TPU v7x, 256 devices: a whole 4x4x8 slice. The times are simulated.
256 devices in a mesh: ctx: 32 (over z, y), fsdp: 4 (over x_lo, core), tp: 2 (over x_hi).
Axes of the slice: x: 4 (x_hi: 2, x_lo: 2; x = x_hi * 2 + x_lo), y: 4, z: 8, core: 2. Of those that a mesh axis runs over, the one named last changes fastest.
Arguments:
- features: bfloat16 [4608, 3, 4096], P('ctx', None, ('fsdp', 'tp')), may hold values from -6 to 6
- short_filter: float32 [3, 7, 256], replicated, may hold values from -2 to 2
- long_filter_taps: float32 [128, 256], replicated, may hold values from -0.5 to 0.5
- queries: bfloat16 [4608, 4096], P('ctx', ('fsdp', 'tp')), may hold values from -4.5 to 4.5
- key_vectors: bfloat16 [4608, 4096], P('ctx', ('fsdp', 'tp')), may hold values from -4.5 to 4.5
- value_vectors: bfloat16 [4608, 4096], P('ctx', ('fsdp', 'tp')), may hold values from -6 to 6
- grad_mixed: bfloat16 [4608, 4096], P('ctx', ('fsdp', 'tp')), may hold values from -6 to 6
- grad_attended: bfloat16 [4608, 4096], P('ctx', ('fsdp', 'tp')), may hold values from -6 to 6
Outputs:
- mixed_tokens: bfloat16 [4608, 4096], P('ctx', ('fsdp', 'tp'))
- attended: bfloat16 [4608, 4096], P('ctx', ('fsdp', 'tp'))
- grad_features: float32 [4608, 3, 4096], P('ctx', None, ('fsdp', 'tp'))
- grad_short: float32 [3, 7, 256], replicated
- grad_long: float32 [128, 256], replicated
- grad_queries: float32 [4608, 4096], P('ctx', ('fsdp', 'tp'))
- grad_key_vectors: float32 [4608, 4096], P('ctx', ('fsdp', 'tp'))
- grad_value_vectors: float32 [4608, 4096], P('ctx', ('fsdp', 'tp'))
All inputs are finite; a program needn't handle non-finite values.
Results may differ from a plain program's by a relative error of at most 0.01.
Values may be sent and summed in bfloat16 or wider, within the bound.
No kernel may reach another device: no remote copies, remote signals or barrier semaphores. Data moves between devices by JAX's collectives and lax.ppermute only.
A program may use at most 128 MiB of HBM per device.

v0:
```python
import jax
import jax.numpy as jnp
from jax import lax
from jax.sharding import PartitionSpec as P

HD = 128


def from_behind(value, axis, steps):
    count = lax.axis_size(axis)
    leading, last = (max(0, -steps), min(count, count - steps))
    return lax.ppermute(value, axis, [(source, source + steps) for source in range(leading, last)])


def from_behind_2(value, axis, by):
    peers = lax.axis_size(axis)
    return lax.ppermute(value, axis, [(i, (i + by) % peers) for i in range(peers)])


def tile_filter(filters, width_cols):
    return jnp.tile(filters, (1, width_cols // filters.shape[1]))


def conv_apply(padded, kernel, row_total, turn_taps):
    length = kernel.shape[0]

    def advance(turn_index, summed):
        for offset_tap in range(turn_taps):
            tap_index = turn_index * turn_taps + offset_tap
            window = lax.dynamic_slice_in_dim(padded, length - 1 - tap_index, row_total, 0)
            summed = summed + lax.dynamic_index_in_dim(kernel, tap_index, 0, False) * window
        return summed

    return lax.fori_loop(
        0, length // turn_taps, advance, jnp.zeros((row_total, padded.shape[1]), jnp.float32)
    )


def conv_adjoint(grad_out, kernel, turn_taps):
    length = kernel.shape[0]
    border = jnp.zeros((length - 1, grad_out.shape[1]), jnp.float32)
    extended = jnp.concatenate([border, grad_out, border], 0)
    out_rows = grad_out.shape[0] + length - 1

    def advance(turn_index, summed):
        for offset_tap in range(turn_taps):
            tap_index = turn_index * turn_taps + offset_tap
            window = lax.dynamic_slice_in_dim(extended, tap_index, out_rows, 0)
            summed = summed + lax.dynamic_index_in_dim(kernel, tap_index, 0, False) * window
        return summed

    return lax.fori_loop(
        0, length // turn_taps, advance, jnp.zeros((out_rows, grad_out.shape[1]), jnp.float32)
    )


def kernel_adjoint(grad_out, padded, filter_count, turn_taps):
    row_total = grad_out.shape[0]
    length = padded.shape[0] - row_total + 1

    def advance(turn_index, result):
        for offset_tap in range(turn_taps):
            tap_index = turn_index * turn_taps + offset_tap
            window = lax.dynamic_slice_in_dim(padded, length - 1 - tap_index, row_total, 0)
            column = jnp.sum(grad_out * window, axis=0)
            folded = jnp.sum(column.reshape(-1, filter_count), axis=0)
            result = lax.dynamic_update_index_in_dim(result, folded, tap_index, 0)
        return result

    return lax.fori_loop(
        0, length // turn_taps, advance, jnp.zeros((length, filter_count), jnp.float32)
    )


def block_rows(piece_rows, shard_rows):
    shards = piece_rows // shard_rows
    wanted = max(1, -(-512 // shard_rows))
    chosen = 1
    for candidate_value in range(1, min(shards, wanted) + 1):
        if shards % candidate_value == 0:
            chosen = candidate_value
    return chosen * shard_rows


def across_blocks(visitor, running, sections, shard_rows):
    piece_rows = sections[0].shape[0]
    span_rows = block_rows(piece_rows, shard_rows)

    def advance(turn_index, current_value):
        offset = turn_index * span_rows
        window = tuple((lax.dynamic_slice_in_dim(x, offset, span_rows, 0) for x in sections))
        return visitor(current_value, window, offset)

    return lax.fori_loop(0, piece_rows // span_rows, advance, running)


def halves_of(x, shard_rows):
    rows = x.shape[0]
    parts = x.reshape((rows // shard_rows, 2, shard_rows // 2) + x.shape[1:])
    return [parts[:, g].reshape((rows // 2,) + x.shape[1:]) for g in range(2)]


def hyena_block(features, short_filter, long_filter_taps, grad_mixed):
    row_count = features.shape[0]
    channels = features.shape[2]
    short_taps = short_filter.shape[1]
    long_taps = long_filter_taps.shape[0]
    filter_count = long_filter_taps.shape[1]
    rim_rows = long_taps + short_taps - 2
    previous = from_behind(features[row_count - rim_rows :], "ctx", 1)
    joined = jnp.concatenate([previous, features], 0).astype(jnp.float32)
    joined_rows = joined.shape[0]
    leading = jnp.zeros((short_taps - 1, channels), jnp.float32)
    short_tiles = [tile_filter(short_filter[g], channels) for g in range(3)]
    padded_in = [jnp.concatenate([leading, joined[:, g]], 0) for g in range(3)]
    featured = [conv_apply(padded_in[g], short_tiles[g], joined_rows, short_taps) for g in range(3)]
    product = featured[0] * featured[2]
    long_tile = tile_filter(long_filter_taps, channels)
    history = product[short_taps - 1 :]
    memory = conv_apply(history, long_tile, row_count, 8)
    gating = featured[1][rim_rows:]
    mixed_tokens = (gating * memory).astype(jnp.bfloat16)
    upstream = grad_mixed.astype(jnp.float32)
    grad_memory = upstream * gating
    grad_gate = upstream * memory
    grad_history = conv_adjoint(grad_memory, long_tile, 8)
    grad_long = kernel_adjoint(grad_memory, history, filter_count, 8)
    grad_product = jnp.concatenate(
        [jnp.zeros((short_taps - 1, channels), jnp.float32), grad_history], 0
    )
    grad_feat = [
        grad_product * featured[2],
        jnp.concatenate([jnp.zeros((rim_rows, channels), jnp.float32), grad_gate], 0),
        grad_product * featured[0],
    ]
    grad_inputs = [
        conv_adjoint(grad_feat[g], short_tiles[g], short_taps)[short_taps - 1 :] for g in range(3)
    ]
    grad_short = jnp.stack(
        [kernel_adjoint(grad_feat[g], padded_in[g], filter_count, short_taps) for g in range(3)], 0
    )
    grad_joined = jnp.stack(grad_inputs, 1)
    incoming = from_behind(grad_joined[:rim_rows].astype(jnp.bfloat16), "ctx", -1).astype(
        jnp.float32
    )
    own_rows = grad_joined[rim_rows:]
    grad_features = jnp.concatenate(
        [own_rows[: row_count - rim_rows], own_rows[row_count - rim_rows :] + incoming], 0
    )
    return (mixed_tokens, grad_features, grad_short, grad_long)


def attention_block(queries, key_vectors, value_vectors, grad_attended):
    row_count, lane_count = queries.shape
    head_count = lane_count // HD
    score_scale = HD ** (-0.5)
    axis_size = lax.axis_size("ctx")
    device_index = lax.axis_index("ctx")

    def positions_of(first_row, count):
        return first_row + jnp.arange(count, dtype=jnp.int32)

    local_rows = positions_of(device_index * row_count, row_count)
    query_heads = queries.reshape(row_count, head_count, HD)
    key_heads = key_vectors.reshape(row_count, head_count, HD)
    value_heads = value_vectors.reshape(row_count, head_count, HD)
    grad_heads = grad_attended.reshape(row_count, head_count, HD)
    local_query = halves_of(query_heads, row_count)
    local_key = halves_of(key_heads, row_count)
    local_value = halves_of(value_heads, row_count)
    local_spots = halves_of(local_rows, row_count)
    group_rows = local_query[0].shape[0]

    def masked_scores(query_part, key_part, query_rows, key_rows):
        scores = (
            jnp.einsum("qhd,khd->hqk", query_part, key_part, preferred_element_type=jnp.float32)
            * score_scale
        )
        return jnp.where((query_rows[:, None] >= key_rows[None, :])[None], scores, -jnp.inf)

    def stat_update(state, query_part, query_rows, key_part, key_rows):
        row_max, row_sum = state
        scores = masked_scores(query_part, key_part, query_rows, key_rows)
        new_max = jnp.maximum(row_max, jnp.max(scores, axis=-1, keepdims=True))
        anchor = jnp.where(new_max == -jnp.inf, 0.0, new_max)
        row_sum = row_sum * jnp.exp(row_max - anchor) + jnp.sum(
            jnp.exp(scores - anchor), axis=-1, keepdims=True
        )
        return (new_max, row_sum)

    def stats_block(running, sections, first_row):
        key_part = sections[0]
        piece_rows = key_part.shape[0]
        key_groups = halves_of(key_part.reshape(piece_rows, head_count, HD), row_count)
        spot_groups = halves_of(positions_of(first_row, piece_rows), row_count)
        updated = []
        for qg in range(len(local_query)):
            state = running[qg]
            for kg in range(len(key_groups)):
                needed = jnp.min(spot_groups[kg]) <= jnp.max(local_spots[qg])
                state = lax.cond(
                    needed,
                    lambda s, qg=qg, kg=kg: stat_update(
                        s, local_query[qg], local_spots[qg], key_groups[kg], spot_groups[kg]
                    ),
                    lambda s: s,
                    state,
                )
            updated.append(state)
        return tuple(updated)

    start_stats = tuple(
        (
            (
                jnp.full((head_count, group_rows, 1), -jnp.inf, jnp.float32),
                jnp.zeros((head_count, group_rows, 1), jnp.float32),
            )
            for g in range(len(local_query))
        )
    )

    def output_maker(log_groups):

        def output_block(running, sections, first_row):
            key_part, value_part = sections
            piece_rows = key_part.shape[0]
            key_groups = halves_of(key_part.reshape(piece_rows, head_count, HD), row_count)
            value_groups = halves_of(value_part.reshape(piece_rows, head_count, HD), row_count)
            spot_groups = halves_of(positions_of(first_row, piece_rows), row_count)
            updated = list(running)
            for qg in range(len(local_query)):
                for kg in range(len(key_groups)):
                    needed = jnp.min(spot_groups[kg]) <= jnp.max(local_spots[qg])

                    def output_accumulate(total, qg=qg, kg=kg):
                        scores = masked_scores(
                            local_query[qg], key_groups[kg], local_spots[qg], spot_groups[kg]
                        )
                        weights_low = jnp.exp(scores - log_groups[qg]).astype(jnp.bfloat16)
                        return total + jnp.einsum(
                            "hqk,khd->hqd",
                            weights_low,
                            value_groups[kg],
                            preferred_element_type=jnp.float32,
                        )

                    updated[qg] = lax.cond(needed, output_accumulate, lambda t: t, updated[qg])
            return tuple(updated)

        return output_block

    start_output = tuple(
        (jnp.zeros((head_count, group_rows, HD), jnp.float32) for g in range(len(local_query)))
    )
    finished_stats = across_blocks(
        stats_block,
        start_stats,
        (lax.all_gather(key_vectors, "ctx", axis=0, tiled=True),),
        row_count,
    )
    log_groups = [state[0] + jnp.log(state[1]) for state in finished_stats]
    finished_out = across_blocks(
        output_maker(log_groups),
        start_output,
        (
            lax.all_gather(key_vectors, "ctx", axis=0, tiled=True),
            lax.all_gather(value_vectors, "ctx", axis=0, tiled=True),
        ),
        row_count,
    )
    log_total = jnp.concatenate(log_groups, 1)
    attended_heads = jnp.concatenate(list(finished_out), 1).astype(jnp.bfloat16)
    attended = attended_heads.transpose(1, 0, 2).reshape(row_count, lane_count)
    kept_output = lax.optimization_barrier(attended).reshape(row_count, head_count, HD)
    row_delta = jnp.sum(grad_heads.astype(jnp.float32) * kept_output.astype(jnp.float32), axis=-1)
    log_rows = log_total[:, :, 0].T

    def pair_grads(
        query_part, grad_part, log_part, delta_part, query_rows, key_part, value_part, key_rows
    ):
        scores = masked_scores(query_part, key_part, query_rows, key_rows)
        weights = jnp.exp(scores - log_part)
        grad_weights = jnp.einsum(
            "qhd,khd->hqk", grad_part, value_part, preferred_element_type=jnp.float32
        )
        grad_scores = (weights * (grad_weights - delta_part)).astype(jnp.bfloat16)
        grad_query = score_scale * jnp.einsum(
            "hqk,khd->qhd", grad_scores, key_part, preferred_element_type=jnp.float32
        )
        grad_key = score_scale * jnp.einsum(
            "hqk,qhd->khd", grad_scores, query_part, preferred_element_type=jnp.float32
        )
        grad_value = jnp.einsum(
            "hqk,qhd->khd",
            weights.astype(jnp.bfloat16),
            grad_part,
            preferred_element_type=jnp.float32,
        )
        return (grad_query, grad_key, grad_value)

    def stat_heads(rows_by_head):
        return rows_by_head.T[:, :, None]

    def visit_block(turn_index, running):
        query_part, grad_part, grad_query, visiting_log, visiting_delta, grad_key, grad_value = (
            running
        )
        root = (device_index - turn_index) % axis_size
        query_rows = positions_of(root * row_count, row_count)
        query_groups = halves_of(query_part.reshape(row_count, head_count, HD), row_count)
        grad_groups = halves_of(grad_part.reshape(row_count, head_count, HD), row_count)
        log_parts = halves_of(visiting_log, row_count)
        delta_parts = halves_of(visiting_delta, row_count)
        spot_groups = halves_of(query_rows, row_count)
        query_sums = halves_of(grad_query.reshape(row_count, head_count, HD), row_count)
        key_sums = halves_of(grad_key, row_count)
        value_sums = halves_of(grad_value, row_count)
        for qa in range(len(query_groups)):
            for kb in range(len(local_key)):
                needed = jnp.min(local_spots[kb]) <= jnp.max(spot_groups[qa])

                def visit_accumulate(totals, qa=qa, kb=kb):
                    adds = pair_grads(
                        query_groups[qa],
                        grad_groups[qa],
                        stat_heads(log_parts[qa]),
                        stat_heads(delta_parts[qa]),
                        spot_groups[qa],
                        local_key[kb],
                        local_value[kb],
                        local_spots[kb],
                    )
                    return tuple((a + b for a, b in zip(totals, adds)))

                query_sums[qa], key_sums[kb], value_sums[kb] = lax.cond(
                    needed,
                    visit_accumulate,
                    lambda t: t,
                    (query_sums[qa], key_sums[kb], value_sums[kb]),
                )
        grad_query = jnp.concatenate(query_sums, 0).reshape(row_count, lane_count)
        grad_key = jnp.concatenate(key_sums, 0)
        grad_value = jnp.concatenate(value_sums, 0)
        query_part, grad_part = from_behind_2((query_part, grad_part), "ctx", 1)
        grad_query, visiting_log, visiting_delta = from_behind_2(
            (grad_query, visiting_log, visiting_delta), "ctx", 1
        )
        return (
            query_part,
            grad_part,
            grad_query,
            visiting_log,
            visiting_delta,
            grad_key,
            grad_value,
        )

    begin_state = (
        queries,
        grad_attended,
        jnp.zeros((row_count, lane_count), jnp.float32),
        log_rows,
        row_delta,
        jnp.zeros((row_count, head_count, HD), jnp.float32),
        jnp.zeros((row_count, head_count, HD), jnp.float32),
    )
    finished_rows = lax.fori_loop(0, axis_size, visit_block, begin_state)
    grad_queries = finished_rows[2]
    grad_key_vectors = finished_rows[5].reshape(row_count, lane_count)
    grad_value_vectors = finished_rows[6].reshape(row_count, lane_count)
    return (attended, grad_queries, grad_key_vectors, grad_value_vectors)


def body(
    features,
    short_filter,
    long_filter_taps,
    queries,
    key_vectors,
    value_vectors,
    grad_mixed,
    grad_attended,
):
    mixed_tokens, grad_features, grad_short, grad_long = hyena_block(
        features, short_filter, long_filter_taps, grad_mixed
    )
    attended, grad_queries, grad_key_vectors, grad_value_vectors = attention_block(
        queries, key_vectors, value_vectors, grad_attended
    )
    grad_short, grad_long = lax.psum((grad_short, grad_long), ("ctx", "fsdp", "tp"))
    return (
        mixed_tokens,
        attended,
        grad_features,
        grad_short,
        grad_long,
        grad_queries,
        grad_key_vectors,
        grad_value_vectors,
    )


def solution(mesh):
    in_specs = (
        P("ctx", None, ("fsdp", "tp")),
        P(),
        P(),
        P("ctx", ("fsdp", "tp")),
        P("ctx", ("fsdp", "tp")),
        P("ctx", ("fsdp", "tp")),
        P("ctx", ("fsdp", "tp")),
        P("ctx", ("fsdp", "tp")),
    )
    out_specs = (
        P("ctx", ("fsdp", "tp")),
        P("ctx", ("fsdp", "tp")),
        P("ctx", None, ("fsdp", "tp")),
        P(),
        P(),
        P("ctx", ("fsdp", "tp")),
        P("ctx", ("fsdp", "tp")),
        P("ctx", ("fsdp", "tp")),
    )
    return jax.shard_map(body, mesh=mesh, in_specs=in_specs, out_specs=out_specs, check_vma=False)
```

profile of v0, /device:TPU:2, one launch (start us, length us, event | category | flops | bytes accessed | tf_op | source)
XLA Modules:
  0.0 1294.4 jit_solution(4932520840999401755)
XLA Ops:
  39.4 29.3 %while.85 = (s32[]{:T(128)}, f32[271,512]{1,0:T(8,128)S(1)}, f32[128,512]{1,0:T(8,128)}, f32[398,512]{1,0:T(8,128)S(1)}, s32[]{:T(128)}, /*index=5*/s32[]{:T(128...) while((s32[]{:T(128)}, f32[271,512]{1,0:T(8,128)S(1)}, ...), condition=%wide.region_37.38_spmd.clone, body=%wide.region_36.37_spmd.clone.sunk | while | flops 2358835 | bytes 5600135 | solution.py:52
  83.5 18.8 %while.82 = (s32[]{:T(128)}, f32[128,256]{1,0:T(8,128)S(1)}, f32[271,512]{1,0:T(8,128)S(1)}, f32[144,512]{1,0:T(8,128)S(1)}, s32[]{:T(128)}, /*index=5*/s32[]{:T...) while((s32[]{:T(128)}, f32[128,256]{1,0:T(8,128)S(1)}, ...), condition=%wide.region_98.99_spmd, body=%wide.region_81.98_spmd.sunk | while | flops 1177666 | bytes 2745365 | solution.py:70
  105.0 83.0 %psum.14 = f32[3,7,256]{2,1,0:T(8,128)} all-reduce(f32[3,7,256]{2,1,0:T(8,128)S(1)} %pad_maximum_fusion.13), channel_id=1, replica_groups=mesh['ctx'=32,'fsdp'=4,'tp'=2] {'ctx','fsdp','tp'}, use_global_device_ids=true, to_apply=%region_80.81 | all-reduce | flops 5376 | bytes 43008 | tf_op jit(solution)/shard_map/psum | solution.py:390
  191.1 63.9 %while.80 = (s32[]{:T(128)}, f32[4,72,1]{1,0,2:T(4,128)S(1)}, f32[4,72,1]{1,0,2:T(4,128)S(1)}, f32[4,72,1]{1,0,2:T(4,128)S(1)}, f32[4,72,1]{1,0,2:T(4,128)S(1)},...) while((s32[]{:T(128)}, f32[4,72,1]{1,0,2:T(4,128)S(1)}, ...), condition=%wide.region_23.24_spmd, body=%wide.region_4.23_spmd.sunk | while | flops 86686856 | bytes 7929851 | solution.py:94
  255.1 67.7 %while.81 = (s32[]{:T(128)}, f32[4,72,128]{2,1,0:T(8,128)S(1)}, f32[4,72,128]{2,1,0:T(8,128)S(1)}, s32[]{:T(128)}, bf16[4608,512]{1,0:T(8,128)(2,1)}, /*index=5*...) while((s32[]{:T(128)}, f32[4,72,128]{2,1,0:T(8,128)S(1)}, ...), condition=%wide.region_35.36_spmd, body=%wide.region_24.35_spmd.sunk | while | flops 171430272 | bytes 11113923 | solution.py:94
  323.8 959.3 %while.83 = (s32[]{:T(128)}, bf16[144,512]{1,0:T(8,128)(2,1)S(1)}, bf16[144,512]{1,0:T(8,128)(2,1)S(1)}, f32[144,512]{1,0:T(8,128)S(1)}, f32[144,4]{0,1:T(4,128)...) while((s32[]{:T(128)}, bf16[144,512]{1,0:T(8,128)(2,1)S(1)}, ...), condition=%wide.region_114.115_spmd, body=%wide.region_103.114_spmd.sunk | while | flops 107728720 | bytes 15455814 | solution.py:367
  342.1 12.1 collective-permute-start
  358.6 100.2 %collective-permute-done.3 = f32[144,4]{0,1:T(4,128)S(1)} collective-permute-done((f32[144,4]{0,1:T(4,128)S(1)}, f32[144,4]{0,1:T(4,128)S(1)}, u32[]{:S(2)}, u32[]{:S(2)}) %collective-permute-start.3) | collective-permute-done | bytes 2336 | tf_op jit(solution)/shard_map/while/body/eval_jaxpr/ppermute | solution.py:17
  475.6 12.9 collective-permute-done.3
  504.4 12.8 collective-permute-done.3
  532.3 11.8 collective-permute-done.3
  559.2 10.9 collective-permute-done.3
  585.2 10.0 collective-permute-done.3
  610.3 9.6 collective-permute-done.3
  635.1 9.6 collective-permute-done.3
  659.8 9.6 collective-permute-done.3
  684.6 9.6 collective-permute-done.3
  709.3 9.6 collective-permute-done.3
  734.1 9.6 collective-permute-done.3
  758.8 9.6 collective-permute-done.3
  783.6 9.6 collective-permute-done.3
  808.3 9.6 collective-permute-done.3
  910.9 9.8 collective-permute-done.3
  939.1 10.9 collective-permute-done.3
  968.3 12.1 collective-permute-done.3
  998.7 12.8 collective-permute-done.3
  1029.5 12.9 collective-permute-done.3
  1059.5 12.9 collective-permute-done.3
  1088.6 12.9 collective-permute-done.3
  1116.9 12.2 collective-permute-done.3
  1144.2 11.3 collective-permute-done.3
  1170.6 10.4 collective-permute-done.3
  (2753 shorter events, 718.9 us)
Async XLA Ops:
  8.0 183.0 %all-gather.3.cloned.1.call-start = ((), (), s32[]{:S(2)}) async-start(), calls=%async_computation | async-start | bytes 4866048 | tf_op jit(solution)/shard_map/all_gather | solution.py:266
  10.7 244.4 %all-gather.5.cloned.1.call-start = ((), (), s32[]{:S(2)}) async-start(), calls=%async_computation.1 | async-start | bytes 4866048 | tf_op jit(solution)/shard_map/all_gather | solution.py:267
  15.5 1269.1 %all-reduce.14.cloned.1.call-start = ((), (), s32[]{:S(2)}) async-start(), calls=%async_computation.2 | async-start | bytes 262144 | tf_op jit(solution)/shard_map/psum | solution.py:390
  82.0 106.7 %collective-permute-start.6 = (bf16[133,3,512]{2,0,1:T(8,128)(2,1)S(1)}, bf16[133,3,512]{2,0,1:T(8,128)(2,1)S(1)}, u32[]{:S(2)}, u32[]{:S(2)}) collective-permute-start(bf16[133,3,512]{2,0,1:T(8,128)(2,1)S(1)} %slice.693), channel_id=1, source_target_pairs={{8,0},{16,8},{24,16},{32,24},{40,32},{48,40},{56,48},{64,56},{72,6... | collective-permute-start | bytes 1225736 | tf_op jit(solution)/shard_map/ppermute | solution.py:12
  334.2 129.6 %collective-permute-start.2 = (f32[144,512]{1,0:T(8,128)S(1)}, f32[144,512]{1,0:T(8,128)S(1)}, u32[]{:S(2)}, u32[]{:S(2)}) collective-permute-start(f32[144,512]{1,0:T(8,128)S(1)} %copy_bitcast_fusion.5), channel_id=1, source_target_pairs={{0,8},{8,16},{16,24},{24,32},{32,40},{40,48},{48,56},{56,64},{64,7... | collective-permute-start | bytes 884744 | tf_op jit(solution)/shard_map/while/body/eval_jaxpr/ppermute | solution.py:17
  338.7 120.2 %collective-permute-start.3 = (f32[144,4]{0,1:T(4,128)S(1)}, f32[144,4]{0,1:T(4,128)S(1)}, u32[]{:S(2)}, u32[]{:S(2)}) collective-permute-start(f32[144,4]{0,1:T(4,128)S(1)} %copy.438), channel_id=1, source_target_pairs={{0,8},{8,16},{16,24},{24,32},{32,40},{40,48},{48,56},{56,64},{64,7... | collective-permute-start | bytes 6920 | tf_op jit(solution)/shard_map/while/body/eval_jaxpr/ppermute | solution.py:17
  340.1 118.9 %collective-permute-start.4 = (f32[144,4]{0,1:T(4,128)S(1)}, f32[144,4]{0,1:T(4,128)S(1)}, u32[]{:S(2)}, u32[]{:S(2)}) collective-permute-start(f32[144,4]{0,1:T(4,128)S(1)} %copy.439), channel_id=1, source_target_pairs={{0,8},{8,16},{16,24},{24,32},{32,40},{40,48},{48,56},{56,64},{64,7... | collective-permute-start | bytes 6920 | tf_op jit(solution)/shard_map/while/body/eval_jaxpr/ppermute | solution.py:17
  342.1 120.0 %collective-permute-start = (bf16[144,512]{1,0:T(8,128)(2,1)S(1)}, bf16[144,512]{1,0:T(8,128)(2,1)S(1)}, u32[]{:S(2)}, u32[]{:S(2)}) collective-permute-start(bf16[144,512]{1,0:T(8,128)(2,1)S(1)} %copy.435), channel_id=1, source_target_pairs={{0,8},{8,16},{16,24},{24,32},{32,40},{40,48},{48,56},{56,64},{64,7... | collective-permute-start | bytes 442376 | tf_op jit(solution)/shard_map/while/body/eval_jaxpr/ppermute | solution.py:17
  354.2 109.6 %collective-permute-start.1 = (bf16[144,512]{1,0:T(8,128)(2,1)S(1)}, bf16[144,512]{1,0:T(8,128)(2,1)S(1)}, u32[]{:S(2)}, u32[]{:S(2)}) collective-permute-start(bf16[144,512]{1,0:T(8,128)(2,1)S(1)} %copy.436), channel_id=1, source_target_pairs={{0,8},{8,16},{16,24},{24,32},{32,40},{40,48},{48,56},{56,64},{64,7... | collective-permute-start | bytes 442376 | tf_op jit(solution)/shard_map/while/body/eval_jaxpr/ppermute | solution.py:17
  475.1 17.4 %collective-permute-start.2 = (f32[144,512]{1,0:T(8,128)S(1)}, f32[144,512]{1,0:T(8,128)S(1)}, u32[]{:S(2)}, u32[]{:S(2)}) collective-permute-start(f32[144,512]{1,0:T(8,128)S(1)} %copy_bitcast_fusion.5), channel_id=1, source_target_pairs={{0,8},{8,16},{16,24},{24,32},{32,40},{40,48},{48,56},{56,64},{64,7... | collective-permute-start | bytes 884744 | tf_op jit(solution)/shard_map/while/body/eval_jaxpr/ppermute | solution.py:17
  475.5 17.0 %collective-permute-start.1 = (bf16[144,512]{1,0:T(8,128)(2,1)S(1)}, bf16[144,512]{1,0:T(8,128)(2,1)S(1)}, u32[]{:S(2)}, u32[]{:S(2)}) collective-permute-start(bf16[144,512]{1,0:T(8,128)(2,1)S(1)} %copy.436), channel_id=1, source_target_pairs={{0,8},{8,16},{16,24},{24,32},{32,40},{40,48},{48,56},{56,64},{64,7... | collective-permute-start | bytes 442376 | tf_op jit(solution)/shard_map/while/body/eval_jaxpr/ppermute | solution.py:17
  503.9 16.5 %collective-permute-start.2 = (f32[144,512]{1,0:T(8,128)S(1)}, f32[144,512]{1,0:T(8,128)S(1)}, u32[]{:S(2)}, u32[]{:S(2)}) collective-permute-start(f32[144,512]{1,0:T(8,128)S(1)} %copy_bitcast_fusion.5), channel_id=1, source_target_pairs={{0,8},{8,16},{16,24},{24,32},{32,40},{40,48},{48,56},{56,64},{64,7... | collective-permute-start | bytes 884744 | tf_op jit(solution)/shard_map/while/body/eval_jaxpr/ppermute | solution.py:17
  504.3 16.1 %collective-permute-start.1 = (bf16[144,512]{1,0:T(8,128)(2,1)S(1)}, bf16[144,512]{1,0:T(8,128)(2,1)S(1)}, u32[]{:S(2)}, u32[]{:S(2)}) collective-permute-start(bf16[144,512]{1,0:T(8,128)(2,1)S(1)} %copy.436), channel_id=1, source_target_pairs={{0,8},{8,16},{16,24},{24,32},{32,40},{40,48},{48,56},{56,64},{64,7... | collective-permute-start | bytes 442376 | tf_op jit(solution)/shard_map/while/body/eval_jaxpr/ppermute | solution.py:17
  883.4 15.7 %collective-permute-start.2 = (f32[144,512]{1,0:T(8,128)S(1)}, f32[144,512]{1,0:T(8,128)S(1)}, u32[]{:S(2)}, u32[]{:S(2)}) collective-permute-start(f32[144,512]{1,0:T(8,128)S(1)} %copy_bitcast_fusion.5), channel_id=1, source_target_pairs={{0,8},{8,16},{16,24},{24,32},{32,40},{40,48},{48,56},{56,64},{64,7... | collective-permute-start | bytes 884744 | tf_op jit(solution)/shard_map/while/body/eval_jaxpr/ppermute | solution.py:17
  910.4 16.7 %collective-permute-start.2 = (f32[144,512]{1,0:T(8,128)S(1)}, f32[144,512]{1,0:T(8,128)S(1)}, u32[]{:S(2)}, u32[]{:S(2)}) collective-permute-start(f32[144,512]{1,0:T(8,128)S(1)} %copy_bitcast_fusion.5), channel_id=1, source_target_pairs={{0,8},{8,16},{16,24},{24,32},{32,40},{40,48},{48,56},{56,64},{64,7... | collective-permute-start | bytes 884744 | tf_op jit(solution)/shard_map/while/body/eval_jaxpr/ppermute | solution.py:17
  910.8 16.4 %collective-permute-start.1 = (bf16[144,512]{1,0:T(8,128)(2,1)S(1)}, bf16[144,512]{1,0:T(8,128)(2,1)S(1)}, u32[]{:S(2)}, u32[]{:S(2)}) collective-permute-start(bf16[144,512]{1,0:T(8,128)(2,1)S(1)} %copy.436), channel_id=1, source_target_pairs={{0,8},{8,16},{16,24},{24,32},{32,40},{40,48},{48,56},{56,64},{64,7... | collective-permute-start | bytes 442376 | tf_op jit(solution)/shard_map/while/body/eval_jaxpr/ppermute | solution.py:17
  938.5 17.8 %collective-permute-start.2 = (f32[144,512]{1,0:T(8,128)S(1)}, f32[144,512]{1,0:T(8,128)S(1)}, u32[]{:S(2)}, u32[]{:S(2)}) collective-permute-start(f32[144,512]{1,0:T(8,128)S(1)} %copy_bitcast_fusion.5), channel_id=1, source_target_pairs={{0,8},{8,16},{16,24},{24,32},{32,40},{40,48},{48,56},{56,64},{64,7... | collective-permute-start | bytes 884744 | tf_op jit(solution)/shard_map/while/body/eval_jaxpr/ppermute | solution.py:17
  938.9 17.5 %collective-permute-start.1 = (bf16[144,512]{1,0:T(8,128)(2,1)S(1)}, bf16[144,512]{1,0:T(8,128)(2,1)S(1)}, u32[]{:S(2)}, u32[]{:S(2)}) collective-permute-start(bf16[144,512]{1,0:T(8,128)(2,1)S(1)} %copy.436), channel_id=1, source_target_pairs={{0,8},{8,16},{16,24},{24,32},{32,40},{40,48},{48,56},{56,64},{64,7... | collective-permute-start | bytes 442376 | tf_op jit(solution)/shard_map/while/body/eval_jaxpr/ppermute | solution.py:17
  967.7 19.0 %collective-permute-start.2 = (f32[144,512]{1,0:T(8,128)S(1)}, f32[144,512]{1,0:T(8,128)S(1)}, u32[]{:S(2)}, u32[]{:S(2)}) collective-permute-start(f32[144,512]{1,0:T(8,128)S(1)} %copy_bitcast_fusion.5), channel_id=1, source_target_pairs={{0,8},{8,16},{16,24},{24,32},{32,40},{40,48},{48,56},{56,64},{64,7... | collective-permute-start | bytes 884744 | tf_op jit(solution)/shard_map/while/body/eval_jaxpr/ppermute | solution.py:17
  968.1 18.6 %collective-permute-start.1 = (bf16[144,512]{1,0:T(8,128)(2,1)S(1)}, bf16[144,512]{1,0:T(8,128)(2,1)S(1)}, u32[]{:S(2)}, u32[]{:S(2)}) collective-permute-start(bf16[144,512]{1,0:T(8,128)(2,1)S(1)} %copy.436), channel_id=1, source_target_pairs={{0,8},{8,16},{16,24},{24,32},{32,40},{40,48},{48,56},{56,64},{64,7... | collective-permute-start | bytes 442376 | tf_op jit(solution)/shard_map/while/body/eval_jaxpr/ppermute | solution.py:17
  998.1 19.4 %collective-permute-start.2 = (f32[144,512]{1,0:T(8,128)S(1)}, f32[144,512]{1,0:T(8,128)S(1)}, u32[]{:S(2)}, u32[]{:S(2)}) collective-permute-start(f32[144,512]{1,0:T(8,128)S(1)} %copy_bitcast_fusion.5), channel_id=1, source_target_pairs={{0,8},{8,16},{16,24},{24,32},{32,40},{40,48},{48,56},{56,64},{64,7... | collective-permute-start | bytes 884744 | tf_op jit(solution)/shard_map/while/body/eval_jaxpr/ppermute | solution.py:17
  998.4 16.2 %collective-permute-start = (bf16[144,512]{1,0:T(8,128)(2,1)S(1)}, bf16[144,512]{1,0:T(8,128)(2,1)S(1)}, u32[]{:S(2)}, u32[]{:S(2)}) collective-permute-start(bf16[144,512]{1,0:T(8,128)(2,1)S(1)} %copy.435), channel_id=1, source_target_pairs={{0,8},{8,16},{16,24},{24,32},{32,40},{40,48},{48,56},{56,64},{64,7... | collective-permute-start | bytes 442376 | tf_op jit(solution)/shard_map/while/body/eval_jaxpr/ppermute | solution.py:17
  998.5 19.1 %collective-permute-start.1 = (bf16[144,512]{1,0:T(8,128)(2,1)S(1)}, bf16[144,512]{1,0:T(8,128)(2,1)S(1)}, u32[]{:S(2)}, u32[]{:S(2)}) collective-permute-start(bf16[144,512]{1,0:T(8,128)(2,1)S(1)} %copy.436), channel_id=1, source_target_pairs={{0,8},{8,16},{16,24},{24,32},{32,40},{40,48},{48,56},{56,64},{64,7... | collective-permute-start | bytes 442376 | tf_op jit(solution)/shard_map/while/body/eval_jaxpr/ppermute | solution.py:17
  1028.9 18.7 %collective-permute-start.2 = (f32[144,512]{1,0:T(8,128)S(1)}, f32[144,512]{1,0:T(8,128)S(1)}, u32[]{:S(2)}, u32[]{:S(2)}) collective-permute-start(f32[144,512]{1,0:T(8,128)S(1)} %copy_bitcast_fusion.5), channel_id=1, source_target_pairs={{0,8},{8,16},{16,24},{24,32},{32,40},{40,48},{48,56},{56,64},{64,7... | collective-permute-start | bytes 884744 | tf_op jit(solution)/shard_map/while/body/eval_jaxpr/ppermute | solution.py:17
  1029.2 16.4 %collective-permute-start = (bf16[144,512]{1,0:T(8,128)(2,1)S(1)}, bf16[144,512]{1,0:T(8,128)(2,1)S(1)}, u32[]{:S(2)}, u32[]{:S(2)}) collective-permute-start(bf16[144,512]{1,0:T(8,128)(2,1)S(1)} %copy.435), channel_id=1, source_target_pairs={{0,8},{8,16},{16,24},{24,32},{32,40},{40,48},{48,56},{56,64},{64,7... | collective-permute-start | bytes 442376 | tf_op jit(solution)/shard_map/while/body/eval_jaxpr/ppermute | solution.py:17
  1029.3 18.3 %collective-permute-start.1 = (bf16[144,512]{1,0:T(8,128)(2,1)S(1)}, bf16[144,512]{1,0:T(8,128)(2,1)S(1)}, u32[]{:S(2)}, u32[]{:S(2)}) collective-permute-start(bf16[144,512]{1,0:T(8,128)(2,1)S(1)} %copy.436), channel_id=1, source_target_pairs={{0,8},{8,16},{16,24},{24,32},{32,40},{40,48},{48,56},{56,64},{64,7... | collective-permute-start | bytes 442376 | tf_op jit(solution)/shard_map/while/body/eval_jaxpr/ppermute | solution.py:17
  1059.0 17.8 %collective-permute-start.2 = (f32[144,512]{1,0:T(8,128)S(1)}, f32[144,512]{1,0:T(8,128)S(1)}, u32[]{:S(2)}, u32[]{:S(2)}) collective-permute-start(f32[144,512]{1,0:T(8,128)S(1)} %copy_bitcast_fusion.5), channel_id=1, source_target_pairs={{0,8},{8,16},{16,24},{24,32},{32,40},{40,48},{48,56},{56,64},{64,7... | collective-permute-start | bytes 884744 | tf_op jit(solution)/shard_map/while/body/eval_jaxpr/ppermute | solution.py:17
  1059.2 15.9 %collective-permute-start = (bf16[144,512]{1,0:T(8,128)(2,1)S(1)}, bf16[144,512]{1,0:T(8,128)(2,1)S(1)}, u32[]{:S(2)}, u32[]{:S(2)}) collective-permute-start(bf16[144,512]{1,0:T(8,128)(2,1)S(1)} %copy.435), channel_id=1, source_target_pairs={{0,8},{8,16},{16,24},{24,32},{32,40},{40,48},{48,56},{56,64},{64,7... | collective-permute-start | bytes 442376 | tf_op jit(solution)/shard_map/while/body/eval_jaxpr/ppermute | solution.py:17
  1059.3 17.4 %collective-permute-start.1 = (bf16[144,512]{1,0:T(8,128)(2,1)S(1)}, bf16[144,512]{1,0:T(8,128)(2,1)S(1)}, u32[]{:S(2)}, u32[]{:S(2)}) collective-permute-start(bf16[144,512]{1,0:T(8,128)(2,1)S(1)} %copy.436), channel_id=1, source_target_pairs={{0,8},{8,16},{16,24},{24,32},{32,40},{40,48},{48,56},{56,64},{64,7... | collective-permute-start | bytes 442376 | tf_op jit(solution)/shard_map/while/body/eval_jaxpr/ppermute | solution.py:17
  1088.1 16.9 %collective-permute-start.2 = (f32[144,512]{1,0:T(8,128)S(1)}, f32[144,512]{1,0:T(8,128)S(1)}, u32[]{:S(2)}, u32[]{:S(2)}) collective-permute-start(f32[144,512]{1,0:T(8,128)S(1)} %copy_bitcast_fusion.5), channel_id=1, source_target_pairs={{0,8},{8,16},{16,24},{24,32},{32,40},{40,48},{48,56},{56,64},{64,7... | collective-permute-start | bytes 884744 | tf_op jit(solution)/shard_map/while/body/eval_jaxpr/ppermute | solution.py:17
  1088.5 16.5 %collective-permute-start.1 = (bf16[144,512]{1,0:T(8,128)(2,1)S(1)}, bf16[144,512]{1,0:T(8,128)(2,1)S(1)}, u32[]{:S(2)}, u32[]{:S(2)}) collective-permute-start(bf16[144,512]{1,0:T(8,128)(2,1)S(1)} %copy.436), channel_id=1, source_target_pairs={{0,8},{8,16},{16,24},{24,32},{32,40},{40,48},{48,56},{56,64},{64,7... | collective-permute-start | bytes 442376 | tf_op jit(solution)/shard_map/while/body/eval_jaxpr/ppermute | solution.py:17
  1116.4 15.9 %collective-permute-start.2 = (f32[144,512]{1,0:T(8,128)S(1)}, f32[144,512]{1,0:T(8,128)S(1)}, u32[]{:S(2)}, u32[]{:S(2)}) collective-permute-start(f32[144,512]{1,0:T(8,128)S(1)} %copy_bitcast_fusion.5), channel_id=1, source_target_pairs={{0,8},{8,16},{16,24},{24,32},{32,40},{40,48},{48,56},{56,64},{64,7... | collective-permute-start | bytes 884744 | tf_op jit(solution)/shard_map/while/body/eval_jaxpr/ppermute | solution.py:17
  (167 other events, 2113.6 us)
Sparse Core Ops, SparseCore 0:
  11.4 91.6 all-gather.2
  105.7 77.5 all-gather.4
Sparse Core Ops, SparseCore 1:
  103.9 254.6 all-reduce.13
where the time goes:
time: 1300 us; the launch traced here: 1290 us
  waiting for transfers between devices  560 us (43%)
  loops' own time  270 us (21%)
  matrix products  135 us (10%)
  other arithmetic  94.1 us (7%)
  local copies, waits for them, and re-layouts  92.6 us (7%)
  blocking collectives  83 us (6%)
  starting transfers between devices  42.3 us (3%)
  between operations  16.8 us (1%)
    ppermute x160, waiting for transfers between devices, from_behind_2(): lax.ppermute(value, axis, [(i, (i + by) % peers) for i in range(peers)])  556 us
    another operation x1, loops' own time, attention_block(): finished_rows = lax.fori_loop(0, axis_size, visit_block, begin_state)  176 us
    psum x1, blocking collectives, body(): lax.psum((grad_short, grad_long), ('ctx', 'fsdp', 'tp'))  83 us
    another operation x2, loops' own time, across_blocks(): return lax.fori_loop(0, piece_rows // span_rows, advance, running)  80.5 us
    ppermute x160, starting transfers between devices, from_behind_2(): lax.ppermute(value, axis, [(i, (i + by) % peers) for i in range(peers)])  37.3 us
    dot_general x127, matrix products, pair_grads(): jnp.einsum('hqk,qhd->khd', grad_scores, query_part, preferred_element_typ...  31.4 us
    dot_general x127, matrix products, pair_grads(): jnp.einsum('hqk,qhd->khd', weights.astype(jnp.bfloat16), grad_part, prefe...  31.1 us
  transfers between devices with their start and end apart: 165, of which 106 were waited for; matrix products, arithmetic and copies ran while one was open for 24% of the time, Pallas kernels for 0%

commit v1 on v0

v1 whole, which is shorter than its diff:
```python
import jax
import jax.numpy as jnp
import numpy as np
from jax import lax
from jax.experimental import pallas as pl
from jax.experimental.pallas import tpu as pltpu
from jax.sharding import Mesh, PartitionSpec as P

HD = 128
ROWS = 144
GROUP = 576
SEQ = 4608
CHUNK = 512
CHUNKS = SEQ // CHUNK
LOG2E = 1.4426950408889634
SCALE = HD ** -0.5
VMEM_BYTES = 56 * 1024 * 1024
F32 = jnp.float32
BF16 = jnp.bfloat16
CTX = ("cz", "cy")
FT = ("fsdp", "tp")


def after(value, *others):
    return lax.optimization_barrier((value,) + others)[0]


def call(body, out_shape, name, **options):
    return pl.pallas_call(
        body,
        out_shape=out_shape,
        name=name,
        compiler_params=pltpu.CompilerParams(vmem_limit_bytes=VMEM_BYTES),
        **options,
    )


def struct(shape, dtype):
    return jax.ShapeDtypeStruct(shape, dtype)


def nt(a, b):
    return lax.dot_general(a, b, (((1,), (1,)), ((), ())), preferred_element_type=F32)


def nn(a, b):
    return lax.dot_general(a, b, (((1,), (0,)), ((), ())), preferred_element_type=F32)


def pack_body(a_ref, b_ref, out_ref):
    for h in range(4):
        out_ref[h, :, :HD] = a_ref[:, h * HD : (h + 1) * HD]
        out_ref[h, :, HD:] = b_ref[:, h * HD : (h + 1) * HD]


def pack(a, b):
    return call(pack_body, struct((4, ROWS, 2 * HD), BF16), "pack")(a, b)


def unpack_body(x_ref, a_ref, b_ref):
    for h in range(4):
        a_ref[:, h * HD : (h + 1) * HD] = x_ref[h, :, :HD].astype(a_ref.dtype)
        b_ref[:, h * HD : (h + 1) * HD] = x_ref[h, :, HD:].astype(b_ref.dtype)


def unpack(x, kind_a, kind_b):
    return call(
        unpack_body,
        (struct((ROWS, 4 * HD), kind_a), struct((ROWS, 4 * HD), kind_b)),
        "unpack",
    )(x)


def hyena_body(
    feat_ref, prev_ref, next_ref, up_ref, short_ref, long_ref,
    mixed_ref, gfeat_ref, glong_ref, gshort_ref,
    x_ref, x1_ref, p_ref, ps_ref, gm_ref, gs_ref, f_ref, gf_ref, wb_ref, gl_ref,
):
    turn = pl.program_id(1)
    for slot, g in enumerate((0, 2)):
        x_ref[slot, 0:136] = prev_ref[g].astype(F32)
        x_ref[slot, 136:280] = feat_ref[g].astype(F32)
        x_ref[slot, 280:288] = next_ref[272 + 8 * slot : 280 + 8 * slot].astype(F32)
    x1_ref[0:136] = prev_ref[1].astype(F32)
    x1_ref[136:280] = feat_ref[1].astype(F32)
    x1_ref[280:416] = next_ref[0:136].astype(F32)
    taps = [[short_ref[g, s : s + 1, :] for s in range(7)] for g in range(3)]

    def featured(read, g):
        total = taps[g][0] * read(0)
        for s in range(1, 7):
            total = total + taps[g][s] * read(s)
        return total

    f0 = featured(lambda s: x_ref[0, 8 - s : 288 - s], 0)
    f2 = featured(lambda s: x_ref[1, 8 - s : 288 - s], 2)
    p_ref[8:288] = f0 * f2
    f_ref[0] = f0[128:280]
    f_ref[2] = f2[128:280]
    f1 = featured(lambda s: x1_ref[136 - s : 416 - s], 1)
    f_ref[1] = f1[0:152]
    gm_ref[0:144] = up_ref[...].astype(F32) * f1[0:144]
    gm_ref[144:280] = next_ref[136:272].astype(F32) * f1[144:280]
    for b in range(8):
        ps_ref[b, 16:288] = p_ref[16 - b : 288 - b]
        gs_ref[b] = gm_ref[b : 272 + b]
    wb_ref[...] = jnp.broadcast_to(long_ref[...][:, None, :], (128, 8, 128))

    def forward(a, total):
        base = pl.multiple_of(136 - 8 * a, 8)
        for b in range(8):
            tap = 8 * a + b
            x = ps_ref[b, pl.ds(base, 152), :].reshape(19, 8, 128)
            total = total + wb_ref[tap][None] * x
            gm = gm_ref[0:144].reshape(18, 8, 128)
            gl_ref[tap] = jnp.sum(gm * x[:18], axis=0)
        return total

    memory = lax.fori_loop(0, 16, forward, jnp.zeros((19, 8, 128), F32)).reshape(152, 128)
    mixed_ref[...] = (f_ref[1, 0:144] * memory[0:144]).astype(BF16)
    gf_ref[1, 0:144] = up_ref[...].astype(F32) * memory[0:144]
    gf_ref[1, 144:152] = next_ref[136:144].astype(F32) * memory[144:152]

    def backward(a, total):
        base = pl.multiple_of(8 * a, 8)
        for b in range(8):
            y = gs_ref[b, pl.ds(base, 152), :].reshape(19, 8, 128)
            total = total + wb_ref[8 * a + b][None] * y
        return total

    gp = lax.fori_loop(0, 16, backward, jnp.zeros((19, 8, 128), F32)).reshape(152, 128)
    gf_ref[0] = gp * f_ref[2]
    gf_ref[2] = gp * f_ref[0]
    glong = jnp.sum(gl_ref[...], axis=1)

    @pl.when(turn == 0)
    def _():
        glong_ref[...] = glong
        gshort_ref[...] = jnp.zeros_like(gshort_ref)

    @pl.when(turn != 0)
    def _():
        glong_ref[...] += glong

    for g in range(3):
        total = taps[g][0] * gf_ref[g, 0:144]
        for s in range(1, 7):
            total = total + taps[g][s] * gf_ref[g, s : 144 + s]
        gfeat_ref[g] = total
        own = gf_ref[g, 0:144]
        for s in range(7):
            if g == 1:
                x = x1_ref[136 - s : 280 - s]
            else:
                x = x_ref[g // 2, 136 - s : 280 - s]
            column = jnp.sum((own * x).reshape(18, 8, 128), axis=0)
            gshort_ref[g, s : s + 1, :] += jnp.sum(column, axis=0, keepdims=True)


def hyena(feat, prev, nxt, up, short8, long_taps):
    def cols(*lead):
        return pl.BlockSpec(lead + (128,), lambda f, k: (0,) * len(lead) + (2 * k + f,))

    def filters(*lead):
        return pl.BlockSpec(lead + (128,), lambda f, k: (0,) * len(lead) + (f,))

    return call(
        hyena_body,
        (
            struct((ROWS, 512), BF16),
            struct((3, ROWS, 512), F32),
            struct((128, 256), F32),
            struct((3, 8, 256), F32),
        ),
        "hyena",
        grid=(2, 2),
        in_specs=[
            cols(3, ROWS), cols(3, 136), cols(288), cols(ROWS), filters(3, 8), filters(128),
        ],
        out_specs=(cols(ROWS), cols(3, ROWS), filters(128), filters(3, 8)),
        scratch_shapes=[
            pltpu.VMEM((2, 288, 128), F32),
            pltpu.VMEM((416, 128), F32),
            pltpu.VMEM((288, 128), F32),
            pltpu.VMEM((8, 288, 128), F32),
            pltpu.VMEM((280, 128), F32),
            pltpu.VMEM((8, 272, 128), F32),
            pltpu.VMEM((3, 152, 128), F32),
            pltpu.VMEM((3, 152, 128), F32),
            pltpu.VMEM((128, 8, 128), F32),
            pltpu.VMEM((128, 8, 128), F32),
        ],
    )(feat, prev, nxt, up, short8, long_taps)


def lane_max(x):
    best = x[:, 0:128]
    for j in range(1, CHUNK // 128):
        best = jnp.maximum(best, x[:, j * 128 : (j + 1) * 128])
    return best


def lane_sum(x):
    total = x[:, 0:128]
    for j in range(1, CHUNK // 128):
        total = total + x[:, j * 128 : (j + 1) * 128]
    return total


def query_body(where_ref, own_ref, kv_ref, out_ref, stat_ref, s_ref, mx_ref, l_ref, o_ref, st_ref):
    first = where_ref[0] * GROUP
    clear = first // CHUNK
    total = (first + GROUP + CHUNK - 1) // CHUNK
    mx_ref[...] = jnp.full_like(mx_ref, -jnp.inf)
    l_ref[...] = jnp.zeros_like(l_ref)
    o_ref[...] = jnp.zeros_like(o_ref)

    def rows_of(c):
        return pl.ds(pl.multiple_of(c * CHUNK, CHUNK), CHUNK)

    def scores(c, masked):
        s = nt(own_ref[:, :HD], kv_ref[rows_of(c), :HD]) * (SCALE * LOG2E)
        if masked:
            q = first + lax.broadcasted_iota(jnp.int32, (GROUP, CHUNK), 0)
            k = c * CHUNK + lax.broadcasted_iota(jnp.int32, (GROUP, CHUNK), 1)
            s = jnp.where(q >= k, s, -jnp.inf)
        s_ref[c] = s
        mx_ref[...] = jnp.maximum(mx_ref[...], lane_max(s))

    @pl.loop(0, clear)
    def _(c):
        scores(c, False)

    @pl.loop(clear, total)
    def _(c):
        scores(c, True)

    peak = jnp.max(mx_ref[...], axis=1, keepdims=True)

    @pl.loop(0, total)
    def _(c):
        p = jnp.exp2(s_ref[c] - peak)
        s_ref[c] = p
        l_ref[...] += lane_sum(p)
        o_ref[...] += nn(p.astype(BF16), kv_ref[rows_of(c), HD:])

    norm = jnp.sum(l_ref[...], axis=1, keepdims=True)
    inverse = 1.0 / norm
    attended = (o_ref[...] * inverse).astype(BF16)
    out_ref[:, :HD] = attended
    delta = jnp.sum(
        own_ref[:, HD:].astype(F32) * attended.astype(F32), axis=1, keepdims=True
    )
    o_ref[...] = jnp.zeros_like(o_ref)

    @pl.loop(0, total)
    def _(c):
        rows = rows_of(c)
        gw = nt(own_ref[:, HD:], kv_ref[rows, HD:])
        gs = (s_ref[c] * (gw - delta)).astype(BF16)
        o_ref[...] += nn(gs, kv_ref[rows, :HD])

    out_ref[:, HD:] = (o_ref[...] * (inverse * SCALE)).astype(BF16)
    lane = lax.broadcasted_iota(jnp.int32, (GROUP, HD), 1)
    st_ref[0:GROUP] = jnp.where(lane == 0, peak + jnp.log2(norm), delta)
    st_ref[GROUP:640] = jnp.zeros((640 - GROUP, HD), F32)
    stat_ref[...] = st_ref[...].T[0:8]


def query_pass(where, own, kv):
    return call(
        query_body,
        (struct((GROUP, 2 * HD), BF16), struct((8, 640), F32)),
        "query_pass",
        in_specs=[
            pl.BlockSpec(memory_space=pltpu.SMEM),
            pl.BlockSpec(memory_space=pltpu.VMEM),
            pl.BlockSpec(memory_space=pltpu.VMEM),
        ],
        scratch_shapes=[
            pltpu.VMEM((CHUNKS, GROUP, CHUNK), F32),
            pltpu.VMEM((GROUP, HD), F32),
            pltpu.VMEM((GROUP, HD), F32),
            pltpu.VMEM((GROUP, HD), F32),
            pltpu.VMEM((640, HD), F32),
        ],
    )(where, own, kv)


def key_body(where_ref, own_ref, qd_ref, stat_ref, out_ref, gk_ref, gv_ref):
    first = where_ref[0] * GROUP
    begin = first // CHUNK
    clear = (first + GROUP - 1 + CHUNK - 1) // CHUNK
    gk_ref[...] = jnp.zeros_like(gk_ref)
    gv_ref[...] = jnp.zeros_like(gv_ref)

    def visit(c, masked):
        rows = pl.ds(pl.multiple_of(c * CHUNK, CHUNK), CHUNK)
        log_row = stat_ref[c, 0:1, :]
        delta_row = stat_ref[c, 1:2, :]
        q = qd_ref[rows, :HD]
        d = qd_ref[rows, HD:]
        s = nt(own_ref[:, :HD], q) * (SCALE * LOG2E)
        p = jnp.exp2(s - log_row)
        if masked:
            k_at = first + lax.broadcasted_iota(jnp.int32, (GROUP, CHUNK), 0)
            q_at = c * CHUNK + lax.broadcasted_iota(jnp.int32, (GROUP, CHUNK), 1)
            p = jnp.where(q_at >= k_at, p, 0.0)
        gv_ref[...] += nn(p.astype(BF16), d)
        gw = nt(own_ref[:, HD:], d)
        gs = (p * (gw - delta_row)).astype(BF16)
        gk_ref[...] += nn(gs, q)

    @pl.loop(begin, jnp.minimum(clear, CHUNKS))
    def _(c):
        visit(c, True)

    @pl.loop(clear, CHUNKS)
    def _(c):
        visit(c, False)

    out_ref[:, :HD] = (gk_ref[...] * SCALE).astype(BF16)
    out_ref[:, HD:] = gv_ref[...].astype(BF16)


def key_pass(where, own, qd, stats):
    return call(
        key_body,
        struct((GROUP, 2 * HD), BF16),
        "key_pass",
        in_specs=[
            pl.BlockSpec(memory_space=pltpu.SMEM),
            pl.BlockSpec(memory_space=pltpu.VMEM),
            pl.BlockSpec(memory_space=pltpu.VMEM),
            pl.BlockSpec(memory_space=pltpu.VMEM),
        ],
        scratch_shapes=[pltpu.VMEM((GROUP, HD), F32), pltpu.VMEM((GROUP, HD), F32)],
    )(where, own, qd, stats)


def exchange(x, axis):
    return lax.all_to_all(x, axis, 0, 0, tiled=True)


def share(x, axis, count):
    return exchange(jnp.broadcast_to(x[None], (count,) + x.shape), axis)


def body(
    features, short_filter, long_filter_taps, queries, key_vectors, value_vectors,
    grad_mixed, grad_attended,
):
    feat = features.transpose(1, 0, 2)
    prev = lax.ppermute(feat[:, 8:], CTX, [(i, i + 1) for i in range(31)])
    rim = jnp.concatenate([feat[1, :136], grad_mixed[:136], feat[0, :8], feat[2, :8]], 0)
    nxt = lax.ppermute(rim, CTX, [(i + 1, i) for i in range(31)])

    where = lax.axis_index("cz").astype(jnp.int32).reshape(1)
    own_kv = exchange(pack(key_vectors, value_vectors), "cy").reshape(GROUP, 2 * HD)
    all_kv = lax.all_gather(own_kv, "cz", axis=0, tiled=True)
    own_qd = exchange(pack(queries, grad_attended), "cy").reshape(GROUP, 2 * HD)
    all_qd = lax.all_gather(own_qd, "cz", axis=0, tiled=True)

    short8 = jnp.pad(short_filter, ((0, 0), (0, 1), (0, 0)))
    mixed, gfeat, glong, gshort = hyena(
        feat, prev, nxt, after(grad_mixed, own_qd), short8, long_filter_taps
    )
    grads = jnp.concatenate([glong, gshort.reshape(24, 256), jnp.zeros((8, 256), F32)], 0)
    part = jnp.sum(exchange(grads.reshape(8, 40, HD), FT), axis=0)

    out_q, stats = query_pass(where, after(own_qd, part), all_kv)
    small = jnp.concatenate([stats[:2].reshape(10, HD), part], 0)
    small = share(small, "cz", 8)
    part = jnp.sum(small[:, 10:], axis=0)
    stats = small[:, :10].reshape(8, 2, 640)[:, :, :GROUP].transpose(1, 0, 2)
    stats = stats.reshape(2, CHUNKS, CHUNK).transpose(1, 0, 2)

    out_q = exchange(after(out_q, small).reshape(4, ROWS, 2 * HD), "cy")
    attended, grad_queries = unpack(out_q, BF16, F32)
    part = jnp.sum(share(after(part, out_q), "cy", 4), axis=0)
    grads = share(part, FT, 8).reshape(160, 256)
    grad_long = grads[:128]
    grad_short = grads[128:152].reshape(3, 8, 256)[:, :7]

    out_k = key_pass(where, after(own_kv, grads), all_qd, stats)
    out_k = exchange(out_k.reshape(4, ROWS, 2 * HD), "cy")
    grad_keys, grad_values = unpack(out_k, F32, F32)
    return (
        mixed, attended, gfeat.transpose(1, 0, 2), grad_short, grad_long,
        grad_queries, grad_keys, grad_values,
    )


def solution(mesh):
    fine = Mesh(np.asarray(mesh.devices).reshape(8, 4, 4, 2), ("cz", "cy", "fsdp", "tp"))
    rows = P(CTX, FT)
    wide = P(CTX, None, FT)
    return jax.shard_map(
        body,
        mesh=fine,
        in_specs=(wide, P(), P(), rows, rows, rows, rows, rows),
        out_specs=(rows, rows, wide, P(), P(), rows, rows, rows),
        check_vma=False,
    )
```

time: 1300 us -> 181 us (0.14)
  waiting for transfers between devices: 560 us -> 32.8 us
  loops' own time: 270 us -> 0 us
  matrix products: 135 us -> 0 us
  other arithmetic: 94.1 us -> 1.09 us
  local copies, waits for them, and re-layouts: 92.6 us -> 7.86 us
  Pallas kernels: 0 us -> 37.9 us
  blocking collectives: 83 us -> 61 us
  starting transfers between devices: 42.3 us -> 24.1 us
    ppermute x162 -> x2, waiting for transfers between devices: 560 us -> 6.62 us  [the longest x1 6.61 us: body(): nxt = lax.ppermute(rim, CTX, [(i + 1, i) for i in range(31)])]
    another operation x198 -> x0, loops' own time: 270 us -> none  [the longest x1 176 us: attention_block(): finished_rows = lax.fori_loop(0, axis_size, visit_block, begin_state)]
    dot_general x641 -> x0, matrix products: 135 us -> none  [the longest x127 31.4 us: pair_grads(): jnp.einsum('hqk,qhd->khd', grad_scores, query_part, preferred_element_typ...]
    psum x1 -> x0, blocking collectives: 83 us -> none  [body(): lax.psum((grad_short, grad_long), ('ctx', 'fsdp', 'tp'))]
    all_to_all x0 -> x3, blocking collectives: none -> 61 us  [exchange(): return lax.all_to_all(x, axis, 0, 0, tiled=True)]
    ppermute x162 -> x2, starting transfers between devices: 42.2 us -> 3.79 us  [the longest x1 2.5 us: body(): prev = lax.ppermute(feat[:, 8:], CTX, [(i, i + 1) for i in range(31)])]
    pallas_call x0 -> x7, Pallas kernels: none -> 37.9 us  [the longest x1 15.8 us: hyena(): call(hyena_body, (struct((ROWS, 512), BF16), struct((3, ROWS, 512), F32),...]
    dynamic_slice x50 -> x0, local copies, waits for them, and re-layouts: 37 us -> none  [the longest x16 19.5 us: advance(): lax.dynamic_slice_in_dim(x, offset, span_rows, 0)]
  transfers between devices with their start and end apart: 165 -> 9, of which waited for: 106 -> 6; matrix products, arithmetic and copies ran while one was open for 24% -> 4% of each run, Pallas kernels for 0% -> 14%
where the time goes in v1:
time: 181 us; the launch traced here: 179 us
  blocking collectives  61 us (34%)
  Pallas kernels  37.9 us (21%)
  waiting for transfers between devices  32.8 us (18%)
  starting transfers between devices  24.1 us (13%)
  between operations  14.2 us (8%)
  local copies, waits for them, and re-layouts  7.86 us (4%)
    all_to_all x3, blocking collectives, exchange(): return lax.all_to_all(x, axis, 0, 0, tiled=True)  61 us
    all_to_all x5, waiting for transfers between devices, exchange(): return lax.all_to_all(x, axis, 0, 0, tiled=True)  26.1 us
    all_to_all x5, starting transfers between devices, exchange(): return lax.all_to_all(x, axis, 0, 0, tiled=True)  20.2 us
    pallas_call x1, Pallas kernels, hyena(): call(hyena_body, (struct((ROWS, 512), BF16), struct((3, ROWS, 512), F32),...  15.8 us
    pallas_call x1, Pallas kernels, key_pass(): call(key_body, struct((GROUP, 2 * HD), BF16), 'key_pass', in_specs=[pl.Bl...  9.64 us
    ppermute x1, waiting for transfers between devices, body(): nxt = lax.ppermute(rim, CTX, [(i + 1, i) for i in range(31)])  6.61 us
    pallas_call x1, Pallas kernels, query_pass(): call(query_body, (struct((GROUP, 2 * HD), BF16), struct((8, 640), F32)),...  5.35 us
  transfers between devices with their start and end apart: 9, of which 6 were waited for; matrix products, arithmetic and copies ran while one was open for 4% of the time, Pallas kernels for 14%

profile of v1, /device:TPU:2, one launch (start us, length us, event | category | flops | bytes accessed | tf_op | source)
XLA Modules:
  0.0 179.0 jit_solution(9789764439955122371)
XLA Ops:
  7.2 1.8 %pack.3 = bf16[4,144,256]{2,1,0:T(8,128)(2,1)} custom-call(bf16[144,512]{1,0:T(8,128)(2,1)} %a_ref.3, bf16[144,512]{1,0:T(8,128)(2,1)} %b_ref.3), custom_call_target="tpu_custom_call" | custom-call | tf_op jit(solution)/shard_map/pack/pallas_call | solution.py:57
  9.0 11.6 %all_to_all.40 = bf16[4,144,256]{2,1,0:T(8,128)(2,1)} all-to-all(bf16[4,144,256]{2,1,0:T(8,128)(2,1)} %pack.3), channel_id=1, replica_groups=mesh['cz'=8,'cy'=4,'fsdp'=4,'tp'=2] {'cy'}, dimensions={0} | all-to-all | bytes 589824 | tf_op jit(solution)/shard_map/all_to_all | solution.py:342
  20.7 1.7 pack.2
  22.5 11.0 %all_to_all.41 = bf16[4,144,256]{2,1,0:T(8,128)(2,1)} all-to-all(bf16[4,144,256]{2,1,0:T(8,128)(2,1)} %pack.2), channel_id=1, replica_groups=mesh['cz'=8,'cy'=4,'fsdp'=4,'tp'=2] {'cy'}, dimensions={0} | all-to-all | bytes 589824 | tf_op jit(solution)/shard_map/all_to_all | solution.py:342
  33.5 2.5 %collective-permute-start = (bf16[3,136,512]{2,1,0:T(8,128)(2,1)S(1)}, bf16[3,136,512]{2,1,0:T(8,128)(2,1)S(1)}, u32[]{:S(2)}, u32[]{:S(2)}) collective-permute-start(bf16[3,136,512]{2,1,0:T(8,128)(2,1)S(1)} %slice.48), channel_id=1, source_target_pairs={{0,8},{8,16},{16,24},{24,32},{32,40},{40,48},{48,56},{56,64},{64,7... | collective-permute-start | bytes 1253384 | tf_op jit(solution)/shard_map/ppermute | solution.py:354
  36.1 1.3 collective-permute-start.1
  38.1 6.6 %collective-permute-done.1.next_ref = bf16[288,512]{1,0:T(8,128)(2,1)S(1)} collective-permute-done((bf16[288,512]{1,0:T(8,128)(2,1)S(1)}, bf16[288,512]{1,0:T(8,128)(2,1)S(1)}, u32[]{:S(2)}, u32[]{:S(2)}) %collective-permute-start.1) | collective-permute-done | bytes 294944 | tf_op jit(solution)/shard_map/ppermute | solution.py:356
  44.7 0.7 copy-done.4
  45.4 0.8 copy-done.3
  46.2 15.8 %hyena.1 = (bf16[144,512]{1,0:T(8,128)(2,1)}, f32[3,144,512]{2,1,0:T(8,128)}, f32[128,256]{1,0:T(8,128)}, f32[3,8,256]{2,1,0:T(8,128)}) custom-call(bf16[3,144,512]{2,1,0:T(8,128)(2,1)} %bitcast.26, bf16[3,136,512]{2,1,0:T(8,128)(2,1)} %copy-done.3, bf16[288,512]{1,0:T(8,128)(2,1)} %copy-done.4, bf16[144,512]{1,0:T(8,128)(2,1)} %up_ref, ...), custom_call_target="tpu_custom_call" | custom-call | tf_op jit(solution)/shard_map/hyena/pallas_call | solution.py:167
  62.0 1.0 maximum_maximum_fusion
  63.0 0.7 reshape.58
  63.7 5.0 %all-to-all-start.1 = ((f32[8,40,128]{2,1,0:T(8,128)}), f32[8,40,128]{2,1,0:T(8,128)S(1)}, u32[]{:S(2)}, u32[]{:S(2)}) async-start(f32[8,40,128]{2,1,0:T(8,128)} %reshape.58), calls=%async_computation.1 | async-start | bytes 327680 | tf_op jit(solution)/shard_map/all_to_all | solution.py:342
  68.7 4.2 %all-to-all-done.1 = f32[8,40,128]{2,1,0:T(8,128)S(1)} async-done(((f32[8,40,128]{2,1,0:T(8,128)}), f32[8,40,128]{2,1,0:T(8,128)S(1)}, u32[]{:S(2)}, u32[]{:S(2)}) %all-to-all-start.1) | async-done | bytes 163872 | tf_op jit(solution)/shard_map/all_to_all | solution.py:342
  72.9 5.4 %query_pass.1 = (bf16[576,256]{1,0:T(8,128)(2,1)}, f32[8,640]{1,0:T(8,128)}) custom-call(s32[1]{0:T(128)} %bitcast.5.where_ref, bf16[576,256]{1,0:T(8,128)(2,1)} %bitcast.25, bf16[4608,256]{1,0:T(8,128)(2,1)} %all-gather.3.cloned.1.call-done.kv_ref), custom_call_target="tpu_custom_call" | custom-call | tf_op jit(solution)/shard_map/query_pass/pallas_call | solution.py:271
  78.3 0.7 slice.41
  79.1 38.4 %all_to_all.42 = f32[8,50,128]{2,1,0:T(8,128)S(1)} all-to-all(f32[8,50,128]{2,1,0:T(8,128)S(1)} %broadcast_in_dim.9), channel_id=1, replica_groups=mesh['cz'=8,'cy'=4,'fsdp'=4,'tp'=2] {'cz'}, dimensions={0} | all-to-all | bytes 409600 | tf_op jit(solution)/shard_map/all_to_all | solution.py:342
  117.5 3.5 %all-to-all-start.4 = ((bf16[4,144,256]{2,1,0:T(8,128)(2,1)}), bf16[4,144,256]{2,1,0:T(8,128)(2,1)S(1)}, u32[]{:S(2)}, u32[]{:S(2)}) async-start(bf16[4,144,256]{2,1,0:T(8,128)(2,1)} %bitcast.31), calls=%async_computation.4 | async-start | bytes 589824 | tf_op jit(solution)/shard_map/all_to_all | solution.py:342
  121.0 7.4 %all-to-all-done.4.x_ref = bf16[4,144,256]{2,1,0:T(8,128)(2,1)S(1)} async-done(((bf16[4,144,256]{2,1,0:T(8,128)(2,1)}), bf16[4,144,256]{2,1,0:T(8,128)(2,1)S(1)}, u32[]{:S(2)}, u32[]{:S(2)}) %all-to-all-start.4) | async-done | bytes 294944 | tf_op jit(solution)/shard_map/all_to_all | solution.py:342
  128.3 0.7 broadcast_in_dim.10
  129.0 3.3 %all-to-all-start.5 = ((f32[4,40,128]{2,1,0:T(8,128)}), f32[4,40,128]{2,1,0:T(8,128)S(1)}, u32[]{:S(2)}, u32[]{:S(2)}) async-start(f32[4,40,128]{2,1,0:T(8,128)} %broadcast_in_dim.10), calls=%async_computation.5 | async-start | bytes 163840 | tf_op jit(solution)/shard_map/all_to_all | solution.py:342
  132.4 5.6 %all-to-all-done.5 = f32[4,40,128]{2,1,0:T(8,128)S(1)} async-done(((f32[4,40,128]{2,1,0:T(8,128)}), f32[4,40,128]{2,1,0:T(8,128)S(1)}, u32[]{:S(2)}, u32[]{:S(2)}) %all-to-all-start.5) | async-done | bytes 81952 | tf_op jit(solution)/shard_map/all_to_all | solution.py:342
  138.0 0.7 broadcast_in_dim.11
  138.7 5.0 %all-to-all-start.6 = ((f32[8,40,128]{2,1,0:T(8,128)}), f32[8,40,128]{2,1,0:T(8,128)S(1)}, u32[]{:S(2)}, u32[]{:S(2)}) async-start(f32[8,40,128]{2,1,0:T(8,128)} %broadcast_in_dim.11), calls=%async_computation.6 | async-start | bytes 327680 | tf_op jit(solution)/shard_map/all_to_all | solution.py:342
  144.5 1.8 unpack.2
  146.3 1.7 all-to-all-done.6
  148.0 0.7 slice.55
  148.7 9.6 %key_pass.1 = bf16[576,256]{1,0:T(8,128)(2,1)} custom-call(s32[1]{0:T(128)} %bitcast.5.where_ref, bf16[576,256]{1,0:T(8,128)(2,1)} %bitcast.23, bf16[4608,256]{1,0:T(8,128)(2,1)} %all-gather.5.cloned.1.call-done.qd_ref, f32[9,2,512]{2,1,0:T(2,128)} %bitcast.32), custom_call_target="tpu_custom_call" | custom-call | tf_op jit(solution)/shard_map/key_pass/pallas_call | solution.py:327
  158.3 3.5 %all-to-all-start.7 = ((bf16[4,144,256]{2,1,0:T(8,128)(2,1)}), bf16[4,144,256]{2,1,0:T(8,128)(2,1)S(1)}, u32[]{:S(2)}, u32[]{:S(2)}) async-start(bf16[4,144,256]{2,1,0:T(8,128)(2,1)} %bitcast.30), calls=%async_computation.7 | async-start | bytes 589824 | tf_op jit(solution)/shard_map/all_to_all | solution.py:342
  162.4 7.3 %all-to-all-done.7.x_ref = bf16[4,144,256]{2,1,0:T(8,128)(2,1)S(1)} async-done(((bf16[4,144,256]{2,1,0:T(8,128)(2,1)}), bf16[4,144,256]{2,1,0:T(8,128)(2,1)S(1)}, u32[]{:S(2)}, u32[]{:S(2)}) %all-to-all-start.7) | async-done | bytes 294944 | tf_op jit(solution)/shard_map/all_to_all | solution.py:342
  169.6 0.7 copy-done.2
  170.4 1.8 %unpack.3 = (f32[144,512]{1,0:T(8,128)}, f32[144,512]{1,0:T(8,128)}) custom-call(bf16[4,144,256]{2,1,0:T(8,128)(2,1)} %copy-done.2), custom_call_target="tpu_custom_call" | custom-call | tf_op jit(solution)/shard_map/unpack/pallas_call | solution.py:67
  (39 shorter events, 2.4 us)
Async XLA Ops:
  7.2 26.3 %copy-start = (bf16[144,3,512]{2,0,1:T(8,128)(2,1)S(1)}, bf16[144,3,512]{2,0,1:T(8,128)(2,1)}, u32[]{:S(2)}) copy-start(bf16[144,3,512]{2,0,1:T(8,128)(2,1)} %param.8) | copy-start | bytes 1327108
  7.2 28.9 %slice-start = ((bf16[144,512]{1,0:T(8,128)(2,1)}), bf16[136,512]{1,0:T(8,128)(2,1)S(1)}, s32[]{:S(2)}) async-start(bf16[144,512]{1,0:T(8,128)(2,1)} %up_ref), calls=%async_computation.10 | async-start | bytes 278528 | tf_op jit(solution)/shard_map/slice | solution.py:355
  7.2 30.2 %copy-start.5 = (f32[3,7,256]{2,1,0:T(8,128)S(1)}, f32[3,7,256]{2,1,0:T(8,128)}, u32[]{:S(2)}) copy-start(f32[3,7,256]{2,1,0:T(8,128)} %param.9) | copy-start | bytes 64516
  7.2 65.7 %all-gather.3.cloned.1.call-start = ((), (), s32[]{:S(2)}) async-start(), calls=%async_computation.8 | async-start | bytes 2654208 | tf_op jit(solution)/shard_map/all_gather | solution.py:360
  20.7 128.0 %all-gather.5.cloned.1.call-start = ((), (), s32[]{:S(2)}) async-start(), calls=%async_computation.9 | async-start | bytes 2654208 | tf_op jit(solution)/shard_map/all_gather | solution.py:362
  33.5 11.2 %collective-permute-start = (bf16[3,136,512]{2,1,0:T(8,128)(2,1)S(1)}, bf16[3,136,512]{2,1,0:T(8,128)(2,1)S(1)}, u32[]{:S(2)}, u32[]{:S(2)}) collective-permute-start(bf16[3,136,512]{2,1,0:T(8,128)(2,1)S(1)} %slice.48), channel_id=1, source_target_pairs={{0,8},{8,16},{16,24},{24,32},{32,40},{40,48},{48,56},{56,64},{64,7... | collective-permute-start | bytes 1253384 | tf_op jit(solution)/shard_map/ppermute | solution.py:354
  36.1 8.6 %collective-permute-start.1 = (bf16[288,512]{1,0:T(8,128)(2,1)S(1)}, bf16[288,512]{1,0:T(8,128)(2,1)S(1)}, u32[]{:S(2)}, u32[]{:S(2)}) collective-permute-start(bf16[288,512]{1,0:T(8,128)(2,1)S(1)} %pad_maximum_fusion), channel_id=1, source_target_pairs={{8,0},{16,8},{24,16},{32,24},{40,32},{48,40},{56,48},{64,56},{72,6... | collective-permute-start | bytes 884744 | tf_op jit(solution)/shard_map/ppermute | solution.py:356
  44.7 0.7 copy-start.4
  45.4 0.8 copy-start.3
  63.7 9.2 %all-to-all-start.1 = ((f32[8,40,128]{2,1,0:T(8,128)}), f32[8,40,128]{2,1,0:T(8,128)S(1)}, u32[]{:S(2)}, u32[]{:S(2)}) async-start(f32[8,40,128]{2,1,0:T(8,128)} %reshape.58), calls=%async_computation.1 | async-start | bytes 327680 | tf_op jit(solution)/shard_map/all_to_all | solution.py:342
  117.5 10.9 %all-to-all-start.4 = ((bf16[4,144,256]{2,1,0:T(8,128)(2,1)}), bf16[4,144,256]{2,1,0:T(8,128)(2,1)S(1)}, u32[]{:S(2)}, u32[]{:S(2)}) async-start(bf16[4,144,256]{2,1,0:T(8,128)(2,1)} %bitcast.31), calls=%async_computation.4 | async-start | bytes 589824 | tf_op jit(solution)/shard_map/all_to_all | solution.py:342
  128.3 16.2 %copy-start.1 = (bf16[4,144,256]{2,1,0:T(8,128)(2,1)}, bf16[4,144,256]{2,1,0:T(8,128)(2,1)S(1)}, u32[]{:S(2)}) copy-start(bf16[4,144,256]{2,1,0:T(8,128)(2,1)S(1)} %all-to-all-done.4.x_ref) | copy-start | bytes 884740
  129.0 9.0 %all-to-all-start.5 = ((f32[4,40,128]{2,1,0:T(8,128)}), f32[4,40,128]{2,1,0:T(8,128)S(1)}, u32[]{:S(2)}, u32[]{:S(2)}) async-start(f32[4,40,128]{2,1,0:T(8,128)} %broadcast_in_dim.10), calls=%async_computation.5 | async-start | bytes 163840 | tf_op jit(solution)/shard_map/all_to_all | solution.py:342
  138.7 9.2 %all-to-all-start.6 = ((f32[8,40,128]{2,1,0:T(8,128)}), f32[8,40,128]{2,1,0:T(8,128)S(1)}, u32[]{:S(2)}, u32[]{:S(2)}) async-start(f32[8,40,128]{2,1,0:T(8,128)} %broadcast_in_dim.11), calls=%async_computation.6 | async-start | bytes 327680 | tf_op jit(solution)/shard_map/all_to_all | solution.py:342
  158.3 11.3 %all-to-all-start.7 = ((bf16[4,144,256]{2,1,0:T(8,128)(2,1)}), bf16[4,144,256]{2,1,0:T(8,128)(2,1)S(1)}, u32[]{:S(2)}, u32[]{:S(2)}) async-start(bf16[4,144,256]{2,1,0:T(8,128)(2,1)} %bitcast.30), calls=%async_computation.7 | async-start | bytes 589824 | tf_op jit(solution)/shard_map/all_to_all | solution.py:342
  169.6 0.7 copy-start.2
Sparse Core Ops, SparseCore 0:
  20.8 47.0 all-gather.2
  69.7 43.2 all-gather.4

commit v2 on v1

--- a/solution.py
+++ b/solution.py
@@ -47,14 +47,15 @@
     return lax.dot_general(a, b, (((1,), (0,)), ((), ())), preferred_element_type=F32)
 
 
-def pack_body(a_ref, b_ref, out_ref):
+def pack_body(*refs):
+    out_ref = refs[-1]
     for h in range(4):
-        out_ref[h, :, :HD] = a_ref[:, h * HD : (h + 1) * HD]
-        out_ref[h, :, HD:] = b_ref[:, h * HD : (h + 1) * HD]
-
-
-def pack(a, b):
-    return call(pack_body, struct((4, ROWS, 2 * HD), BF16), "pack")(a, b)
+        for slot, ref in enumerate(refs[:-1]):
+            out_ref[h, :, slot * HD : (slot + 1) * HD] = ref[:, h * HD : (h + 1) * HD]
+
+
+def pack(*parts):
+    return call(pack_body, struct((4, ROWS, len(parts) * HD), BF16), "pack")(*parts)
 
 
 def unpack_body(x_ref, a_ref, b_ref):
@@ -193,6 +194,10 @@
     )(feat, prev, nxt, up, short8, long_taps)
 
 
+def half(rows, side):
+    return pl.BlockSpec((rows, 2 * HD), lambda i: (0, side), pipeline_mode=pl.Buffered(1))
+
+
 def lane_max(x):
     best = x[:, 0:128]
     for j in range(1, CHUNK // 128):
@@ -272,10 +277,11 @@
         query_body,
         (struct((GROUP, 2 * HD), BF16), struct((8, 640), F32)),
         "query_pass",
+        grid=(1,),
         in_specs=[
             pl.BlockSpec(memory_space=pltpu.SMEM),
-            pl.BlockSpec(memory_space=pltpu.VMEM),
-            pl.BlockSpec(memory_space=pltpu.VMEM),
+            half(GROUP, 0),
+            half(SEQ, 1),
         ],
         scratch_shapes=[
             pltpu.VMEM((CHUNKS, GROUP, CHUNK), F32),
@@ -328,10 +334,11 @@
         key_body,
         struct((GROUP, 2 * HD), BF16),
         "key_pass",
+        grid=(1,),
         in_specs=[
             pl.BlockSpec(memory_space=pltpu.SMEM),
-            pl.BlockSpec(memory_space=pltpu.VMEM),
-            pl.BlockSpec(memory_space=pltpu.VMEM),
+            half(GROUP, 1),
+            half(SEQ, 0),
             pl.BlockSpec(memory_space=pltpu.VMEM),
         ],
         scratch_shapes=[pltpu.VMEM((GROUP, HD), F32), pltpu.VMEM((GROUP, HD), F32)],
@@ -356,34 +363,30 @@
     nxt = lax.ppermute(rim, CTX, [(i + 1, i) for i in range(31)])
 
     where = lax.axis_index("cz").astype(jnp.int32).reshape(1)
-    own_kv = exchange(pack(key_vectors, value_vectors), "cy").reshape(GROUP, 2 * HD)
-    all_kv = lax.all_gather(own_kv, "cz", axis=0, tiled=True)
-    own_qd = exchange(pack(queries, grad_attended), "cy").reshape(GROUP, 2 * HD)
-    all_qd = lax.all_gather(own_qd, "cz", axis=0, tiled=True)
+    packed = pack(queries, grad_attended, key_vectors, value_vectors)
+    own = exchange(packed, "cy").reshape(GROUP, 4 * HD)
+    everything = lax.all_gather(own, "cz", axis=0, tiled=True)
 
     short8 = jnp.pad(short_filter, ((0, 0), (0, 1), (0, 0)))
     mixed, gfeat, glong, gshort = hyena(
-        feat, prev, nxt, after(grad_mixed, own_qd), short8, long_filter_taps
+        feat, prev, nxt, after(grad_mixed, own), short8, long_filter_taps
     )
     grads = jnp.concatenate([glong, gshort.reshape(24, 256), jnp.zeros((8, 256), F32)], 0)
     part = jnp.sum(exchange(grads.reshape(8, 40, HD), FT), axis=0)
-
-    out_q, stats = query_pass(where, after(own_qd, part), all_kv)
-    small = jnp.concatenate([stats[:2].reshape(10, HD), part], 0)
-    small = share(small, "cz", 8)
-    part = jnp.sum(small[:, 10:], axis=0)
-    stats = small[:, :10].reshape(8, 2, 640)[:, :, :GROUP].transpose(1, 0, 2)
-    stats = stats.reshape(2, CHUNKS, CHUNK).transpose(1, 0, 2)
-
-    out_q = exchange(after(out_q, small).reshape(4, ROWS, 2 * HD), "cy")
-    attended, grad_queries = unpack(out_q, BF16, F32)
-    part = jnp.sum(share(after(part, out_q), "cy", 4), axis=0)
+    part = jnp.sum(share(part, "cz", 8), axis=0)
+    part = jnp.sum(share(part, "cy", 4), axis=0)
     grads = share(part, FT, 8).reshape(160, 256)
     grad_long = grads[:128]
     grad_short = grads[128:152].reshape(3, 8, 256)[:, :7]
 
-    out_k = key_pass(where, after(own_kv, grads), all_qd, stats)
+    out_q, stats = query_pass(where, after(own, grads), everything)
+    stats = share(stats[:2, :GROUP], "cz", 8).transpose(1, 0, 2)
+    stats = stats.reshape(2, CHUNKS, CHUNK).transpose(1, 0, 2)
+    out_q = exchange(after(out_q, stats).reshape(4, ROWS, 2 * HD), "cy")
+
+    out_k = key_pass(where, own, everything, stats)
     out_k = exchange(out_k.reshape(4, ROWS, 2 * HD), "cy")
+    attended, grad_queries = unpack(out_q, BF16, F32)
     grad_keys, grad_values = unpack(out_k, F32, F32)
     return (
         mixed, attended, gfeat.transpose(1, 0, 2), grad_short, grad_long,

time: 181 us -> 175 us (0.967)
  blocking collectives: 61 us -> 79.8 us
  waiting for transfers between devices: 32.8 us -> 15.6 us
  starting transfers between devices: 24.1 us -> 16.5 us
  local copies, waits for them, and re-layouts: 7.86 us -> 10 us
    all_to_all x3 -> x5, blocking collectives: 61 us -> 79.8 us  [exchange(): return lax.all_to_all(x, axis, 0, 0, tiled=True)]
    all_to_all x5 -> x3, waiting for transfers between devices: 26.1 us -> 8.67 us  [exchange(): return lax.all_to_all(x, axis, 0, 0, tiled=True)]
    all_to_all x5 -> x3, starting transfers between devices: 20.2 us -> 12.7 us  [exchange(): return lax.all_to_all(x, axis, 0, 0, tiled=True)]
    pallas_call x3 -> x2, Pallas kernels: 13.2 us -> 11.7 us  [the longest x1 9.64 us: key_pass(): call(key_body, struct((GROUP, 2 * HD), BF16), 'key_pass', grid=(1,), in_s...]
  transfers between devices with their start and end apart: 9 -> 6, of which waited for: 6 -> 3; matrix products, arithmetic and copies ran while one was open for 4% -> 4% of each run, Pallas kernels for 14% -> 16%
where the time goes in v2:
time: 175 us; the launch traced here: 174 us
  blocking collectives  79.8 us (46%)
  Pallas kernels  36.4 us (21%)
  starting transfers between devices  16.5 us (9%)
  waiting for transfers between devices  15.6 us (9%)
  between operations  14.2 us (8%)
  local copies, waits for them, and re-layouts  10 us (6%)
    all_to_all x5, blocking collectives, exchange(): return lax.all_to_all(x, axis, 0, 0, tiled=True)  79.8 us
    pallas_call x1, Pallas kernels, hyena(): call(hyena_body, (struct((ROWS, 512), BF16), struct((3, ROWS, 512), F32),...  15.8 us
    all_to_all x3, starting transfers between devices, exchange(): return lax.all_to_all(x, axis, 0, 0, tiled=True)  12.7 us
    pallas_call x1, Pallas kernels, key_pass(): call(key_body, struct((GROUP, 2 * HD), BF16), 'key_pass', grid=(1,), in_s...  9.64 us
    all_to_all x3, waiting for transfers between devices, exchange(): return lax.all_to_all(x, axis, 0, 0, tiled=True)  8.67 us
    ppermute x1, waiting for transfers between devices, body(): nxt = lax.ppermute(rim, CTX, [(i + 1, i) for i in range(31)])  6.89 us
    pallas_call x1, Pallas kernels, query_pass(): call(query_body, (struct((GROUP, 2 * HD), BF16), struct((8, 640), F32)),...  5.34 us
    pallas_call x2, Pallas kernels, unpack(): call(unpack_body, (struct((ROWS, 4 * HD), kind_a), struct((ROWS, 4 * HD),...  3.61 us
  transfers between devices with their start and end apart: 6, of which 3 were waited for; matrix products, arithmetic and copies ran while one was open for 4% of the time, Pallas kernels for 16%

profile of v2, /device:TPU:2, one launch (start us, length us, event | category | flops | bytes accessed | tf_op | source)
XLA Modules:
  0.0 173.6 jit_solution(12053787351640213672)
XLA Ops:
  7.2 2.0 %pack.1 = bf16[4,144,512]{2,1,0:T(8,128)(2,1)} custom-call(bf16[144,512]{1,0:T(8,128)(2,1)} %refs_0_.1, bf16[144,512]{1,0:T(8,128)(2,1)} %refs_1_.1, bf16[144,512]{1,0:T(8,128)(2,1)} %refs_2_.1, bf16[144,512]{1,0:T(8,128)(2,1)} %refs_3_.1), custom_call_target="tpu_custom_call" | custom-call | tf_op jit(solution)/shard_map/pack/pallas_call | solution.py:58
  9.3 14.7 %all_to_all.40 = bf16[4,144,512]{2,1,0:T(8,128)(2,1)} all-to-all(bf16[4,144,512]{2,1,0:T(8,128)(2,1)} %pack.1), channel_id=1, replica_groups=mesh['cz'=8,'cy'=4,'fsdp'=4,'tp'=2] {'cy'}, dimensions={0} | all-to-all | bytes 1179648 | tf_op jit(solution)/shard_map/all_to_all | solution.py:349
  24.0 1.0 slice.36
  25.1 2.5 %collective-permute-start = (bf16[3,136,512]{2,1,0:T(8,128)(2,1)S(1)}, bf16[3,136,512]{2,1,0:T(8,128)(2,1)S(1)}, u32[]{:S(2)}, u32[]{:S(2)}) collective-permute-start(bf16[3,136,512]{2,1,0:T(8,128)(2,1)S(1)} %slice.36), channel_id=1, source_target_pairs={{0,8},{8,16},{16,24},{24,32},{32,40},{40,48},{48,56},{56,64},{64,7... | collective-permute-start | bytes 1253384 | tf_op jit(solution)/shard_map/ppermute | solution.py:361
  27.6 0.9 slice_bitcast_fusion
  28.5 0.7 slice_bitcast_fusion.3
  29.2 0.9 slice.29
  30.2 1.3 collective-permute-start.1
  31.5 0.6 pad.4.short_ref
  32.2 6.9 %collective-permute-done.1.next_ref = bf16[288,512]{1,0:T(8,128)(2,1)S(1)} collective-permute-done((bf16[288,512]{1,0:T(8,128)(2,1)S(1)}, bf16[288,512]{1,0:T(8,128)(2,1)S(1)}, u32[]{:S(2)}, u32[]{:S(2)}) %collective-permute-start.1) | collective-permute-done | bytes 294944 | tf_op jit(solution)/shard_map/ppermute | solution.py:363
  39.1 0.7 copy-done.3
  39.8 0.8 copy-done.2
  40.6 15.8 %hyena.1 = (bf16[144,512]{1,0:T(8,128)(2,1)}, f32[3,144,512]{2,1,0:T(8,128)}, f32[128,256]{1,0:T(8,128)}, f32[3,8,256]{2,1,0:T(8,128)}) custom-call(bf16[3,144,512]{2,1,0:T(8,128)(2,1)} %bitcast.26, bf16[3,136,512]{2,1,0:T(8,128)(2,1)} %copy-done.2, bf16[288,512]{1,0:T(8,128)(2,1)} %copy-done.3, bf16[144,512]{1,0:T(8,128)(2,1)} %up_ref, ...), custom_call_target="tpu_custom_call" | custom-call | tf_op jit(solution)/shard_map/hyena/pallas_call | solution.py:168
  56.4 1.0 maximum_maximum_fusion
  57.4 8.8 %all_to_all.41 = f32[8,40,128]{2,1,0:T(8,128)S(1)} all-to-all(f32[8,40,128]{2,1,0:T(8,128)S(1)} %reshape.50), channel_id=1, replica_groups=mesh['cz'=8,'cy'=4,'fsdp'=4,'tp'=2] {'fsdp','tp'}, dimensions={0} | all-to-all | bytes 327680 | tf_op jit(solution)/shard_map/all_to_all | solution.py:349
  66.3 29.4 %all_to_all.42 = f32[8,40,128]{2,1,0:T(8,128)S(1)} all-to-all(f32[8,40,128]{2,1,0:T(8,128)S(1)} %broadcast_in_dim.11), channel_id=1, replica_groups=mesh['cz'=8,'cy'=4,'fsdp'=4,'tp'=2] {'cz'}, dimensions={0} | all-to-all | bytes 327680 | tf_op jit(solution)/shard_map/all_to_all | solution.py:349
  95.7 10.5 %all_to_all.43 = f32[4,40,128]{2,1,0:T(8,128)S(1)} all-to-all(f32[4,40,128]{2,1,0:T(8,128)S(1)} %broadcast_in_dim.12), channel_id=1, replica_groups=mesh['cz'=8,'cy'=4,'fsdp'=4,'tp'=2] {'cy'}, dimensions={0} | all-to-all | bytes 163840 | tf_op jit(solution)/shard_map/all_to_all | solution.py:349
  106.2 0.7 broadcast_in_dim.13
  106.9 4.5 %all-to-all-start.4 = ((f32[8,40,128]{2,1,0:T(8,128)}), f32[8,40,128]{2,1,0:T(8,128)S(1)}, u32[]{:S(2)}, u32[]{:S(2)}) async-start(f32[8,40,128]{2,1,0:T(8,128)} %broadcast_in_dim.13), calls=%async_computation.4 | async-start | bytes 327680 | tf_op jit(solution)/shard_map/all_to_all | solution.py:349
  111.4 4.2 %all-to-all-done.4 = f32[8,40,128]{2,1,0:T(8,128)S(1)} async-done(((f32[8,40,128]{2,1,0:T(8,128)}), f32[8,40,128]{2,1,0:T(8,128)S(1)}, u32[]{:S(2)}, u32[]{:S(2)}) %all-to-all-start.4) | async-done | bytes 163872 | tf_op jit(solution)/shard_map/all_to_all | solution.py:349
  115.7 5.3 %query_pass.1 = (bf16[576,256]{1,0:T(8,128)(2,1)}, f32[8,640]{1,0:T(8,128)}) custom-call(s32[1]{0:T(128)} %bitcast.5.where_ref, bf16[576,512]{1,0:T(8,128)(2,1)} %bitcast.21, bf16[4608,512]{1,0:T(8,128)(2,1)} %all-gather.2.cloned.1.call-done.kv_ref.qd_ref), custom_call_target="tpu_custom_call" | custom-call | tf_op jit(solution)/shard_map/query_pass/pallas_call | solution.py:276
  121.0 0.7 slice.32
  121.7 16.3 %all_to_all.44 = f32[8,2,576]{2,1,0:T(2,128)S(1)} all-to-all(f32[8,2,576]{2,1,0:T(2,128)S(1)} %broadcast_in_dim.14), channel_id=1, replica_groups=mesh['cz'=8,'cy'=4,'fsdp'=4,'tp'=2] {'cz'}, dimensions={0} | all-to-all | bytes 73728 | tf_op jit(solution)/shard_map/all_to_all | solution.py:349
  138.2 0.6 copy.22
  138.8 3.5 %all-to-all-start.6 = ((bf16[4,144,256]{2,1,0:T(8,128)(2,1)}), bf16[4,144,256]{2,1,0:T(8,128)(2,1)S(1)}, u32[]{:S(2)}, u32[]{:S(2)}) async-start(bf16[4,144,256]{2,1,0:T(8,128)(2,1)} %bitcast.28), calls=%async_computation.6 | async-start | bytes 589824 | tf_op jit(solution)/shard_map/all_to_all | solution.py:349
  142.3 0.7 slice.42
  143.0 9.6 %key_pass.1 = bf16[576,256]{1,0:T(8,128)(2,1)} custom-call(s32[1]{0:T(128)} %bitcast.5.where_ref, bf16[576,512]{1,0:T(8,128)(2,1)} %bitcast.22, bf16[4608,512]{1,0:T(8,128)(2,1)} %all-gather.2.cloned.1.call-done.kv_ref.qd_ref, f32[9,2,512]{2,1,0:T(2,128)} %bitcast.30), custom_call_target="tpu_custom_call" | custom-call | tf_op jit(solution)/shard_map/key_pass/pallas_call | solution.py:333
  152.6 4.8 %all-to-all-start.7 = ((bf16[4,144,256]{2,1,0:T(8,128)(2,1)}), bf16[4,144,256]{2,1,0:T(8,128)(2,1)S(1)}, u32[]{:S(2)}, u32[]{:S(2)}) async-start(bf16[4,144,256]{2,1,0:T(8,128)(2,1)} %bitcast.27), calls=%async_computation.7 | async-start | bytes 589824 | tf_op jit(solution)/shard_map/all_to_all | solution.py:349
  158.0 1.8 %unpack.2 = (bf16[144,512]{1,0:T(8,128)(2,1)}, f32[144,512]{1,0:T(8,128)}) custom-call(bf16[4,144,256]{2,1,0:T(8,128)(2,1)} %copy-done), custom_call_target="tpu_custom_call" | custom-call | tf_op jit(solution)/shard_map/unpack/pallas_call | solution.py:68
  159.8 4.5 %all-to-all-done.7.x_ref = bf16[4,144,256]{2,1,0:T(8,128)(2,1)S(1)} async-done(((bf16[4,144,256]{2,1,0:T(8,128)(2,1)}), bf16[4,144,256]{2,1,0:T(8,128)(2,1)S(1)}, u32[]{:S(2)}, u32[]{:S(2)}) %all-to-all-start.7) | async-done | bytes 294944 | tf_op jit(solution)/shard_map/all_to_all | solution.py:349
  164.2 0.7 copy-done.1
  164.9 1.8 %unpack.3 = (f32[144,512]{1,0:T(8,128)}, f32[144,512]{1,0:T(8,128)}) custom-call(bf16[4,144,256]{2,1,0:T(8,128)(2,1)} %copy-done.1), custom_call_target="tpu_custom_call" | custom-call | tf_op jit(solution)/shard_map/unpack/pallas_call | solution.py:68
  (26 shorter events, 1.0 us)
Async XLA Ops:
  7.2 24.3 %copy-start.4 = (f32[3,7,256]{2,1,0:T(8,128)S(1)}, f32[3,7,256]{2,1,0:T(8,128)}, u32[]{:S(2)}) copy-start(f32[3,7,256]{2,1,0:T(8,128)} %param.9) | copy-start | bytes 64516
  7.2 108.5 %all-gather.2.cloned.1.call-start = ((), (), s32[]{:S(2)}) async-start(), calls=%async_computation.8 | async-start | bytes 5308416 | tf_op jit(solution)/shard_map/all_gather | solution.py:368
  25.1 14.0 %collective-permute-start = (bf16[3,136,512]{2,1,0:T(8,128)(2,1)S(1)}, bf16[3,136,512]{2,1,0:T(8,128)(2,1)S(1)}, u32[]{:S(2)}, u32[]{:S(2)}) collective-permute-start(bf16[3,136,512]{2,1,0:T(8,128)(2,1)S(1)} %slice.36), channel_id=1, source_target_pairs={{0,8},{8,16},{16,24},{24,32},{32,40},{40,48},{48,56},{56,64},{64,7... | collective-permute-start | bytes 1253384 | tf_op jit(solution)/shard_map/ppermute | solution.py:361
  30.2 8.9 %collective-permute-start.1 = (bf16[288,512]{1,0:T(8,128)(2,1)S(1)}, bf16[288,512]{1,0:T(8,128)(2,1)S(1)}, u32[]{:S(2)}, u32[]{:S(2)}) collective-permute-start(bf16[288,512]{1,0:T(8,128)(2,1)S(1)} %pad_maximum_fusion), channel_id=1, source_target_pairs={{8,0},{16,8},{24,16},{32,24},{40,32},{48,40},{56,48},{64,56},{72,6... | collective-permute-start | bytes 884744 | tf_op jit(solution)/shard_map/ppermute | solution.py:363
  39.1 0.7 copy-start.3
  39.8 0.8 copy-start.2
  106.9 8.7 %all-to-all-start.4 = ((f32[8,40,128]{2,1,0:T(8,128)}), f32[8,40,128]{2,1,0:T(8,128)S(1)}, u32[]{:S(2)}, u32[]{:S(2)}) async-start(f32[8,40,128]{2,1,0:T(8,128)} %broadcast_in_dim.13), calls=%async_computation.4 | async-start | bytes 327680 | tf_op jit(solution)/shard_map/all_to_all | solution.py:349
  138.8 13.8 %all-to-all-start.6 = ((bf16[4,144,256]{2,1,0:T(8,128)(2,1)}), bf16[4,144,256]{2,1,0:T(8,128)(2,1)S(1)}, u32[]{:S(2)}, u32[]{:S(2)}) async-start(bf16[4,144,256]{2,1,0:T(8,128)(2,1)} %bitcast.28), calls=%async_computation.6 | async-start | bytes 589824 | tf_op jit(solution)/shard_map/all_to_all | solution.py:349
  152.6 5.4 %copy-start = (bf16[4,144,256]{2,1,0:T(8,128)(2,1)}, bf16[4,144,256]{2,1,0:T(8,128)(2,1)S(1)}, u32[]{:S(2)}) copy-start(bf16[4,144,256]{2,1,0:T(8,128)(2,1)S(1)} %all-to-all-done.6.x_ref) | copy-start | bytes 884740
  152.6 11.6 %all-to-all-start.7 = ((bf16[4,144,256]{2,1,0:T(8,128)(2,1)}), bf16[4,144,256]{2,1,0:T(8,128)(2,1)S(1)}, u32[]{:S(2)}, u32[]{:S(2)}) async-start(bf16[4,144,256]{2,1,0:T(8,128)(2,1)} %bitcast.27), calls=%async_computation.7 | async-start | bytes 589824 | tf_op jit(solution)/shard_map/all_to_all | solution.py:349
  164.2 0.7 copy-start.1
Sparse Core Ops, SparseCore 0:
  24.2 63.1 all-gather.1

commit v3 on v2

--- a/solution.py
+++ b/solution.py
@@ -1,3 +1,5 @@
+import functools
+
 import jax
 import jax.numpy as jnp
 import numpy as np
@@ -9,6 +11,7 @@
 HD = 128
 ROWS = 144
 GROUP = 576
+KEYS = GROUP // 2
 SEQ = 4608
 CHUNK = 512
 CHUNKS = SEQ // CHUNK
@@ -19,6 +22,7 @@
 BF16 = jnp.bfloat16
 CTX = ("cz", "cy")
 FT = ("fsdp", "tp")
+YFT = ("cy", "fsdp", "tp")
 
 
 def after(value, *others):
@@ -293,10 +297,10 @@
     )(where, own, kv)
 
 
-def key_body(where_ref, own_ref, qd_ref, stat_ref, out_ref, gk_ref, gv_ref):
-    first = where_ref[0] * GROUP
+def key_body(part, where_ref, own_ref, qd_ref, stat_ref, out_ref, gk_ref, gv_ref):
+    first = where_ref[0] * GROUP + part * KEYS
     begin = first // CHUNK
-    clear = (first + GROUP - 1 + CHUNK - 1) // CHUNK
+    clear = (first + KEYS - 1 + CHUNK - 1) // CHUNK
     gk_ref[...] = jnp.zeros_like(gk_ref)
     gv_ref[...] = jnp.zeros_like(gv_ref)
 
@@ -309,8 +313,8 @@
         s = nt(own_ref[:, :HD], q) * (SCALE * LOG2E)
         p = jnp.exp2(s - log_row)
         if masked:
-            k_at = first + lax.broadcasted_iota(jnp.int32, (GROUP, CHUNK), 0)
-            q_at = c * CHUNK + lax.broadcasted_iota(jnp.int32, (GROUP, CHUNK), 1)
+            k_at = first + lax.broadcasted_iota(jnp.int32, (KEYS, CHUNK), 0)
+            q_at = c * CHUNK + lax.broadcasted_iota(jnp.int32, (KEYS, CHUNK), 1)
             p = jnp.where(q_at >= k_at, p, 0.0)
         gv_ref[...] += nn(p.astype(BF16), d)
         gw = nt(own_ref[:, HD:], d)
@@ -329,19 +333,22 @@
     out_ref[:, HD:] = gv_ref[...].astype(BF16)
 
 
-def key_pass(where, own, qd, stats):
+def key_pass(part, where, own, qd, stats):
     return call(
-        key_body,
-        struct((GROUP, 2 * HD), BF16),
+        functools.partial(key_body, part),
+        struct((KEYS, 2 * HD), BF16),
         "key_pass",
+        cost_estimate=pl.CostEstimate(
+            flops=8 * KEYS * SEQ * HD, transcendentals=KEYS * SEQ, bytes_accessed=16 << 20
+        ),
         grid=(1,),
         in_specs=[
             pl.BlockSpec(memory_space=pltpu.SMEM),
-            half(GROUP, 1),
+            pl.BlockSpec((KEYS, 2 * HD), lambda i: (part, 1)),
             half(SEQ, 0),
             pl.BlockSpec(memory_space=pltpu.VMEM),
         ],
-        scratch_shapes=[pltpu.VMEM((GROUP, HD), F32), pltpu.VMEM((GROUP, HD), F32)],
+        scratch_shapes=[pltpu.VMEM((KEYS, HD), F32), pltpu.VMEM((KEYS, HD), F32)],
     )(where, own, qd, stats)
 
 
@@ -372,20 +379,21 @@
         feat, prev, nxt, after(grad_mixed, own), short8, long_filter_taps
     )
     grads = jnp.concatenate([glong, gshort.reshape(24, 256), jnp.zeros((8, 256), F32)], 0)
-    part = jnp.sum(exchange(grads.reshape(8, 40, HD), FT), axis=0)
-    part = jnp.sum(share(part, "cz", 8), axis=0)
-    part = jnp.sum(share(part, "cy", 4), axis=0)
-    grads = share(part, FT, 8).reshape(160, 256)
+    part = jnp.sum(exchange(grads.reshape(32, 10, HD), YFT), axis=0)
+
+    out_q, stats = query_pass(where, after(own, part), everything)
+    small = jnp.concatenate([stats[:2].reshape(10, HD), part], 0)
+    small = share(small, "cz", 8)
+    stats = small[:, :10].reshape(8, 2, 640)[:, :, :GROUP].transpose(1, 0, 2)
+    stats = stats.reshape(2, CHUNKS, CHUNK).transpose(1, 0, 2)
+    part = jnp.sum(small[:, 10:], axis=0)
+    grads = share(part, YFT, 32).reshape(160, 256)
     grad_long = grads[:128]
     grad_short = grads[128:152].reshape(3, 8, 256)[:, :7]
-
-    out_q, stats = query_pass(where, after(own, grads), everything)
-    stats = share(stats[:2, :GROUP], "cz", 8).transpose(1, 0, 2)
-    stats = stats.reshape(2, CHUNKS, CHUNK).transpose(1, 0, 2)
-    out_q = exchange(after(out_q, stats).reshape(4, ROWS, 2 * HD), "cy")
-
-    out_k = key_pass(where, own, everything, stats)
-    out_k = exchange(out_k.reshape(4, ROWS, 2 * HD), "cy")
+    out_k0 = key_pass(0, where, own, everything, stats)
+    out_q = exchange(out_q.reshape(4, ROWS, 2 * HD), "cy")
+    out_k1 = key_pass(1, where, own, everything, stats)
+    out_k = exchange(jnp.concatenate([out_k0, out_k1], 0).reshape(4, ROWS, 2 * HD), "cy")
     attended, grad_queries = unpack(out_q, BF16, F32)
     grad_keys, grad_values = unpack(out_k, F32, F32)
     return (

time: 175 us -> 169 us (0.966)
  blocking collectives: 79.8 us -> 36.6 us
  starting transfers between devices: 16.5 us -> 36.5 us
  waiting for transfers between devices: 15.6 us -> 25.1 us
  Pallas kernels: 36.4 us -> 42.5 us
    all_to_all x5 -> x2, blocking collectives: 79.8 us -> 36.6 us  [exchange(): return lax.all_to_all(x, axis, 0, 0, tiled=True)]
    all_to_all x3 -> x4, starting transfers between devices: 12.7 us -> 32.6 us  [exchange(): return lax.all_to_all(x, axis, 0, 0, tiled=True)]
    pallas_call x1 -> x2, Pallas kernels: 9.64 us -> 15.8 us  [key_pass(): call(functools.partial(key_body, part), struct((KEYS, 2 * HD), BF16), 'ke...]
    all_to_all x3 -> x4, waiting for transfers between devices: 8.67 us -> 14.1 us  [exchange(): return lax.all_to_all(x, axis, 0, 0, tiled=True)]
    all_gather x1, waiting for transfers between devices: 0.02 us -> 4.04 us  [body(): everything = lax.all_gather(own, 'cz', axis=0, tiled=True)]
  transfers between devices with their start and end apart: 6 -> 7, of which waited for: 3 -> 4; matrix products, arithmetic and copies ran while one was open for 4% -> 6% of each run, Pallas kernels for 16% -> 20%
where the time goes in v3:
time: 169 us; the launch traced here: 168 us
  Pallas kernels  42.5 us (25%)
  blocking collectives  36.6 us (22%)
  starting transfers between devices  36.5 us (22%)
  waiting for transfers between devices  25.1 us (15%)
  between operations  14.2 us (8%)
  local copies, waits for them, and re-layouts  10.8 us (6%)
  other arithmetic  2.73 us (2%)
    all_to_all x2, blocking collectives, exchange(): return lax.all_to_all(x, axis, 0, 0, tiled=True)  36.6 us
    all_to_all x4, starting transfers between devices, exchange(): return lax.all_to_all(x, axis, 0, 0, tiled=True)  32.6 us
    pallas_call x1, Pallas kernels, hyena(): call(hyena_body, (struct((ROWS, 512), BF16), struct((3, ROWS, 512), F32),...  15.8 us
    pallas_call x2, Pallas kernels, key_pass(): call(functools.partial(key_body, part), struct((KEYS, 2 * HD), BF16), 'ke...  15.8 us
    all_to_all x4, waiting for transfers between devices, exchange(): return lax.all_to_all(x, axis, 0, 0, tiled=True)  14.1 us
    ppermute x1, waiting for transfers between devices, body(): nxt = lax.ppermute(rim, CTX, [(i + 1, i) for i in range(31)])  6.89 us
    pallas_call x1, Pallas kernels, query_pass(): call(query_body, (struct((GROUP, 2 * HD), BF16), struct((8, 640), F32)),...  5.34 us
    all_gather x1, waiting for transfers between devices, body(): everything = lax.all_gather(own, 'cz', axis=0, tiled=True)  4.04 us
  transfers between devices with their start and end apart: 7, of which 4 were waited for; matrix products, arithmetic and copies ran while one was open for 6% of the time, Pallas kernels for 20%

profile of v3, /device:TPU:2, one launch (start us, length us, event | category | flops | bytes accessed | tf_op | source)
XLA Modules:
  0.0 168.4 jit_solution(15548383566482830808)
XLA Ops:
  7.2 2.0 %pack.1 = bf16[4,144,512]{2,1,0:T(8,128)(2,1)} custom-call(bf16[144,512]{1,0:T(8,128)(2,1)} %refs_0_.1, bf16[144,512]{1,0:T(8,128)(2,1)} %refs_1_.1, bf16[144,512]{1,0:T(8,128)(2,1)} %refs_2_.1, bf16[144,512]{1,0:T(8,128)(2,1)} %refs_3_.1), custom_call_target="tpu_custom_call" | custom-call | tf_op jit(solution)/shard_map/pack/pallas_call | solution.py:62
  9.3 14.7 %all_to_all.30 = bf16[4,144,512]{2,1,0:T(8,128)(2,1)} all-to-all(bf16[4,144,512]{2,1,0:T(8,128)(2,1)} %pack.1), channel_id=1, replica_groups=mesh['cz'=8,'cy'=4,'fsdp'=4,'tp'=2] {'cy'}, dimensions={0} | all-to-all | bytes 1179648 | tf_op jit(solution)/shard_map/all_to_all | solution.py:356
  24.0 1.0 slice.48
  25.1 2.5 %collective-permute-start = (bf16[3,136,512]{2,1,0:T(8,128)(2,1)S(1)}, bf16[3,136,512]{2,1,0:T(8,128)(2,1)S(1)}, u32[]{:S(2)}, u32[]{:S(2)}) collective-permute-start(bf16[3,136,512]{2,1,0:T(8,128)(2,1)S(1)} %slice.48), channel_id=1, source_target_pairs={{0,8},{8,16},{16,24},{24,32},{32,40},{40,48},{48,56},{56,64},{64,7... | collective-permute-start | bytes 1253384 | tf_op jit(solution)/shard_map/ppermute | solution.py:368
  27.6 0.9 slice_bitcast_fusion
  28.5 0.7 slice_bitcast_fusion.4
  29.2 0.9 slice.38
  30.2 1.3 collective-permute-start.1
  32.2 6.9 %collective-permute-done.1.next_ref = bf16[288,512]{1,0:T(8,128)(2,1)S(1)} collective-permute-done((bf16[288,512]{1,0:T(8,128)(2,1)S(1)}, bf16[288,512]{1,0:T(8,128)(2,1)S(1)}, u32[]{:S(2)}, u32[]{:S(2)}) %collective-permute-start.1) | collective-permute-done | bytes 294944 | tf_op jit(solution)/shard_map/ppermute | solution.py:370
  39.1 0.7 copy-done.4
  39.8 0.8 copy-done.3
  40.6 15.8 %hyena.1 = (bf16[144,512]{1,0:T(8,128)(2,1)}, f32[3,144,512]{2,1,0:T(8,128)}, f32[128,256]{1,0:T(8,128)}, f32[3,8,256]{2,1,0:T(8,128)}) custom-call(bf16[3,144,512]{2,1,0:T(8,128)(2,1)} %bitcast.28, bf16[3,136,512]{2,1,0:T(8,128)(2,1)} %copy-done.3, bf16[288,512]{1,0:T(8,128)(2,1)} %copy-done.4, bf16[144,512]{1,0:T(8,128)(2,1)} %up_ref, ...), custom_call_target="tpu_custom_call" | custom-call | tf_op jit(solution)/shard_map/hyena/pallas_call | solution.py:172
  56.4 1.0 maximum_maximum_fusion
  57.4 0.7 reshape.54
  58.1 17.0 %all-to-all-start.1 = ((f32[32,10,128]{2,1,0:T(8,128)}), f32[32,10,128]{2,1,0:T(8,128)S(1)}, u32[]{:S(2)}, u32[]{:S(2)}) async-start(f32[32,10,128]{2,1,0:T(8,128)} %reshape.54), calls=%async_computation.1 | async-start | bytes 524288 | tf_op jit(solution)/shard_map/all_to_all | solution.py:356
  75.1 8.1 %all-to-all-done.1 = f32[32,10,128]{2,1,0:T(8,128)S(1)} async-done(((f32[32,10,128]{2,1,0:T(8,128)}), f32[32,10,128]{2,1,0:T(8,128)S(1)}, u32[]{:S(2)}, u32[]{:S(2)}) %all-to-all-start.1) | async-done | bytes 163872 | tf_op jit(solution)/shard_map/all_to_all | solution.py:356
  83.3 4.0 %all-gather.2.cloned.1.call-done.kv_ref.qd_ref = bf16[4608,512]{1,0:T(8,128)(2,1)} async-done(((bf16[576,512]{1,0:T(8,128)(2,1)}), bf16[4608,512]{1,0:T(8,128)(2,1)}) %all-gather.2.cloned.1.call-update) | async-done | bytes 4718608 | tf_op jit(solution)/shard_map/all_gather | solution.py:375
  87.3 5.3 %query_pass.1 = (bf16[576,256]{1,0:T(8,128)(2,1)}, f32[8,640]{1,0:T(8,128)}) custom-call(s32[1]{0:T(128)} %bitcast.5.where_ref, bf16[576,512]{1,0:T(8,128)(2,1)} %bitcast.22, bf16[4608,512]{1,0:T(8,128)(2,1)} %all-gather.2.cloned.1.call-done.kv_ref.qd_ref), custom_call_target="tpu_custom_call" | custom-call | tf_op jit(solution)/shard_map/query_pass/pallas_call | solution.py:280
  92.7 0.7 slice.41
  93.4 21.9 %all_to_all.31 = f32[8,20,128]{2,1,0:T(8,128)S(1)} all-to-all(f32[8,20,128]{2,1,0:T(8,128)S(1)} %broadcast_in_dim.7), channel_id=1, replica_groups=mesh['cz'=8,'cy'=4,'fsdp'=4,'tp'=2] {'cz'}, dimensions={0} | all-to-all | bytes 163840 | tf_op jit(solution)/shard_map/all_to_all | solution.py:356
  115.3 3.5 %all-to-all-start.2 = ((bf16[4,144,256]{2,1,0:T(8,128)(2,1)}), bf16[4,144,256]{2,1,0:T(8,128)(2,1)S(1)}, u32[]{:S(2)}, u32[]{:S(2)}) async-start(bf16[4,144,256]{2,1,0:T(8,128)(2,1)} %bitcast.31), calls=%async_computation.2 | async-start | bytes 589824 | tf_op jit(solution)/shard_map/all_to_all | solution.py:356
  119.6 7.9 %key_pass.2 = bf16[288,256]{1,0:T(8,128)(2,1)} custom-call(s32[1]{0:T(128)} %bitcast.5.where_ref, bf16[576,512]{1,0:T(8,128)(2,1)} %bitcast.23, bf16[4608,512]{1,0:T(8,128)(2,1)} %all-gather.2.cloned.1.call-done.kv_ref.qd_ref, f32[9,2,512]{2,1,0:T(2,128)} %bitcast.29), custom_call_target="tpu_custom_call" | custom-call | flops 1358954496 | bytes 16777216 | tf_op jit(solution)/shard_map/key_pass/pallas_call | solution.py:337
  127.5 0.7 broadcast_in_dim.8
  128.2 7.9 %all-to-all-start.4 = ((f32[32,10,128]{2,1,0:T(8,128)}), f32[32,10,128]{2,1,0:T(8,128)S(1)}, u32[]{:S(2)}, u32[]{:S(2)}) async-start(f32[32,10,128]{2,1,0:T(8,128)} %broadcast_in_dim.8), calls=%async_computation.4 | async-start | bytes 524288 | tf_op jit(solution)/shard_map/all_to_all | solution.py:356
  136.1 7.9 %key_pass.3 = bf16[288,256]{1,0:T(8,128)(2,1)} custom-call(s32[1]{0:T(128)} %bitcast.5.where_ref, bf16[576,512]{1,0:T(8,128)(2,1)} %bitcast.24, bf16[4608,512]{1,0:T(8,128)(2,1)} %all-gather.2.cloned.1.call-done.kv_ref.qd_ref, f32[9,2,512]{2,1,0:T(2,128)} %bitcast.30), custom_call_target="tpu_custom_call" | custom-call | flops 1358954496 | bytes 16777216 | tf_op jit(solution)/shard_map/key_pass/pallas_call | solution.py:337
  144.0 1.6 pad_maximum_fusion.1
  145.6 1.8 %unpack.2 = (bf16[144,512]{1,0:T(8,128)(2,1)}, f32[144,512]{1,0:T(8,128)}) custom-call(bf16[4,144,256]{2,1,0:T(8,128)(2,1)} %copy-done), custom_call_target="tpu_custom_call" | custom-call | tf_op jit(solution)/shard_map/unpack/pallas_call | solution.py:72
  147.4 4.3 %all-to-all-start.5 = ((bf16[4,144,256]{2,1,0:T(8,128)(2,1)}), bf16[4,144,256]{2,1,0:T(8,128)(2,1)S(1)}, u32[]{:S(2)}, u32[]{:S(2)}) async-start(bf16[4,144,256]{2,1,0:T(8,128)(2,1)} %bitcast.12), calls=%async_computation.5 | async-start | bytes 589824 | tf_op jit(solution)/shard_map/all_to_all | solution.py:356
  151.7 0.7 slice.55
  153.0 6.0 %all-to-all-done.5.x_ref = bf16[4,144,256]{2,1,0:T(8,128)(2,1)S(1)} async-done(((bf16[4,144,256]{2,1,0:T(8,128)(2,1)}), bf16[4,144,256]{2,1,0:T(8,128)(2,1)S(1)}, u32[]{:S(2)}, u32[]{:S(2)}) %all-to-all-start.5) | async-done | bytes 294944 | tf_op jit(solution)/shard_map/all_to_all | solution.py:356
  159.0 0.7 copy-done.1
  159.7 1.8 %unpack.3 = (f32[144,512]{1,0:T(8,128)}, f32[144,512]{1,0:T(8,128)}) custom-call(bf16[4,144,256]{2,1,0:T(8,128)(2,1)} %copy-done.1), custom_call_target="tpu_custom_call" | custom-call | tf_op jit(solution)/shard_map/unpack/pallas_call | solution.py:72
  (30 shorter events, 2.3 us)
Async XLA Ops:
  7.2 24.3 %copy-start.5 = (f32[3,7,256]{2,1,0:T(8,128)S(1)}, f32[3,7,256]{2,1,0:T(8,128)}, u32[]{:S(2)}) copy-start(f32[3,7,256]{2,1,0:T(8,128)} %param.9) | copy-start | bytes 64516
  7.2 80.1 %all-gather.2.cloned.1.call-start = ((), (), s32[]{:S(2)}) async-start(), calls=%async_computation.6 | async-start | bytes 5308416 | tf_op jit(solution)/shard_map/all_gather | solution.py:375
  25.1 14.0 %collective-permute-start = (bf16[3,136,512]{2,1,0:T(8,128)(2,1)S(1)}, bf16[3,136,512]{2,1,0:T(8,128)(2,1)S(1)}, u32[]{:S(2)}, u32[]{:S(2)}) collective-permute-start(bf16[3,136,512]{2,1,0:T(8,128)(2,1)S(1)} %slice.48), channel_id=1, source_target_pairs={{0,8},{8,16},{16,24},{24,32},{32,40},{40,48},{48,56},{56,64},{64,7... | collective-permute-start | bytes 1253384 | tf_op jit(solution)/shard_map/ppermute | solution.py:368
  30.2 8.9 %collective-permute-start.1 = (bf16[288,512]{1,0:T(8,128)(2,1)S(1)}, bf16[288,512]{1,0:T(8,128)(2,1)S(1)}, u32[]{:S(2)}, u32[]{:S(2)}) collective-permute-start(bf16[288,512]{1,0:T(8,128)(2,1)S(1)} %pad_maximum_fusion), channel_id=1, source_target_pairs={{8,0},{16,8},{24,16},{32,24},{40,32},{48,40},{56,48},{64,56},{72,6... | collective-permute-start | bytes 884744 | tf_op jit(solution)/shard_map/ppermute | solution.py:370
  39.1 0.7 copy-start.4
  39.8 0.8 copy-start.3
  58.1 25.2 %all-to-all-start.1 = ((f32[32,10,128]{2,1,0:T(8,128)}), f32[32,10,128]{2,1,0:T(8,128)S(1)}, u32[]{:S(2)}, u32[]{:S(2)}) async-start(f32[32,10,128]{2,1,0:T(8,128)} %reshape.54), calls=%async_computation.1 | async-start | bytes 524288 | tf_op jit(solution)/shard_map/all_to_all | solution.py:356
  115.3 12.2 %all-to-all-start.2 = ((bf16[4,144,256]{2,1,0:T(8,128)(2,1)}), bf16[4,144,256]{2,1,0:T(8,128)(2,1)S(1)}, u32[]{:S(2)}, u32[]{:S(2)}) async-start(bf16[4,144,256]{2,1,0:T(8,128)(2,1)} %bitcast.31), calls=%async_computation.2 | async-start | bytes 589824 | tf_op jit(solution)/shard_map/all_to_all | solution.py:356
  127.5 16.5 %copy-start.2 = (bf16[288,256]{1,0:T(8,128)(2,1)S(1)}, bf16[288,256]{1,0:T(8,128)(2,1)}, u32[]{:S(2)}) copy-start(bf16[288,256]{1,0:T(8,128)(2,1)} %key_pass.2) | copy-start | bytes 442372
  127.5 18.2 %copy-start = (bf16[4,144,256]{2,1,0:T(8,128)(2,1)}, bf16[4,144,256]{2,1,0:T(8,128)(2,1)S(1)}, u32[]{:S(2)}) copy-start(bf16[4,144,256]{2,1,0:T(8,128)(2,1)S(1)} %all-to-all-done.2.x_ref) | copy-start | bytes 884740
  128.2 19.2 %all-to-all-start.4 = ((f32[32,10,128]{2,1,0:T(8,128)}), f32[32,10,128]{2,1,0:T(8,128)S(1)}, u32[]{:S(2)}, u32[]{:S(2)}) async-start(f32[32,10,128]{2,1,0:T(8,128)} %broadcast_in_dim.8), calls=%async_computation.4 | async-start | bytes 524288 | tf_op jit(solution)/shard_map/all_to_all | solution.py:356
  147.4 11.6 %all-to-all-start.5 = ((bf16[4,144,256]{2,1,0:T(8,128)(2,1)}), bf16[4,144,256]{2,1,0:T(8,128)(2,1)S(1)}, u32[]{:S(2)}, u32[]{:S(2)}) async-start(bf16[4,144,256]{2,1,0:T(8,128)(2,1)} %bitcast.12), calls=%async_computation.5 | async-start | bytes 589824 | tf_op jit(solution)/shard_map/all_to_all | solution.py:356
  159.0 0.7 copy-start.1
Sparse Core Ops, SparseCore 0:
  24.2 63.1 all-gather.1

commit v4 on v2

--- a/solution.py
+++ b/solution.py
@@ -19,6 +19,7 @@
 BF16 = jnp.bfloat16
 CTX = ("cz", "cy")
 FT = ("fsdp", "tp")
+YFT = ("cy", "fsdp", "tp")
 
 
 def after(value, *others):
@@ -58,16 +59,24 @@
     return call(pack_body, struct((4, ROWS, len(parts) * HD), BF16), "pack")(*parts)
 
 
-def unpack_body(x_ref, a_ref, b_ref):
+def unpack_body(x_ref, attended_ref, gq_ref, gk_ref, gv_ref, grads_ref):
     for h in range(4):
-        a_ref[:, h * HD : (h + 1) * HD] = x_ref[h, :, :HD].astype(a_ref.dtype)
-        b_ref[:, h * HD : (h + 1) * HD] = x_ref[h, :, HD:].astype(b_ref.dtype)
-
-
-def unpack(x, kind_a, kind_b):
+        at = slice(h * HD, (h + 1) * HD)
+        attended_ref[:, at] = x_ref[h, :ROWS, 0:HD]
+        gq_ref[:, at] = x_ref[h, :ROWS, HD : 2 * HD].astype(F32)
+        gk_ref[:, at] = x_ref[h, :ROWS, 2 * HD : 3 * HD].astype(F32)
+        gv_ref[:, at] = x_ref[h, :ROWS, 3 * HD :].astype(F32)
+        for side in range(2):
+            high = x_ref[h, ROWS:, side * HD : (side + 1) * HD].astype(F32)
+            low = x_ref[h, ROWS:, (side + 2) * HD : (side + 3) * HD].astype(F32)
+            grads_ref[h, side * 40 : (side + 1) * 40] = high + low
+
+
+def unpack(x):
+    whole = struct((ROWS, 4 * HD), F32)
     return call(
         unpack_body,
-        (struct((ROWS, 4 * HD), kind_a), struct((ROWS, 4 * HD), kind_b)),
+        (struct((ROWS, 4 * HD), BF16), whole, whole, whole, struct((4, 80, HD), F32)),
         "unpack",
     )(x)
 
@@ -293,7 +302,7 @@
     )(where, own, kv)
 
 
-def key_body(where_ref, own_ref, qd_ref, stat_ref, out_ref, gk_ref, gv_ref):
+def key_body(where_ref, own_ref, qd_ref, stat_ref, oq_ref, part_ref, out_ref, gk_ref, gv_ref):
     first = where_ref[0] * GROUP
     begin = first // CHUNK
     clear = (first + GROUP - 1 + CHUNK - 1) // CHUNK
@@ -325,24 +334,38 @@
     def _(c):
         visit(c, False)
 
-    out_ref[:, :HD] = (gk_ref[...] * SCALE).astype(BF16)
-    out_ref[:, HD:] = gv_ref[...].astype(BF16)
-
-
-def key_pass(where, own, qd, stats):
+    for j in range(4):
+        at = slice(j * ROWS, (j + 1) * ROWS)
+        out_ref[j, :ROWS, : 2 * HD] = oq_ref[at]
+        out_ref[j, :ROWS, 2 * HD : 3 * HD] = (gk_ref[at] * SCALE).astype(BF16)
+        out_ref[j, :ROWS, 3 * HD :] = gv_ref[at].astype(BF16)
+        for side in range(2):
+            value = part_ref[side * 40 : (side + 1) * 40]
+            high = value.astype(BF16)
+            out_ref[j, ROWS:, side * HD : (side + 1) * HD] = high
+            low = (value - high.astype(F32)).astype(BF16)
+            out_ref[j, ROWS:, (side + 2) * HD : (side + 3) * HD] = low
+
+
+def key_pass(where, own, qd, stats, out_q, part):
     return call(
         key_body,
-        struct((GROUP, 2 * HD), BF16),
+        struct((4, ROWS + 40, 4 * HD), BF16),
         "key_pass",
+        cost_estimate=pl.CostEstimate(
+            flops=8 * GROUP * SEQ * HD, transcendentals=GROUP * SEQ, bytes_accessed=16 << 20
+        ),
         grid=(1,),
         in_specs=[
             pl.BlockSpec(memory_space=pltpu.SMEM),
             half(GROUP, 1),
             half(SEQ, 0),
             pl.BlockSpec(memory_space=pltpu.VMEM),
+            pl.BlockSpec(memory_space=pltpu.VMEM),
+            pl.BlockSpec(memory_space=pltpu.VMEM),
         ],
         scratch_shapes=[pltpu.VMEM((GROUP, HD), F32), pltpu.VMEM((GROUP, HD), F32)],
-    )(where, own, qd, stats)
+    )(where, own, qd, stats, out_q, part)
 
 
 def exchange(x, axis):
@@ -365,6 +388,7 @@
     where = lax.axis_index("cz").astype(jnp.int32).reshape(1)
     packed = pack(queries, grad_attended, key_vectors, value_vectors)
     own = exchange(packed, "cy").reshape(GROUP, 4 * HD)
+    own, prev, nxt = lax.optimization_barrier((own, prev, nxt))
     everything = lax.all_gather(own, "cz", axis=0, tiled=True)
 
     short8 = jnp.pad(short_filter, ((0, 0), (0, 1), (0, 0)))
@@ -372,22 +396,18 @@
         feat, prev, nxt, after(grad_mixed, own), short8, long_filter_taps
     )
     grads = jnp.concatenate([glong, gshort.reshape(24, 256), jnp.zeros((8, 256), F32)], 0)
-    part = jnp.sum(exchange(grads.reshape(8, 40, HD), FT), axis=0)
+    part = jnp.sum(exchange(grads.reshape(32, 10, HD), YFT), axis=0)
     part = jnp.sum(share(part, "cz", 8), axis=0)
-    part = jnp.sum(share(part, "cy", 4), axis=0)
-    grads = share(part, FT, 8).reshape(160, 256)
+    part = share(part, FT, 8)
+
+    out_q, stats = query_pass(where, after(own, part), everything)
+    stats = share(stats[:2, :GROUP], "cz", 8).transpose(1, 0, 2)
+    stats = stats.reshape(2, CHUNKS, CHUNK).transpose(1, 0, 2)
+    result = key_pass(where, own, everything, stats, out_q, part.reshape(80, HD))
+    attended, grad_queries, grad_keys, grad_values, grads = unpack(exchange(result, "cy"))
+    grads = grads.reshape(160, 256)
     grad_long = grads[:128]
     grad_short = grads[128:152].reshape(3, 8, 256)[:, :7]
-
-    out_q, stats = query_pass(where, after(own, grads), everything)
-    stats = share(stats[:2, :GROUP], "cz", 8).transpose(1, 0, 2)
-    stats = stats.reshape(2, CHUNKS, CHUNK).transpose(1, 0, 2)
-    out_q = exchange(after(out_q, stats).reshape(4, ROWS, 2 * HD), "cy")
-
-    out_k = key_pass(where, own, everything, stats)
-    out_k = exchange(out_k.reshape(4, ROWS, 2 * HD), "cy")
-    attended, grad_queries = unpack(out_q, BF16, F32)
-    grad_keys, grad_values = unpack(out_k, F32, F32)
     return (
         mixed, attended, gfeat.transpose(1, 0, 2), grad_short, grad_long,
         grad_queries, grad_keys, grad_values,

time: 175 us -> 162 us (0.926)
  blocking collectives: 79.8 us -> 48.3 us
  waiting for transfers between devices: 15.6 us -> 26.7 us
  starting transfers between devices: 16.5 us -> 24.4 us
    all_to_all x5 -> x3, blocking collectives: 79.8 us -> 48.3 us  [exchange(): return lax.all_to_all(x, axis, 0, 0, tiled=True)]
    all_to_all x3, starting transfers between devices: 12.7 us -> 19.6 us  [exchange(): return lax.all_to_all(x, axis, 0, 0, tiled=True)]
    all_gather x1, waiting for transfers between devices: 0.02 us -> 4.48 us  [body(): everything = lax.all_gather(own, 'cz', axis=0, tiled=True)]
    ppermute x1, waiting for transfers between devices: 6.89 us -> 10.8 us  [body(): nxt = lax.ppermute(rim, CTX, [(i + 1, i) for i in range(31)])]
    all_to_all x3, waiting for transfers between devices: 8.67 us -> 11.4 us  [exchange(): return lax.all_to_all(x, axis, 0, 0, tiled=True)]
    pallas_call x3 -> x2, Pallas kernels: 13.2 us -> 12.1 us  [the longest x1 9.94 us: key_pass(): call(key_body, struct((4, ROWS + 40, 4 * HD), BF16), 'key_pass', cost_est...]
  transfers between devices with their start and end apart: 6 -> 6, of which waited for: 3 -> 4; matrix products, arithmetic and copies ran while one was open for 4% -> 3% of each run, Pallas kernels for 16% -> 11%
where the time goes in v4:
time: 162 us; the launch traced here: 161 us
  blocking collectives  48.3 us (30%)
  Pallas kernels  35.3 us (22%)
  waiting for transfers between devices  26.7 us (16%)
  starting transfers between devices  24.4 us (15%)
  between operations  14.1 us (9%)
  local copies, waits for them, and re-layouts  10.8 us (7%)
    all_to_all x3, blocking collectives, exchange(): return lax.all_to_all(x, axis, 0, 0, tiled=True)  48.3 us
    all_to_all x3, starting transfers between devices, exchange(): return lax.all_to_all(x, axis, 0, 0, tiled=True)  19.6 us
    pallas_call x1, Pallas kernels, hyena(): call(hyena_body, (struct((ROWS, 512), BF16), struct((3, ROWS, 512), F32),...  15.8 us
    all_to_all x3, waiting for transfers between devices, exchange(): return lax.all_to_all(x, axis, 0, 0, tiled=True)  11.4 us
    ppermute x1, waiting for transfers between devices, body(): nxt = lax.ppermute(rim, CTX, [(i + 1, i) for i in range(31)])  10.8 us
    pallas_call x1, Pallas kernels, key_pass(): call(key_body, struct((4, ROWS + 40, 4 * HD), BF16), 'key_pass', cost_est...  9.94 us
    pallas_call x1, Pallas kernels, query_pass(): call(query_body, (struct((GROUP, 2 * HD), BF16), struct((8, 640), F32)),...  5.33 us
    all_gather x1, waiting for transfers between devices, body(): everything = lax.all_gather(own, 'cz', axis=0, tiled=True)  4.48 us
  transfers between devices with their start and end apart: 6, of which 4 were waited for; matrix products, arithmetic and copies ran while one was open for 3% of the time, Pallas kernels for 11%

profile of v4, /device:TPU:2, one launch (start us, length us, event | category | flops | bytes accessed | tf_op | source)
XLA Modules:
  0.0 160.7 jit_solution(7050233009231944749)
XLA Ops:
  7.2 1.0 slice.36
  8.2 3.5 %collective-permute-start = (bf16[3,136,512]{2,1,0:T(8,128)(2,1)S(1)}, bf16[3,136,512]{2,1,0:T(8,128)(2,1)S(1)}, u32[]{:S(2)}, u32[]{:S(2)}) collective-permute-start(bf16[3,136,512]{2,1,0:T(8,128)(2,1)S(1)} %slice.36), channel_id=1, source_target_pairs={{0,8},{8,16},{16,24},{24,32},{32,40},{40,48},{48,56},{56,64},{64,7... | collective-permute-start | bytes 1253384 | tf_op jit(solution)/shard_map/ppermute | solution.py:384
  11.7 2.0 %pack.1 = bf16[4,144,512]{2,1,0:T(8,128)(2,1)} custom-call(bf16[144,512]{1,0:T(8,128)(2,1)} %refs_0_.1, bf16[144,512]{1,0:T(8,128)(2,1)} %refs_1_.1, bf16[144,512]{1,0:T(8,128)(2,1)} %refs_2_.1, bf16[144,512]{1,0:T(8,128)(2,1)} %refs_3_.1), custom_call_target="tpu_custom_call" | custom-call | tf_op jit(solution)/shard_map/pack/pallas_call | solution.py:59
  13.8 4.3 %all-to-all-start = ((bf16[4,144,512]{2,1,0:T(8,128)(2,1)}), bf16[4,144,512]{2,1,0:T(8,128)(2,1)S(1)}, u32[]{:S(2)}, u32[]{:S(2)}) async-start(bf16[4,144,512]{2,1,0:T(8,128)(2,1)} %pack.1), calls=%async_computation | async-start | bytes 1179648 | tf_op jit(solution)/shard_map/all_to_all | solution.py:372
  18.0 0.9 slice_bitcast_fusion
  19.0 0.7 slice_bitcast_fusion.3
  19.7 0.9 slice.29
  20.6 1.3 collective-permute-start.1
  21.9 10.8 %collective-permute-done.1.next_ref = bf16[288,512]{1,0:T(8,128)(2,1)S(1)} collective-permute-done((bf16[288,512]{1,0:T(8,128)(2,1)S(1)}, bf16[288,512]{1,0:T(8,128)(2,1)S(1)}, u32[]{:S(2)}, u32[]{:S(2)}) %collective-permute-start.1) | collective-permute-done | bytes 294944 | tf_op jit(solution)/shard_map/ppermute | solution.py:386
  32.8 0.9 copy-done
  33.7 0.6 pad.4.short_ref
  34.4 15.8 %hyena.1 = (bf16[144,512]{1,0:T(8,128)(2,1)}, f32[3,144,512]{2,1,0:T(8,128)}, f32[128,256]{1,0:T(8,128)}, f32[3,8,256]{2,1,0:T(8,128)}) custom-call(bf16[3,144,512]{2,1,0:T(8,128)(2,1)} %bitcast.24, bf16[3,136,512]{2,1,0:T(8,128)(2,1)} %copy-done.1, bf16[288,512]{1,0:T(8,128)(2,1)} %copy-done.2, bf16[144,512]{1,0:T(8,128)(2,1)} %up_ref, ...), custom_call_target="tpu_custom_call" | custom-call | tf_op jit(solution)/shard_map/hyena/pallas_call | solution.py:177
  50.2 1.0 maximum_maximum_fusion
  51.2 16.1 %all_to_all.30 = f32[32,10,128]{2,1,0:T(8,128)S(1)} all-to-all(f32[32,10,128]{2,1,0:T(8,128)S(1)} %reshape.46), channel_id=1, replica_groups=mesh['cz'=8,'cy'=4,'fsdp'=4,'tp'=2] {'cy','fsdp','tp'}, dimensions={0} | all-to-all | bytes 327680 | tf_op jit(solution)/shard_map/all_to_all | solution.py:372
  67.4 17.2 %all_to_all.31 = f32[8,10,128]{2,1,0:T(8,128)S(1)} all-to-all(f32[8,10,128]{2,1,0:T(8,128)S(1)} %broadcast_in_dim.9), channel_id=1, replica_groups=mesh['cz'=8,'cy'=4,'fsdp'=4,'tp'=2] {'cz'}, dimensions={0} | all-to-all | bytes 81920 | tf_op jit(solution)/shard_map/all_to_all | solution.py:372
  84.6 0.6 broadcast_in_dim.10
  85.2 4.7 %all-to-all-start.3 = ((f32[8,10,128]{2,1,0:T(8,128)}), f32[8,10,128]{2,1,0:T(8,128)S(1)}, u32[]{:S(2)}, u32[]{:S(2)}) async-start(f32[8,10,128]{2,1,0:T(8,128)} %broadcast_in_dim.10), calls=%async_computation.3 | async-start | bytes 131072 | tf_op jit(solution)/shard_map/all_to_all | solution.py:372
  89.9 3.9 %all-to-all-done.3 = f32[8,10,128]{2,1,0:T(8,128)S(1)} async-done(((f32[8,10,128]{2,1,0:T(8,128)}), f32[8,10,128]{2,1,0:T(8,128)S(1)}, u32[]{:S(2)}, u32[]{:S(2)}) %all-to-all-start.3) | async-done | bytes 40992 | tf_op jit(solution)/shard_map/all_to_all | solution.py:372
  93.9 4.5 %all-gather.2.cloned.1.call-done.kv_ref.qd_ref = bf16[4608,512]{1,0:T(8,128)(2,1)} async-done(((bf16[576,512]{1,0:T(8,128)(2,1)}), bf16[4608,512]{1,0:T(8,128)(2,1)}) %all-gather.2.cloned.1.call-update) | async-done | bytes 4718608 | tf_op jit(solution)/shard_map/all_gather | solution.py:392
  98.3 5.3 %query_pass.1 = (bf16[576,256]{1,0:T(8,128)(2,1)}, f32[8,640]{1,0:T(8,128)}) custom-call(s32[1]{0:T(128)} %bitcast.5.where_ref, bf16[576,512]{1,0:T(8,128)(2,1)} %bitcast.19, bf16[4608,512]{1,0:T(8,128)(2,1)} %all-gather.2.cloned.1.call-done.kv_ref.qd_ref), custom_call_target="tpu_custom_call" | custom-call | tf_op jit(solution)/shard_map/query_pass/pallas_call | solution.py:285
  103.7 0.7 slice.32
  104.4 0.6 broadcast_in_dim.11
  105.0 10.6 %all-to-all-start.4 = ((f32[8,2,576]{2,1,0:T(2,128)}), f32[8,2,576]{2,1,0:T(2,128)S(1)}, u32[]{:S(2)}, u32[]{:S(2)}) async-start(f32[8,2,576]{2,1,0:T(2,128)} %broadcast_in_dim.11), calls=%async_computation.4 | async-start | bytes 81920 | tf_op jit(solution)/shard_map/all_to_all | solution.py:372
  115.6 0.6 reshape.48.part_ref
  116.2 7.5 %all-to-all-done.4 = f32[8,2,576]{2,1,0:T(2,128)S(1)} async-done(((f32[8,2,576]{2,1,0:T(2,128)}), f32[8,2,576]{2,1,0:T(2,128)S(1)}, u32[]{:S(2)}, u32[]{:S(2)}) %all-to-all-start.4) | async-done | bytes 36896 | tf_op jit(solution)/shard_map/all_to_all | solution.py:372
  123.8 0.6 copy.26
  124.5 9.9 %key_pass.1 = bf16[4,184,512]{2,1,0:T(8,128)(2,1)} custom-call(s32[1]{0:T(128)} %bitcast.5.where_ref, bf16[576,512]{1,0:T(8,128)(2,1)} %bitcast.20, bf16[4608,512]{1,0:T(8,128)(2,1)} %all-gather.2.cloned.1.call-done.kv_ref.qd_ref, f32[9,2,512]{2,1,0:T(2,128)} %bitcast.26, bf16[576,256]{1,0:T(8,128)(2,1)} %get-tuple-element.33.oq_ref, f32[80,128]{1,0:T(8,128)} %reshape.48.part_ref), custom_call_target="tpu_custom_call" | custom-call | flops 2717908992 | bytes 16777216 | tf_op jit(solution)/shard_map/key_pass/pallas_call | solution.py:351
  134.4 15.0 %all_to_all.32.x_ref = bf16[4,184,512]{2,1,0:T(8,128)(2,1)} all-to-all(bf16[4,184,512]{2,1,0:T(8,128)(2,1)} %key_pass.1), channel_id=1, replica_groups=mesh['cz'=8,'cy'=4,'fsdp'=4,'tp'=2] {'cy'}, dimensions={0} | all-to-all | bytes 1507328 | tf_op jit(solution)/shard_map/all_to_all | solution.py:372
  149.4 2.2 %unpack.1 = (bf16[144,512]{1,0:T(8,128)(2,1)}, f32[144,512]{1,0:T(8,128)}, f32[144,512]{1,0:T(8,128)}, f32[144,512]{1,0:T(8,128)}, f32[4,80,128]{2,1,0:T(8,128)}) custom-call(bf16[4,184,512]{2,1,0:T(8,128)(2,1)} %all_to_all.32.x_ref), custom_call_target="tpu_custom_call" | custom-call | tf_op jit(solution)/shard_map/unpack/pallas_call | solution.py:77
  151.6 1.0 reshape.49
  152.6 0.6 slice_bitcast_fusion.1
  153.2 0.7 slice.42
  (20 shorter events, 0.3 us)
Async XLA Ops:
  7.2 26.5 %copy-start.3 = (f32[3,7,256]{2,1,0:T(8,128)S(1)}, f32[3,7,256]{2,1,0:T(8,128)}, u32[]{:S(2)}) copy-start(f32[3,7,256]{2,1,0:T(8,128)} %param.9) | copy-start | bytes 64516
  8.2 24.5 %collective-permute-start = (bf16[3,136,512]{2,1,0:T(8,128)(2,1)S(1)}, bf16[3,136,512]{2,1,0:T(8,128)(2,1)S(1)}, u32[]{:S(2)}, u32[]{:S(2)}) collective-permute-start(bf16[3,136,512]{2,1,0:T(8,128)(2,1)S(1)} %slice.36), channel_id=1, source_target_pairs={{0,8},{8,16},{16,24},{24,32},{32,40},{40,48},{48,56},{56,64},{64,7... | collective-permute-start | bytes 1253384 | tf_op jit(solution)/shard_map/ppermute | solution.py:384
  13.8 19.0 %all-to-all-start = ((bf16[4,144,512]{2,1,0:T(8,128)(2,1)}), bf16[4,144,512]{2,1,0:T(8,128)(2,1)S(1)}, u32[]{:S(2)}, u32[]{:S(2)}) async-start(bf16[4,144,512]{2,1,0:T(8,128)(2,1)} %pack.1), calls=%async_computation | async-start | bytes 1179648 | tf_op jit(solution)/shard_map/all_to_all | solution.py:372
  18.0 80.3 %all-gather.2.cloned.1.call-start = ((), (), s32[]{:S(2)}) async-start(), calls=%async_computation.6 | async-start | bytes 5308416 | tf_op jit(solution)/shard_map/all_gather | solution.py:392
  20.6 12.1 %collective-permute-start.1 = (bf16[288,512]{1,0:T(8,128)(2,1)S(1)}, bf16[288,512]{1,0:T(8,128)(2,1)S(1)}, u32[]{:S(2)}, u32[]{:S(2)}) collective-permute-start(bf16[288,512]{1,0:T(8,128)(2,1)S(1)} %pad_maximum_fusion), channel_id=1, source_target_pairs={{8,0},{16,8},{24,16},{32,24},{40,32},{48,40},{56,48},{64,56},{72,6... | collective-permute-start | bytes 884744 | tf_op jit(solution)/shard_map/ppermute | solution.py:386
  32.8 1.6 %copy-start.2 = (bf16[288,512]{1,0:T(8,128)(2,1)}, bf16[288,512]{1,0:T(8,128)(2,1)S(1)}, u32[]{:S(2)}) copy-start(bf16[288,512]{1,0:T(8,128)(2,1)S(1)} %collective-permute-done.1.next_ref) | copy-start | bytes 884740
  32.8 1.6 %copy-start.1 = (bf16[3,136,512]{2,1,0:T(8,128)(2,1)}, bf16[3,136,512]{2,1,0:T(8,128)(2,1)S(1)}, u32[]{:S(2)}) copy-start(bf16[3,136,512]{2,1,0:T(8,128)(2,1)S(1)} %collective-permute-done.prev_ref) | copy-start | bytes 1253380
  32.8 0.9 copy-start
  85.2 8.6 %all-to-all-start.3 = ((f32[8,10,128]{2,1,0:T(8,128)}), f32[8,10,128]{2,1,0:T(8,128)S(1)}, u32[]{:S(2)}, u32[]{:S(2)}) async-start(f32[8,10,128]{2,1,0:T(8,128)} %broadcast_in_dim.10), calls=%async_computation.3 | async-start | bytes 131072 | tf_op jit(solution)/shard_map/all_to_all | solution.py:372
  105.0 18.7 %all-to-all-start.4 = ((f32[8,2,576]{2,1,0:T(2,128)}), f32[8,2,576]{2,1,0:T(2,128)S(1)}, u32[]{:S(2)}, u32[]{:S(2)}) async-start(f32[8,2,576]{2,1,0:T(2,128)} %broadcast_in_dim.11), calls=%async_computation.4 | async-start | bytes 81920 | tf_op jit(solution)/shard_map/all_to_all | solution.py:372
Sparse Core Ops, SparseCore 0:
  33.8 64.4 all-gather.1

commit v5 on v4

--- a/solution.py
+++ b/solution.py
@@ -81,12 +81,12 @@
     )(x)
 
 
-def hyena_body(
-    feat_ref, prev_ref, next_ref, up_ref, short_ref, long_ref,
-    mixed_ref, gfeat_ref, glong_ref, gshort_ref,
-    x_ref, x1_ref, p_ref, ps_ref, gm_ref, gs_ref, f_ref, gf_ref, wb_ref, gl_ref,
-):
-    turn = pl.program_id(1)
+def hyena_body(feat_ref, prev_ref, next_ref, up_ref, short_ref, long_ref, *refs):
+    (
+        mixed_ref, gfeat_ref, glong_ref, gshort_ref,
+        x_ref, x1_ref, p_ref, ps_ref, gm_ref, gs_ref, f_ref, gf_ref, wb_ref, gl_ref,
+    ) = refs[-14:]
+    turn = pl.program_id(0)
     for slot, g in enumerate((0, 2)):
         x_ref[slot, 0:136] = prev_ref[g].astype(F32)
         x_ref[slot, 136:280] = feat_ref[g].astype(F32)
@@ -167,27 +167,32 @@
             gshort_ref[g, s : s + 1, :] += jnp.sum(column, axis=0, keepdims=True)
 
 
-def hyena(feat, prev, nxt, up, short8, long_taps):
+def hyena(side, feat, prev, nxt, up, short8, long_taps, earlier):
     def cols(*lead):
-        return pl.BlockSpec(lead + (128,), lambda f, k: (0,) * len(lead) + (2 * k + f,))
+        return pl.BlockSpec(lead + (128,), lambda k: (0,) * len(lead) + (2 * k + side,))
 
     def filters(*lead):
-        return pl.BlockSpec(lead + (128,), lambda f, k: (0,) * len(lead) + (f,))
-
+        return pl.BlockSpec(lead + (128,), lambda k: (0,) * len(lead) + (side,))
+
+    def sums(*lead):
+        return pl.BlockSpec(lead + (128,), lambda k: (0,) * (len(lead) + 1))
+
+    kept = pl.BlockSpec(memory_space=pl.ANY)
     return call(
         hyena_body,
         (
             struct((ROWS, 512), BF16),
             struct((3, ROWS, 512), F32),
-            struct((128, 256), F32),
-            struct((3, 8, 256), F32),
+            struct((128, 128), F32),
+            struct((3, 8, 128), F32),
         ),
         "hyena",
-        grid=(2, 2),
+        grid=(2,),
         in_specs=[
             cols(3, ROWS), cols(3, 136), cols(288), cols(ROWS), filters(3, 8), filters(128),
-        ],
-        out_specs=(cols(ROWS), cols(3, ROWS), filters(128), filters(3, 8)),
+        ] + [kept] * len(earlier),
+        out_specs=(cols(ROWS), cols(3, ROWS), sums(128), sums(3, 8)),
+        input_output_aliases={6 + i: i for i in range(len(earlier))},
         scratch_shapes=[
             pltpu.VMEM((2, 288, 128), F32),
             pltpu.VMEM((416, 128), F32),
@@ -200,11 +205,24 @@
             pltpu.VMEM((128, 8, 128), F32),
             pltpu.VMEM((128, 8, 128), F32),
         ],
-    )(feat, prev, nxt, up, short8, long_taps)
-
-
-def half(rows, side):
-    return pl.BlockSpec((rows, 2 * HD), lambda i: (0, side), pipeline_mode=pl.Buffered(1))
+    )(feat, prev, nxt, up, short8, long_taps, *earlier)
+
+
+def assemble(where_ref, pieces, out_ref, step):
+    for t, piece in enumerate(pieces):
+        block = where_ref[0] + step * t
+
+        @pl.when((block >= 0) & (block < len(pieces)))
+        def _():
+            out_ref[pl.ds(pl.multiple_of(block * GROUP, 64), GROUP), :] = piece[...]
+
+    spare = where_ref[0] - step
+
+    @pl.when((spare >= 0) & (spare < len(pieces)))
+    def _():
+        out_ref[pl.ds(pl.multiple_of(spare * GROUP, 64), GROUP), :] = jnp.zeros(
+            (GROUP, 2 * HD), BF16
+        )
 
 
 def lane_max(x):
@@ -221,7 +239,9 @@
     return total
 
 
-def query_body(where_ref, own_ref, kv_ref, out_ref, stat_ref, s_ref, mx_ref, l_ref, o_ref, st_ref):
+def query_body(where_ref, own_ref, *refs):
+    out_ref, stat_ref, s_ref, mx_ref, l_ref, o_ref, st_ref, kv_ref = refs[8:]
+    assemble(where_ref, refs[:8], kv_ref, -1)
     first = where_ref[0] * GROUP
     clear = first // CHUNK
     total = (first + GROUP + CHUNK - 1) // CHUNK
@@ -286,23 +306,22 @@
         query_body,
         (struct((GROUP, 2 * HD), BF16), struct((8, 640), F32)),
         "query_pass",
-        grid=(1,),
-        in_specs=[
-            pl.BlockSpec(memory_space=pltpu.SMEM),
-            half(GROUP, 0),
-            half(SEQ, 1),
-        ],
+        in_specs=[pl.BlockSpec(memory_space=pltpu.SMEM)]
+        + [pl.BlockSpec(memory_space=pltpu.VMEM)] * 9,
         scratch_shapes=[
             pltpu.VMEM((CHUNKS, GROUP, CHUNK), F32),
             pltpu.VMEM((GROUP, HD), F32),
             pltpu.VMEM((GROUP, HD), F32),
             pltpu.VMEM((GROUP, HD), F32),
             pltpu.VMEM((640, HD), F32),
+            pltpu.VMEM((SEQ, 2 * HD), BF16),
         ],
-    )(where, own, kv)
-
-
-def key_body(where_ref, own_ref, qd_ref, stat_ref, oq_ref, part_ref, out_ref, gk_ref, gv_ref):
+    )(where, own, *kv)
+
+
+def key_body(where_ref, own_ref, stat_ref, oq_ref, part_ref, *refs):
+    out_ref, gk_ref, gv_ref, qd_ref = refs[8:]
+    assemble(where_ref, refs[:8], qd_ref, 1)
     first = where_ref[0] * GROUP
     begin = first // CHUNK
     clear = (first + GROUP - 1 + CHUNK - 1) // CHUNK
@@ -352,20 +371,14 @@
         key_body,
         struct((4, ROWS + 40, 4 * HD), BF16),
         "key_pass",
-        cost_estimate=pl.CostEstimate(
-            flops=8 * GROUP * SEQ * HD, transcendentals=GROUP * SEQ, bytes_accessed=16 << 20
-        ),
-        grid=(1,),
-        in_specs=[
-            pl.BlockSpec(memory_space=pltpu.SMEM),
-            half(GROUP, 1),
-            half(SEQ, 0),
-            pl.BlockSpec(memory_space=pltpu.VMEM),
-            pl.BlockSpec(memory_space=pltpu.VMEM),
-            pl.BlockSpec(memory_space=pltpu.VMEM),
+        in_specs=[pl.BlockSpec(memory_space=pltpu.SMEM)]
+        + [pl.BlockSpec(memory_space=pltpu.VMEM)] * 12,
+        scratch_shapes=[
+            pltpu.VMEM((GROUP, HD), F32),
+            pltpu.VMEM((GROUP, HD), F32),
+            pltpu.VMEM((SEQ, 2 * HD), BF16),
         ],
-        scratch_shapes=[pltpu.VMEM((GROUP, HD), F32), pltpu.VMEM((GROUP, HD), F32)],
-    )(where, own, qd, stats, out_q, part)
+    )(where, own, stats, out_q, part, *qd)
 
 
 def exchange(x, axis):
@@ -388,22 +401,46 @@
     where = lax.axis_index("cz").astype(jnp.int32).reshape(1)
     packed = pack(queries, grad_attended, key_vectors, value_vectors)
     own = exchange(packed, "cy").reshape(GROUP, 4 * HD)
-    own, prev, nxt = lax.optimization_barrier((own, prev, nxt))
-    everything = lax.all_gather(own, "cz", axis=0, tiled=True)
+    kv = [own[:, 2 * HD :]]
+    qd = [own[:, : 2 * HD]]
+
+    def step():
+        t = len(kv)
+        kv.append(lax.ppermute(kv[-1], "cz", [(i, i + 1) for i in range(t - 1, 7)]))
+        qd.append(lax.ppermute(qd[-1], "cz", [(i, i - 1) for i in range(1, 9 - t)]))
+
+    def order(*values):
+        held = lax.optimization_barrier((kv[-1], qd[-1]) + values)
+        kv[-1], qd[-1] = held[:2]
+        return held[2:]
 
     short8 = jnp.pad(short_filter, ((0, 0), (0, 1), (0, 0)))
-    mixed, gfeat, glong, gshort = hyena(
-        feat, prev, nxt, after(grad_mixed, own), short8, long_filter_taps
-    )
-    grads = jnp.concatenate([glong, gshort.reshape(24, 256), jnp.zeros((8, 256), F32)], 0)
+    step()
+    prev, nxt = order(prev, nxt)
+    step()
+    first = hyena(0, feat, prev, nxt, grad_mixed, short8, long_filter_taps, ())
+    first = order(*first)
+    step()
+    second = hyena(1, feat, prev, nxt, grad_mixed, short8, long_filter_taps, first[:2])
+    mixed, gfeat, glong, gshort = order(*second)
+    glong = jnp.concatenate([first[2], glong], 1)
+    gshort = jnp.concatenate([first[3], gshort], 2).reshape(24, 256)
+    grads = jnp.concatenate([glong, gshort, jnp.zeros((8, 256), F32)], 0)
+    step()
     part = jnp.sum(exchange(grads.reshape(32, 10, HD), YFT), axis=0)
+    (part,) = order(part)
+    step()
     part = jnp.sum(share(part, "cz", 8), axis=0)
+    (part,) = order(part)
+    step()
     part = share(part, FT, 8)
-
-    out_q, stats = query_pass(where, after(own, part), everything)
+    (part,) = order(part)
+    step()
+
+    out_q, stats = query_pass(where, qd[0], kv)
     stats = share(stats[:2, :GROUP], "cz", 8).transpose(1, 0, 2)
     stats = stats.reshape(2, CHUNKS, CHUNK).transpose(1, 0, 2)
-    result = key_pass(where, own, everything, stats, out_q, part.reshape(80, HD))
+    result = key_pass(where, kv[0], qd, stats, out_q, part.reshape(80, HD))
     attended, grad_queries, grad_keys, grad_values, grads = unpack(exchange(result, "cy"))
     grads = grads.reshape(160, 256)
     grad_long = grads[:128]

time: 162 us -> 186 us (1.15)
  starting transfers between devices: 24.4 us -> 47 us
  blocking collectives: 48.3 us -> 70.8 us
  between operations: 14.1 us -> 1.13 us
  waiting for transfers between devices: 26.7 us -> 19.1 us
  local copies, waits for them, and re-layouts: 10.8 us -> 8.13 us
  Pallas kernels: 35.3 us -> 37.4 us
    all_to_all x3 -> x4, blocking collectives: 48.3 us -> 70.8 us  [exchange(): return lax.all_to_all(x, axis, 0, 0, tiled=True)]
    ppermute x0 -> x14, starting transfers between devices: none -> 17.7 us  [the longest x7 9.04 us: step(): qd.append(lax.ppermute(qd[-1], 'cz', [(i, i - 1) for i in range(1, 9 - t)]))]
    ppermute x1, waiting for transfers between devices: 10.8 us -> 0.01 us  [body(): nxt = lax.ppermute(rim, CTX, [(i + 1, i) for i in range(31)])]
    ppermute x0 -> x14, waiting for transfers between devices: none -> 8.04 us  [the longest x7 8.02 us: step(): qd.append(lax.ppermute(qd[-1], 'cz', [(i, i - 1) for i in range(1, 9 - t)]))]
    all_gather x1 -> x0, waiting for transfers between devices: 4.48 us -> none  [body(): everything = lax.all_gather(own, 'cz', axis=0, tiled=True)]
    all_to_all x3 -> x2, starting transfers between devices: 19.6 us -> 23.5 us  [exchange(): return lax.all_to_all(x, axis, 0, 0, tiled=True)]
    pallas_call x1 -> x2, Pallas kernels: 15.8 us -> 17.6 us  [hyena(): call(hyena_body, (struct((ROWS, 512), BF16), struct((3, ROWS, 512), F32),...]
    all_to_all x3 -> x2, waiting for transfers between devices: 11.4 us -> 11 us  [exchange(): return lax.all_to_all(x, axis, 0, 0, tiled=True)]
  transfers between devices with their start and end apart: 6 -> 18, of which waited for: 4 -> 5; matrix products, arithmetic and copies ran while one was open for 3% -> 3% of each run, Pallas kernels for 11% -> 12%
where the time goes in v5:
time: 186 us; the launch traced here: 185 us
  blocking collectives  70.8 us (38%)
  starting transfers between devices  47 us (25%)
  Pallas kernels  37.4 us (20%)
  waiting for transfers between devices  19.1 us (10%)
  local copies, waits for them, and re-layouts  8.13 us (4%)
    all_to_all x4, blocking collectives, exchange(): return lax.all_to_all(x, axis, 0, 0, tiled=True)  70.8 us
    all_to_all x2, starting transfers between devices, exchange(): return lax.all_to_all(x, axis, 0, 0, tiled=True)  23.5 us
    pallas_call x2, Pallas kernels, hyena(): call(hyena_body, (struct((ROWS, 512), BF16), struct((3, ROWS, 512), F32),...  17.6 us
    all_to_all x2, waiting for transfers between devices, exchange(): return lax.all_to_all(x, axis, 0, 0, tiled=True)  11 us
    pallas_call x1, Pallas kernels, key_pass(): call(key_body, struct((4, ROWS + 40, 4 * HD), BF16), 'key_pass', in_specs...  10.2 us
    ppermute x7, starting transfers between devices, step(): qd.append(lax.ppermute(qd[-1], 'cz', [(i, i - 1) for i in range(1, 9 - t)]))  9.04 us
    ppermute x7, starting transfers between devices, step(): kv.append(lax.ppermute(kv[-1], 'cz', [(i, i + 1) for i in range(t - 1, 7)]))  8.61 us
    ppermute x7, waiting for transfers between devices, step(): qd.append(lax.ppermute(qd[-1], 'cz', [(i, i - 1) for i in range(1, 9 - t)]))  8.02 us
  transfers between devices with their start and end apart: 18, of which 5 were waited for; matrix products, arithmetic and copies ran while one was open for 3% of the time, Pallas kernels for 12%

profile of v5, /device:TPU:2, one launch (start us, length us, event | category | flops | bytes accessed | tf_op | source)
XLA Modules:
  0.0 185.2 jit_solution(316954507974537185)
XLA Ops:
  0.6 2.0 %pack.1 = bf16[4,144,512]{2,1,0:T(8,128)(2,1)} custom-call(bf16[144,512]{1,0:T(8,128)(2,1)} %refs_0_.1, bf16[144,512]{1,0:T(8,128)(2,1)} %refs_1_.1, bf16[144,512]{1,0:T(8,128)(2,1)} %refs_2_.1, bf16[144,512]{1,0:T(8,128)(2,1)} %refs_3_.1), custom_call_target="tpu_custom_call" | custom-call | tf_op jit(solution)/shard_map/pack/pallas_call | solution.py:59
  2.7 4.6 %all-to-all-start = ((bf16[4,144,512]{2,1,0:T(8,128)(2,1)}), bf16[4,144,512]{2,1,0:T(8,128)(2,1)S(1)}, u32[]{:S(2)}, u32[]{:S(2)}) async-start(bf16[4,144,512]{2,1,0:T(8,128)(2,1)} %pack.1), calls=%async_computation | async-start | bytes 1179648 | tf_op jit(solution)/shard_map/all_to_all | solution.py:385
  7.3 0.9 slice-done
  8.2 1.3 collective-permute-start.3
  9.5 4.6 %collective-permute-start.2 = (bf16[3,136,512]{2,1,0:T(8,128)(2,1)S(1)}, bf16[3,136,512]{2,1,0:T(8,128)(2,1)S(1)}, u32[]{:S(2)}, u32[]{:S(2)}) collective-permute-start(bf16[3,136,512]{2,1,0:T(8,128)(2,1)S(1)} %slice.46), channel_id=1, source_target_pairs={{0,8},{8,16},{16,24},{24,32},{32,40},{40,48},{48,56},{56,64},{64,7... | collective-permute-start | bytes 1253384 | tf_op jit(solution)/shard_map/ppermute | solution.py:397
  14.1 3.5 %all-to-all-done = bf16[4,144,512]{2,1,0:T(8,128)(2,1)S(1)} async-done(((bf16[4,144,512]{2,1,0:T(8,128)(2,1)}), bf16[4,144,512]{2,1,0:T(8,128)(2,1)S(1)}, u32[]{:S(2)}, u32[]{:S(2)}) %all-to-all-start) | async-done | bytes 589856 | tf_op jit(solution)/shard_map/all_to_all | solution.py:385
  17.7 1.3 collective-permute-start.1
  19.0 4.6 %collective-permute-start = (bf16[576,256]{1,0:T(8,128)(2,1)S(1)}, bf16[576,256]{1,0:T(8,128)(2,1)S(1)}, u32[]{:S(2)}, u32[]{:S(2)}) collective-permute-start(bf16[576,256]{1,0:T(8,128)(2,1)S(1)} %get-tuple-element.89.refs_0_.own_ref), channel_id=1, source_target_pairs={{0,32},{32,64},{64,96},{96,128},{128,160},{160,192},{192,224},{1,3... | collective-permute-start | bytes 884744 | tf_op jit(solution)/shard_map/ppermute | solution.py:409
  23.6 5.0 %collective-permute-done.1.refs_1_ = bf16[576,256]{1,0:T(8,128)(2,1)S(1)} collective-permute-done((bf16[576,256]{1,0:T(8,128)(2,1)S(1)}, bf16[576,256]{1,0:T(8,128)(2,1)S(1)}, u32[]{:S(2)}, u32[]{:S(2)}) %collective-permute-start.1) | collective-permute-done | bytes 294944 | tf_op jit(solution)/shard_map/ppermute | solution.py:410
  29.3 1.3 collective-permute-start.5
  31.2 8.8 %hyena.2 = (bf16[144,512]{1,0:T(8,128)(2,1)}, f32[3,144,512]{2,1,0:T(8,128)}, f32[128,128]{1,0:T(8,128)}, f32[3,8,128]{2,1,0:T(8,128)}) custom-call(bf16[3,144,512]{2,1,0:T(8,128)(2,1)} %bitcast.19, bf16[3,136,512]{2,1,0:T(8,128)(2,1)} %copy-done.3, bf16[288,512]{1,0:T(8,128)(2,1)} %copy-done.4, bf16[144,512]{1,0:T(8,128)(2,1)} %up_ref.3, ...), custom_call_target="tpu_custom_call" | custom-call | tf_op jit(solution)/shard_map/hyena/pallas_call | solution.py:181
  40.0 1.9 %collective-permute-done.5.refs_2_ = bf16[576,256]{1,0:T(8,128)(2,1)S(1)} collective-permute-done((bf16[576,256]{1,0:T(8,128)(2,1)S(1)}, bf16[576,256]{1,0:T(8,128)(2,1)S(1)}, u32[]{:S(2)}, u32[]{:S(2)}) %collective-permute-start.5) | collective-permute-done | bytes 294944 | tf_op jit(solution)/shard_map/ppermute | solution.py:410
  42.6 1.3 collective-permute-start.7
  44.0 8.8 %hyena.3 = (bf16[144,512]{1,0:T(8,128)(2,1)}, f32[3,144,512]{2,1,0:T(8,128)}, f32[128,128]{1,0:T(8,128)}, f32[3,8,128]{2,1,0:T(8,128)}) custom-call(bf16[3,144,512]{2,1,0:T(8,128)(2,1)} %bitcast.20, bf16[3,136,512]{2,1,0:T(8,128)(2,1)} %copy-done.3, bf16[288,512]{1,0:T(8,128)(2,1)} %copy-done.4, ...), custom_call_target="tpu_custom_call", output_to_operand_aliasing={{0}: (6, {}), {1}: (7, {})} | custom-call | tf_op jit(solution)/shard_map/hyena/pallas_call | solution.py:181
  52.8 1.2 collective-permute-done.7.refs_3_
  54.7 1.3 collective-permute-start.9
  56.7 0.9 maximum_maximum_fusion
  57.7 17.4 %all_to_all.30 = f32[32,10,128]{2,1,0:T(8,128)S(1)} all-to-all(f32[32,10,128]{2,1,0:T(8,128)S(1)} %reshape.46), channel_id=1, replica_groups=mesh['cz'=8,'cy'=4,'fsdp'=4,'tp'=2] {'cy','fsdp','tp'}, dimensions={0} | all-to-all | bytes 327680 | tf_op jit(solution)/shard_map/all_to_all | solution.py:385
  75.9 1.3 collective-permute-start.11
  77.2 30.8 %all_to_all.31 = f32[8,10,128]{2,1,0:T(8,128)S(1)} all-to-all(f32[8,10,128]{2,1,0:T(8,128)S(1)} %broadcast_in_dim.9), channel_id=1, replica_groups=mesh['cz'=8,'cy'=4,'fsdp'=4,'tp'=2] {'cz'}, dimensions={0} | all-to-all | bytes 81920 | tf_op jit(solution)/shard_map/all_to_all | solution.py:385
  108.8 1.3 collective-permute-start.13
  110.1 7.7 %all_to_all.32 = f32[8,10,128]{2,1,0:T(8,128)S(1)} all-to-all(f32[8,10,128]{2,1,0:T(8,128)S(1)} %broadcast_in_dim.10), channel_id=1, replica_groups=mesh['cz'=8,'cy'=4,'fsdp'=4,'tp'=2] {'fsdp','tp'}, dimensions={0} | all-to-all | bytes 81920 | tf_op jit(solution)/shard_map/all_to_all | solution.py:385
  118.5 1.3 collective-permute-start.15
  120.5 5.4 %query_pass.1 = (bf16[576,256]{1,0:T(8,128)(2,1)}, f32[8,640]{1,0:T(8,128)}) custom-call(s32[1]{0:T(128)} %bitcast.5.where_ref, bf16[576,256]{1,0:T(8,128)(2,1)} %copy-done.1, bf16[576,256]{1,0:T(8,128)(2,1)} %copy-done.2, bf16[576,256]{1,0:T(8,128)(2,1)} %copy-done.12, bf16[576,256]{1,0:T(8,128)(2,1)} %copy-done.13, bf16[576,256]{1,0:T(8,128)(2,1)} %copy-done.14, ...), custom_call_target="tpu_custom_call" | custom-call | tf_op jit(solution)/shard_map/query_pass/pallas_call | solution.py:305
  125.9 0.7 slice.40
  127.3 18.9 %all-to-all-start.4 = ((f32[8,2,576]{2,1,0:T(2,128)}), f32[8,2,576]{2,1,0:T(2,128)S(1)}, u32[]{:S(2)}, u32[]{:S(2)}) async-start(f32[8,2,576]{2,1,0:T(2,128)} %broadcast_in_dim.11), calls=%async_computation.4 | async-start | bytes 81920 | tf_op jit(solution)/shard_map/all_to_all | solution.py:385
  146.8 7.5 %all-to-all-done.4 = f32[8,2,576]{2,1,0:T(2,128)S(1)} async-done(((f32[8,2,576]{2,1,0:T(2,128)}), f32[8,2,576]{2,1,0:T(2,128)S(1)}, u32[]{:S(2)}, u32[]{:S(2)}) %all-to-all-start.4) | async-done | bytes 36896 | tf_op jit(solution)/shard_map/all_to_all | solution.py:385
  155.1 0.7 copy-done.11
  155.8 10.2 %key_pass.1 = bf16[4,184,512]{2,1,0:T(8,128)(2,1)} custom-call(s32[1]{0:T(128)} %bitcast.5.where_ref, bf16[576,256]{1,0:T(8,128)(2,1)} %copy-done.2, f32[9,2,512]{2,1,0:T(2,128)} %bitcast.27, bf16[576,256]{1,0:T(8,128)(2,1)} %get-tuple-element.79.oq_ref, f32[80,128]{1,0:T(8,128)} %reshape.48.part_ref, bf16[576,256]{1,0:T(8,128)(2,1)} %copy-done.1, ...), custom_call_target="tpu_custom_call" | custom-call | tf_op jit(solution)/shard_map/key_pass/pallas_call | solution.py:370
  166.0 14.8 %all_to_all.33.x_ref = bf16[4,184,512]{2,1,0:T(8,128)(2,1)} all-to-all(bf16[4,184,512]{2,1,0:T(8,128)(2,1)} %key_pass.1), channel_id=1, replica_groups=mesh['cz'=8,'cy'=4,'fsdp'=4,'tp'=2] {'cy'}, dimensions={0} | all-to-all | bytes 1507328 | tf_op jit(solution)/shard_map/all_to_all | solution.py:385
  180.8 2.2 %unpack.1 = (bf16[144,512]{1,0:T(8,128)(2,1)}, f32[144,512]{1,0:T(8,128)}, f32[144,512]{1,0:T(8,128)}, f32[144,512]{1,0:T(8,128)}, f32[4,80,128]{2,1,0:T(8,128)}) custom-call(bf16[4,184,512]{2,1,0:T(8,128)(2,1)} %all_to_all.33.x_ref), custom_call_target="tpu_custom_call" | custom-call | tf_op jit(solution)/shard_map/unpack/pallas_call | solution.py:77
  183.0 1.0 reshape.49
  (84 shorter events, 9.7 us)
Async XLA Ops:
  2.7 15.0 %all-to-all-start = ((bf16[4,144,512]{2,1,0:T(8,128)(2,1)}), bf16[4,144,512]{2,1,0:T(8,128)(2,1)S(1)}, u32[]{:S(2)}, u32[]{:S(2)}) async-start(bf16[4,144,512]{2,1,0:T(8,128)(2,1)} %pack.1), calls=%async_computation | async-start | bytes 1179648 | tf_op jit(solution)/shard_map/all_to_all | solution.py:385
  8.2 15.4 %collective-permute-start.3 = (bf16[288,512]{1,0:T(8,128)(2,1)S(1)}, bf16[288,512]{1,0:T(8,128)(2,1)S(1)}, u32[]{:S(2)}, u32[]{:S(2)}) collective-permute-start(bf16[288,512]{1,0:T(8,128)(2,1)S(1)} %pad_maximum_fusion), channel_id=1, source_target_pairs={{8,0},{16,8},{24,16},{32,24},{40,32},{48,40},{56,48},{64,56},{72,6... | collective-permute-start | bytes 884744 | tf_op jit(solution)/shard_map/ppermute | solution.py:399
  9.5 14.1 %collective-permute-start.2 = (bf16[3,136,512]{2,1,0:T(8,128)(2,1)S(1)}, bf16[3,136,512]{2,1,0:T(8,128)(2,1)S(1)}, u32[]{:S(2)}, u32[]{:S(2)}) collective-permute-start(bf16[3,136,512]{2,1,0:T(8,128)(2,1)S(1)} %slice.46), channel_id=1, source_target_pairs={{0,8},{8,16},{16,24},{24,32},{32,40},{40,48},{48,56},{56,64},{64,7... | collective-permute-start | bytes 1253384 | tf_op jit(solution)/shard_map/ppermute | solution.py:397
  17.7 12.9 %copy-start.20 = (f32[3,7,256]{2,1,0:T(8,128)S(1)}, f32[3,7,256]{2,1,0:T(8,128)}, u32[]{:S(2)}) copy-start(f32[3,7,256]{2,1,0:T(8,128)} %param.9) | copy-start | bytes 64516
  17.7 22.3 %copy-start.1 = (bf16[576,256]{1,0:T(8,128)(2,1)}, bf16[576,256]{1,0:T(8,128)(2,1)S(1)}, u32[]{:S(2)}) copy-start(bf16[576,256]{1,0:T(8,128)(2,1)S(1)} %get-tuple-element.88.own_ref.refs_0_) | copy-start | bytes 884740
  17.7 22.3 %copy-start.2 = (bf16[576,256]{1,0:T(8,128)(2,1)}, bf16[576,256]{1,0:T(8,128)(2,1)S(1)}, u32[]{:S(2)}) copy-start(bf16[576,256]{1,0:T(8,128)(2,1)S(1)} %get-tuple-element.89.refs_0_.own_ref) | copy-start | bytes 884740
  17.7 10.9 %collective-permute-start.1 = (bf16[576,256]{1,0:T(8,128)(2,1)S(1)}, bf16[576,256]{1,0:T(8,128)(2,1)S(1)}, u32[]{:S(2)}, u32[]{:S(2)}) collective-permute-start(bf16[576,256]{1,0:T(8,128)(2,1)S(1)} %get-tuple-element.88.own_ref.refs_0_), channel_id=1, source_target_pairs={{32,0},{64,32},{96,64},{128,96},{160,128},{192,160},{224,192},{33,... | collective-permute-start | bytes 884744 | tf_op jit(solution)/shard_map/ppermute | solution.py:410
  19.0 9.6 %collective-permute-start = (bf16[576,256]{1,0:T(8,128)(2,1)S(1)}, bf16[576,256]{1,0:T(8,128)(2,1)S(1)}, u32[]{:S(2)}, u32[]{:S(2)}) collective-permute-start(bf16[576,256]{1,0:T(8,128)(2,1)S(1)} %get-tuple-element.89.refs_0_.own_ref), channel_id=1, source_target_pairs={{0,32},{32,64},{64,96},{96,128},{128,160},{160,192},{192,224},{1,3... | collective-permute-start | bytes 884744 | tf_op jit(solution)/shard_map/ppermute | solution.py:409
  28.6 11.4 %copy-start.5 = (bf16[576,256]{1,0:T(8,128)(2,1)}, bf16[576,256]{1,0:T(8,128)(2,1)S(1)}, u32[]{:S(2)}) copy-start(bf16[576,256]{1,0:T(8,128)(2,1)S(1)} %collective-permute-done.1.refs_1_) | copy-start | bytes 884740
  28.6 11.4 %copy-start.12 = (bf16[576,256]{1,0:T(8,128)(2,1)}, bf16[576,256]{1,0:T(8,128)(2,1)S(1)}, u32[]{:S(2)}) copy-start(bf16[576,256]{1,0:T(8,128)(2,1)S(1)} %collective-permute-done.refs_1_) | copy-start | bytes 884740
  28.6 11.4 %collective-permute-start.4 = (bf16[576,256]{1,0:T(8,128)(2,1)S(1)}, bf16[576,256]{1,0:T(8,128)(2,1)S(1)}, u32[]{:S(2)}, u32[]{:S(2)}) collective-permute-start(bf16[576,256]{1,0:T(8,128)(2,1)S(1)} %collective-permute-done.refs_1_), channel_id=1, source_target_pairs={{32,64},{64,96},{96,128},{128,160},{160,192},{192,224},{33,65},{65... | collective-permute-start | bytes 884744 | tf_op jit(solution)/shard_map/ppermute | solution.py:409
  29.3 12.6 %collective-permute-start.5 = (bf16[576,256]{1,0:T(8,128)(2,1)S(1)}, bf16[576,256]{1,0:T(8,128)(2,1)S(1)}, u32[]{:S(2)}, u32[]{:S(2)}) collective-permute-start(bf16[576,256]{1,0:T(8,128)(2,1)S(1)} %collective-permute-done.1.refs_1_), channel_id=1, source_target_pairs={{32,0},{64,32},{96,64},{128,96},{160,128},{192,160},{33,1},{65,33}... | collective-permute-start | bytes 884744 | tf_op jit(solution)/shard_map/ppermute | solution.py:410
  40.0 12.8 %copy-start.13 = (bf16[576,256]{1,0:T(8,128)(2,1)}, bf16[576,256]{1,0:T(8,128)(2,1)S(1)}, u32[]{:S(2)}) copy-start(bf16[576,256]{1,0:T(8,128)(2,1)S(1)} %collective-permute-done.4.refs_2_) | copy-start | bytes 884740
  41.9 10.9 %copy-start.6 = (bf16[576,256]{1,0:T(8,128)(2,1)}, bf16[576,256]{1,0:T(8,128)(2,1)S(1)}, u32[]{:S(2)}) copy-start(bf16[576,256]{1,0:T(8,128)(2,1)S(1)} %collective-permute-done.5.refs_2_) | copy-start | bytes 884740
  41.9 10.9 %collective-permute-start.6 = (bf16[576,256]{1,0:T(8,128)(2,1)S(1)}, bf16[576,256]{1,0:T(8,128)(2,1)S(1)}, u32[]{:S(2)}, u32[]{:S(2)}) collective-permute-start(bf16[576,256]{1,0:T(8,128)(2,1)S(1)} %collective-permute-done.4.refs_2_), channel_id=1, source_target_pairs={{64,96},{96,128},{128,160},{160,192},{192,224},{65,97},{97,129},{1... | collective-permute-start | bytes 884744 | tf_op jit(solution)/shard_map/ppermute | solution.py:409
  42.6 11.4 %collective-permute-start.7 = (bf16[576,256]{1,0:T(8,128)(2,1)S(1)}, bf16[576,256]{1,0:T(8,128)(2,1)S(1)}, u32[]{:S(2)}, u32[]{:S(2)}) collective-permute-start(bf16[576,256]{1,0:T(8,128)(2,1)S(1)} %collective-permute-done.5.refs_2_), channel_id=1, source_target_pairs={{32,0},{64,32},{96,64},{128,96},{160,128},{33,1},{65,33},{97,65},{... | collective-permute-start | bytes 884744 | tf_op jit(solution)/shard_map/ppermute | solution.py:410
  44.0 12.0 %copy-start.21 = (f32[3,8,128]{2,1,0:T(8,128)S(1)}, f32[3,8,128]{2,1,0:T(8,128)}, u32[]{:S(2)}) copy-start(f32[3,8,128]{2,1,0:T(8,128)} %get-tuple-element.69) | copy-start | bytes 36868
  44.0 12.7 %copy-start.19 = (f32[128,128]{1,0:T(8,128)S(1)}, f32[128,128]{1,0:T(8,128)}, u32[]{:S(2)}) copy-start(f32[128,128]{1,0:T(8,128)} %get-tuple-element.67) | copy-start | bytes 196612
  54.0 21.2 %collective-permute-start.8 = (bf16[576,256]{1,0:T(8,128)(2,1)S(1)}, bf16[576,256]{1,0:T(8,128)(2,1)S(1)}, u32[]{:S(2)}, u32[]{:S(2)}) collective-permute-start(bf16[576,256]{1,0:T(8,128)(2,1)S(1)} %collective-permute-done.6.refs_3_), channel_id=1, source_target_pairs={{96,128},{128,160},{160,192},{192,224},{97,129},{129,161},{161,193... | collective-permute-start | bytes 884744 | tf_op jit(solution)/shard_map/ppermute | solution.py:409
  54.7 20.5 %collective-permute-start.9 = (bf16[576,256]{1,0:T(8,128)(2,1)S(1)}, bf16[576,256]{1,0:T(8,128)(2,1)S(1)}, u32[]{:S(2)}, u32[]{:S(2)}) collective-permute-start(bf16[576,256]{1,0:T(8,128)(2,1)S(1)} %collective-permute-done.7.refs_3_), channel_id=1, source_target_pairs={{32,0},{64,32},{96,64},{128,96},{33,1},{65,33},{97,65},{129,97},{3... | collective-permute-start | bytes 884744 | tf_op jit(solution)/shard_map/ppermute | solution.py:410
  75.2 44.7 %copy-start.15 = (bf16[576,256]{1,0:T(8,128)(2,1)}, bf16[576,256]{1,0:T(8,128)(2,1)S(1)}, u32[]{:S(2)}) copy-start(bf16[576,256]{1,0:T(8,128)(2,1)S(1)} %collective-permute-done.8.refs_4_) | copy-start | bytes 884740
  75.2 50.7 %copy-start.8 = (bf16[576,256]{1,0:T(8,128)(2,1)}, bf16[576,256]{1,0:T(8,128)(2,1)S(1)}, u32[]{:S(2)}) copy-start(bf16[576,256]{1,0:T(8,128)(2,1)S(1)} %collective-permute-done.9.refs_4_) | copy-start | bytes 884740
  75.2 32.8 %collective-permute-start.10 = (bf16[576,256]{1,0:T(8,128)(2,1)S(1)}, bf16[576,256]{1,0:T(8,128)(2,1)S(1)}, u32[]{:S(2)}, u32[]{:S(2)}) collective-permute-start(bf16[576,256]{1,0:T(8,128)(2,1)S(1)} %collective-permute-done.8.refs_4_), channel_id=1, source_target_pairs={{128,160},{160,192},{192,224},{129,161},{161,193},{193,225},{130,1... | collective-permute-start | bytes 884744 | tf_op jit(solution)/shard_map/ppermute | solution.py:409
  75.9 32.2 %collective-permute-start.11 = (bf16[576,256]{1,0:T(8,128)(2,1)S(1)}, bf16[576,256]{1,0:T(8,128)(2,1)S(1)}, u32[]{:S(2)}, u32[]{:S(2)}) collective-permute-start(bf16[576,256]{1,0:T(8,128)(2,1)S(1)} %collective-permute-done.9.refs_4_), channel_id=1, source_target_pairs={{32,0},{64,32},{96,64},{33,1},{65,33},{97,65},{34,2},{66,34},{98,6... | collective-permute-start | bytes 884744 | tf_op jit(solution)/shard_map/ppermute | solution.py:410
  108.0 11.8 %copy-start.16 = (bf16[576,256]{1,0:T(8,128)(2,1)}, bf16[576,256]{1,0:T(8,128)(2,1)S(1)}, u32[]{:S(2)}) copy-start(bf16[576,256]{1,0:T(8,128)(2,1)S(1)} %collective-permute-done.10.refs_5_) | copy-start | bytes 884740
  108.1 17.9 %copy-start.9 = (bf16[576,256]{1,0:T(8,128)(2,1)}, bf16[576,256]{1,0:T(8,128)(2,1)S(1)}, u32[]{:S(2)}) copy-start(bf16[576,256]{1,0:T(8,128)(2,1)S(1)} %collective-permute-done.11.refs_5_) | copy-start | bytes 884740
  108.1 9.7 %collective-permute-start.12 = (bf16[576,256]{1,0:T(8,128)(2,1)S(1)}, bf16[576,256]{1,0:T(8,128)(2,1)S(1)}, u32[]{:S(2)}, u32[]{:S(2)}) collective-permute-start(bf16[576,256]{1,0:T(8,128)(2,1)S(1)} %collective-permute-done.10.refs_5_), channel_id=1, source_target_pairs={{160,192},{192,224},{161,193},{193,225},{162,194},{194,226},{163,1... | collective-permute-start | bytes 884744 | tf_op jit(solution)/shard_map/ppermute | solution.py:409
  108.8 9.0 %collective-permute-start.13 = (bf16[576,256]{1,0:T(8,128)(2,1)S(1)}, bf16[576,256]{1,0:T(8,128)(2,1)S(1)}, u32[]{:S(2)}, u32[]{:S(2)}) collective-permute-start(bf16[576,256]{1,0:T(8,128)(2,1)S(1)} %collective-permute-done.11.refs_5_), channel_id=1, source_target_pairs={{32,0},{64,32},{33,1},{65,33},{34,2},{66,34},{35,3},{67,35},{36,4}... | collective-permute-start | bytes 884744 | tf_op jit(solution)/shard_map/ppermute | solution.py:410
  117.8 8.1 %copy-start.10 = (bf16[576,256]{1,0:T(8,128)(2,1)}, bf16[576,256]{1,0:T(8,128)(2,1)S(1)}, u32[]{:S(2)}) copy-start(bf16[576,256]{1,0:T(8,128)(2,1)S(1)} %collective-permute-done.13.refs_6_) | copy-start | bytes 884740
  117.8 2.0 %collective-permute-start.14 = (bf16[576,256]{1,0:T(8,128)(2,1)S(1)}, bf16[576,256]{1,0:T(8,128)(2,1)S(1)}, u32[]{:S(2)}, u32[]{:S(2)}) collective-permute-start(bf16[576,256]{1,0:T(8,128)(2,1)S(1)} %collective-permute-done.12.refs_6_), channel_id=1, source_target_pairs={{192,224},{193,225},{194,226},{195,227},{196,228},{197,229},{198,2... | collective-permute-start | bytes 884744 | tf_op jit(solution)/shard_map/ppermute | solution.py:409
  118.5 36.6 %collective-permute-start.15 = (bf16[576,256]{1,0:T(8,128)(2,1)S(1)}, bf16[576,256]{1,0:T(8,128)(2,1)S(1)}, u32[]{:S(2)}, u32[]{:S(2)}) collective-permute-start(bf16[576,256]{1,0:T(8,128)(2,1)S(1)} %collective-permute-done.13.refs_6_), channel_id=1, source_target_pairs={{32,0},{33,1},{34,2},{35,3},{36,4},{37,5},{38,6},{39,7},{40,8},{41... | collective-permute-start | bytes 884744 | tf_op jit(solution)/shard_map/ppermute | solution.py:410
  127.3 27.0 %all-to-all-start.4 = ((f32[8,2,576]{2,1,0:T(2,128)}), f32[8,2,576]{2,1,0:T(2,128)S(1)}, u32[]{:S(2)}, u32[]{:S(2)}) async-start(f32[8,2,576]{2,1,0:T(2,128)} %broadcast_in_dim.11), calls=%async_computation.4 | async-start | bytes 81920 | tf_op jit(solution)/shard_map/all_to_all | solution.py:385
  (9 other events, 32.7 us)

commit v6 on v5

--- a/solution.py
+++ b/solution.py
@@ -86,7 +86,6 @@
         mixed_ref, gfeat_ref, glong_ref, gshort_ref,
         x_ref, x1_ref, p_ref, ps_ref, gm_ref, gs_ref, f_ref, gf_ref, wb_ref, gl_ref,
     ) = refs[-14:]
-    turn = pl.program_id(0)
     for slot, g in enumerate((0, 2)):
         x_ref[slot, 0:136] = prev_ref[g].astype(F32)
         x_ref[slot, 136:280] = feat_ref[g].astype(F32)
@@ -141,17 +140,8 @@
     gp = lax.fori_loop(0, 16, backward, jnp.zeros((19, 8, 128), F32)).reshape(152, 128)
     gf_ref[0] = gp * f_ref[2]
     gf_ref[2] = gp * f_ref[0]
-    glong = jnp.sum(gl_ref[...], axis=1)
-
-    @pl.when(turn == 0)
-    def _():
-        glong_ref[...] = glong
-        gshort_ref[...] = jnp.zeros_like(gshort_ref)
-
-    @pl.when(turn != 0)
-    def _():
-        glong_ref[...] += glong
-
+    glong_ref[...] = jnp.sum(gl_ref[...], axis=1)
+    gshort_ref[...] = jnp.zeros_like(gshort_ref)
     for g in range(3):
         total = taps[g][0] * gf_ref[g, 0:144]
         for s in range(1, 7):
@@ -164,15 +154,15 @@
             else:
                 x = x_ref[g // 2, 136 - s : 280 - s]
             column = jnp.sum((own * x).reshape(18, 8, 128), axis=0)
-            gshort_ref[g, s : s + 1, :] += jnp.sum(column, axis=0, keepdims=True)
-
-
-def hyena(side, feat, prev, nxt, up, short8, long_taps, earlier):
+            gshort_ref[g, s : s + 1, :] = jnp.sum(column, axis=0, keepdims=True)
+
+
+def hyena(tile, feat, prev, nxt, up, short8, long_taps, earlier):
     def cols(*lead):
-        return pl.BlockSpec(lead + (128,), lambda k: (0,) * len(lead) + (2 * k + side,))
+        return pl.BlockSpec(lead + (128,), lambda k: (0,) * len(lead) + (tile,))
 
     def filters(*lead):
-        return pl.BlockSpec(lead + (128,), lambda k: (0,) * len(lead) + (side,))
+        return pl.BlockSpec(lead + (128,), lambda k: (0,) * len(lead) + (tile % 2,))
 
     def sums(*lead):
         return pl.BlockSpec(lead + (128,), lambda k: (0,) * (len(lead) + 1))
@@ -187,7 +177,7 @@
             struct((3, 8, 128), F32),
         ),
         "hyena",
-        grid=(2,),
+        grid=(1,),
         in_specs=[
             cols(3, ROWS), cols(3, 136), cols(288), cols(ROWS), filters(3, 8), filters(128),
         ] + [kept] * len(earlier),
@@ -319,7 +309,7 @@
     )(where, own, *kv)
 
 
-def key_body(where_ref, own_ref, stat_ref, oq_ref, part_ref, *refs):
+def key_body(where_ref, own_ref, stat_ref, *refs):
     out_ref, gk_ref, gv_ref, qd_ref = refs[8:]
     assemble(where_ref, refs[:8], qd_ref, 1)
     first = where_ref[0] * GROUP
@@ -353,11 +343,15 @@
     def _(c):
         visit(c, False)
 
+    out_ref[:, :HD] = (gk_ref[...] * SCALE).astype(BF16)
+    out_ref[:, HD:] = gv_ref[...].astype(BF16)
+
+
+def join_body(oq_ref, ok_ref, part_ref, out_ref):
     for j in range(4):
         at = slice(j * ROWS, (j + 1) * ROWS)
         out_ref[j, :ROWS, : 2 * HD] = oq_ref[at]
-        out_ref[j, :ROWS, 2 * HD : 3 * HD] = (gk_ref[at] * SCALE).astype(BF16)
-        out_ref[j, :ROWS, 3 * HD :] = gv_ref[at].astype(BF16)
+        out_ref[j, :ROWS, 2 * HD :] = ok_ref[at]
         for side in range(2):
             value = part_ref[side * 40 : (side + 1) * 40]
             high = value.astype(BF16)
@@ -366,19 +360,23 @@
             out_ref[j, ROWS:, (side + 2) * HD : (side + 3) * HD] = low
 
 
-def key_pass(where, own, qd, stats, out_q, part):
+def join(out_q, out_k, part):
+    return call(join_body, struct((4, ROWS + 40, 4 * HD), BF16), "join")(out_q, out_k, part)
+
+
+def key_pass(where, own, qd, stats):
     return call(
         key_body,
-        struct((4, ROWS + 40, 4 * HD), BF16),
+        struct((GROUP, 2 * HD), BF16),
         "key_pass",
         in_specs=[pl.BlockSpec(memory_space=pltpu.SMEM)]
-        + [pl.BlockSpec(memory_space=pltpu.VMEM)] * 12,
+        + [pl.BlockSpec(memory_space=pltpu.VMEM)] * 10,
         scratch_shapes=[
             pltpu.VMEM((GROUP, HD), F32),
             pltpu.VMEM((GROUP, HD), F32),
             pltpu.VMEM((SEQ, 2 * HD), BF16),
         ],
-    )(where, own, stats, out_q, part, *qd)
+    )(where, own, stats, *qd)
 
 
 def exchange(x, axis):
@@ -393,17 +391,18 @@
     features, short_filter, long_filter_taps, queries, key_vectors, value_vectors,
     grad_mixed, grad_attended,
 ):
-    feat = features.transpose(1, 0, 2)
-    prev = lax.ppermute(feat[:, 8:], CTX, [(i, i + 1) for i in range(31)])
-    rim = jnp.concatenate([feat[1, :136], grad_mixed[:136], feat[0, :8], feat[2, :8]], 0)
-    nxt = lax.ppermute(rim, CTX, [(i + 1, i) for i in range(31)])
-
     where = lax.axis_index("cz").astype(jnp.int32).reshape(1)
     packed = pack(queries, grad_attended, key_vectors, value_vectors)
     own = exchange(packed, "cy").reshape(GROUP, 4 * HD)
     kv = [own[:, 2 * HD :]]
     qd = [own[:, : 2 * HD]]
 
+    features, upstream = after(features, own), after(grad_mixed, own)
+    feat = features.transpose(1, 0, 2)
+    prev = lax.ppermute(feat[:, 8:], CTX, [(i, i + 1) for i in range(31)])
+    rim = jnp.concatenate([feat[1, :136], upstream[:136], feat[0, :8], feat[2, :8]], 0)
+    nxt = lax.ppermute(rim, CTX, [(i + 1, i) for i in range(31)])
+
     def step():
         t = len(kv)
         kv.append(lax.ppermute(kv[-1], "cz", [(i, i + 1) for i in range(t - 1, 7)]))
@@ -417,30 +416,38 @@
     short8 = jnp.pad(short_filter, ((0, 0), (0, 1), (0, 0)))
     step()
     prev, nxt = order(prev, nxt)
+    kept = ()
+    glong, gshort = [], []
+    for tile in range(4):
+        step()
+        done = hyena(tile, feat, prev, nxt, upstream, short8, long_filter_taps, kept)
+        done = order(*done)
+        kept = done[:2]
+        glong.append(done[2])
+        gshort.append(done[3].reshape(24, HD))
+    mixed, gfeat = kept
+    grads = jnp.concatenate(
+        [
+            jnp.concatenate([glong[0] + glong[2], glong[1] + glong[3]], 1),
+            jnp.concatenate([gshort[0] + gshort[2], gshort[1] + gshort[3]], 1),
+            jnp.zeros((8, 256), F32),
+        ],
+        0,
+    )
+    part = jnp.sum(exchange(grads.reshape(32, 10, HD), YFT), axis=0)
     step()
-    first = hyena(0, feat, prev, nxt, grad_mixed, short8, long_filter_taps, ())
-    first = order(*first)
+    order()
     step()
-    second = hyena(1, feat, prev, nxt, grad_mixed, short8, long_filter_taps, first[:2])
-    mixed, gfeat, glong, gshort = order(*second)
-    glong = jnp.concatenate([first[2], glong], 1)
-    gshort = jnp.concatenate([first[3], gshort], 2).reshape(24, 256)
-    grads = jnp.concatenate([glong, gshort, jnp.zeros((8, 256), F32)], 0)
-    step()
-    part = jnp.sum(exchange(grads.reshape(32, 10, HD), YFT), axis=0)
-    (part,) = order(part)
-    step()
-    part = jnp.sum(share(part, "cz", 8), axis=0)
-    (part,) = order(part)
-    step()
-    part = share(part, FT, 8)
-    (part,) = order(part)
-    step()
+    order()
 
     out_q, stats = query_pass(where, qd[0], kv)
-    stats = share(stats[:2, :GROUP], "cz", 8).transpose(1, 0, 2)
+    small = jnp.concatenate([stats[:2].reshape(10, HD), part], 0)
+    small = share(small, "cz", 8)
+    part = share(jnp.sum(small[:, 10:], axis=0), FT, 8)
+    stats = small[:, :10].reshape(8, 2, 640)[:, :, :GROUP].transpose(1, 0, 2)
     stats = stats.reshape(2, CHUNKS, CHUNK).transpose(1, 0, 2)
-    result = key_pass(where, kv[0], qd, stats, out_q, part.reshape(80, HD))
+    out_k = key_pass(where, kv[0], qd, stats)
+    result = join(out_q, out_k, part.reshape(80, HD))
     attended, grad_queries, grad_keys, grad_values, grads = unpack(exchange(result, "cy"))
     grads = grads.reshape(160, 256)
     grad_long = grads[:128]

time: 186 us -> 178 us (0.957)
  blocking collectives: 70.8 us -> 45.4 us
  waiting for transfers between devices: 19.1 us -> 42.9 us
  starting transfers between devices: 47 us -> 35.2 us
  Pallas kernels: 37.4 us -> 42 us
    ppermute x7, waiting for transfers between devices: 8.02 us -> 34.7 us  [step(): qd.append(lax.ppermute(qd[-1], 'cz', [(i, i - 1) for i in range(1, 9 - t)]))]
    all_to_all x4 -> x3, blocking collectives: 70.8 us -> 45.4 us  [exchange(): return lax.all_to_all(x, axis, 0, 0, tiled=True)]
    all_to_all x2, starting transfers between devices: 23.5 us -> 9.76 us  [exchange(): return lax.all_to_all(x, axis, 0, 0, tiled=True)]
    ppermute x7, starting transfers between devices: 8.61 us -> 12.7 us  [step(): kv.append(lax.ppermute(kv[-1], 'cz', [(i, i + 1) for i in range(t - 1, 7)]))]
    pallas_call x2 -> x4, Pallas kernels: 17.6 us -> 20.5 us  [hyena(): call(hyena_body, (struct((ROWS, 512), BF16), struct((3, ROWS, 512), F32),...]
    all_to_all x2, waiting for transfers between devices: 11 us -> 8.13 us  [exchange(): return lax.all_to_all(x, axis, 0, 0, tiled=True)]
    ppermute x1, starting transfers between devices: 4.58 us -> 2.49 us  [body(): prev = lax.ppermute(feat[:, 8:], CTX, [(i, i + 1) for i in range(31)])]
    pallas_call x1 -> x2, Pallas kernels: 10.2 us -> 11.9 us  [the longest x1 9.87 us: key_pass(): call(key_body, struct((GROUP, 2 * HD), BF16), 'key_pass', in_specs=[pl.Bl...]
  transfers between devices with their start and end apart: 18 -> 18, of which waited for: 5 -> 7; matrix products, arithmetic and copies ran while one was open for 3% -> 1% of each run, Pallas kernels for 12% -> 17%
where the time goes in v6:
time: 178 us; the launch traced here: 177 us
  blocking collectives  45.4 us (26%)
  waiting for transfers between devices  42.9 us (24%)
  Pallas kernels  42 us (24%)
  starting transfers between devices  35.2 us (20%)
  local copies, waits for them, and re-layouts  9.76 us (5%)
    all_to_all x3, blocking collectives, exchange(): return lax.all_to_all(x, axis, 0, 0, tiled=True)  45.4 us
    ppermute x7, waiting for transfers between devices, step(): qd.append(lax.ppermute(qd[-1], 'cz', [(i, i - 1) for i in range(1, 9 - t)]))  34.7 us
    pallas_call x4, Pallas kernels, hyena(): call(hyena_body, (struct((ROWS, 512), BF16), struct((3, ROWS, 512), F32),...  20.5 us
    ppermute x7, starting transfers between devices, step(): kv.append(lax.ppermute(kv[-1], 'cz', [(i, i + 1) for i in range(t - 1, 7)]))  12.7 us
    pallas_call x1, Pallas kernels, key_pass(): call(key_body, struct((GROUP, 2 * HD), BF16), 'key_pass', in_specs=[pl.Bl...  9.87 us
    all_to_all x2, starting transfers between devices, exchange(): return lax.all_to_all(x, axis, 0, 0, tiled=True)  9.76 us
    ppermute x7, starting transfers between devices, step(): qd.append(lax.ppermute(qd[-1], 'cz', [(i, i - 1) for i in range(1, 9 - t)]))  9.04 us
    all_to_all x2, waiting for transfers between devices, exchange(): return lax.all_to_all(x, axis, 0, 0, tiled=True)  8.13 us
  transfers between devices with their start and end apart: 18, of which 7 were waited for; matrix products, arithmetic and copies ran while one was open for 1% of the time, Pallas kernels for 17%

profile of v6, /device:TPU:2, one launch (start us, length us, event | category | flops | bytes accessed | tf_op | source)
XLA Modules:
  0.0 176.6 jit_solution(2027529471789438850)
XLA Ops:
  0.6 2.0 %pack.1 = bf16[4,144,512]{2,1,0:T(8,128)(2,1)} custom-call(bf16[144,512]{1,0:T(8,128)(2,1)} %refs_0_.1, bf16[144,512]{1,0:T(8,128)(2,1)} %refs_1_.1, bf16[144,512]{1,0:T(8,128)(2,1)} %refs_2_.1, bf16[144,512]{1,0:T(8,128)(2,1)} %refs_3_.1), custom_call_target="tpu_custom_call" | custom-call | tf_op jit(solution)/shard_map/pack/pallas_call | solution.py:59
  2.7 14.8 %all_to_all.25 = bf16[4,144,512]{2,1,0:T(8,128)(2,1)S(1)} all-to-all(bf16[4,144,512]{2,1,0:T(8,128)(2,1)} %pack.1), channel_id=1, replica_groups=mesh['cz'=8,'cy'=4,'fsdp'=4,'tp'=2] {'cy'}, dimensions={0} | all-to-all | bytes 1179648 | tf_op jit(solution)/shard_map/all_to_all | solution.py:383
  17.6 2.5 %collective-permute-start.2 = (bf16[3,136,512]{2,1,0:T(8,128)(2,1)S(1)}, bf16[3,136,512]{2,1,0:T(8,128)(2,1)S(1)}, u32[]{:S(2)}, u32[]{:S(2)}) collective-permute-start(bf16[3,136,512]{2,1,0:T(8,128)(2,1)S(1)} %slice.58), channel_id=1, source_target_pairs={{0,8},{8,16},{16,24},{24,32},{32,40},{40,48},{48,56},{56,64},{64,7... | collective-permute-start | bytes 1253384 | tf_op jit(solution)/shard_map/ppermute | solution.py:402
  21.0 1.3 collective-permute-start.3
  22.3 1.3 collective-permute-start.1
  23.6 8.6 %collective-permute-start = (bf16[576,256]{1,0:T(8,128)(2,1)S(1)}, bf16[576,256]{1,0:T(8,128)(2,1)S(1)}, u32[]{:S(2)}, u32[]{:S(2)}) collective-permute-start(bf16[576,256]{1,0:T(8,128)(2,1)S(1)} %get-tuple-element.123.refs_0_.own_ref), channel_id=1, source_target_pairs={{0,32},{32,64},{64,96},{96,128},{128,160},{160,192},{192,224},{1,3... | collective-permute-start | bytes 884744 | tf_op jit(solution)/shard_map/ppermute | solution.py:408
  32.3 7.4 %collective-permute-done.1.refs_1_ = bf16[576,256]{1,0:T(8,128)(2,1)S(1)} collective-permute-done((bf16[576,256]{1,0:T(8,128)(2,1)S(1)}, bf16[576,256]{1,0:T(8,128)(2,1)S(1)}, u32[]{:S(2)}, u32[]{:S(2)}) %collective-permute-start.1) | collective-permute-done | bytes 294944 | tf_op jit(solution)/shard_map/ppermute | solution.py:409
  40.4 1.3 collective-permute-start.5
  42.3 5.1 %hyena.4 = (bf16[144,512]{1,0:T(8,128)(2,1)}, f32[3,144,512]{2,1,0:T(8,128)}, f32[128,128]{1,0:T(8,128)}, f32[3,8,128]{2,1,0:T(8,128)}) custom-call(bf16[3,144,512]{2,1,0:T(8,128)(2,1)} %bitcast.22, bf16[3,136,512]{2,1,0:T(8,128)(2,1)} %copy-done.1, bf16[288,512]{1,0:T(8,128)(2,1)} %copy-done.2, bf16[144,512]{1,0:T(8,128)(2,1)} %up_ref.3, ...), custom_call_target="tpu_custom_call" | custom-call | tf_op jit(solution)/shard_map/hyena/pallas_call | solution.py:171
  47.4 4.6 %collective-permute-done.5.refs_2_ = bf16[576,256]{1,0:T(8,128)(2,1)S(1)} collective-permute-done((bf16[576,256]{1,0:T(8,128)(2,1)S(1)}, bf16[576,256]{1,0:T(8,128)(2,1)S(1)}, u32[]{:S(2)}, u32[]{:S(2)}) %collective-permute-start.5) | collective-permute-done | bytes 294944 | tf_op jit(solution)/shard_map/ppermute | solution.py:409
  52.7 1.3 collective-permute-start.7
  54.0 5.1 %hyena.5 = (bf16[144,512]{1,0:T(8,128)(2,1)}, f32[3,144,512]{2,1,0:T(8,128)}, f32[128,128]{1,0:T(8,128)}, f32[3,8,128]{2,1,0:T(8,128)}) custom-call(bf16[3,144,512]{2,1,0:T(8,128)(2,1)} %bitcast.23, bf16[3,136,512]{2,1,0:T(8,128)(2,1)} %copy-done.1, bf16[288,512]{1,0:T(8,128)(2,1)} %copy-done.2, ...), custom_call_target="tpu_custom_call", output_to_operand_aliasing={{0}: (6, {}), {1}: (7, {})} | custom-call | tf_op jit(solution)/shard_map/hyena/pallas_call | solution.py:171
  59.2 4.5 %collective-permute-done.7.refs_3_ = bf16[576,256]{1,0:T(8,128)(2,1)S(1)} collective-permute-done((bf16[576,256]{1,0:T(8,128)(2,1)S(1)}, bf16[576,256]{1,0:T(8,128)(2,1)S(1)}, u32[]{:S(2)}, u32[]{:S(2)}) %collective-permute-start.7) | collective-permute-done | bytes 294944 | tf_op jit(solution)/shard_map/ppermute | solution.py:409
  64.3 1.3 collective-permute-start.9
  65.6 5.1 %hyena.6 = (bf16[144,512]{1,0:T(8,128)(2,1)}, f32[3,144,512]{2,1,0:T(8,128)}, f32[128,128]{1,0:T(8,128)}, f32[3,8,128]{2,1,0:T(8,128)}) custom-call(bf16[3,144,512]{2,1,0:T(8,128)(2,1)} %bitcast.24, bf16[3,136,512]{2,1,0:T(8,128)(2,1)} %copy-done.1, bf16[288,512]{1,0:T(8,128)(2,1)} %copy-done.2, ...), custom_call_target="tpu_custom_call", output_to_operand_aliasing={{0}: (6, {}), {1}: (7, {})} | custom-call | tf_op jit(solution)/shard_map/hyena/pallas_call | solution.py:171
  70.8 5.9 %collective-permute-done.9.refs_4_ = bf16[576,256]{1,0:T(8,128)(2,1)S(1)} collective-permute-done((bf16[576,256]{1,0:T(8,128)(2,1)S(1)}, bf16[576,256]{1,0:T(8,128)(2,1)S(1)}, u32[]{:S(2)}, u32[]{:S(2)}) %collective-permute-start.9) | collective-permute-done | bytes 294944 | tf_op jit(solution)/shard_map/ppermute | solution.py:409
  77.4 1.3 collective-permute-start.11
  78.8 5.2 %hyena.7 = (bf16[144,512]{1,0:T(8,128)(2,1)}, f32[3,144,512]{2,1,0:T(8,128)}, f32[128,128]{1,0:T(8,128)}, f32[3,8,128]{2,1,0:T(8,128)}) custom-call(bf16[3,144,512]{2,1,0:T(8,128)(2,1)} %bitcast.25, bf16[3,136,512]{2,1,0:T(8,128)(2,1)} %copy-done.1, bf16[288,512]{1,0:T(8,128)(2,1)} %copy-done.2, ...), custom_call_target="tpu_custom_call", output_to_operand_aliasing={{0}: (6, {}), {1}: (7, {})} | custom-call | tf_op jit(solution)/shard_map/hyena/pallas_call | solution.py:171
  84.0 2.0 %collective-permute-done.11.refs_5_ = bf16[576,256]{1,0:T(8,128)(2,1)S(1)} collective-permute-done((bf16[576,256]{1,0:T(8,128)(2,1)S(1)}, bf16[576,256]{1,0:T(8,128)(2,1)S(1)}, u32[]{:S(2)}, u32[]{:S(2)}) %collective-permute-start.11) | collective-permute-done | bytes 294944 | tf_op jit(solution)/shard_map/ppermute | solution.py:409
  86.7 1.3 collective-permute-start.13
  89.6 10.3 %collective-permute-done.13.refs_6_ = bf16[576,256]{1,0:T(8,128)(2,1)S(1)} collective-permute-done((bf16[576,256]{1,0:T(8,128)(2,1)S(1)}, bf16[576,256]{1,0:T(8,128)(2,1)S(1)}, u32[]{:S(2)}, u32[]{:S(2)}) %collective-permute-start.13) | collective-permute-done | bytes 294944 | tf_op jit(solution)/shard_map/ppermute | solution.py:409
  100.7 1.3 collective-permute-start.15
  102.8 5.0 %all-to-all-start.1 = ((f32[32,10,128]{2,1,0:T(8,128)}), f32[32,10,128]{2,1,0:T(8,128)S(1)}, u32[]{:S(2)}, u32[]{:S(2)}) async-start(f32[32,10,128]{2,1,0:T(8,128)} %reshape.54), calls=%async_computation.1 | async-start | bytes 524288 | tf_op jit(solution)/shard_map/all_to_all | solution.py:383
  107.9 8.1 %all-to-all-done.1 = f32[32,10,128]{2,1,0:T(8,128)S(1)} async-done(((f32[32,10,128]{2,1,0:T(8,128)}), f32[32,10,128]{2,1,0:T(8,128)S(1)}, u32[]{:S(2)}, u32[]{:S(2)}) %all-to-all-start.1) | async-done | bytes 163872 | tf_op jit(solution)/shard_map/all_to_all | solution.py:383
  116.8 5.4 %query_pass.1 = (bf16[576,256]{1,0:T(8,128)(2,1)}, f32[8,640]{1,0:T(8,128)}) custom-call(s32[1]{0:T(128)} %bitcast.5.where_ref, bf16[576,256]{1,0:T(8,128)(2,1)} %copy-done.3, bf16[576,256]{1,0:T(8,128)(2,1)} %copy-done.4, bf16[576,256]{1,0:T(8,128)(2,1)} %copy-done.12, bf16[576,256]{1,0:T(8,128)(2,1)} %copy-done.13, bf16[576,256]{1,0:T(8,128)(2,1)} %copy-done.14, ...), custom_call_target="tpu_custom_call" | custom-call | tf_op jit(solution)/shard_map/query_pass/pallas_call | solution.py:295
  122.9 13.8 %all_to_all.26 = f32[8,20,128]{2,1,0:T(8,128)S(1)} all-to-all(f32[8,20,128]{2,1,0:T(8,128)S(1)} %broadcast_in_dim.7), channel_id=1, replica_groups=mesh['cz'=8,'cy'=4,'fsdp'=4,'tp'=2] {'cz'}, dimensions={0} | all-to-all | bytes 163840 | tf_op jit(solution)/shard_map/all_to_all | solution.py:383
  137.4 4.7 %all-to-all-start.3 = ((f32[8,10,128]{2,1,0:T(8,128)}), f32[8,10,128]{2,1,0:T(8,128)S(1)}, u32[]{:S(2)}, u32[]{:S(2)}) async-start(f32[8,10,128]{2,1,0:T(8,128)} %broadcast_in_dim.8), calls=%async_computation.3 | async-start | bytes 131072 | tf_op jit(solution)/shard_map/all_to_all | solution.py:383
  142.9 9.9 %key_pass.1.ok_ref = bf16[576,256]{1,0:T(8,128)(2,1)} custom-call(s32[1]{0:T(128)} %bitcast.5.where_ref, bf16[576,256]{1,0:T(8,128)(2,1)} %copy-done.4, f32[9,2,512]{2,1,0:T(2,128)} %bitcast.31, bf16[576,256]{1,0:T(8,128)(2,1)} %copy-done.3, bf16[576,256]{1,0:T(8,128)(2,1)} %copy-done.5, bf16[576,256]{1,0:T(8,128)(2,1)} %copy-done.6, ...), custom_call_target="tpu_custom_call" | custom-call | tf_op jit(solution)/shard_map/key_pass/pallas_call | solution.py:368
  153.4 2.0 %join.1 = bf16[4,184,512]{2,1,0:T(8,128)(2,1)} custom-call(bf16[576,256]{1,0:T(8,128)(2,1)} %get-tuple-element.105.oq_ref, bf16[576,256]{1,0:T(8,128)(2,1)} %key_pass.1.ok_ref, f32[80,128]{1,0:T(8,128)} %reshape.57.part_ref), custom_call_target="tpu_custom_call" | custom-call | tf_op jit(solution)/shard_map/join/pallas_call | solution.py:364
  155.4 16.8 %all_to_all.27.x_ref = bf16[4,184,512]{2,1,0:T(8,128)(2,1)} all-to-all(bf16[4,184,512]{2,1,0:T(8,128)(2,1)} %join.1), channel_id=1, replica_groups=mesh['cz'=8,'cy'=4,'fsdp'=4,'tp'=2] {'cy'}, dimensions={0} | all-to-all | bytes 1507328 | tf_op jit(solution)/shard_map/all_to_all | solution.py:383
  172.1 2.2 %unpack.1 = (bf16[144,512]{1,0:T(8,128)(2,1)}, f32[144,512]{1,0:T(8,128)}, f32[144,512]{1,0:T(8,128)}, f32[144,512]{1,0:T(8,128)}, f32[4,80,128]{2,1,0:T(8,128)}) custom-call(bf16[4,184,512]{2,1,0:T(8,128)(2,1)} %all_to_all.27.x_ref), custom_call_target="tpu_custom_call" | custom-call | tf_op jit(solution)/shard_map/unpack/pallas_call | solution.py:77
  174.3 1.0 reshape.58
  (104 shorter events, 13.0 us)
Async XLA Ops:
  2.7 14.8 %copy-start = (bf16[144,3,512]{2,0,1:T(8,128)(2,1)S(1)}, bf16[144,3,512]{2,0,1:T(8,128)(2,1)}, u32[]{:S(2)}) copy-start(bf16[144,3,512]{2,0,1:T(8,128)(2,1)} %param.8) | copy-start | bytes 1327108
  17.6 22.1 %collective-permute-start.2 = (bf16[3,136,512]{2,1,0:T(8,128)(2,1)S(1)}, bf16[3,136,512]{2,1,0:T(8,128)(2,1)S(1)}, u32[]{:S(2)}, u32[]{:S(2)}) collective-permute-start(bf16[3,136,512]{2,1,0:T(8,128)(2,1)S(1)} %slice.58), channel_id=1, source_target_pairs={{0,8},{8,16},{16,24},{24,32},{32,40},{40,48},{48,56},{56,64},{64,7... | collective-permute-start | bytes 1253384 | tf_op jit(solution)/shard_map/ppermute | solution.py:402
  21.0 20.7 %copy-start.23 = (f32[3,7,256]{2,1,0:T(8,128)S(1)}, f32[3,7,256]{2,1,0:T(8,128)}, u32[]{:S(2)}) copy-start(f32[3,7,256]{2,1,0:T(8,128)} %param.9) | copy-start | bytes 64516
  21.0 11.3 %collective-permute-start.3 = (bf16[288,512]{1,0:T(8,128)(2,1)S(1)}, bf16[288,512]{1,0:T(8,128)(2,1)S(1)}, u32[]{:S(2)}, u32[]{:S(2)}) collective-permute-start(bf16[288,512]{1,0:T(8,128)(2,1)S(1)} %pad_maximum_fusion), channel_id=1, source_target_pairs={{8,0},{16,8},{24,16},{32,24},{40,32},{48,40},{56,48},{64,56},{72,6... | collective-permute-start | bytes 884744 | tf_op jit(solution)/shard_map/ppermute | solution.py:404
  22.3 17.3 %collective-permute-start.1 = (bf16[576,256]{1,0:T(8,128)(2,1)S(1)}, bf16[576,256]{1,0:T(8,128)(2,1)S(1)}, u32[]{:S(2)}, u32[]{:S(2)}) collective-permute-start(bf16[576,256]{1,0:T(8,128)(2,1)S(1)} %get-tuple-element.122.own_ref.refs_0_), channel_id=1, source_target_pairs={{32,0},{64,32},{96,64},{128,96},{160,128},{192,160},{224,192},{33,... | collective-permute-start | bytes 884744 | tf_op jit(solution)/shard_map/ppermute | solution.py:409
  23.6 16.0 %collective-permute-start = (bf16[576,256]{1,0:T(8,128)(2,1)S(1)}, bf16[576,256]{1,0:T(8,128)(2,1)S(1)}, u32[]{:S(2)}, u32[]{:S(2)}) collective-permute-start(bf16[576,256]{1,0:T(8,128)(2,1)S(1)} %get-tuple-element.123.refs_0_.own_ref), channel_id=1, source_target_pairs={{0,32},{32,64},{64,96},{96,128},{128,160},{160,192},{192,224},{1,3... | collective-permute-start | bytes 884744 | tf_op jit(solution)/shard_map/ppermute | solution.py:408
  32.3 10.0 %copy-start.2 = (bf16[288,512]{1,0:T(8,128)(2,1)}, bf16[288,512]{1,0:T(8,128)(2,1)S(1)}, u32[]{:S(2)}) copy-start(bf16[288,512]{1,0:T(8,128)(2,1)S(1)} %collective-permute-done.3.next_ref) | copy-start | bytes 884740
  39.7 19.5 %copy-start.5 = (bf16[576,256]{1,0:T(8,128)(2,1)}, bf16[576,256]{1,0:T(8,128)(2,1)S(1)}, u32[]{:S(2)}) copy-start(bf16[576,256]{1,0:T(8,128)(2,1)S(1)} %collective-permute-done.1.refs_1_) | copy-start | bytes 884740
  39.7 19.5 %copy-start.12 = (bf16[576,256]{1,0:T(8,128)(2,1)}, bf16[576,256]{1,0:T(8,128)(2,1)S(1)}, u32[]{:S(2)}) copy-start(bf16[576,256]{1,0:T(8,128)(2,1)S(1)} %collective-permute-done.refs_1_) | copy-start | bytes 884740
  39.7 7.7 %collective-permute-start.4 = (bf16[576,256]{1,0:T(8,128)(2,1)S(1)}, bf16[576,256]{1,0:T(8,128)(2,1)S(1)}, u32[]{:S(2)}, u32[]{:S(2)}) collective-permute-start(bf16[576,256]{1,0:T(8,128)(2,1)S(1)} %collective-permute-done.refs_1_), channel_id=1, source_target_pairs={{32,64},{64,96},{96,128},{128,160},{160,192},{192,224},{33,65},{65... | collective-permute-start | bytes 884744 | tf_op jit(solution)/shard_map/ppermute | solution.py:408
  40.4 11.7 %collective-permute-start.5 = (bf16[576,256]{1,0:T(8,128)(2,1)S(1)}, bf16[576,256]{1,0:T(8,128)(2,1)S(1)}, u32[]{:S(2)}, u32[]{:S(2)}) collective-permute-start(bf16[576,256]{1,0:T(8,128)(2,1)S(1)} %collective-permute-done.1.refs_1_), channel_id=1, source_target_pairs={{32,0},{64,32},{96,64},{128,96},{160,128},{192,160},{33,1},{65,33}... | collective-permute-start | bytes 884744 | tf_op jit(solution)/shard_map/ppermute | solution.py:409
  47.4 11.7 %copy-start.13 = (bf16[576,256]{1,0:T(8,128)(2,1)}, bf16[576,256]{1,0:T(8,128)(2,1)S(1)}, u32[]{:S(2)}) copy-start(bf16[576,256]{1,0:T(8,128)(2,1)S(1)} %collective-permute-done.4.refs_2_) | copy-start | bytes 884740
  52.1 7.1 %collective-permute-start.6 = (bf16[576,256]{1,0:T(8,128)(2,1)S(1)}, bf16[576,256]{1,0:T(8,128)(2,1)S(1)}, u32[]{:S(2)}, u32[]{:S(2)}) collective-permute-start(bf16[576,256]{1,0:T(8,128)(2,1)S(1)} %collective-permute-done.4.refs_2_), channel_id=1, source_target_pairs={{64,96},{96,128},{128,160},{160,192},{192,224},{65,97},{97,129},{1... | collective-permute-start | bytes 884744 | tf_op jit(solution)/shard_map/ppermute | solution.py:408
  52.7 10.9 %collective-permute-start.7 = (bf16[576,256]{1,0:T(8,128)(2,1)S(1)}, bf16[576,256]{1,0:T(8,128)(2,1)S(1)}, u32[]{:S(2)}, u32[]{:S(2)}) collective-permute-start(bf16[576,256]{1,0:T(8,128)(2,1)S(1)} %collective-permute-done.5.refs_2_), channel_id=1, source_target_pairs={{32,0},{64,32},{96,64},{128,96},{160,128},{33,1},{65,33},{97,65},{... | collective-permute-start | bytes 884744 | tf_op jit(solution)/shard_map/ppermute | solution.py:409
  59.2 11.6 %copy-start.14 = (bf16[576,256]{1,0:T(8,128)(2,1)}, bf16[576,256]{1,0:T(8,128)(2,1)S(1)}, u32[]{:S(2)}) copy-start(bf16[576,256]{1,0:T(8,128)(2,1)S(1)} %collective-permute-done.6.refs_3_) | copy-start | bytes 884740
  63.7 7.1 %collective-permute-start.8 = (bf16[576,256]{1,0:T(8,128)(2,1)S(1)}, bf16[576,256]{1,0:T(8,128)(2,1)S(1)}, u32[]{:S(2)}, u32[]{:S(2)}) collective-permute-start(bf16[576,256]{1,0:T(8,128)(2,1)S(1)} %collective-permute-done.6.refs_3_), channel_id=1, source_target_pairs={{96,128},{128,160},{160,192},{192,224},{97,129},{129,161},{161,193... | collective-permute-start | bytes 884744 | tf_op jit(solution)/shard_map/ppermute | solution.py:408
  64.3 12.4 %collective-permute-start.9 = (bf16[576,256]{1,0:T(8,128)(2,1)S(1)}, bf16[576,256]{1,0:T(8,128)(2,1)S(1)}, u32[]{:S(2)}, u32[]{:S(2)}) collective-permute-start(bf16[576,256]{1,0:T(8,128)(2,1)S(1)} %collective-permute-done.7.refs_3_), channel_id=1, source_target_pairs={{32,0},{64,32},{96,64},{128,96},{33,1},{65,33},{97,65},{129,97},{3... | collective-permute-start | bytes 884744 | tf_op jit(solution)/shard_map/ppermute | solution.py:409
  70.8 13.1 %copy-start.15 = (bf16[576,256]{1,0:T(8,128)(2,1)}, bf16[576,256]{1,0:T(8,128)(2,1)S(1)}, u32[]{:S(2)}) copy-start(bf16[576,256]{1,0:T(8,128)(2,1)S(1)} %collective-permute-done.8.refs_4_) | copy-start | bytes 884740
  76.7 7.2 %collective-permute-start.10 = (bf16[576,256]{1,0:T(8,128)(2,1)S(1)}, bf16[576,256]{1,0:T(8,128)(2,1)S(1)}, u32[]{:S(2)}, u32[]{:S(2)}) collective-permute-start(bf16[576,256]{1,0:T(8,128)(2,1)S(1)} %collective-permute-done.8.refs_4_), channel_id=1, source_target_pairs={{128,160},{160,192},{192,224},{129,161},{161,193},{193,225},{130,1... | collective-permute-start | bytes 884744 | tf_op jit(solution)/shard_map/ppermute | solution.py:408
  77.4 8.6 %collective-permute-start.11 = (bf16[576,256]{1,0:T(8,128)(2,1)S(1)}, bf16[576,256]{1,0:T(8,128)(2,1)S(1)}, u32[]{:S(2)}, u32[]{:S(2)}) collective-permute-start(bf16[576,256]{1,0:T(8,128)(2,1)S(1)} %collective-permute-done.9.refs_4_), channel_id=1, source_target_pairs={{32,0},{64,32},{96,64},{33,1},{65,33},{97,65},{34,2},{66,34},{98,6... | collective-permute-start | bytes 884744 | tf_op jit(solution)/shard_map/ppermute | solution.py:409
  78.8 9.2 %copy-start.26 = (f32[3,8,128]{2,1,0:T(8,128)S(1)}, f32[3,8,128]{2,1,0:T(8,128)}, u32[]{:S(2)}) copy-start(f32[3,8,128]{2,1,0:T(8,128)} %get-tuple-element.112) | copy-start | bytes 36868
  78.8 9.2 %copy-start.19 = (f32[128,128]{1,0:T(8,128)S(1)}, f32[128,128]{1,0:T(8,128)}, u32[]{:S(2)}) copy-start(f32[128,128]{1,0:T(8,128)} %get-tuple-element.107) | copy-start | bytes 196612
  78.8 9.2 %copy-start.21 = (f32[128,128]{1,0:T(8,128)S(1)}, f32[128,128]{1,0:T(8,128)}, u32[]{:S(2)}) copy-start(f32[128,128]{1,0:T(8,128)} %get-tuple-element.108) | copy-start | bytes 196612
  83.9 18.1 %copy-start.16 = (bf16[576,256]{1,0:T(8,128)(2,1)}, bf16[576,256]{1,0:T(8,128)(2,1)S(1)}, u32[]{:S(2)}) copy-start(bf16[576,256]{1,0:T(8,128)(2,1)S(1)} %collective-permute-done.10.refs_5_) | copy-start | bytes 884740
  86.0 16.1 %copy-start.9 = (bf16[576,256]{1,0:T(8,128)(2,1)}, bf16[576,256]{1,0:T(8,128)(2,1)S(1)}, u32[]{:S(2)}) copy-start(bf16[576,256]{1,0:T(8,128)(2,1)S(1)} %collective-permute-done.11.refs_5_) | copy-start | bytes 884740
  86.0 3.6 %collective-permute-start.12 = (bf16[576,256]{1,0:T(8,128)(2,1)S(1)}, bf16[576,256]{1,0:T(8,128)(2,1)S(1)}, u32[]{:S(2)}, u32[]{:S(2)}) collective-permute-start(bf16[576,256]{1,0:T(8,128)(2,1)S(1)} %collective-permute-done.10.refs_5_), channel_id=1, source_target_pairs={{160,192},{192,224},{161,193},{193,225},{162,194},{194,226},{163,1... | collective-permute-start | bytes 884744 | tf_op jit(solution)/shard_map/ppermute | solution.py:408
  86.7 13.3 %collective-permute-start.13 = (bf16[576,256]{1,0:T(8,128)(2,1)S(1)}, bf16[576,256]{1,0:T(8,128)(2,1)S(1)}, u32[]{:S(2)}, u32[]{:S(2)}) collective-permute-start(bf16[576,256]{1,0:T(8,128)(2,1)S(1)} %collective-permute-done.11.refs_5_), channel_id=1, source_target_pairs={{32,0},{64,32},{33,1},{65,33},{34,2},{66,34},{35,3},{67,35},{36,4}... | collective-permute-start | bytes 884744 | tf_op jit(solution)/shard_map/ppermute | solution.py:409
  89.6 13.2 %copy-start.17 = (bf16[576,256]{1,0:T(8,128)(2,1)}, bf16[576,256]{1,0:T(8,128)(2,1)S(1)}, u32[]{:S(2)}) copy-start(bf16[576,256]{1,0:T(8,128)(2,1)S(1)} %collective-permute-done.12.refs_6_) | copy-start | bytes 884740
  100.0 16.1 %collective-permute-start.14 = (bf16[576,256]{1,0:T(8,128)(2,1)S(1)}, bf16[576,256]{1,0:T(8,128)(2,1)S(1)}, u32[]{:S(2)}, u32[]{:S(2)}) collective-permute-start(bf16[576,256]{1,0:T(8,128)(2,1)S(1)} %collective-permute-done.12.refs_6_), channel_id=1, source_target_pairs={{192,224},{193,225},{194,226},{195,227},{196,228},{197,229},{198,2... | collective-permute-start | bytes 884744 | tf_op jit(solution)/shard_map/ppermute | solution.py:408
  100.7 15.4 %collective-permute-start.15 = (bf16[576,256]{1,0:T(8,128)(2,1)S(1)}, bf16[576,256]{1,0:T(8,128)(2,1)S(1)}, u32[]{:S(2)}, u32[]{:S(2)}) collective-permute-start(bf16[576,256]{1,0:T(8,128)(2,1)S(1)} %collective-permute-done.13.refs_6_), channel_id=1, source_target_pairs={{32,0},{33,1},{34,2},{35,3},{36,4},{37,5},{38,6},{39,7},{40,8},{41... | collective-permute-start | bytes 884744 | tf_op jit(solution)/shard_map/ppermute | solution.py:409
  102.8 13.2 %all-to-all-start.1 = ((f32[32,10,128]{2,1,0:T(8,128)}), f32[32,10,128]{2,1,0:T(8,128)S(1)}, u32[]{:S(2)}, u32[]{:S(2)}) async-start(f32[32,10,128]{2,1,0:T(8,128)} %reshape.54), calls=%async_computation.1 | async-start | bytes 524288 | tf_op jit(solution)/shard_map/all_to_all | solution.py:383
  137.4 15.4 %all-to-all-start.3 = ((f32[8,10,128]{2,1,0:T(8,128)}), f32[8,10,128]{2,1,0:T(8,128)S(1)}, u32[]{:S(2)}, u32[]{:S(2)}) async-start(f32[8,10,128]{2,1,0:T(8,128)} %broadcast_in_dim.8), calls=%async_computation.3 | async-start | bytes 131072 | tf_op jit(solution)/shard_map/all_to_all | solution.py:383
  (15 other events, 57.8 us)

commit v7 on v5

--- a/solution.py
+++ b/solution.py
@@ -208,17 +208,26 @@
     )(feat, prev, nxt, up, short8, long_taps, *earlier)
 
 
-def assemble(where_ref, pieces, out_ref, step):
-    for t, piece in enumerate(pieces):
-        block = where_ref[0] + step * t
-
-        @pl.when((block >= 0) & (block < len(pieces)))
+PLACES = (0, -1, -2, -3, 1, 2, 3, 4)
+
+
+def part_of(side):
+    return pl.BlockSpec((GROUP, 2 * HD), lambda i: (0, side))
+
+
+def assemble(where_ref, pieces, out_ref, below):
+    z = where_ref[0]
+    for place, piece in zip(PLACES, pieces):
+        block = (z + place + 8) % 8
+        needed = (block <= z) if below else (block >= z)
+
+        @pl.when(needed)
         def _():
             out_ref[pl.ds(pl.multiple_of(block * GROUP, 64), GROUP), :] = piece[...]
 
-    spare = where_ref[0] - step
-
-    @pl.when((spare >= 0) & (spare < len(pieces)))
+    spare = z + 1 if below else z - 1
+
+    @pl.when((spare >= 0) & (spare < 8))
     def _():
         out_ref[pl.ds(pl.multiple_of(spare * GROUP, 64), GROUP), :] = jnp.zeros(
             (GROUP, 2 * HD), BF16
@@ -241,7 +250,7 @@
 
 def query_body(where_ref, own_ref, *refs):
     out_ref, stat_ref, s_ref, mx_ref, l_ref, o_ref, st_ref, kv_ref = refs[8:]
-    assemble(where_ref, refs[:8], kv_ref, -1)
+    assemble(where_ref, refs[:8], kv_ref, True)
     first = where_ref[0] * GROUP
     clear = first // CHUNK
     total = (first + GROUP + CHUNK - 1) // CHUNK
@@ -306,8 +315,11 @@
         query_body,
         (struct((GROUP, 2 * HD), BF16), struct((8, 640), F32)),
         "query_pass",
+        grid=(1,),
         in_specs=[pl.BlockSpec(memory_space=pltpu.SMEM)]
-        + [pl.BlockSpec(memory_space=pltpu.VMEM)] * 9,
+        + [part_of(0)]
+        + [part_of(1)] * 7
+        + [part_of(0)],
         scratch_shapes=[
             pltpu.VMEM((CHUNKS, GROUP, CHUNK), F32),
             pltpu.VMEM((GROUP, HD), F32),
@@ -319,9 +331,9 @@
     )(where, own, *kv)
 
 
-def key_body(where_ref, own_ref, stat_ref, oq_ref, part_ref, *refs):
+def key_body(where_ref, own_ref, stat_ref, *refs):
     out_ref, gk_ref, gv_ref, qd_ref = refs[8:]
-    assemble(where_ref, refs[:8], qd_ref, 1)
+    assemble(where_ref, refs[:8], qd_ref, False)
     first = where_ref[0] * GROUP
     begin = first // CHUNK
     clear = (first + GROUP - 1 + CHUNK - 1) // CHUNK
@@ -353,11 +365,15 @@
     def _(c):
         visit(c, False)
 
+    out_ref[:, :HD] = (gk_ref[...] * SCALE).astype(BF16)
+    out_ref[:, HD:] = gv_ref[...].astype(BF16)
+
+
+def join_body(oq_ref, ok_ref, part_ref, out_ref):
     for j in range(4):
         at = slice(j * ROWS, (j + 1) * ROWS)
         out_ref[j, :ROWS, : 2 * HD] = oq_ref[at]
-        out_ref[j, :ROWS, 2 * HD : 3 * HD] = (gk_ref[at] * SCALE).astype(BF16)
-        out_ref[j, :ROWS, 3 * HD :] = gv_ref[at].astype(BF16)
+        out_ref[j, :ROWS, 2 * HD :] = ok_ref[at]
         for side in range(2):
             value = part_ref[side * 40 : (side + 1) * 40]
             high = value.astype(BF16)
@@ -366,19 +382,26 @@
             out_ref[j, ROWS:, (side + 2) * HD : (side + 3) * HD] = low
 
 
-def key_pass(where, own, qd, stats, out_q, part):
+def join(out_q, out_k, part):
+    return call(join_body, struct((4, ROWS + 40, 4 * HD), BF16), "join")(out_q, out_k, part)
+
+
+def key_pass(where, own, qd, stats):
     return call(
         key_body,
-        struct((4, ROWS + 40, 4 * HD), BF16),
+        struct((GROUP, 2 * HD), BF16),
         "key_pass",
+        grid=(1,),
         in_specs=[pl.BlockSpec(memory_space=pltpu.SMEM)]
-        + [pl.BlockSpec(memory_space=pltpu.VMEM)] * 12,
+        + [part_of(1)]
+        + [pl.BlockSpec(memory_space=pltpu.VMEM)]
+        + [part_of(0)] * 8,
         scratch_shapes=[
             pltpu.VMEM((GROUP, HD), F32),
             pltpu.VMEM((GROUP, HD), F32),
             pltpu.VMEM((SEQ, 2 * HD), BF16),
         ],
-    )(where, own, stats, out_q, part, *qd)
+    )(where, own, stats, *qd)
 
 
 def exchange(x, axis):
@@ -393,54 +416,55 @@
     features, short_filter, long_filter_taps, queries, key_vectors, value_vectors,
     grad_mixed, grad_attended,
 ):
-    feat = features.transpose(1, 0, 2)
-    prev = lax.ppermute(feat[:, 8:], CTX, [(i, i + 1) for i in range(31)])
-    rim = jnp.concatenate([feat[1, :136], grad_mixed[:136], feat[0, :8], feat[2, :8]], 0)
-    nxt = lax.ppermute(rim, CTX, [(i + 1, i) for i in range(31)])
-
     where = lax.axis_index("cz").astype(jnp.int32).reshape(1)
     packed = pack(queries, grad_attended, key_vectors, value_vectors)
     own = exchange(packed, "cy").reshape(GROUP, 4 * HD)
-    kv = [own[:, 2 * HD :]]
-    qd = [own[:, : 2 * HD]]
+    features, upstream = after(features, own), after(grad_mixed, own)
+    feat = features.transpose(1, 0, 2)
+    prev = lax.ppermute(feat[:, 8:], CTX, [(i, i + 1) for i in range(31)])
+    rim = jnp.concatenate([feat[1, :136], upstream[:136], feat[0, :8], feat[2, :8]], 0)
+    nxt = lax.ppermute(rim, CTX, [(i + 1, i) for i in range(31)])
+
+    rising, falling = [own], [own]
+
+    def shift(x, by):
+        return lax.ppermute(x, "cz", [(i, (i + by) % 8) for i in range(8)])
 
     def step():
-        t = len(kv)
-        kv.append(lax.ppermute(kv[-1], "cz", [(i, i + 1) for i in range(t - 1, 7)]))
-        qd.append(lax.ppermute(qd[-1], "cz", [(i, i - 1) for i in range(1, 9 - t)]))
+        rising.append(shift(rising[-1], 1))
+        falling.append(shift(falling[-1], -1))
 
     def order(*values):
-        held = lax.optimization_barrier((kv[-1], qd[-1]) + values)
-        kv[-1], qd[-1] = held[:2]
+        held = lax.optimization_barrier((rising[-1], falling[-1]) + values)
+        rising[-1], falling[-1] = held[:2]
         return held[2:]
 
     short8 = jnp.pad(short_filter, ((0, 0), (0, 1), (0, 0)))
     step()
     prev, nxt = order(prev, nxt)
     step()
-    first = hyena(0, feat, prev, nxt, grad_mixed, short8, long_filter_taps, ())
+    first = hyena(0, feat, prev, nxt, upstream, short8, long_filter_taps, ())
     first = order(*first)
     step()
-    second = hyena(1, feat, prev, nxt, grad_mixed, short8, long_filter_taps, first[:2])
+    second = hyena(1, feat, prev, nxt, upstream, short8, long_filter_taps, first[:2])
     mixed, gfeat, glong, gshort = order(*second)
     glong = jnp.concatenate([first[2], glong], 1)
     gshort = jnp.concatenate([first[3], gshort], 2).reshape(24, 256)
     grads = jnp.concatenate([glong, gshort, jnp.zeros((8, 256), F32)], 0)
-    step()
+    far_kv = shift(rising[-1][:, 2 * HD :], 1)
+    far_qd = shift(falling[-1][:, : 2 * HD], -1)
     part = jnp.sum(exchange(grads.reshape(32, 10, HD), YFT), axis=0)
-    (part,) = order(part)
-    step()
-    part = jnp.sum(share(part, "cz", 8), axis=0)
-    (part,) = order(part)
-    step()
-    part = share(part, FT, 8)
-    (part,) = order(part)
-    step()
-
-    out_q, stats = query_pass(where, qd[0], kv)
-    stats = share(stats[:2, :GROUP], "cz", 8).transpose(1, 0, 2)
+    far_kv, far_qd, own = lax.optimization_barrier((far_kv, far_qd, own))
+    pieces = [own] + rising[1:] + falling[1:]
+
+    out_q, stats = query_pass(where, own, pieces + [far_kv])
+    small = jnp.concatenate([stats[:2].reshape(10, HD), part], 0)
+    small = share(small, "cz", 8)
+    part = share(jnp.sum(small[:, 10:], axis=0), FT, 8)
+    stats = small[:, :10].reshape(8, 2, 640)[:, :, :GROUP].transpose(1, 0, 2)
     stats = stats.reshape(2, CHUNKS, CHUNK).transpose(1, 0, 2)
-    result = key_pass(where, kv[0], qd, stats, out_q, part.reshape(80, HD))
+    out_k = key_pass(where, own, pieces + [far_qd], stats)
+    result = join(out_q, out_k, part.reshape(80, HD))
     attended, grad_queries, grad_keys, grad_values, grads = unpack(exchange(result, "cy"))
     grads = grads.reshape(160, 256)
     grad_long = grads[:128]

time: 186 us -> 161 us (0.87)
  blocking collectives: 70.8 us -> 52.6 us
  starting transfers between devices: 47 us -> 37.6 us
    all_to_all x4 -> x3, blocking collectives: 70.8 us -> 52.6 us  [exchange(): return lax.all_to_all(x, axis, 0, 0, tiled=True)]
    all_to_all x2, starting transfers between devices: 23.5 us -> 9.71 us  [exchange(): return lax.all_to_all(x, axis, 0, 0, tiled=True)]
    ppermute x1, waiting for transfers between devices: 0.01 us -> 7.32 us  [body(): nxt = lax.ppermute(rim, CTX, [(i + 1, i) for i in range(31)])]
    ppermute x14 -> x8, starting transfers between devices: 17.7 us -> 24.1 us  [shift(): return lax.ppermute(x, 'cz', [(i, (i + by) % 8) for i in range(8)])]
    ppermute x14 -> x8, waiting for transfers between devices: 8.04 us -> 5.14 us  [shift(): return lax.ppermute(x, 'cz', [(i, (i + by) % 8) for i in range(8)])]
    all_to_all x2, waiting for transfers between devices: 11 us -> 8.13 us  [exchange(): return lax.all_to_all(x, axis, 0, 0, tiled=True)]
    ppermute x1, starting transfers between devices: 4.58 us -> 2.48 us  [body(): prev = lax.ppermute(feat[:, 8:], CTX, [(i, i + 1) for i in range(31)])]
    pallas_call x1 -> x2, Pallas kernels: 10.2 us -> 11.9 us  [the longest x1 9.87 us: key_pass(): call(key_body, struct((GROUP, 2 * HD), BF16), 'key_pass', grid=(1,), in_s...]
  transfers between devices with their start and end apart: 18 -> 12, of which waited for: 5 -> 5; matrix products, arithmetic and copies ran while one was open for 3% -> 1% of each run, Pallas kernels for 12% -> 17%
where the time goes in v7:
time: 161 us; the launch traced here: 160 us
  blocking collectives  52.6 us (33%)
  Pallas kernels  39 us (24%)
  starting transfers between devices  37.6 us (23%)
  waiting for transfers between devices  20.6 us (13%)
  local copies, waits for them, and re-layouts  8.94 us (6%)
    all_to_all x3, blocking collectives, exchange(): return lax.all_to_all(x, axis, 0, 0, tiled=True)  52.6 us
    ppermute x8, starting transfers between devices, shift(): return lax.ppermute(x, 'cz', [(i, (i + by) % 8) for i in range(8)])  24.1 us
    pallas_call x2, Pallas kernels, hyena(): call(hyena_body, (struct((ROWS, 512), BF16), struct((3, ROWS, 512), F32),...  17.5 us
    pallas_call x1, Pallas kernels, key_pass(): call(key_body, struct((GROUP, 2 * HD), BF16), 'key_pass', grid=(1,), in_s...  9.87 us
    all_to_all x2, starting transfers between devices, exchange(): return lax.all_to_all(x, axis, 0, 0, tiled=True)  9.71 us
    all_to_all x2, waiting for transfers between devices, exchange(): return lax.all_to_all(x, axis, 0, 0, tiled=True)  8.13 us
    ppermute x1, waiting for transfers between devices, body(): nxt = lax.ppermute(rim, CTX, [(i + 1, i) for i in range(31)])  7.32 us
    pallas_call x1, Pallas kernels, query_pass(): call(query_body, (struct((GROUP, 2 * HD), BF16), struct((8, 640), F32)),...  5.36 us
  transfers between devices with their start and end apart: 12, of which 5 were waited for; matrix products, arithmetic and copies ran while one was open for 1% of the time, Pallas kernels for 17%

profile of v7, /device:TPU:2, one launch (start us, length us, event | category | flops | bytes accessed | tf_op | source)
XLA Modules:
  0.0 159.9 jit_solution(16631415176942809797)
XLA Ops:
  0.6 2.0 %pack.1 = bf16[4,144,512]{2,1,0:T(8,128)(2,1)} custom-call(bf16[144,512]{1,0:T(8,128)(2,1)} %refs_0_.1, bf16[144,512]{1,0:T(8,128)(2,1)} %refs_1_.1, bf16[144,512]{1,0:T(8,128)(2,1)} %refs_2_.1, bf16[144,512]{1,0:T(8,128)(2,1)} %refs_3_.1), custom_call_target="tpu_custom_call" | custom-call | tf_op jit(solution)/shard_map/pack/pallas_call | solution.py:59
  2.7 14.8 %all_to_all.25 = bf16[4,144,512]{2,1,0:T(8,128)(2,1)S(1)} all-to-all(bf16[4,144,512]{2,1,0:T(8,128)(2,1)} %pack.1), channel_id=1, replica_groups=mesh['cz'=8,'cy'=4,'fsdp'=4,'tp'=2] {'cy'}, dimensions={0} | all-to-all | bytes 1179648 | tf_op jit(solution)/shard_map/all_to_all | solution.py:408
  17.5 5.9 %collective-permute-start.1 = (bf16[576,512]{1,0:T(8,128)(2,1)S(1)}, bf16[576,512]{1,0:T(8,128)(2,1)S(1)}, u32[]{:S(2)}, u32[]{:S(2)}) collective-permute-start(bf16[576,512]{1,0:T(8,128)(2,1)S(1)} %bitcast.20), channel_id=1, source_target_pairs={{0,224},{32,0},{64,32},{96,64},{128,96},{160,128},{192,160},{224,1... | collective-permute-start | bytes 1769480 | tf_op jit(solution)/shard_map/ppermute | solution.py:431
  23.4 2.5 %collective-permute-start.2 = (bf16[3,136,512]{2,1,0:T(8,128)(2,1)S(1)}, bf16[3,136,512]{2,1,0:T(8,128)(2,1)S(1)}, u32[]{:S(2)}, u32[]{:S(2)}) collective-permute-start(bf16[3,136,512]{2,1,0:T(8,128)(2,1)S(1)} %slice.56), channel_id=1, source_target_pairs={{0,8},{8,16},{16,24},{24,32},{32,40},{40,48},{48,56},{56,64},{64,7... | collective-permute-start | bytes 1253384 | tf_op jit(solution)/shard_map/ppermute | solution.py:424
  26.0 0.9 slice-done
  26.9 1.3 collective-permute-start.3
  28.2 7.3 %collective-permute-done.3.next_ref = bf16[288,512]{1,0:T(8,128)(2,1)S(1)} collective-permute-done((bf16[288,512]{1,0:T(8,128)(2,1)S(1)}, bf16[288,512]{1,0:T(8,128)(2,1)S(1)}, u32[]{:S(2)}, u32[]{:S(2)}) %collective-permute-start.3) | collective-permute-done | bytes 294944 | tf_op jit(solution)/shard_map/ppermute | solution.py:426
  35.5 2.4 %collective-permute-done.refs_1_ = bf16[576,512]{1,0:T(8,128)(2,1)S(1)} collective-permute-done((bf16[576,512]{1,0:T(8,128)(2,1)S(1)}, bf16[576,512]{1,0:T(8,128)(2,1)S(1)}, u32[]{:S(2)}, u32[]{:S(2)}) %collective-permute-start) | collective-permute-done | bytes 589856 | tf_op jit(solution)/shard_map/ppermute | solution.py:431
  38.0 10.7 %collective-permute-start.4 = (bf16[576,512]{1,0:T(8,128)(2,1)S(1)}, bf16[576,512]{1,0:T(8,128)(2,1)S(1)}, u32[]{:S(2)}, u32[]{:S(2)}) collective-permute-start(bf16[576,512]{1,0:T(8,128)(2,1)S(1)} %collective-permute-done.refs_1_), channel_id=1, source_target_pairs={{0,32},{32,64},{64,96},{96,128},{128,160},{160,192},{192,224},{224... | collective-permute-start | bytes 1769480 | tf_op jit(solution)/shard_map/ppermute | solution.py:431
  48.7 0.8 collective-permute-start.5
  50.1 8.8 %hyena.2 = (bf16[144,512]{1,0:T(8,128)(2,1)}, f32[3,144,512]{2,1,0:T(8,128)}, f32[128,128]{1,0:T(8,128)}, f32[3,8,128]{2,1,0:T(8,128)}) custom-call(bf16[3,144,512]{2,1,0:T(8,128)(2,1)} %bitcast.26, bf16[3,136,512]{2,1,0:T(8,128)(2,1)} %copy-done.8, bf16[288,512]{1,0:T(8,128)(2,1)} %copy-done.9, bf16[144,512]{1,0:T(8,128)(2,1)} %up_ref.1, ...), custom_call_target="tpu_custom_call" | custom-call | tf_op jit(solution)/shard_map/hyena/pallas_call | solution.py:181
  58.9 1.4 collective-permute-done.5.refs_5_
  60.3 0.7 collective-permute-start.6
  61.0 2.5 %collective-permute-start.7 = (bf16[576,512]{1,0:T(8,128)(2,1)S(1)}, bf16[576,512]{1,0:T(8,128)(2,1)S(1)}, u32[]{:S(2)}, u32[]{:S(2)}) collective-permute-start(bf16[576,512]{1,0:T(8,128)(2,1)S(1)} %collective-permute-done.5.refs_5_), channel_id=1, source_target_pairs={{0,224},{32,0},{64,32},{96,64},{128,96},{160,128},{192,160},{224,1... | collective-permute-start | bytes 1769480 | tf_op jit(solution)/shard_map/ppermute | solution.py:431
  63.6 8.8 %hyena.3 = (bf16[144,512]{1,0:T(8,128)(2,1)}, f32[3,144,512]{2,1,0:T(8,128)}, f32[128,128]{1,0:T(8,128)}, f32[3,8,128]{2,1,0:T(8,128)}) custom-call(bf16[3,144,512]{2,1,0:T(8,128)(2,1)} %bitcast.27, bf16[3,136,512]{2,1,0:T(8,128)(2,1)} %copy-done.8, bf16[288,512]{1,0:T(8,128)(2,1)} %copy-done.9, ...), custom_call_target="tpu_custom_call", output_to_operand_aliasing={{0}: (6, {}), {1}: (7, {})} | custom-call | tf_op jit(solution)/shard_map/hyena/pallas_call | solution.py:181
  72.4 1.3 collective-permute-done.7.refs_6_
  73.8 0.7 copy-done.3
  74.5 3.4 %collective-permute-start.9 = (bf16[576,256]{1,0:T(8,128)(2,1)S(1)}, bf16[576,256]{1,0:T(8,128)(2,1)S(1)}, u32[]{:S(2)}, u32[]{:S(2)}) collective-permute-start(bf16[576,256]{1,0:T(8,128)(2,1)S(1)} %slice.48), channel_id=1, source_target_pairs={{0,224},{32,0},{64,32},{96,64},{128,96},{160,128},{192,160},{224,1... | collective-permute-start | bytes 884744 | tf_op jit(solution)/shard_map/ppermute | solution.py:431
  78.1 0.7 reshape.52
  78.8 5.0 %all-to-all-start.1 = ((f32[32,10,128]{2,1,0:T(8,128)}), f32[32,10,128]{2,1,0:T(8,128)S(1)}, u32[]{:S(2)}, u32[]{:S(2)}) async-start(f32[32,10,128]{2,1,0:T(8,128)} %reshape.52), calls=%async_computation.1 | async-start | bytes 524288 | tf_op jit(solution)/shard_map/all_to_all | solution.py:408
  83.8 8.1 %all-to-all-done.1 = f32[32,10,128]{2,1,0:T(8,128)S(1)} async-done(((f32[32,10,128]{2,1,0:T(8,128)}), f32[32,10,128]{2,1,0:T(8,128)S(1)}, u32[]{:S(2)}, u32[]{:S(2)}) %all-to-all-start.1) | async-done | bytes 163872 | tf_op jit(solution)/shard_map/all_to_all | solution.py:408
  92.0 0.7 copy-done.11
  92.8 5.4 %query_pass.1 = (bf16[576,256]{1,0:T(8,128)(2,1)}, f32[8,640]{1,0:T(8,128)}) custom-call(s32[1]{0:T(128)} %bitcast.5.where_ref, bf16[576,512]{1,0:T(8,128)(2,1)} %bitcast.22, bf16[576,512]{1,0:T(8,128)(2,1)} %bitcast.23, bf16[576,512]{1,0:T(8,128)(2,1)} %copy-done.5, bf16[576,512]{1,0:T(8,128)(2,1)} %copy-done.6, bf16[576,512]{1,0:T(8,128)(2,1)} %copy-done.2, ...), custom_call_target="tpu_custom_call" | custom-call | tf_op jit(solution)/shard_map/query_pass/pallas_call | solution.py:314
  98.1 0.7 slice.49
  98.9 21.0 %all_to_all.26 = f32[8,20,128]{2,1,0:T(8,128)S(1)} all-to-all(f32[8,20,128]{2,1,0:T(8,128)S(1)} %broadcast_in_dim.7), channel_id=1, replica_groups=mesh['cz'=8,'cy'=4,'fsdp'=4,'tp'=2] {'cz'}, dimensions={0} | all-to-all | bytes 163840 | tf_op jit(solution)/shard_map/all_to_all | solution.py:408
  120.6 4.7 %all-to-all-start.3 = ((f32[8,10,128]{2,1,0:T(8,128)}), f32[8,10,128]{2,1,0:T(8,128)S(1)}, u32[]{:S(2)}, u32[]{:S(2)}) async-start(f32[8,10,128]{2,1,0:T(8,128)} %broadcast_in_dim.8), calls=%async_computation.3 | async-start | bytes 131072 | tf_op jit(solution)/shard_map/all_to_all | solution.py:408
  126.1 9.9 %key_pass.1.ok_ref = bf16[576,256]{1,0:T(8,128)(2,1)} custom-call(s32[1]{0:T(128)} %bitcast.5.where_ref, bf16[576,512]{1,0:T(8,128)(2,1)} %bitcast.24, f32[9,2,512]{2,1,0:T(2,128)} %bitcast.32, bf16[576,512]{1,0:T(8,128)(2,1)} %bitcast.25, bf16[576,512]{1,0:T(8,128)(2,1)} %copy-done.5, bf16[576,512]{1,0:T(8,128)(2,1)} %copy-done.6, ...), custom_call_target="tpu_custom_call" | custom-call | tf_op jit(solution)/shard_map/key_pass/pallas_call | solution.py:390
  136.6 2.0 %join.1 = bf16[4,184,512]{2,1,0:T(8,128)(2,1)} custom-call(bf16[576,256]{1,0:T(8,128)(2,1)} %get-tuple-element.67.oq_ref, bf16[576,256]{1,0:T(8,128)(2,1)} %key_pass.1.ok_ref, f32[80,128]{1,0:T(8,128)} %reshape.55.part_ref), custom_call_target="tpu_custom_call" | custom-call | tf_op jit(solution)/shard_map/join/pallas_call | solution.py:386
  138.6 16.8 %all_to_all.27.x_ref = bf16[4,184,512]{2,1,0:T(8,128)(2,1)} all-to-all(bf16[4,184,512]{2,1,0:T(8,128)(2,1)} %join.1), channel_id=1, replica_groups=mesh['cz'=8,'cy'=4,'fsdp'=4,'tp'=2] {'cy'}, dimensions={0} | all-to-all | bytes 1507328 | tf_op jit(solution)/shard_map/all_to_all | solution.py:408
  155.4 2.2 %unpack.1 = (bf16[144,512]{1,0:T(8,128)(2,1)}, f32[144,512]{1,0:T(8,128)}, f32[144,512]{1,0:T(8,128)}, f32[144,512]{1,0:T(8,128)}, f32[4,80,128]{2,1,0:T(8,128)}) custom-call(bf16[4,184,512]{2,1,0:T(8,128)(2,1)} %all_to_all.27.x_ref), custom_call_target="tpu_custom_call" | custom-call | tf_op jit(solution)/shard_map/unpack/pallas_call | solution.py:77
  157.6 1.0 reshape.56
  159.2 0.7 slice.65
  (66 shorter events, 3.7 us)
Async XLA Ops:
  2.7 14.8 %copy-start.1 = (bf16[144,3,512]{2,0,1:T(8,128)(2,1)S(1)}, bf16[144,3,512]{2,0,1:T(8,128)(2,1)}, u32[]{:S(2)}) copy-start(bf16[144,3,512]{2,0,1:T(8,128)(2,1)} %param.8) | copy-start | bytes 1327108
  17.5 8.5 %copy-start = (bf16[4,144,512]{2,1,0:T(8,128)(2,1)}, bf16[4,144,512]{2,1,0:T(8,128)(2,1)S(1)}, u32[]{:S(2)}) copy-start(bf16[4,144,512]{2,1,0:T(8,128)(2,1)S(1)} %all_to_all.25) | copy-start | bytes 1769476
  17.5 18.0 %collective-permute-start.1 = (bf16[576,512]{1,0:T(8,128)(2,1)S(1)}, bf16[576,512]{1,0:T(8,128)(2,1)S(1)}, u32[]{:S(2)}, u32[]{:S(2)}) collective-permute-start(bf16[576,512]{1,0:T(8,128)(2,1)S(1)} %bitcast.20), channel_id=1, source_target_pairs={{0,224},{32,0},{64,32},{96,64},{128,96},{160,128},{192,160},{224,1... | collective-permute-start | bytes 1769480 | tf_op jit(solution)/shard_map/ppermute | solution.py:431
  23.4 14.5 %collective-permute-start = (bf16[576,512]{1,0:T(8,128)(2,1)S(1)}, bf16[576,512]{1,0:T(8,128)(2,1)S(1)}, u32[]{:S(2)}, u32[]{:S(2)}) collective-permute-start(bf16[576,512]{1,0:T(8,128)(2,1)S(1)} %bitcast.21), channel_id=1, source_target_pairs={{0,32},{32,64},{64,96},{96,128},{128,160},{160,192},{192,224},{224... | collective-permute-start | bytes 1769480 | tf_op jit(solution)/shard_map/ppermute | solution.py:431
  23.4 12.1 %collective-permute-start.2 = (bf16[3,136,512]{2,1,0:T(8,128)(2,1)S(1)}, bf16[3,136,512]{2,1,0:T(8,128)(2,1)S(1)}, u32[]{:S(2)}, u32[]{:S(2)}) collective-permute-start(bf16[3,136,512]{2,1,0:T(8,128)(2,1)S(1)} %slice.56), channel_id=1, source_target_pairs={{0,8},{8,16},{16,24},{24,32},{32,40},{40,48},{48,56},{56,64},{64,7... | collective-permute-start | bytes 1253384 | tf_op jit(solution)/shard_map/ppermute | solution.py:424
  25.9 0.9 slice-start
  26.9 22.6 %copy-start.14 = (f32[3,7,256]{2,1,0:T(8,128)S(1)}, f32[3,7,256]{2,1,0:T(8,128)}, u32[]{:S(2)}) copy-start(f32[3,7,256]{2,1,0:T(8,128)} %param.9) | copy-start | bytes 64516
  26.9 8.6 %collective-permute-start.3 = (bf16[288,512]{1,0:T(8,128)(2,1)S(1)}, bf16[288,512]{1,0:T(8,128)(2,1)S(1)}, u32[]{:S(2)}, u32[]{:S(2)}) collective-permute-start(bf16[288,512]{1,0:T(8,128)(2,1)S(1)} %pad_maximum_fusion), channel_id=1, source_target_pairs={{8,0},{16,8},{24,16},{32,24},{40,32},{48,40},{56,48},{64,56},{72,6... | collective-permute-start | bytes 884744 | tf_op jit(solution)/shard_map/ppermute | solution.py:426
  35.5 14.6 %copy-start.9 = (bf16[288,512]{1,0:T(8,128)(2,1)}, bf16[288,512]{1,0:T(8,128)(2,1)S(1)}, u32[]{:S(2)}) copy-start(bf16[288,512]{1,0:T(8,128)(2,1)S(1)} %collective-permute-done.3.next_ref) | copy-start | bytes 884740
  35.5 14.6 %copy-start.8 = (bf16[3,136,512]{2,1,0:T(8,128)(2,1)}, bf16[3,136,512]{2,1,0:T(8,128)(2,1)S(1)}, u32[]{:S(2)}) copy-start(bf16[3,136,512]{2,1,0:T(8,128)(2,1)S(1)} %collective-permute-done.2.prev_ref) | copy-start | bytes 1253380
  35.5 23.4 %copy-start.4 = (bf16[576,512]{1,0:T(8,128)(2,1)}, bf16[576,512]{1,0:T(8,128)(2,1)S(1)}, u32[]{:S(2)}) copy-start(bf16[576,512]{1,0:T(8,128)(2,1)S(1)} %collective-permute-done.1.refs_4_) | copy-start | bytes 1769476
  38.0 20.9 %copy-start.5 = (bf16[576,512]{1,0:T(8,128)(2,1)}, bf16[576,512]{1,0:T(8,128)(2,1)S(1)}, u32[]{:S(2)}) copy-start(bf16[576,512]{1,0:T(8,128)(2,1)S(1)} %collective-permute-done.refs_1_) | copy-start | bytes 1769476
  38.0 20.9 %collective-permute-start.4 = (bf16[576,512]{1,0:T(8,128)(2,1)S(1)}, bf16[576,512]{1,0:T(8,128)(2,1)S(1)}, u32[]{:S(2)}, u32[]{:S(2)}) collective-permute-start(bf16[576,512]{1,0:T(8,128)(2,1)S(1)} %collective-permute-done.refs_1_), channel_id=1, source_target_pairs={{0,32},{32,64},{64,96},{96,128},{128,160},{160,192},{192,224},{224... | collective-permute-start | bytes 1769480 | tf_op jit(solution)/shard_map/ppermute | solution.py:431
  48.7 11.6 %collective-permute-start.5 = (bf16[576,512]{1,0:T(8,128)(2,1)S(1)}, bf16[576,512]{1,0:T(8,128)(2,1)S(1)}, u32[]{:S(2)}, u32[]{:S(2)}) collective-permute-start(bf16[576,512]{1,0:T(8,128)(2,1)S(1)} %collective-permute-done.1.refs_4_), channel_id=1, source_target_pairs={{0,224},{32,0},{64,32},{96,64},{128,96},{160,128},{192,160},{224,1... | collective-permute-start | bytes 1769480 | tf_op jit(solution)/shard_map/ppermute | solution.py:431
  58.9 13.5 %copy-start.6 = (bf16[576,512]{1,0:T(8,128)(2,1)}, bf16[576,512]{1,0:T(8,128)(2,1)S(1)}, u32[]{:S(2)}) copy-start(bf16[576,512]{1,0:T(8,128)(2,1)S(1)} %collective-permute-done.4.refs_2_) | copy-start | bytes 1769476
  60.3 12.1 %copy-start.7 = (bf16[576,512]{1,0:T(8,128)(2,1)}, bf16[576,512]{1,0:T(8,128)(2,1)S(1)}, u32[]{:S(2)}) copy-start(bf16[576,512]{1,0:T(8,128)(2,1)S(1)} %collective-permute-done.5.refs_5_) | copy-start | bytes 1769476
  60.3 12.1 %collective-permute-start.6 = (bf16[576,512]{1,0:T(8,128)(2,1)S(1)}, bf16[576,512]{1,0:T(8,128)(2,1)S(1)}, u32[]{:S(2)}, u32[]{:S(2)}) collective-permute-start(bf16[576,512]{1,0:T(8,128)(2,1)S(1)} %collective-permute-done.4.refs_2_), channel_id=1, source_target_pairs={{0,32},{32,64},{64,96},{96,128},{128,160},{160,192},{192,224},{224... | collective-permute-start | bytes 1769480 | tf_op jit(solution)/shard_map/ppermute | solution.py:431
  61.0 12.7 %collective-permute-start.7 = (bf16[576,512]{1,0:T(8,128)(2,1)S(1)}, bf16[576,512]{1,0:T(8,128)(2,1)S(1)}, u32[]{:S(2)}, u32[]{:S(2)}) collective-permute-start(bf16[576,512]{1,0:T(8,128)(2,1)S(1)} %collective-permute-done.5.refs_5_), channel_id=1, source_target_pairs={{0,224},{32,0},{64,32},{96,64},{128,96},{160,128},{192,160},{224,1... | collective-permute-start | bytes 1769480 | tf_op jit(solution)/shard_map/ppermute | solution.py:431
  72.4 1.4 copy-start.2
  73.7 0.8 copy-start.3
  73.7 4.2 %copy-start.15 = (f32[3,8,128]{2,1,0:T(8,128)S(1)}, f32[3,8,128]{2,1,0:T(8,128)}, u32[]{:S(2)}) copy-start(f32[3,8,128]{2,1,0:T(8,128)} %get-tuple-element.71) | copy-start | bytes 36868
  73.7 4.2 %copy-start.16 = (f32[3,8,128]{2,1,0:T(8,128)S(1)}, f32[3,8,128]{2,1,0:T(8,128)}, u32[]{:S(2)}) copy-start(f32[3,8,128]{2,1,0:T(8,128)} %get-tuple-element.72) | copy-start | bytes 36868
  73.8 4.2 %copy-start.12 = (f32[128,128]{1,0:T(8,128)S(1)}, f32[128,128]{1,0:T(8,128)}, u32[]{:S(2)}) copy-start(f32[128,128]{1,0:T(8,128)} %get-tuple-element.69) | copy-start | bytes 196612
  73.8 4.2 %copy-start.13 = (f32[128,128]{1,0:T(8,128)S(1)}, f32[128,128]{1,0:T(8,128)}, u32[]{:S(2)}) copy-start(f32[128,128]{1,0:T(8,128)} %get-tuple-element.70) | copy-start | bytes 196612
  74.5 17.5 %collective-permute-start.9 = (bf16[576,256]{1,0:T(8,128)(2,1)S(1)}, bf16[576,256]{1,0:T(8,128)(2,1)S(1)}, u32[]{:S(2)}, u32[]{:S(2)}) collective-permute-start(bf16[576,256]{1,0:T(8,128)(2,1)S(1)} %slice.48), channel_id=1, source_target_pairs={{0,224},{32,0},{64,32},{96,64},{128,96},{160,128},{192,160},{224,1... | collective-permute-start | bytes 884744 | tf_op jit(solution)/shard_map/ppermute | solution.py:431
  78.0 14.1 %collective-permute-start.8 = (bf16[576,256]{1,0:T(8,128)(2,1)S(1)}, bf16[576,256]{1,0:T(8,128)(2,1)S(1)}, u32[]{:S(2)}, u32[]{:S(2)}) collective-permute-start(bf16[576,256]{1,0:T(8,128)(2,1)S(1)} %slice.47), channel_id=1, source_target_pairs={{0,32},{32,64},{64,96},{96,128},{128,160},{160,192},{192,224},{224... | collective-permute-start | bytes 884744 | tf_op jit(solution)/shard_map/ppermute | solution.py:431
  78.8 13.1 %all-to-all-start.1 = ((f32[32,10,128]{2,1,0:T(8,128)}), f32[32,10,128]{2,1,0:T(8,128)S(1)}, u32[]{:S(2)}, u32[]{:S(2)}) async-start(f32[32,10,128]{2,1,0:T(8,128)} %reshape.52), calls=%async_computation.1 | async-start | bytes 524288 | tf_op jit(solution)/shard_map/all_to_all | solution.py:408
  92.0 6.1 %copy-start.10 = (bf16[576,256]{1,0:T(8,128)(2,1)}, bf16[576,256]{1,0:T(8,128)(2,1)S(1)}, u32[]{:S(2)}) copy-start(bf16[576,256]{1,0:T(8,128)(2,1)S(1)} %collective-permute-done.9.refs_7_) | copy-start | bytes 884740
  92.0 0.8 copy-start.11
  120.6 15.4 %all-to-all-start.3 = ((f32[8,10,128]{2,1,0:T(8,128)}), f32[8,10,128]{2,1,0:T(8,128)S(1)}, u32[]{:S(2)}, u32[]{:S(2)}) async-start(f32[8,10,128]{2,1,0:T(8,128)} %broadcast_in_dim.8), calls=%async_computation.3 | async-start | bytes 131072 | tf_op jit(solution)/shard_map/all_to_all | solution.py:408

commit v8 on v7

--- a/solution.py
+++ b/solution.py
@@ -48,15 +48,27 @@
     return lax.dot_general(a, b, (((1,), (0,)), ((), ())), preferred_element_type=F32)
 
 
-def pack_body(*refs):
-    out_ref = refs[-1]
+def pack_body(q_ref, d_ref, k_ref, v_ref, feat_ref, up_ref, out_ref, tail_ref, rim_ref):
     for h in range(4):
-        for slot, ref in enumerate(refs[:-1]):
+        for slot, ref in enumerate((q_ref, d_ref, k_ref, v_ref)):
             out_ref[h, :, slot * HD : (slot + 1) * HD] = ref[:, h * HD : (h + 1) * HD]
+    tail_ref[...] = feat_ref[:, 8:]
+    rim_ref[0:136] = feat_ref[1, 0:136]
+    rim_ref[136:272] = up_ref[0:136]
+    rim_ref[272:280] = feat_ref[0, 0:8]
+    rim_ref[280:288] = feat_ref[2, 0:8]
 
 
 def pack(*parts):
-    return call(pack_body, struct((4, ROWS, len(parts) * HD), BF16), "pack")(*parts)
+    return call(
+        pack_body,
+        (
+            struct((4, ROWS, 4 * HD), BF16),
+            struct((3, 136, 4 * HD), BF16),
+            struct((288, 4 * HD), BF16),
+        ),
+        "pack",
+    )(*parts)
 
 
 def unpack_body(x_ref, attended_ref, gq_ref, gk_ref, gv_ref, grads_ref):
@@ -416,15 +428,15 @@
     features, short_filter, long_filter_taps, queries, key_vectors, value_vectors,
     grad_mixed, grad_attended,
 ):
+    feat = features.transpose(1, 0, 2)
     where = lax.axis_index("cz").astype(jnp.int32).reshape(1)
-    packed = pack(queries, grad_attended, key_vectors, value_vectors)
+    packed, tail, rim = pack(
+        queries, grad_attended, key_vectors, value_vectors, feat, grad_mixed
+    )
+    prev = lax.ppermute(tail, CTX, [(i, i + 1) for i in range(31)])
+    nxt = lax.ppermute(rim, CTX, [(i + 1, i) for i in range(31)])
     own = exchange(packed, "cy").reshape(GROUP, 4 * HD)
-    features, upstream = after(features, own), after(grad_mixed, own)
-    feat = features.transpose(1, 0, 2)
-    prev = lax.ppermute(feat[:, 8:], CTX, [(i, i + 1) for i in range(31)])
-    rim = jnp.concatenate([feat[1, :136], upstream[:136], feat[0, :8], feat[2, :8]], 0)
-    nxt = lax.ppermute(rim, CTX, [(i + 1, i) for i in range(31)])
-
+    own, prev, nxt = lax.optimization_barrier((own, prev, nxt))
     rising, falling = [own], [own]
 
     def shift(x, by):
@@ -441,19 +453,19 @@
 
     short8 = jnp.pad(short_filter, ((0, 0), (0, 1), (0, 0)))
     step()
-    prev, nxt = order(prev, nxt)
-    step()
-    first = hyena(0, feat, prev, nxt, upstream, short8, long_filter_taps, ())
+    first = hyena(0, feat, prev, nxt, grad_mixed, short8, long_filter_taps, ())
     first = order(*first)
     step()
-    second = hyena(1, feat, prev, nxt, upstream, short8, long_filter_taps, first[:2])
+    second = hyena(1, feat, prev, nxt, grad_mixed, short8, long_filter_taps, first[:2])
     mixed, gfeat, glong, gshort = order(*second)
+    step()
     glong = jnp.concatenate([first[2], glong], 1)
     gshort = jnp.concatenate([first[3], gshort], 2).reshape(24, 256)
     grads = jnp.concatenate([glong, gshort, jnp.zeros((8, 256), F32)], 0)
+    part = jnp.sum(exchange(grads.reshape(32, 10, HD), YFT), axis=0)
+    (part,) = order(part)
     far_kv = shift(rising[-1][:, 2 * HD :], 1)
     far_qd = shift(falling[-1][:, : 2 * HD], -1)
-    part = jnp.sum(exchange(grads.reshape(32, 10, HD), YFT), axis=0)
     far_kv, far_qd, own = lax.optimization_barrier((far_kv, far_qd, own))
     pieces = [own] + rising[1:] + falling[1:]
 

time: 161 us -> 159 us (0.988)
  starting transfers between devices: 37.6 us -> 32.6 us
  waiting for transfers between devices: 20.6 us -> 24.8 us
  blocking collectives: 52.6 us -> 50.6 us
    ppermute x8, waiting for transfers between devices: 5.14 us -> 14.7 us  [shift(): return lax.ppermute(x, 'cz', [(i, (i + by) % 8) for i in range(8)])]
    all_to_all x2, waiting for transfers between devices: 8.13 us -> 0.01 us  [exchange(): return lax.all_to_all(x, axis, 0, 0, tiled=True)]
    ppermute x8, starting transfers between devices: 24.1 us -> 17.8 us  [shift(): return lax.ppermute(x, 'cz', [(i, (i + by) % 8) for i in range(8)])]
    ppermute x1, waiting for transfers between devices: 7.32 us -> 9.73 us  [body(): nxt = lax.ppermute(rim, CTX, [(i + 1, i) for i in range(31)])]
    all_to_all x3, blocking collectives: 52.6 us -> 50.6 us  [exchange(): return lax.all_to_all(x, axis, 0, 0, tiled=True)]
  transfers between devices with their start and end apart: 12 -> 12, of which waited for: 5 -> 7; matrix products, arithmetic and copies ran while one was open for 1% -> 2% of each run, Pallas kernels for 17% -> 17%
where the time goes in v8:
time: 159 us; the launch traced here: 157 us
  blocking collectives  50.6 us (32%)
  Pallas kernels  39.5 us (25%)
  starting transfers between devices  32.6 us (21%)
  waiting for transfers between devices  24.8 us (16%)
  local copies, waits for them, and re-layouts  7.48 us (5%)
  other arithmetic  1.69 us (1%)
    all_to_all x3, blocking collectives, exchange(): return lax.all_to_all(x, axis, 0, 0, tiled=True)  50.6 us
    ppermute x8, starting transfers between devices, shift(): return lax.ppermute(x, 'cz', [(i, (i + by) % 8) for i in range(8)])  17.8 us
    pallas_call x2, Pallas kernels, hyena(): call(hyena_body, (struct((ROWS, 512), BF16), struct((3, ROWS, 512), F32),...  17.6 us
    ppermute x8, waiting for transfers between devices, shift(): return lax.ppermute(x, 'cz', [(i, (i + by) % 8) for i in range(8)])  14.7 us
    pallas_call x1, Pallas kernels, key_pass(): call(key_body, struct((GROUP, 2 * HD), BF16), 'key_pass', grid=(1,), in_s...  9.87 us
    ppermute x1, waiting for transfers between devices, body(): nxt = lax.ppermute(rim, CTX, [(i + 1, i) for i in range(31)])  9.73 us
    all_to_all x2, starting transfers between devices, exchange(): return lax.all_to_all(x, axis, 0, 0, tiled=True)  9.52 us
    pallas_call x1, Pallas kernels, query_pass(): call(query_body, (struct((GROUP, 2 * HD), BF16), struct((8, 640), F32)),...  5.34 us
  transfers between devices with their start and end apart: 12, of which 7 were waited for; matrix products, arithmetic and copies ran while one was open for 2% of the time, Pallas kernels for 17%

profile of v8, /device:TPU:2, one launch (start us, length us, event | category | flops | bytes accessed | tf_op | source)
XLA Modules:
  0.0 157.5 jit_solution(4526432135836453912)
XLA Ops:
  0.6 2.5 %pack.1 = (bf16[4,144,512]{2,1,0:T(8,128)(2,1)}, bf16[3,136,512]{2,1,0:T(8,128)(2,1)}, bf16[288,512]{1,0:T(8,128)(2,1)}) custom-call(bf16[144,512]{1,0:T(8,128)(2,1)} %q_ref.1, bf16[144,512]{1,0:T(8,128)(2,1)} %d_ref.1, bf16[144,512]{1,0:T(8,128)(2,1)} %k_ref.1, bf16[144,512]{1,0:T(8,128)(2,1)} %v_ref.1, bf16[3,144,512]{2,1,0:T(8,128)(2,1)} %bitcast.20, ...), custom_call_target="tpu_custom_call" | custom-call | tf_op jit(solution)/shard_map/pack/pallas_call | solution.py:63
  3.2 4.6 %all-to-all-start = ((bf16[4,144,512]{2,1,0:T(8,128)(2,1)}), bf16[4,144,512]{2,1,0:T(8,128)(2,1)S(1)}, u32[]{:S(2)}, u32[]{:S(2)}) async-start(bf16[4,144,512]{2,1,0:T(8,128)(2,1)} %get-tuple-element.47), calls=%async_computation | async-start | bytes 1179648 | tf_op jit(solution)/shard_map/all_to_all | solution.py:420
  7.8 3.9 %collective-permute-start = (bf16[3,136,512]{2,1,0:T(8,128)(2,1)S(1)}, bf16[3,136,512]{2,1,0:T(8,128)(2,1)S(1)}, u32[]{:S(2)}, u32[]{:S(2)}) collective-permute-start(bf16[3,136,512]{2,1,0:T(8,128)(2,1)S(1)} %copy-done.14), channel_id=1, source_target_pairs={{0,8},{8,16},{16,24},{24,32},{32,40},{40,48},{48,56},{56,64},{64,7... | collective-permute-start | bytes 1253384 | tf_op jit(solution)/shard_map/ppermute | solution.py:436
  11.7 1.3 collective-permute-start.1
  13.0 9.7 %collective-permute-done.1.next_ref = bf16[288,512]{1,0:T(8,128)(2,1)S(1)} collective-permute-done((bf16[288,512]{1,0:T(8,128)(2,1)S(1)}, bf16[288,512]{1,0:T(8,128)(2,1)S(1)}, u32[]{:S(2)}, u32[]{:S(2)}) %collective-permute-start.1) | collective-permute-done | bytes 294944 | tf_op jit(solution)/shard_map/ppermute | solution.py:437
  23.2 9.3 %collective-permute-start.3 = (bf16[576,512]{1,0:T(8,128)(2,1)S(1)}, bf16[576,512]{1,0:T(8,128)(2,1)S(1)}, u32[]{:S(2)}, u32[]{:S(2)}) collective-permute-start(bf16[576,512]{1,0:T(8,128)(2,1)S(1)} %bitcast.14), channel_id=1, source_target_pairs={{0,224},{32,0},{64,32},{96,64},{128,96},{160,128},{192,160},{224,1... | collective-permute-start | bytes 1769480 | tf_op jit(solution)/shard_map/ppermute | solution.py:443
  33.1 8.8 %hyena.2 = (bf16[144,512]{1,0:T(8,128)(2,1)}, f32[3,144,512]{2,1,0:T(8,128)}, f32[128,128]{1,0:T(8,128)}, f32[3,8,128]{2,1,0:T(8,128)}) custom-call(bf16[3,144,512]{2,1,0:T(8,128)(2,1)} %bitcast.21, bf16[3,136,512]{2,1,0:T(8,128)(2,1)} %copy-done.7, bf16[288,512]{1,0:T(8,128)(2,1)} %copy-done.8, bf16[144,512]{1,0:T(8,128)(2,1)} %up_ref.5, ...), custom_call_target="tpu_custom_call" | custom-call | tf_op jit(solution)/shard_map/hyena/pallas_call | solution.py:193
  41.8 1.4 collective-permute-done.3.refs_4_
  43.3 3.4 %collective-permute-done.2.refs_1_ = bf16[576,512]{1,0:T(8,128)(2,1)S(1)} collective-permute-done((bf16[576,512]{1,0:T(8,128)(2,1)S(1)}, bf16[576,512]{1,0:T(8,128)(2,1)S(1)}, u32[]{:S(2)}, u32[]{:S(2)}) %collective-permute-start.2) | collective-permute-done | bytes 589856 | tf_op jit(solution)/shard_map/ppermute | solution.py:443
  46.7 3.2 %collective-permute-start.5 = (bf16[576,512]{1,0:T(8,128)(2,1)S(1)}, bf16[576,512]{1,0:T(8,128)(2,1)S(1)}, u32[]{:S(2)}, u32[]{:S(2)}) collective-permute-start(bf16[576,512]{1,0:T(8,128)(2,1)S(1)} %collective-permute-done.3.refs_4_), channel_id=1, source_target_pairs={{0,224},{32,0},{64,32},{96,64},{128,96},{160,128},{192,160},{224,1... | collective-permute-start | bytes 1769480 | tf_op jit(solution)/shard_map/ppermute | solution.py:443
  49.9 8.8 %hyena.3 = (bf16[144,512]{1,0:T(8,128)(2,1)}, f32[3,144,512]{2,1,0:T(8,128)}, f32[128,128]{1,0:T(8,128)}, f32[3,8,128]{2,1,0:T(8,128)}) custom-call(bf16[3,144,512]{2,1,0:T(8,128)(2,1)} %bitcast.22, bf16[3,136,512]{2,1,0:T(8,128)(2,1)} %copy-done.7, bf16[288,512]{1,0:T(8,128)(2,1)} %copy-done.8, ...), custom_call_target="tpu_custom_call", output_to_operand_aliasing={{0}: (6, {}), {1}: (7, {})} | custom-call | tf_op jit(solution)/shard_map/hyena/pallas_call | solution.py:193
  58.8 1.4 collective-permute-done.4.refs_2_
  60.2 3.2 %collective-permute-start.7 = (bf16[576,512]{1,0:T(8,128)(2,1)S(1)}, bf16[576,512]{1,0:T(8,128)(2,1)S(1)}, u32[]{:S(2)}, u32[]{:S(2)}) collective-permute-start(bf16[576,512]{1,0:T(8,128)(2,1)S(1)} %collective-permute-done.5.refs_5_), channel_id=1, source_target_pairs={{0,224},{32,0},{64,32},{96,64},{128,96},{160,128},{192,160},{224,1... | collective-permute-start | bytes 1769480 | tf_op jit(solution)/shard_map/ppermute | solution.py:443
  63.5 0.7 maximum_bitcast_fusion
  64.2 0.9 maximum_maximum_fusion
  65.2 15.7 %all_to_all.25 = f32[32,10,128]{2,1,0:T(8,128)S(1)} all-to-all(f32[32,10,128]{2,1,0:T(8,128)S(1)} %reshape.51), channel_id=1, replica_groups=mesh['cz'=8,'cy'=4,'fsdp'=4,'tp'=2] {'cy','fsdp','tp'}, dimensions={0} | all-to-all | bytes 327680 | tf_op jit(solution)/shard_map/all_to_all | solution.py:420
  81.0 0.7 copy-done.1
  81.9 1.7 %collective-permute-start.9 = (bf16[576,256]{1,0:T(8,128)(2,1)S(1)}, bf16[576,256]{1,0:T(8,128)(2,1)S(1)}, u32[]{:S(2)}, u32[]{:S(2)}) collective-permute-start(bf16[576,256]{1,0:T(8,128)(2,1)S(1)} %slice.28), channel_id=1, source_target_pairs={{0,224},{32,0},{64,32},{96,64},{128,96},{160,128},{192,160},{224,1... | collective-permute-start | bytes 884744 | tf_op jit(solution)/shard_map/ppermute | solution.py:443
  84.0 5.9 %collective-permute-done.9.refs_7_ = bf16[576,256]{1,0:T(8,128)(2,1)S(1)} collective-permute-done((bf16[576,256]{1,0:T(8,128)(2,1)S(1)}, bf16[576,256]{1,0:T(8,128)(2,1)S(1)}, u32[]{:S(2)}, u32[]{:S(2)}) %collective-permute-start.9) | collective-permute-done | bytes 294944 | tf_op jit(solution)/shard_map/ppermute | solution.py:443
  89.8 2.6 %collective-permute-done.8.refs_7_ = bf16[576,256]{1,0:T(8,128)(2,1)S(1)} collective-permute-done((bf16[576,256]{1,0:T(8,128)(2,1)S(1)}, bf16[576,256]{1,0:T(8,128)(2,1)S(1)}, u32[]{:S(2)}, u32[]{:S(2)}) %collective-permute-start.8) | collective-permute-done | bytes 294944 | tf_op jit(solution)/shard_map/ppermute | solution.py:443
  92.4 0.7 copy-done.10
  93.1 5.3 %query_pass.1 = (bf16[576,256]{1,0:T(8,128)(2,1)}, f32[8,640]{1,0:T(8,128)}) custom-call(s32[1]{0:T(128)} %bitcast.2.where_ref, bf16[576,512]{1,0:T(8,128)(2,1)} %bitcast.16, bf16[576,512]{1,0:T(8,128)(2,1)} %bitcast.17, bf16[576,512]{1,0:T(8,128)(2,1)} %copy-done.4, bf16[576,512]{1,0:T(8,128)(2,1)} %copy-done.5, bf16[576,512]{1,0:T(8,128)(2,1)} %copy-done.1, ...), custom_call_target="tpu_custom_call" | custom-call | tf_op jit(solution)/shard_map/query_pass/pallas_call | solution.py:326
  98.5 0.7 slice.29
  99.2 18.1 %all_to_all.26 = f32[8,20,128]{2,1,0:T(8,128)S(1)} all-to-all(f32[8,20,128]{2,1,0:T(8,128)S(1)} %broadcast_in_dim.7), channel_id=1, replica_groups=mesh['cz'=8,'cy'=4,'fsdp'=4,'tp'=2] {'cz'}, dimensions={0} | all-to-all | bytes 163840 | tf_op jit(solution)/shard_map/all_to_all | solution.py:420
  118.1 4.9 %all-to-all-start.3 = ((f32[8,10,128]{2,1,0:T(8,128)}), f32[8,10,128]{2,1,0:T(8,128)S(1)}, u32[]{:S(2)}, u32[]{:S(2)}) async-start(f32[8,10,128]{2,1,0:T(8,128)} %broadcast_in_dim.8), calls=%async_computation.3 | async-start | bytes 131072 | tf_op jit(solution)/shard_map/all_to_all | solution.py:420
  123.1 0.6 copy.21
  123.7 9.9 %key_pass.1.ok_ref = bf16[576,256]{1,0:T(8,128)(2,1)} custom-call(s32[1]{0:T(128)} %bitcast.2.where_ref, bf16[576,512]{1,0:T(8,128)(2,1)} %bitcast.18, f32[9,2,512]{2,1,0:T(2,128)} %bitcast.24, bf16[576,512]{1,0:T(8,128)(2,1)} %bitcast.19, bf16[576,512]{1,0:T(8,128)(2,1)} %copy-done.4, bf16[576,512]{1,0:T(8,128)(2,1)} %copy-done.5, ...), custom_call_target="tpu_custom_call" | custom-call | tf_op jit(solution)/shard_map/key_pass/pallas_call | solution.py:402
  134.2 2.0 %join.1 = bf16[4,184,512]{2,1,0:T(8,128)(2,1)} custom-call(bf16[576,256]{1,0:T(8,128)(2,1)} %get-tuple-element.76.oq_ref, bf16[576,256]{1,0:T(8,128)(2,1)} %key_pass.1.ok_ref, f32[80,128]{1,0:T(8,128)} %reshape.55.part_ref), custom_call_target="tpu_custom_call" | custom-call | tf_op jit(solution)/shard_map/join/pallas_call | solution.py:398
  136.3 16.8 %all_to_all.27.x_ref = bf16[4,184,512]{2,1,0:T(8,128)(2,1)} all-to-all(bf16[4,184,512]{2,1,0:T(8,128)(2,1)} %join.1), channel_id=1, replica_groups=mesh['cz'=8,'cy'=4,'fsdp'=4,'tp'=2] {'cy'}, dimensions={0} | all-to-all | bytes 1507328 | tf_op jit(solution)/shard_map/all_to_all | solution.py:420
  153.0 2.2 %unpack.1 = (bf16[144,512]{1,0:T(8,128)(2,1)}, f32[144,512]{1,0:T(8,128)}, f32[144,512]{1,0:T(8,128)}, f32[144,512]{1,0:T(8,128)}, f32[4,80,128]{2,1,0:T(8,128)}) custom-call(bf16[4,184,512]{2,1,0:T(8,128)(2,1)} %all_to_all.27.x_ref), custom_call_target="tpu_custom_call" | custom-call | tf_op jit(solution)/shard_map/unpack/pallas_call | solution.py:89
  155.2 1.0 reshape.56
  156.8 0.7 slice.41
  (58 shorter events, 4.0 us)
Async XLA Ops:
  3.1 4.6 %copy-start.14 = (bf16[3,136,512]{2,1,0:T(8,128)(2,1)S(1)}, bf16[3,136,512]{2,1,0:T(8,128)(2,1)}, u32[]{:S(2)}) copy-start(bf16[3,136,512]{2,1,0:T(8,128)(2,1)} %get-tuple-element.48) | copy-start | bytes 1253380
  3.1 8.6 %copy-start.15 = (bf16[288,512]{1,0:T(8,128)(2,1)S(1)}, bf16[288,512]{1,0:T(8,128)(2,1)}, u32[]{:S(2)}) copy-start(bf16[288,512]{1,0:T(8,128)(2,1)} %get-tuple-element.49) | copy-start | bytes 884740
  3.1 29.3 %copy-start.12 = (f32[3,7,256]{2,1,0:T(8,128)S(1)}, f32[3,7,256]{2,1,0:T(8,128)}, u32[]{:S(2)}) copy-start(f32[3,7,256]{2,1,0:T(8,128)} %param.9) | copy-start | bytes 64516
  3.2 20.0 %all-to-all-start = ((bf16[4,144,512]{2,1,0:T(8,128)(2,1)}), bf16[4,144,512]{2,1,0:T(8,128)(2,1)S(1)}, u32[]{:S(2)}, u32[]{:S(2)}) async-start(bf16[4,144,512]{2,1,0:T(8,128)(2,1)} %get-tuple-element.47), calls=%async_computation | async-start | bytes 1179648 | tf_op jit(solution)/shard_map/all_to_all | solution.py:420
  7.8 15.4 %collective-permute-start = (bf16[3,136,512]{2,1,0:T(8,128)(2,1)S(1)}, bf16[3,136,512]{2,1,0:T(8,128)(2,1)S(1)}, u32[]{:S(2)}, u32[]{:S(2)}) collective-permute-start(bf16[3,136,512]{2,1,0:T(8,128)(2,1)S(1)} %copy-done.14), channel_id=1, source_target_pairs={{0,8},{8,16},{16,24},{24,32},{32,40},{40,48},{48,56},{56,64},{64,7... | collective-permute-start | bytes 1253384 | tf_op jit(solution)/shard_map/ppermute | solution.py:436
  11.7 11.0 %collective-permute-start.1 = (bf16[288,512]{1,0:T(8,128)(2,1)S(1)}, bf16[288,512]{1,0:T(8,128)(2,1)S(1)}, u32[]{:S(2)}, u32[]{:S(2)}) collective-permute-start(bf16[288,512]{1,0:T(8,128)(2,1)S(1)} %copy-done.15), channel_id=1, source_target_pairs={{8,0},{16,8},{24,16},{32,24},{40,32},{48,40},{56,48},{64,56},{72,6... | collective-permute-start | bytes 884744 | tf_op jit(solution)/shard_map/ppermute | solution.py:437
  22.8 10.3 %copy-start.8 = (bf16[288,512]{1,0:T(8,128)(2,1)}, bf16[288,512]{1,0:T(8,128)(2,1)S(1)}, u32[]{:S(2)}) copy-start(bf16[288,512]{1,0:T(8,128)(2,1)S(1)} %collective-permute-done.1.next_ref) | copy-start | bytes 884740
  23.2 9.9 %copy-start.7 = (bf16[3,136,512]{2,1,0:T(8,128)(2,1)}, bf16[3,136,512]{2,1,0:T(8,128)(2,1)S(1)}, u32[]{:S(2)}) copy-start(bf16[3,136,512]{2,1,0:T(8,128)(2,1)S(1)} %collective-permute-done.prev_ref) | copy-start | bytes 1253380
  23.2 18.6 %copy-start = (bf16[4,144,512]{2,1,0:T(8,128)(2,1)}, bf16[4,144,512]{2,1,0:T(8,128)(2,1)S(1)}, u32[]{:S(2)}) copy-start(bf16[4,144,512]{2,1,0:T(8,128)(2,1)S(1)} %all-to-all-done) | copy-start | bytes 1769476
  23.2 20.1 %collective-permute-start.3 = (bf16[576,512]{1,0:T(8,128)(2,1)S(1)}, bf16[576,512]{1,0:T(8,128)(2,1)S(1)}, u32[]{:S(2)}, u32[]{:S(2)}) collective-permute-start(bf16[576,512]{1,0:T(8,128)(2,1)S(1)} %bitcast.14), channel_id=1, source_target_pairs={{0,224},{32,0},{64,32},{96,64},{128,96},{160,128},{192,160},{224,1... | collective-permute-start | bytes 1769480 | tf_op jit(solution)/shard_map/ppermute | solution.py:443
  32.5 14.2 %collective-permute-start.2 = (bf16[576,512]{1,0:T(8,128)(2,1)S(1)}, bf16[576,512]{1,0:T(8,128)(2,1)S(1)}, u32[]{:S(2)}, u32[]{:S(2)}) collective-permute-start(bf16[576,512]{1,0:T(8,128)(2,1)S(1)} %bitcast.15), channel_id=1, source_target_pairs={{0,32},{32,64},{64,96},{96,128},{128,160},{160,192},{192,224},{224... | collective-permute-start | bytes 1769480 | tf_op jit(solution)/shard_map/ppermute | solution.py:443
  43.3 15.5 %copy-start.3 = (bf16[576,512]{1,0:T(8,128)(2,1)}, bf16[576,512]{1,0:T(8,128)(2,1)S(1)}, u32[]{:S(2)}) copy-start(bf16[576,512]{1,0:T(8,128)(2,1)S(1)} %collective-permute-done.3.refs_4_) | copy-start | bytes 1769476
  46.7 12.1 %copy-start.4 = (bf16[576,512]{1,0:T(8,128)(2,1)}, bf16[576,512]{1,0:T(8,128)(2,1)S(1)}, u32[]{:S(2)}) copy-start(bf16[576,512]{1,0:T(8,128)(2,1)S(1)} %collective-permute-done.2.refs_1_) | copy-start | bytes 1769476
  46.7 13.4 %collective-permute-start.4 = (bf16[576,512]{1,0:T(8,128)(2,1)S(1)}, bf16[576,512]{1,0:T(8,128)(2,1)S(1)}, u32[]{:S(2)}, u32[]{:S(2)}) collective-permute-start(bf16[576,512]{1,0:T(8,128)(2,1)S(1)} %collective-permute-done.2.refs_1_), channel_id=1, source_target_pairs={{0,32},{32,64},{64,96},{96,128},{128,160},{160,192},{192,224},{224... | collective-permute-start | bytes 1769480 | tf_op jit(solution)/shard_map/ppermute | solution.py:443
  46.7 13.4 %collective-permute-start.5 = (bf16[576,512]{1,0:T(8,128)(2,1)S(1)}, bf16[576,512]{1,0:T(8,128)(2,1)S(1)}, u32[]{:S(2)}, u32[]{:S(2)}) collective-permute-start(bf16[576,512]{1,0:T(8,128)(2,1)S(1)} %collective-permute-done.3.refs_4_), channel_id=1, source_target_pairs={{0,224},{32,0},{64,32},{96,64},{128,96},{160,128},{192,160},{224,1... | collective-permute-start | bytes 1769480 | tf_op jit(solution)/shard_map/ppermute | solution.py:443
  49.9 13.6 %copy-start.13 = (f32[3,8,128]{2,1,0:T(8,128)S(1)}, f32[3,8,128]{2,1,0:T(8,128)}, u32[]{:S(2)}) copy-start(f32[3,8,128]{2,1,0:T(8,128)} %get-tuple-element.70) | copy-start | bytes 36868
  49.9 14.3 %copy-start.11 = (f32[128,128]{1,0:T(8,128)S(1)}, f32[128,128]{1,0:T(8,128)}, u32[]{:S(2)}) copy-start(f32[128,128]{1,0:T(8,128)} %get-tuple-element.68) | copy-start | bytes 196612
  60.1 20.8 %copy-start.5 = (bf16[576,512]{1,0:T(8,128)(2,1)}, bf16[576,512]{1,0:T(8,128)(2,1)S(1)}, u32[]{:S(2)}) copy-start(bf16[576,512]{1,0:T(8,128)(2,1)S(1)} %collective-permute-done.4.refs_2_) | copy-start | bytes 1769476
  60.1 20.8 %copy-start.6 = (bf16[576,512]{1,0:T(8,128)(2,1)}, bf16[576,512]{1,0:T(8,128)(2,1)S(1)}, u32[]{:S(2)}) copy-start(bf16[576,512]{1,0:T(8,128)(2,1)S(1)} %collective-permute-done.5.refs_5_) | copy-start | bytes 1769476
  60.1 20.8 %collective-permute-start.6 = (bf16[576,512]{1,0:T(8,128)(2,1)S(1)}, bf16[576,512]{1,0:T(8,128)(2,1)S(1)}, u32[]{:S(2)}, u32[]{:S(2)}) collective-permute-start(bf16[576,512]{1,0:T(8,128)(2,1)S(1)} %collective-permute-done.4.refs_2_), channel_id=1, source_target_pairs={{0,32},{32,64},{64,96},{96,128},{128,160},{160,192},{192,224},{224... | collective-permute-start | bytes 1769480 | tf_op jit(solution)/shard_map/ppermute | solution.py:443
  60.2 20.7 %collective-permute-start.7 = (bf16[576,512]{1,0:T(8,128)(2,1)S(1)}, bf16[576,512]{1,0:T(8,128)(2,1)S(1)}, u32[]{:S(2)}, u32[]{:S(2)}) collective-permute-start(bf16[576,512]{1,0:T(8,128)(2,1)S(1)} %collective-permute-done.5.refs_5_), channel_id=1, source_target_pairs={{0,224},{32,0},{64,32},{96,64},{128,96},{160,128},{192,160},{224,1... | collective-permute-start | bytes 1769480 | tf_op jit(solution)/shard_map/ppermute | solution.py:443
  80.9 0.8 copy-start.1
  80.9 1.0 copy-start.2
  81.9 7.9 %collective-permute-start.9 = (bf16[576,256]{1,0:T(8,128)(2,1)S(1)}, bf16[576,256]{1,0:T(8,128)(2,1)S(1)}, u32[]{:S(2)}, u32[]{:S(2)}) collective-permute-start(bf16[576,256]{1,0:T(8,128)(2,1)S(1)} %slice.28), channel_id=1, source_target_pairs={{0,224},{32,0},{64,32},{96,64},{128,96},{160,128},{192,160},{224,1... | collective-permute-start | bytes 884744 | tf_op jit(solution)/shard_map/ppermute | solution.py:443
  83.6 8.8 %collective-permute-start.8 = (bf16[576,256]{1,0:T(8,128)(2,1)S(1)}, bf16[576,256]{1,0:T(8,128)(2,1)S(1)}, u32[]{:S(2)}, u32[]{:S(2)}) collective-permute-start(bf16[576,256]{1,0:T(8,128)(2,1)S(1)} %slice.27), channel_id=1, source_target_pairs={{0,32},{32,64},{64,96},{96,128},{128,160},{160,192},{192,224},{224... | collective-permute-start | bytes 884744 | tf_op jit(solution)/shard_map/ppermute | solution.py:443
  89.8 8.7 %copy-start.9 = (bf16[576,256]{1,0:T(8,128)(2,1)}, bf16[576,256]{1,0:T(8,128)(2,1)S(1)}, u32[]{:S(2)}) copy-start(bf16[576,256]{1,0:T(8,128)(2,1)S(1)} %collective-permute-done.9.refs_7_) | copy-start | bytes 884740
  92.4 0.7 copy-start.10
  118.1 15.5 %all-to-all-start.3 = ((f32[8,10,128]{2,1,0:T(8,128)}), f32[8,10,128]{2,1,0:T(8,128)S(1)}, u32[]{:S(2)}, u32[]{:S(2)}) async-start(f32[8,10,128]{2,1,0:T(8,128)} %broadcast_in_dim.8), calls=%async_computation.3 | async-start | bytes 131072 | tf_op jit(solution)/shard_map/all_to_all | solution.py:420

commit v9 on v8

--- a/solution.py
+++ b/solution.py
@@ -52,7 +52,9 @@
     for h in range(4):
         for slot, ref in enumerate((q_ref, d_ref, k_ref, v_ref)):
             out_ref[h, :, slot * HD : (slot + 1) * HD] = ref[:, h * HD : (h + 1) * HD]
-    tail_ref[...] = feat_ref[:, 8:]
+    tail_ref[0:136] = feat_ref[0, 8:]
+    tail_ref[136:272] = feat_ref[2, 8:]
+    tail_ref[272:280] = feat_ref[1, 136:]
     rim_ref[0:136] = feat_ref[1, 0:136]
     rim_ref[136:272] = up_ref[0:136]
     rim_ref[272:280] = feat_ref[0, 0:8]
@@ -64,14 +66,14 @@
         pack_body,
         (
             struct((4, ROWS, 4 * HD), BF16),
-            struct((3, 136, 4 * HD), BF16),
+            struct((280, 4 * HD), BF16),
             struct((288, 4 * HD), BF16),
         ),
         "pack",
     )(*parts)
 
 
-def unpack_body(x_ref, attended_ref, gq_ref, gk_ref, gv_ref, grads_ref):
+def unpack_body(x_ref, attended_ref, gq_ref, gk_ref, gv_ref, glong_ref, gshort_ref, grads_ref):
     for h in range(4):
         at = slice(h * HD, (h + 1) * HD)
         attended_ref[:, at] = x_ref[h, :ROWS, 0:HD]
@@ -81,15 +83,26 @@
         for side in range(2):
             high = x_ref[h, ROWS:, side * HD : (side + 1) * HD].astype(F32)
             low = x_ref[h, ROWS:, (side + 2) * HD : (side + 3) * HD].astype(F32)
-            grads_ref[h, side * 40 : (side + 1) * 40] = high + low
+            first = 80 * h + 40 * side
+            grads_ref[first : first + 40] = high + low
+    for side in range(2):
+        at = slice(side * HD, (side + 1) * HD)
+        glong_ref[:, at] = grads_ref[128 * side : 128 * (side + 1)]
+        for g in range(3):
+            first = 256 + 24 * side + 8 * g
+            gshort_ref[g, :, at] = grads_ref[first : first + 7]
 
 
 def unpack(x):
     whole = struct((ROWS, 4 * HD), F32)
     return call(
         unpack_body,
-        (struct((ROWS, 4 * HD), BF16), whole, whole, whole, struct((4, 80, HD), F32)),
+        (
+            struct((ROWS, 4 * HD), BF16), whole, whole, whole,
+            struct((128, 256), F32), struct((3, 7, 256), F32),
+        ),
         "unpack",
+        scratch_shapes=[pltpu.VMEM((320, HD), F32)],
     )(x)
 
 
@@ -100,10 +113,10 @@
     ) = refs[-14:]
     turn = pl.program_id(0)
     for slot, g in enumerate((0, 2)):
-        x_ref[slot, 0:136] = prev_ref[g].astype(F32)
+        x_ref[slot, 0:136] = prev_ref[136 * slot : 136 * (slot + 1)].astype(F32)
         x_ref[slot, 136:280] = feat_ref[g].astype(F32)
         x_ref[slot, 280:288] = next_ref[272 + 8 * slot : 280 + 8 * slot].astype(F32)
-    x1_ref[0:136] = prev_ref[1].astype(F32)
+    x1_ref[128:136] = prev_ref[272:280].astype(F32)
     x1_ref[136:280] = feat_ref[1].astype(F32)
     x1_ref[280:416] = next_ref[0:136].astype(F32)
     taps = [[short_ref[g, s : s + 1, :] for s in range(7)] for g in range(3)]
@@ -201,7 +214,7 @@
         "hyena",
         grid=(2,),
         in_specs=[
-            cols(3, ROWS), cols(3, 136), cols(288), cols(ROWS), filters(3, 8), filters(128),
+            cols(3, ROWS), cols(280), cols(288), cols(ROWS), filters(3, 8), filters(128),
         ] + [kept] * len(earlier),
         out_specs=(cols(ROWS), cols(3, ROWS), sums(128), sums(3, 8)),
         input_output_aliases={6 + i: i for i in range(len(earlier))},
@@ -260,8 +273,8 @@
     return total
 
 
-def query_body(where_ref, own_ref, *refs):
-    out_ref, stat_ref, s_ref, mx_ref, l_ref, o_ref, st_ref, kv_ref = refs[8:]
+def query_body(where_ref, part_ref, own_ref, *refs):
+    out_ref, small_ref, s_ref, mx_ref, l_ref, o_ref, st_ref, kv_ref = refs[8:]
     assemble(where_ref, refs[:8], kv_ref, True)
     first = where_ref[0] * GROUP
     clear = first // CHUNK
@@ -319,19 +332,26 @@
     lane = lax.broadcasted_iota(jnp.int32, (GROUP, HD), 1)
     st_ref[0:GROUP] = jnp.where(lane == 0, peak + jnp.log2(norm), delta)
     st_ref[GROUP:640] = jnp.zeros((640 - GROUP, HD), F32)
-    stat_ref[...] = st_ref[...].T[0:8]
-
-
-def query_pass(where, own, kv):
+    rows = st_ref[...].T
+    for line in range(2):
+        for j in range(5):
+            row = rows[line : line + 1, j * 128 : (j + 1) * 128]
+            small_ref[:, 5 * line + j : 5 * line + j + 1, :] = jnp.broadcast_to(
+                row[None], (8, 1, 128)
+            )
+    for n in range(8):
+        small_ref[n, 10:20] = part_ref[...]
+
+
+def query_pass(where, part, own, kv):
     return call(
         query_body,
-        (struct((GROUP, 2 * HD), BF16), struct((8, 640), F32)),
+        (struct((GROUP, 2 * HD), BF16), struct((8, 20, HD), F32)),
         "query_pass",
         grid=(1,),
         in_specs=[pl.BlockSpec(memory_space=pltpu.SMEM)]
-        + [part_of(0)]
-        + [part_of(1)] * 7
-        + [part_of(0)],
+        + [pl.BlockSpec(memory_space=pltpu.VMEM)]
+        + [part_of(side) for side in (0, 1, 1, 1, 0, 1, 1, 0, 0)],
         scratch_shapes=[
             pltpu.VMEM((CHUNKS, GROUP, CHUNK), F32),
             pltpu.VMEM((GROUP, HD), F32),
@@ -340,7 +360,7 @@
             pltpu.VMEM((640, HD), F32),
             pltpu.VMEM((SEQ, 2 * HD), BF16),
         ],
-    )(where, own, *kv)
+    )(where, part, own, *kv)
 
 
 def key_body(where_ref, own_ref, stat_ref, *refs):
@@ -381,7 +401,9 @@
     out_ref[:, HD:] = gv_ref[...].astype(BF16)
 
 
-def join_body(oq_ref, ok_ref, part_ref, out_ref):
+def join_body(oq_ref, ok_ref, slices_ref, out_ref, part_ref):
+    for n in range(8):
+        part_ref[10 * n : 10 * (n + 1)] = slices_ref[n]
     for j in range(4):
         at = slice(j * ROWS, (j + 1) * ROWS)
         out_ref[j, :ROWS, : 2 * HD] = oq_ref[at]
@@ -395,7 +417,8 @@
 
 
 def join(out_q, out_k, part):
-    return call(join_body, struct((4, ROWS + 40, 4 * HD), BF16), "join")(out_q, out_k, part)
+    return call(join_body, struct((4, ROWS + 40, 4 * HD), BF16), "join",
+                scratch_shapes=[pltpu.VMEM((80, HD), F32)])(out_q, out_k, part)
 
 
 def key_pass(where, own, qd, stats):
@@ -458,29 +481,33 @@
     step()
     second = hyena(1, feat, prev, nxt, grad_mixed, short8, long_filter_taps, first[:2])
     mixed, gfeat, glong, gshort = order(*second)
-    step()
-    glong = jnp.concatenate([first[2], glong], 1)
-    gshort = jnp.concatenate([first[3], gshort], 2).reshape(24, 256)
-    grads = jnp.concatenate([glong, gshort, jnp.zeros((8, 256), F32)], 0)
+    z = where[0]
+    low, high = 0, 2 * HD
+    up_side = jnp.where((z >= 2) & (z <= 6), high, low)
+    down_side = jnp.where((z >= 1) & (z <= 5), low, high)
+    rising.append(shift(lax.dynamic_slice(rising[2], (0, up_side), (GROUP, 2 * HD)), 1))
+    falling.append(shift(lax.dynamic_slice(falling[2], (0, down_side), (GROUP, 2 * HD)), -1))
+    grads = jnp.concatenate(
+        [first[2], glong, first[3].reshape(24, HD), gshort.reshape(24, HD), jnp.zeros((16, HD), F32)],
+        0,
+    )
     part = jnp.sum(exchange(grads.reshape(32, 10, HD), YFT), axis=0)
-    (part,) = order(part)
-    far_kv = shift(rising[-1][:, 2 * HD :], 1)
-    far_qd = shift(falling[-1][:, : 2 * HD], -1)
+    order()
+    far_kv = lax.ppermute(rising[3], "cz", [(i, i + 1) for i in range(3, 7)])
+    far_qd = lax.ppermute(falling[3], "cz", [(i, i - 1) for i in range(1, 5)])
     far_kv, far_qd, own = lax.optimization_barrier((far_kv, far_qd, own))
     pieces = [own] + rising[1:] + falling[1:]
 
-    out_q, stats = query_pass(where, own, pieces + [far_kv])
-    small = jnp.concatenate([stats[:2].reshape(10, HD), part], 0)
-    small = share(small, "cz", 8)
+    out_q, small = query_pass(where, part, own, pieces + [far_kv])
+    small = exchange(small, "cz")
     part = share(jnp.sum(small[:, 10:], axis=0), FT, 8)
     stats = small[:, :10].reshape(8, 2, 640)[:, :, :GROUP].transpose(1, 0, 2)
     stats = stats.reshape(2, CHUNKS, CHUNK).transpose(1, 0, 2)
     out_k = key_pass(where, own, pieces + [far_qd], stats)
-    result = join(out_q, out_k, part.reshape(80, HD))
-    attended, grad_queries, grad_keys, grad_values, grads = unpack(exchange(result, "cy"))
-    grads = grads.reshape(160, 256)
-    grad_long = grads[:128]
-    grad_short = grads[128:152].reshape(3, 8, 256)[:, :7]
+    result = join(out_q, out_k, part)
+    attended, grad_queries, grad_keys, grad_values, grad_long, grad_short = unpack(
+        exchange(result, "cy")
+    )
     return (
         mixed, attended, gfeat.transpose(1, 0, 2), grad_short, grad_long,
         grad_queries, grad_keys, grad_values,

time: 159 us -> 153 us (0.962)
  local copies, waits for them, and re-layouts: 7.48 us -> 4.08 us
  waiting for transfers between devices: 24.8 us -> 22.5 us
    ppermute x1, waiting for transfers between devices: 9.73 us -> 2.37 us  [body(): nxt = lax.ppermute(rim, CTX, [(i + 1, i) for i in range(31)])]
    ppermute x1, waiting for transfers between devices: 0.43 us -> 6.74 us  [body(): prev = lax.ppermute(tail, CTX, [(i, i + 1) for i in range(31)])]
    ppermute x8 -> x6, starting transfers between devices: 17.8 us -> 15.1 us  [shift(): return lax.ppermute(x, 'cz', [(i, (i + by) % 8) for i in range(8)])]
    reshape x4 -> x0, local copies, waits for them, and re-layouts: 2.21 us -> none  [the longest x1 0.96 us: body(): grads = grads.reshape(160, 256)]
    ppermute x0 -> x2, starting transfers between devices: none -> 1.96 us  [the longest x1 1.29 us: body(): far_qd = lax.ppermute(falling[3], 'cz', [(i, i - 1) for i in range(1, 5)])]
    ppermute x8 -> x6, waiting for transfers between devices: 14.7 us -> 13.4 us  [shift(): return lax.ppermute(x, 'cz', [(i, (i + by) % 8) for i in range(8)])]
  transfers between devices with their start and end apart: 12 -> 12, of which waited for: 7 -> 7; matrix products, arithmetic and copies ran while one was open for 2% -> 1% of each run, Pallas kernels for 17% -> 18%
where the time goes in v9:
time: 153 us; the launch traced here: 152 us
  blocking collectives  51.9 us (34%)
  Pallas kernels  39.4 us (26%)
  starting transfers between devices  32.2 us (21%)
  waiting for transfers between devices  22.5 us (15%)
  local copies, waits for them, and re-layouts  4.08 us (3%)
    all_to_all x3, blocking collectives, exchange(): return lax.all_to_all(x, axis, 0, 0, tiled=True)  51.9 us
    pallas_call x2, Pallas kernels, hyena(): call(hyena_body, (struct((ROWS, 512), BF16), struct((3, ROWS, 512), F32),...  17.5 us
    ppermute x6, starting transfers between devices, shift(): return lax.ppermute(x, 'cz', [(i, (i + by) % 8) for i in range(8)])  15.1 us
    ppermute x6, waiting for transfers between devices, shift(): return lax.ppermute(x, 'cz', [(i, (i + by) % 8) for i in range(8)])  13.4 us
    pallas_call x1, Pallas kernels, key_pass(): call(key_body, struct((GROUP, 2 * HD), BF16), 'key_pass', grid=(1,), in_s...  9.87 us
    all_to_all x2, starting transfers between devices, exchange(): return lax.all_to_all(x, axis, 0, 0, tiled=True)  9.33 us
    ppermute x1, waiting for transfers between devices, body(): prev = lax.ppermute(tail, CTX, [(i, i + 1) for i in range(31)])  6.74 us
    pallas_call x1, Pallas kernels, query_pass(): call(query_body, (struct((GROUP, 2 * HD), BF16), struct((8, 20, HD), F32)...  5.4 us
  transfers between devices with their start and end apart: 12, of which 7 were waited for; matrix products, arithmetic and copies ran while one was open for 1% of the time, Pallas kernels for 18%

profile of v9, /device:TPU:2, one launch (start us, length us, event | category | flops | bytes accessed | tf_op | source)
XLA Modules:
  0.0 151.6 jit_solution(2580295040139235702)
XLA Ops:
  0.6 2.5 %pack.1 = (bf16[4,144,512]{2,1,0:T(8,128)(2,1)}, bf16[280,512]{1,0:T(8,128)(2,1)}, bf16[288,512]{1,0:T(8,128)(2,1)}) custom-call(bf16[144,512]{1,0:T(8,128)(2,1)} %q_ref.1, bf16[144,512]{1,0:T(8,128)(2,1)} %d_ref.1, bf16[144,512]{1,0:T(8,128)(2,1)} %k_ref.1, bf16[144,512]{1,0:T(8,128)(2,1)} %v_ref.1, bf16[3,144,512]{2,1,0:T(8,128)(2,1)} %bitcast.19, ...), custom_call_target="tpu_custom_call" | custom-call | tf_op jit(solution)/shard_map/pack/pallas_call | solution.py:65
  3.1 4.6 %all-to-all-start = ((bf16[4,144,512]{2,1,0:T(8,128)(2,1)}), bf16[4,144,512]{2,1,0:T(8,128)(2,1)S(1)}, u32[]{:S(2)}, u32[]{:S(2)}) async-start(bf16[4,144,512]{2,1,0:T(8,128)(2,1)} %get-tuple-element.47), calls=%async_computation | async-start | bytes 1179648 | tf_op jit(solution)/shard_map/all_to_all | solution.py:443
  7.7 1.3 collective-permute-start.1
  9.0 4.6 %collective-permute-start = (bf16[280,512]{1,0:T(8,128)(2,1)S(1)}, bf16[280,512]{1,0:T(8,128)(2,1)S(1)}, u32[]{:S(2)}, u32[]{:S(2)}) collective-permute-start(bf16[280,512]{1,0:T(8,128)(2,1)S(1)} %copy-done.18), channel_id=1, source_target_pairs={{0,8},{8,16},{16,24},{24,32},{32,40},{40,48},{48,56},{56,64},{64,7... | collective-permute-start | bytes 860168 | tf_op jit(solution)/shard_map/ppermute | solution.py:459
  13.6 6.7 %collective-permute-done.prev_ref = bf16[280,512]{1,0:T(8,128)(2,1)S(1)} collective-permute-done((bf16[280,512]{1,0:T(8,128)(2,1)S(1)}, bf16[280,512]{1,0:T(8,128)(2,1)S(1)}, u32[]{:S(2)}, u32[]{:S(2)}) %collective-permute-start) | collective-permute-done | bytes 286752 | tf_op jit(solution)/shard_map/ppermute | solution.py:459
  20.3 2.4 %collective-permute-done.1.next_ref = bf16[288,512]{1,0:T(8,128)(2,1)S(1)} collective-permute-done((bf16[288,512]{1,0:T(8,128)(2,1)S(1)}, bf16[288,512]{1,0:T(8,128)(2,1)S(1)}, u32[]{:S(2)}, u32[]{:S(2)}) %collective-permute-start.1) | collective-permute-done | bytes 294944 | tf_op jit(solution)/shard_map/ppermute | solution.py:460
  22.7 8.4 %collective-permute-start.3 = (bf16[576,512]{1,0:T(8,128)(2,1)S(1)}, bf16[576,512]{1,0:T(8,128)(2,1)S(1)}, u32[]{:S(2)}, u32[]{:S(2)}) collective-permute-start(bf16[576,512]{1,0:T(8,128)(2,1)S(1)} %bitcast.13), channel_id=1, source_target_pairs={{0,224},{32,0},{64,32},{96,64},{128,96},{160,128},{192,160},{224,1... | collective-permute-start | bytes 1769480 | tf_op jit(solution)/shard_map/ppermute | solution.py:466
  31.1 0.6 pad.4.short_ref
  31.7 8.7 %hyena.2 = (bf16[144,512]{1,0:T(8,128)(2,1)}, f32[3,144,512]{2,1,0:T(8,128)}, f32[128,128]{1,0:T(8,128)}, f32[3,8,128]{2,1,0:T(8,128)}) custom-call(bf16[3,144,512]{2,1,0:T(8,128)(2,1)} %bitcast.20, bf16[280,512]{1,0:T(8,128)(2,1)} %copy-done.8, bf16[288,512]{1,0:T(8,128)(2,1)} %copy-done.7, bf16[144,512]{1,0:T(8,128)(2,1)} %up_ref.5, ...), custom_call_target="tpu_custom_call" | custom-call | tf_op jit(solution)/shard_map/hyena/pallas_call | solution.py:206
  40.4 1.4 collective-permute-done.3.refs_4_
  41.9 3.4 %collective-permute-done.2.refs_1_ = bf16[576,512]{1,0:T(8,128)(2,1)S(1)} collective-permute-done((bf16[576,512]{1,0:T(8,128)(2,1)S(1)}, bf16[576,512]{1,0:T(8,128)(2,1)S(1)}, u32[]{:S(2)}, u32[]{:S(2)}) %collective-permute-start.2) | collective-permute-done | bytes 589856 | tf_op jit(solution)/shard_map/ppermute | solution.py:466
  45.3 3.2 %collective-permute-start.5 = (bf16[576,512]{1,0:T(8,128)(2,1)S(1)}, bf16[576,512]{1,0:T(8,128)(2,1)S(1)}, u32[]{:S(2)}, u32[]{:S(2)}) collective-permute-start(bf16[576,512]{1,0:T(8,128)(2,1)S(1)} %collective-permute-done.3.refs_4_), channel_id=1, source_target_pairs={{0,224},{32,0},{64,32},{96,64},{128,96},{160,128},{192,160},{224,1... | collective-permute-start | bytes 1769480 | tf_op jit(solution)/shard_map/ppermute | solution.py:466
  48.5 8.8 %hyena.3 = (bf16[144,512]{1,0:T(8,128)(2,1)}, f32[3,144,512]{2,1,0:T(8,128)}, f32[128,128]{1,0:T(8,128)}, f32[3,8,128]{2,1,0:T(8,128)}) custom-call(bf16[3,144,512]{2,1,0:T(8,128)(2,1)} %bitcast.21, bf16[280,512]{1,0:T(8,128)(2,1)} %copy-done.8, bf16[288,512]{1,0:T(8,128)(2,1)} %copy-done.7, ...), custom_call_target="tpu_custom_call", output_to_operand_aliasing={{0}: (6, {}), {1}: (7, {})} | custom-call | tf_op jit(solution)/shard_map/hyena/pallas_call | solution.py:206
  57.3 1.2 collective-permute-done.4.refs_2_
  58.6 3.4 %collective-permute-start.7 = (bf16[576,256]{1,0:T(8,128)(2,1)S(1)}, bf16[576,256]{1,0:T(8,128)(2,1)S(1)}, u32[]{:S(2)}, u32[]{:S(2)}) collective-permute-start(bf16[576,256]{1,0:T(8,128)(2,1)S(1)} %constant_dynamic-slice_fusion), channel_id=1, source_target_pairs={{0,224},{32,0},{64,32},{96,64},{128,96},{160,128},{192,160},{224,1... | collective-permute-start | bytes 884744 | tf_op jit(solution)/shard_map/ppermute | solution.py:466
  62.8 3.5 %collective-permute-done.7.refs_6_ = bf16[576,256]{1,0:T(8,128)(2,1)S(1)} collective-permute-done((bf16[576,256]{1,0:T(8,128)(2,1)S(1)}, bf16[576,256]{1,0:T(8,128)(2,1)S(1)}, u32[]{:S(2)}, u32[]{:S(2)}) %collective-permute-start.7) | collective-permute-done | bytes 294944 | tf_op jit(solution)/shard_map/ppermute | solution.py:466
  66.3 3.8 %collective-permute-done.6.refs_3_ = bf16[576,256]{1,0:T(8,128)(2,1)S(1)} collective-permute-done((bf16[576,256]{1,0:T(8,128)(2,1)S(1)}, bf16[576,256]{1,0:T(8,128)(2,1)S(1)}, u32[]{:S(2)}, u32[]{:S(2)}) %collective-permute-start.6) | collective-permute-done | bytes 294944 | tf_op jit(solution)/shard_map/ppermute | solution.py:466
  70.1 0.7 collective-permute-start.8
  70.8 1.3 collective-permute-start.9
  72.1 13.4 %all_to_all.25 = f32[32,10,128]{2,1,0:T(8,128)S(1)} all-to-all(f32[32,10,128]{2,1,0:T(8,128)S(1)} %reshape.42), channel_id=1, replica_groups=mesh['cz'=8,'cy'=4,'fsdp'=4,'tp'=2] {'cy','fsdp','tp'}, dimensions={0} | all-to-all | bytes 327680 | tf_op jit(solution)/shard_map/all_to_all | solution.py:443
  85.6 0.6 reduce_sum.18.part_ref
  86.2 0.7 copy-done.10
  86.9 5.4 %query_pass.1 = (bf16[576,256]{1,0:T(8,128)(2,1)}, f32[8,20,128]{2,1,0:T(8,128)}) custom-call(s32[1]{0:T(128)} %bitcast.2.where_ref, f32[10,128]{1,0:T(8,128)} %reduce_sum.18.part_ref, bf16[576,512]{1,0:T(8,128)(2,1)} %bitcast.15, bf16[576,512]{1,0:T(8,128)(2,1)} %bitcast.16, bf16[576,512]{1,0:T(8,128)(2,1)} %copy-done.4, bf16[576,512]{1,0:T(8,128)(2,1)} %copy-done.1, ...), custom_call_target="tpu_custom_call" | custom-call | tf_op jit(solution)/shard_map/query_pass/pallas_call | solution.py:347
  92.3 21.7 %all_to_all.26 = f32[8,20,128]{2,1,0:T(8,128)S(1)} all-to-all(f32[8,20,128]{2,1,0:T(8,128)} %get-tuple-element.77), channel_id=1, replica_groups=mesh['cz'=8,'cy'=4,'fsdp'=4,'tp'=2] {'cz'}, dimensions={0} | all-to-all | bytes 163840 | tf_op jit(solution)/shard_map/all_to_all | solution.py:443
  114.0 0.6 broadcast_in_dim.10
  114.7 4.7 %all-to-all-start.3 = ((f32[8,10,128]{2,1,0:T(8,128)}), f32[8,10,128]{2,1,0:T(8,128)S(1)}, u32[]{:S(2)}, u32[]{:S(2)}) async-start(f32[8,10,128]{2,1,0:T(8,128)} %broadcast_in_dim.10), calls=%async_computation.3 | async-start | bytes 131072 | tf_op jit(solution)/shard_map/all_to_all | solution.py:443
  119.5 0.6 copy.21
  120.1 9.9 %key_pass.1.ok_ref = bf16[576,256]{1,0:T(8,128)(2,1)} custom-call(s32[1]{0:T(128)} %bitcast.2.where_ref, bf16[576,512]{1,0:T(8,128)(2,1)} %bitcast.17, f32[9,2,512]{2,1,0:T(2,128)} %bitcast.23, bf16[576,512]{1,0:T(8,128)(2,1)} %bitcast.18, bf16[576,512]{1,0:T(8,128)(2,1)} %copy-done.4, bf16[576,512]{1,0:T(8,128)(2,1)} %copy-done.1, ...), custom_call_target="tpu_custom_call" | custom-call | tf_op jit(solution)/shard_map/key_pass/pallas_call | solution.py:425
  130.0 0.6 copy-done.11
  130.6 2.0 %join.1 = bf16[4,184,512]{2,1,0:T(8,128)(2,1)} custom-call(bf16[576,256]{1,0:T(8,128)(2,1)} %get-tuple-element.76.oq_ref, bf16[576,256]{1,0:T(8,128)(2,1)} %key_pass.1.ok_ref, f32[8,10,128]{2,1,0:T(8,128)} %copy-done.11), custom_call_target="tpu_custom_call" | custom-call | tf_op jit(solution)/shard_map/join/pallas_call | solution.py:420
  132.6 16.8 %all_to_all.27.x_ref = bf16[4,184,512]{2,1,0:T(8,128)(2,1)} all-to-all(bf16[4,184,512]{2,1,0:T(8,128)(2,1)} %join.1), channel_id=1, replica_groups=mesh['cz'=8,'cy'=4,'fsdp'=4,'tp'=2] {'cy'}, dimensions={0} | all-to-all | bytes 1507328 | tf_op jit(solution)/shard_map/all_to_all | solution.py:443
  149.4 2.2 %unpack.1 = (bf16[144,512]{1,0:T(8,128)(2,1)}, f32[144,512]{1,0:T(8,128)}, f32[144,512]{1,0:T(8,128)}, f32[144,512]{1,0:T(8,128)}, f32[128,256]{1,0:T(8,128)}, /*index=5*/f32[3,7,256]{2,1,0:T(8,128)}) custom-call(bf16[4,184,512]{2,1,0:T(8,128)(2,1)} %all_to_all.27.x_ref), custom_call_target="tpu_custom_call" | custom-call | tf_op jit(solution)/shard_map/unpack/pallas_call | solution.py:98
  (57 shorter events, 1.0 us)
Async XLA Ops:
  3.1 4.6 %copy-start.17 = (bf16[288,512]{1,0:T(8,128)(2,1)S(1)}, bf16[288,512]{1,0:T(8,128)(2,1)}, u32[]{:S(2)}) copy-start(bf16[288,512]{1,0:T(8,128)(2,1)} %get-tuple-element.49) | copy-start | bytes 884740
  3.1 5.9 %copy-start.18 = (bf16[280,512]{1,0:T(8,128)(2,1)S(1)}, bf16[280,512]{1,0:T(8,128)(2,1)}, u32[]{:S(2)}) copy-start(bf16[280,512]{1,0:T(8,128)(2,1)} %get-tuple-element.48) | copy-start | bytes 860164
  3.1 28.0 %copy-start.14 = (f32[3,7,256]{2,1,0:T(8,128)S(1)}, f32[3,7,256]{2,1,0:T(8,128)}, u32[]{:S(2)}) copy-start(f32[3,7,256]{2,1,0:T(8,128)} %param.9) | copy-start | bytes 64516
  3.1 19.6 %all-to-all-start = ((bf16[4,144,512]{2,1,0:T(8,128)(2,1)}), bf16[4,144,512]{2,1,0:T(8,128)(2,1)S(1)}, u32[]{:S(2)}, u32[]{:S(2)}) async-start(bf16[4,144,512]{2,1,0:T(8,128)(2,1)} %get-tuple-element.47), calls=%async_computation | async-start | bytes 1179648 | tf_op jit(solution)/shard_map/all_to_all | solution.py:443
  7.7 15.0 %collective-permute-start.1 = (bf16[288,512]{1,0:T(8,128)(2,1)S(1)}, bf16[288,512]{1,0:T(8,128)(2,1)S(1)}, u32[]{:S(2)}, u32[]{:S(2)}) collective-permute-start(bf16[288,512]{1,0:T(8,128)(2,1)S(1)} %copy-done.17), channel_id=1, source_target_pairs={{8,0},{16,8},{24,16},{32,24},{40,32},{48,40},{56,48},{64,56},{72,6... | collective-permute-start | bytes 884744 | tf_op jit(solution)/shard_map/ppermute | solution.py:460
  9.0 11.3 %collective-permute-start = (bf16[280,512]{1,0:T(8,128)(2,1)S(1)}, bf16[280,512]{1,0:T(8,128)(2,1)S(1)}, u32[]{:S(2)}, u32[]{:S(2)}) collective-permute-start(bf16[280,512]{1,0:T(8,128)(2,1)S(1)} %copy-done.18), channel_id=1, source_target_pairs={{0,8},{8,16},{16,24},{24,32},{32,40},{40,48},{48,56},{56,64},{64,7... | collective-permute-start | bytes 860168 | tf_op jit(solution)/shard_map/ppermute | solution.py:459
  20.3 11.4 %copy-start.8 = (bf16[280,512]{1,0:T(8,128)(2,1)}, bf16[280,512]{1,0:T(8,128)(2,1)S(1)}, u32[]{:S(2)}) copy-start(bf16[280,512]{1,0:T(8,128)(2,1)S(1)} %collective-permute-done.prev_ref) | copy-start | bytes 860164
  22.7 9.0 %copy-start.7 = (bf16[288,512]{1,0:T(8,128)(2,1)}, bf16[288,512]{1,0:T(8,128)(2,1)S(1)}, u32[]{:S(2)}) copy-start(bf16[288,512]{1,0:T(8,128)(2,1)S(1)} %collective-permute-done.1.next_ref) | copy-start | bytes 884740
  22.7 17.7 %copy-start = (bf16[4,144,512]{2,1,0:T(8,128)(2,1)}, bf16[4,144,512]{2,1,0:T(8,128)(2,1)S(1)}, u32[]{:S(2)}) copy-start(bf16[4,144,512]{2,1,0:T(8,128)(2,1)S(1)} %all-to-all-done) | copy-start | bytes 1769476
  22.7 19.2 %collective-permute-start.3 = (bf16[576,512]{1,0:T(8,128)(2,1)S(1)}, bf16[576,512]{1,0:T(8,128)(2,1)S(1)}, u32[]{:S(2)}, u32[]{:S(2)}) collective-permute-start(bf16[576,512]{1,0:T(8,128)(2,1)S(1)} %bitcast.13), channel_id=1, source_target_pairs={{0,224},{32,0},{64,32},{96,64},{128,96},{160,128},{192,160},{224,1... | collective-permute-start | bytes 1769480 | tf_op jit(solution)/shard_map/ppermute | solution.py:466
  31.1 14.2 %collective-permute-start.2 = (bf16[576,512]{1,0:T(8,128)(2,1)S(1)}, bf16[576,512]{1,0:T(8,128)(2,1)S(1)}, u32[]{:S(2)}, u32[]{:S(2)}) collective-permute-start(bf16[576,512]{1,0:T(8,128)(2,1)S(1)} %bitcast.14), channel_id=1, source_target_pairs={{0,32},{32,64},{64,96},{96,128},{128,160},{160,192},{192,224},{224... | collective-permute-start | bytes 1769480 | tf_op jit(solution)/shard_map/ppermute | solution.py:466
  41.9 15.4 %copy-start.3 = (bf16[576,512]{1,0:T(8,128)(2,1)}, bf16[576,512]{1,0:T(8,128)(2,1)S(1)}, u32[]{:S(2)}) copy-start(bf16[576,512]{1,0:T(8,128)(2,1)S(1)} %collective-permute-done.3.refs_4_) | copy-start | bytes 1769476
  45.3 12.0 %copy-start.4 = (bf16[576,512]{1,0:T(8,128)(2,1)}, bf16[576,512]{1,0:T(8,128)(2,1)S(1)}, u32[]{:S(2)}) copy-start(bf16[576,512]{1,0:T(8,128)(2,1)S(1)} %collective-permute-done.2.refs_1_) | copy-start | bytes 1769476
  45.3 13.3 %collective-permute-start.4 = (bf16[576,512]{1,0:T(8,128)(2,1)S(1)}, bf16[576,512]{1,0:T(8,128)(2,1)S(1)}, u32[]{:S(2)}, u32[]{:S(2)}) collective-permute-start(bf16[576,512]{1,0:T(8,128)(2,1)S(1)} %collective-permute-done.2.refs_1_), channel_id=1, source_target_pairs={{0,32},{32,64},{64,96},{96,128},{128,160},{160,192},{192,224},{224... | collective-permute-start | bytes 1769480 | tf_op jit(solution)/shard_map/ppermute | solution.py:466
  45.3 13.3 %collective-permute-start.5 = (bf16[576,512]{1,0:T(8,128)(2,1)S(1)}, bf16[576,512]{1,0:T(8,128)(2,1)S(1)}, u32[]{:S(2)}, u32[]{:S(2)}) collective-permute-start(bf16[576,512]{1,0:T(8,128)(2,1)S(1)} %collective-permute-done.3.refs_4_), channel_id=1, source_target_pairs={{0,224},{32,0},{64,32},{96,64},{128,96},{160,128},{192,160},{224,1... | collective-permute-start | bytes 1769480 | tf_op jit(solution)/shard_map/ppermute | solution.py:466
  48.5 8.8 %copy-start.12 = (f32[128,128]{1,0:T(8,128)S(1)}, f32[128,128]{1,0:T(8,128)}, u32[]{:S(2)}) copy-start(f32[128,128]{1,0:T(8,128)} %get-tuple-element.66) | copy-start | bytes 196612
  58.6 3.5 %copy-start.1 = (bf16[576,512]{1,0:T(8,128)(2,1)}, bf16[576,512]{1,0:T(8,128)(2,1)S(1)}, u32[]{:S(2)}) copy-start(bf16[576,512]{1,0:T(8,128)(2,1)S(1)} %collective-permute-done.4.refs_2_) | copy-start | bytes 1769476
  58.6 3.5 %copy-start.2 = (bf16[576,512]{1,0:T(8,128)(2,1)}, bf16[576,512]{1,0:T(8,128)(2,1)S(1)}, u32[]{:S(2)}) copy-start(bf16[576,512]{1,0:T(8,128)(2,1)S(1)} %collective-permute-done.5.refs_5_) | copy-start | bytes 1769476
  58.6 3.6 %copy-start.13 = (f32[128,128]{1,0:T(8,128)S(1)}, f32[128,128]{1,0:T(8,128)}, u32[]{:S(2)}) copy-start(f32[128,128]{1,0:T(8,128)} %get-tuple-element.67) | copy-start | bytes 196612
  58.6 7.6 %collective-permute-start.7 = (bf16[576,256]{1,0:T(8,128)(2,1)S(1)}, bf16[576,256]{1,0:T(8,128)(2,1)S(1)}, u32[]{:S(2)}, u32[]{:S(2)}) collective-permute-start(bf16[576,256]{1,0:T(8,128)(2,1)S(1)} %constant_dynamic-slice_fusion), channel_id=1, source_target_pairs={{0,224},{32,0},{64,32},{96,64},{128,96},{160,128},{192,160},{224,1... | collective-permute-start | bytes 884744 | tf_op jit(solution)/shard_map/ppermute | solution.py:466
  62.1 0.7 copy-start.15
  62.1 8.0 %collective-permute-start.6 = (bf16[576,256]{1,0:T(8,128)(2,1)S(1)}, bf16[576,256]{1,0:T(8,128)(2,1)S(1)}, u32[]{:S(2)}, u32[]{:S(2)}) collective-permute-start(bf16[576,256]{1,0:T(8,128)(2,1)S(1)} %constant_dynamic-slice_fusion.1), channel_id=1, source_target_pairs={{0,32},{32,64},{64,96},{96,128},{128,160},{160,192},{192,224},{224... | collective-permute-start | bytes 884744 | tf_op jit(solution)/shard_map/ppermute | solution.py:466
  62.8 9.3 %copy-start.16 = (f32[3,8,128]{2,1,0:T(8,128)S(1)}, f32[3,8,128]{2,1,0:T(8,128)}, u32[]{:S(2)}) copy-start(f32[3,8,128]{2,1,0:T(8,128)} %get-tuple-element.69) | copy-start | bytes 36868
  66.3 19.3 %copy-start.5 = (bf16[576,256]{1,0:T(8,128)(2,1)}, bf16[576,256]{1,0:T(8,128)(2,1)S(1)}, u32[]{:S(2)}) copy-start(bf16[576,256]{1,0:T(8,128)(2,1)S(1)} %collective-permute-done.7.refs_6_) | copy-start | bytes 884740
  70.1 15.5 %copy-start.6 = (bf16[576,256]{1,0:T(8,128)(2,1)}, bf16[576,256]{1,0:T(8,128)(2,1)S(1)}, u32[]{:S(2)}) copy-start(bf16[576,256]{1,0:T(8,128)(2,1)S(1)} %collective-permute-done.6.refs_3_) | copy-start | bytes 884740
  70.1 16.1 %collective-permute-start.8 = (bf16[576,256]{1,0:T(8,128)(2,1)S(1)}, bf16[576,256]{1,0:T(8,128)(2,1)S(1)}, u32[]{:S(2)}, u32[]{:S(2)}) collective-permute-start(bf16[576,256]{1,0:T(8,128)(2,1)S(1)} %collective-permute-done.6.refs_3_), channel_id=1, source_target_pairs={{96,128},{128,160},{160,192},{192,224},{97,129},{129,161},{161,193... | collective-permute-start | bytes 884744 | tf_op jit(solution)/shard_map/ppermute | solution.py:496
  70.8 15.4 %collective-permute-start.9 = (bf16[576,256]{1,0:T(8,128)(2,1)S(1)}, bf16[576,256]{1,0:T(8,128)(2,1)S(1)}, u32[]{:S(2)}, u32[]{:S(2)}) collective-permute-start(bf16[576,256]{1,0:T(8,128)(2,1)S(1)} %collective-permute-done.7.refs_6_), channel_id=1, source_target_pairs={{32,0},{64,32},{96,64},{128,96},{33,1},{65,33},{97,65},{129,97},{3... | collective-permute-start | bytes 884744 | tf_op jit(solution)/shard_map/ppermute | solution.py:497
  86.2 0.7 copy-start.10
  86.2 6.1 %copy-start.9 = (bf16[576,256]{1,0:T(8,128)(2,1)}, bf16[576,256]{1,0:T(8,128)(2,1)S(1)}, u32[]{:S(2)}) copy-start(bf16[576,256]{1,0:T(8,128)(2,1)S(1)} %collective-permute-done.9.refs_7_) | copy-start | bytes 884740
  114.7 15.3 %all-to-all-start.3 = ((f32[8,10,128]{2,1,0:T(8,128)}), f32[8,10,128]{2,1,0:T(8,128)S(1)}, u32[]{:S(2)}, u32[]{:S(2)}) async-start(f32[8,10,128]{2,1,0:T(8,128)} %broadcast_in_dim.10), calls=%async_computation.3 | async-start | bytes 131072 | tf_op jit(solution)/shard_map/all_to_all | solution.py:443
  130.0 0.6 copy-start.11

commit v10 on v9

--- a/solution.py
+++ b/solution.py
@@ -80,11 +80,10 @@
         gq_ref[:, at] = x_ref[h, :ROWS, HD : 2 * HD].astype(F32)
         gk_ref[:, at] = x_ref[h, :ROWS, 2 * HD : 3 * HD].astype(F32)
         gv_ref[:, at] = x_ref[h, :ROWS, 3 * HD :].astype(F32)
-        for side in range(2):
-            high = x_ref[h, ROWS:, side * HD : (side + 1) * HD].astype(F32)
-            low = x_ref[h, ROWS:, (side + 2) * HD : (side + 3) * HD].astype(F32)
-            first = 80 * h + 40 * side
-            grads_ref[first : first + 40] = high + low
+        for c in range(4):
+            first = 80 * h + 20 * c
+            piece = x_ref[h, ROWS : ROWS + 20, c * HD : (c + 1) * HD]
+            grads_ref[first : first + 20] = piece.astype(F32)
     for side in range(2):
         at = slice(side * HD, (side + 1) * HD)
         glong_ref[:, at] = grads_ref[128 * side : 128 * (side + 1)]
@@ -273,7 +272,7 @@
     return total
 
 
-def query_body(where_ref, part_ref, own_ref, *refs):
+def query_body(where_ref, own_ref, *refs):
     out_ref, small_ref, s_ref, mx_ref, l_ref, o_ref, st_ref, kv_ref = refs[8:]
     assemble(where_ref, refs[:8], kv_ref, True)
     first = where_ref[0] * GROUP
@@ -339,18 +338,15 @@
             small_ref[:, 5 * line + j : 5 * line + j + 1, :] = jnp.broadcast_to(
                 row[None], (8, 1, 128)
             )
-    for n in range(8):
-        small_ref[n, 10:20] = part_ref[...]
-
-
-def query_pass(where, part, own, kv):
+
+
+def query_pass(where, own, kv):
     return call(
         query_body,
-        (struct((GROUP, 2 * HD), BF16), struct((8, 20, HD), F32)),
+        (struct((GROUP, 2 * HD), BF16), struct((8, 10, HD), F32)),
         "query_pass",
         grid=(1,),
         in_specs=[pl.BlockSpec(memory_space=pltpu.SMEM)]
-        + [pl.BlockSpec(memory_space=pltpu.VMEM)]
         + [part_of(side) for side in (0, 1, 1, 1, 0, 1, 1, 0, 0)],
         scratch_shapes=[
             pltpu.VMEM((CHUNKS, GROUP, CHUNK), F32),
@@ -360,7 +356,7 @@
             pltpu.VMEM((640, HD), F32),
             pltpu.VMEM((SEQ, 2 * HD), BF16),
         ],
-    )(where, part, own, *kv)
+    )(where, own, *kv)
 
 
 def key_body(where_ref, own_ref, stat_ref, *refs):
@@ -408,16 +404,14 @@
         at = slice(j * ROWS, (j + 1) * ROWS)
         out_ref[j, :ROWS, : 2 * HD] = oq_ref[at]
         out_ref[j, :ROWS, 2 * HD :] = ok_ref[at]
-        for side in range(2):
-            value = part_ref[side * 40 : (side + 1) * 40]
-            high = value.astype(BF16)
-            out_ref[j, ROWS:, side * HD : (side + 1) * HD] = high
-            low = (value - high.astype(F32)).astype(BF16)
-            out_ref[j, ROWS:, (side + 2) * HD : (side + 3) * HD] = low
+        for c in range(4):
+            value = part_ref[20 * c : 20 * (c + 1)].astype(BF16)
+            out_ref[j, ROWS : ROWS + 20, c * HD : (c + 1) * HD] = value
+        out_ref[j, ROWS + 20 :] = jnp.zeros((4, 4 * HD), BF16)
 
 
 def join(out_q, out_k, part):
-    return call(join_body, struct((4, ROWS + 40, 4 * HD), BF16), "join",
+    return call(join_body, struct((4, ROWS + 24, 4 * HD), BF16), "join",
                 scratch_shapes=[pltpu.VMEM((80, HD), F32)])(out_q, out_k, part)
 
 
@@ -491,14 +485,16 @@
         [first[2], glong, first[3].reshape(24, HD), gshort.reshape(24, HD), jnp.zeros((16, HD), F32)],
         0,
     )
-    part = jnp.sum(exchange(grads.reshape(32, 10, HD), YFT), axis=0)
     order()
     far_kv = lax.ppermute(rising[3], "cz", [(i, i + 1) for i in range(3, 7)])
     far_qd = lax.ppermute(falling[3], "cz", [(i, i - 1) for i in range(1, 5)])
     far_kv, far_qd, own = lax.optimization_barrier((far_kv, far_qd, own))
     pieces = [own] + rising[1:] + falling[1:]
 
-    out_q, small = query_pass(where, part, own, pieces + [far_kv])
+    received = exchange(after(grads, own).reshape(32, 10, HD), YFT)
+    out_q, small = query_pass(where, own, pieces + [far_kv])
+    part = jnp.sum(received, axis=0)
+    small = jnp.concatenate([small, jnp.broadcast_to(part[None], (8, 10, HD))], 1)
     small = exchange(small, "cz")
     part = share(jnp.sum(small[:, 10:], axis=0), FT, 8)
     stats = small[:, :10].reshape(8, 2, 640)[:, :, :GROUP].transpose(1, 0, 2)

time: 153 us -> 148 us (0.967)
  blocking collectives: 51.9 us -> 33.8 us
  waiting for transfers between devices: 22.5 us -> 29.9 us
  starting transfers between devices: 32.2 us -> 39 us
    all_to_all x3 -> x2, blocking collectives: 51.9 us -> 33.8 us  [exchange(): return lax.all_to_all(x, axis, 0, 0, tiled=True)]
    ppermute x1, waiting for transfers between devices: 0.01 us -> 7.26 us  [body(): far_qd = lax.ppermute(falling[3], 'cz', [(i, i - 1) for i in range(1, 5)])]
    all_to_all x2 -> x3, starting transfers between devices: 9.33 us -> 15.3 us  [exchange(): return lax.all_to_all(x, axis, 0, 0, tiled=True)]
    all_to_all x2 -> x3, waiting for transfers between devices: 0.01 us -> 2.74 us  [exchange(): return lax.all_to_all(x, axis, 0, 0, tiled=True)]
    ppermute x6, waiting for transfers between devices: 13.4 us -> 10.8 us  [shift(): return lax.ppermute(x, 'cz', [(i, (i + by) % 8) for i in range(8)])]
  transfers between devices with their start and end apart: 12 -> 13, of which waited for: 7 -> 8; matrix products, arithmetic and copies ran while one was open for 1% -> 1% of each run, Pallas kernels for 18% -> 22%
where the time goes in v10:
time: 148 us; the launch traced here: 147 us
  Pallas kernels  39.3 us (27%)
  starting transfers between devices  39 us (26%)
  blocking collectives  33.8 us (23%)
  waiting for transfers between devices  29.9 us (20%)
  local copies, waits for them, and re-layouts  4.4 us (3%)
    all_to_all x2, blocking collectives, exchange(): return lax.all_to_all(x, axis, 0, 0, tiled=True)  33.8 us
    pallas_call x2, Pallas kernels, hyena(): call(hyena_body, (struct((ROWS, 512), BF16), struct((3, ROWS, 512), F32),...  17.5 us
    ppermute x6, starting transfers between devices, shift(): return lax.ppermute(x, 'cz', [(i, (i + by) % 8) for i in range(8)])  15.9 us
    all_to_all x3, starting transfers between devices, exchange(): return lax.all_to_all(x, axis, 0, 0, tiled=True)  15.3 us
    ppermute x6, waiting for transfers between devices, shift(): return lax.ppermute(x, 'cz', [(i, (i + by) % 8) for i in range(8)])  10.8 us
    pallas_call x1, Pallas kernels, key_pass(): call(key_body, struct((GROUP, 2 * HD), BF16), 'key_pass', grid=(1,), in_s...  9.87 us
    ppermute x1, waiting for transfers between devices, body(): far_qd = lax.ppermute(falling[3], 'cz', [(i, i - 1) for i in range(1, 5)])  7.26 us
    ppermute x1, waiting for transfers between devices, body(): prev = lax.ppermute(tail, CTX, [(i, i + 1) for i in range(31)])  6.74 us
  transfers between devices with their start and end apart: 13, of which 8 were waited for; matrix products, arithmetic and copies ran while one was open for 1% of the time, Pallas kernels for 22%

profile of v10, /device:TPU:2, one launch (start us, length us, event | category | flops | bytes accessed | tf_op | source)
XLA Modules:
  0.0 147.3 jit_solution(7116662809377554931)
XLA Ops:
  0.6 2.5 %pack.1 = (bf16[4,144,512]{2,1,0:T(8,128)(2,1)}, bf16[280,512]{1,0:T(8,128)(2,1)}, bf16[288,512]{1,0:T(8,128)(2,1)}) custom-call(bf16[144,512]{1,0:T(8,128)(2,1)} %q_ref.1, bf16[144,512]{1,0:T(8,128)(2,1)} %d_ref.1, bf16[144,512]{1,0:T(8,128)(2,1)} %k_ref.1, bf16[144,512]{1,0:T(8,128)(2,1)} %v_ref.1, bf16[3,144,512]{2,1,0:T(8,128)(2,1)} %bitcast.19, ...), custom_call_target="tpu_custom_call" | custom-call | tf_op jit(solution)/shard_map/pack/pallas_call | solution.py:65
  3.1 4.6 %all-to-all-start = ((bf16[4,144,512]{2,1,0:T(8,128)(2,1)}), bf16[4,144,512]{2,1,0:T(8,128)(2,1)S(1)}, u32[]{:S(2)}, u32[]{:S(2)}) async-start(bf16[4,144,512]{2,1,0:T(8,128)(2,1)} %get-tuple-element.48), calls=%async_computation | async-start | bytes 1179648 | tf_op jit(solution)/shard_map/all_to_all | solution.py:437
  7.7 1.3 collective-permute-start.1
  9.0 4.6 %collective-permute-start = (bf16[280,512]{1,0:T(8,128)(2,1)S(1)}, bf16[280,512]{1,0:T(8,128)(2,1)S(1)}, u32[]{:S(2)}, u32[]{:S(2)}) collective-permute-start(bf16[280,512]{1,0:T(8,128)(2,1)S(1)} %copy-done.19), channel_id=1, source_target_pairs={{0,8},{8,16},{16,24},{24,32},{32,40},{40,48},{48,56},{56,64},{64,7... | collective-permute-start | bytes 860168 | tf_op jit(solution)/shard_map/ppermute | solution.py:453
  13.6 6.7 %collective-permute-done.prev_ref = bf16[280,512]{1,0:T(8,128)(2,1)S(1)} collective-permute-done((bf16[280,512]{1,0:T(8,128)(2,1)S(1)}, bf16[280,512]{1,0:T(8,128)(2,1)S(1)}, u32[]{:S(2)}, u32[]{:S(2)}) %collective-permute-start) | collective-permute-done | bytes 286752 | tf_op jit(solution)/shard_map/ppermute | solution.py:453
  20.3 2.4 %collective-permute-done.1.next_ref = bf16[288,512]{1,0:T(8,128)(2,1)S(1)} collective-permute-done((bf16[288,512]{1,0:T(8,128)(2,1)S(1)}, bf16[288,512]{1,0:T(8,128)(2,1)S(1)}, u32[]{:S(2)}, u32[]{:S(2)}) %collective-permute-start.1) | collective-permute-done | bytes 294944 | tf_op jit(solution)/shard_map/ppermute | solution.py:454
  22.7 4.0 %collective-permute-start.2 = (bf16[576,512]{1,0:T(8,128)(2,1)S(1)}, bf16[576,512]{1,0:T(8,128)(2,1)S(1)}, u32[]{:S(2)}, u32[]{:S(2)}) collective-permute-start(bf16[576,512]{1,0:T(8,128)(2,1)S(1)} %bitcast.13), channel_id=1, source_target_pairs={{0,32},{32,64},{64,96},{96,128},{128,160},{160,192},{192,224},{224... | collective-permute-start | bytes 1769480 | tf_op jit(solution)/shard_map/ppermute | solution.py:460
  26.7 4.5 %collective-permute-start.3 = (bf16[576,512]{1,0:T(8,128)(2,1)S(1)}, bf16[576,512]{1,0:T(8,128)(2,1)S(1)}, u32[]{:S(2)}, u32[]{:S(2)}) collective-permute-start(bf16[576,512]{1,0:T(8,128)(2,1)S(1)} %bitcast.14), channel_id=1, source_target_pairs={{0,224},{32,0},{64,32},{96,64},{128,96},{160,128},{192,160},{224,1... | collective-permute-start | bytes 1769480 | tf_op jit(solution)/shard_map/ppermute | solution.py:460
  31.8 8.7 %hyena.2 = (bf16[144,512]{1,0:T(8,128)(2,1)}, f32[3,144,512]{2,1,0:T(8,128)}, f32[128,128]{1,0:T(8,128)}, f32[3,8,128]{2,1,0:T(8,128)}) custom-call(bf16[3,144,512]{2,1,0:T(8,128)(2,1)} %bitcast.20, bf16[280,512]{1,0:T(8,128)(2,1)} %copy-done.8, bf16[288,512]{1,0:T(8,128)(2,1)} %copy-done.7, bf16[144,512]{1,0:T(8,128)(2,1)} %up_ref.5, ...), custom_call_target="tpu_custom_call" | custom-call | tf_op jit(solution)/shard_map/hyena/pallas_call | solution.py:205
  40.5 2.1 %collective-permute-done.2.refs_1_ = bf16[576,512]{1,0:T(8,128)(2,1)S(1)} collective-permute-done((bf16[576,512]{1,0:T(8,128)(2,1)S(1)}, bf16[576,512]{1,0:T(8,128)(2,1)S(1)}, u32[]{:S(2)}, u32[]{:S(2)}) %collective-permute-start.2) | collective-permute-done | bytes 589856 | tf_op jit(solution)/shard_map/ppermute | solution.py:460
  42.7 3.2 %collective-permute-start.5 = (bf16[576,512]{1,0:T(8,128)(2,1)S(1)}, bf16[576,512]{1,0:T(8,128)(2,1)S(1)}, u32[]{:S(2)}, u32[]{:S(2)}) collective-permute-start(bf16[576,512]{1,0:T(8,128)(2,1)S(1)} %collective-permute-done.3.refs_4_), channel_id=1, source_target_pairs={{0,224},{32,0},{64,32},{96,64},{128,96},{160,128},{192,160},{224,1... | collective-permute-start | bytes 1769480 | tf_op jit(solution)/shard_map/ppermute | solution.py:460
  45.9 8.8 %hyena.3 = (bf16[144,512]{1,0:T(8,128)(2,1)}, f32[3,144,512]{2,1,0:T(8,128)}, f32[128,128]{1,0:T(8,128)}, f32[3,8,128]{2,1,0:T(8,128)}) custom-call(bf16[3,144,512]{2,1,0:T(8,128)(2,1)} %bitcast.21, bf16[280,512]{1,0:T(8,128)(2,1)} %copy-done.8, bf16[288,512]{1,0:T(8,128)(2,1)} %copy-done.7, ...), custom_call_target="tpu_custom_call", output_to_operand_aliasing={{0}: (6, {}), {1}: (7, {})} | custom-call | tf_op jit(solution)/shard_map/hyena/pallas_call | solution.py:205
  54.7 1.8 %collective-permute-done.4.refs_2_ = bf16[576,512]{1,0:T(8,128)(2,1)S(1)} collective-permute-done((bf16[576,512]{1,0:T(8,128)(2,1)S(1)}, bf16[576,512]{1,0:T(8,128)(2,1)S(1)}, u32[]{:S(2)}, u32[]{:S(2)}) %collective-permute-start.4) | collective-permute-done | bytes 589856 | tf_op jit(solution)/shard_map/ppermute | solution.py:460
  56.6 3.0 %collective-permute-start.7 = (bf16[576,256]{1,0:T(8,128)(2,1)S(1)}, bf16[576,256]{1,0:T(8,128)(2,1)S(1)}, u32[]{:S(2)}, u32[]{:S(2)}) collective-permute-start(bf16[576,256]{1,0:T(8,128)(2,1)S(1)} %constant_dynamic-slice_fusion), channel_id=1, source_target_pairs={{0,224},{32,0},{64,32},{96,64},{128,96},{160,128},{192,160},{224,1... | collective-permute-start | bytes 884744 | tf_op jit(solution)/shard_map/ppermute | solution.py:460
  59.7 1.1 collective-permute-start.6
  60.8 4.0 %collective-permute-done.7.refs_6_ = bf16[576,256]{1,0:T(8,128)(2,1)S(1)} collective-permute-done((bf16[576,256]{1,0:T(8,128)(2,1)S(1)}, bf16[576,256]{1,0:T(8,128)(2,1)S(1)}, u32[]{:S(2)}, u32[]{:S(2)}) %collective-permute-start.7) | collective-permute-done | bytes 294944 | tf_op jit(solution)/shard_map/ppermute | solution.py:460
  64.7 2.9 %collective-permute-done.6.refs_3_ = bf16[576,256]{1,0:T(8,128)(2,1)S(1)} collective-permute-done((bf16[576,256]{1,0:T(8,128)(2,1)S(1)}, bf16[576,256]{1,0:T(8,128)(2,1)S(1)}, u32[]{:S(2)}, u32[]{:S(2)}) %collective-permute-start.6) | collective-permute-done | bytes 294944 | tf_op jit(solution)/shard_map/ppermute | solution.py:460
  67.7 0.7 collective-permute-start.8
  68.4 1.3 collective-permute-start.9
  69.7 7.3 %collective-permute-done.9.refs_7_ = bf16[576,256]{1,0:T(8,128)(2,1)S(1)} collective-permute-done((bf16[576,256]{1,0:T(8,128)(2,1)S(1)}, bf16[576,256]{1,0:T(8,128)(2,1)S(1)}, u32[]{:S(2)}, u32[]{:S(2)}) %collective-permute-start.9) | collective-permute-done | bytes 294944 | tf_op jit(solution)/shard_map/ppermute | solution.py:490
  77.0 0.7 reshape.43
  77.8 5.9 %all-to-all-start.1 = ((f32[32,10,128]{2,1,0:T(8,128)}), f32[32,10,128]{2,1,0:T(8,128)S(1)}, u32[]{:S(2)}, u32[]{:S(2)}) async-start(f32[32,10,128]{2,1,0:T(8,128)} %reshape.43), calls=%async_computation.1 | async-start | bytes 524288 | tf_op jit(solution)/shard_map/all_to_all | solution.py:437
  83.7 5.4 %query_pass.1 = (bf16[576,256]{1,0:T(8,128)(2,1)}, f32[8,10,128]{2,1,0:T(8,128)}) custom-call(s32[1]{0:T(128)} %bitcast.2.where_ref, bf16[576,512]{1,0:T(8,128)(2,1)} %bitcast.15, bf16[576,512]{1,0:T(8,128)(2,1)} %bitcast.16, bf16[576,512]{1,0:T(8,128)(2,1)} %copy-done.3, bf16[576,512]{1,0:T(8,128)(2,1)} %copy-done.1, bf16[576,256]{1,0:T(8,128)(2,1)} %copy-done.6, ...), custom_call_target="tpu_custom_call" | custom-call | tf_op jit(solution)/shard_map/query_pass/pallas_call | solution.py:344
  89.0 2.7 %all-to-all-done.1 = f32[32,10,128]{2,1,0:T(8,128)S(1)} async-done(((f32[32,10,128]{2,1,0:T(8,128)}), f32[32,10,128]{2,1,0:T(8,128)S(1)}, u32[]{:S(2)}, u32[]{:S(2)}) %all-to-all-start.1) | async-done | bytes 163872 | tf_op jit(solution)/shard_map/all_to_all | solution.py:437
  91.8 0.8 copy-done.12
  92.7 17.7 %all_to_all.25 = f32[8,20,128]{2,1,0:T(8,128)S(1)} all-to-all(f32[8,20,128]{2,1,0:T(8,128)S(1)} %pad_maximum_fusion), channel_id=1, replica_groups=mesh['cz'=8,'cy'=4,'fsdp'=4,'tp'=2] {'cz'}, dimensions={0} | all-to-all | bytes 163840 | tf_op jit(solution)/shard_map/all_to_all | solution.py:437
  111.1 4.8 %all-to-all-start.3 = ((f32[8,10,128]{2,1,0:T(8,128)}), f32[8,10,128]{2,1,0:T(8,128)S(1)}, u32[]{:S(2)}, u32[]{:S(2)}) async-start(f32[8,10,128]{2,1,0:T(8,128)} %broadcast_in_dim.8), calls=%async_computation.3 | async-start | bytes 131072 | tf_op jit(solution)/shard_map/all_to_all | solution.py:437
  116.0 0.6 copy.21
  116.7 9.9 %key_pass.1.ok_ref = bf16[576,256]{1,0:T(8,128)(2,1)} custom-call(s32[1]{0:T(128)} %bitcast.2.where_ref, bf16[576,512]{1,0:T(8,128)(2,1)} %bitcast.17, f32[9,2,512]{2,1,0:T(2,128)} %bitcast.23, bf16[576,512]{1,0:T(8,128)(2,1)} %bitcast.18, bf16[576,512]{1,0:T(8,128)(2,1)} %copy-done.3, bf16[576,512]{1,0:T(8,128)(2,1)} %copy-done.1, ...), custom_call_target="tpu_custom_call" | custom-call | tf_op jit(solution)/shard_map/key_pass/pallas_call | solution.py:419
  127.2 2.0 %join.1 = bf16[4,168,512]{2,1,0:T(8,128)(2,1)} custom-call(bf16[576,256]{1,0:T(8,128)(2,1)} %get-tuple-element.73.oq_ref, bf16[576,256]{1,0:T(8,128)(2,1)} %key_pass.1.ok_ref, f32[8,10,128]{2,1,0:T(8,128)} %copy-done.11), custom_call_target="tpu_custom_call" | custom-call | tf_op jit(solution)/shard_map/join/pallas_call | solution.py:414
  129.1 16.1 %all_to_all.26.x_ref = bf16[4,168,512]{2,1,0:T(8,128)(2,1)} all-to-all(bf16[4,168,512]{2,1,0:T(8,128)(2,1)} %join.1), channel_id=1, replica_groups=mesh['cz'=8,'cy'=4,'fsdp'=4,'tp'=2] {'cy'}, dimensions={0} | all-to-all | bytes 1376256 | tf_op jit(solution)/shard_map/all_to_all | solution.py:437
  145.2 2.1 %unpack.1 = (bf16[144,512]{1,0:T(8,128)(2,1)}, f32[144,512]{1,0:T(8,128)}, f32[144,512]{1,0:T(8,128)}, f32[144,512]{1,0:T(8,128)}, f32[128,256]{1,0:T(8,128)}, /*index=5*/f32[3,7,256]{2,1,0:T(8,128)}) custom-call(bf16[4,168,512]{2,1,0:T(8,128)(2,1)} %all_to_all.26.x_ref), custom_call_target="tpu_custom_call" | custom-call | tf_op jit(solution)/shard_map/unpack/pallas_call | solution.py:97
  (62 shorter events, 2.3 us)
Async XLA Ops:
  3.1 4.6 %copy-start.18 = (bf16[288,512]{1,0:T(8,128)(2,1)S(1)}, bf16[288,512]{1,0:T(8,128)(2,1)}, u32[]{:S(2)}) copy-start(bf16[288,512]{1,0:T(8,128)(2,1)} %get-tuple-element.50) | copy-start | bytes 884740
  3.1 5.9 %copy-start.19 = (bf16[280,512]{1,0:T(8,128)(2,1)S(1)}, bf16[280,512]{1,0:T(8,128)(2,1)}, u32[]{:S(2)}) copy-start(bf16[280,512]{1,0:T(8,128)(2,1)} %get-tuple-element.49) | copy-start | bytes 860164
  3.1 28.1 %copy-start.15 = (f32[3,7,256]{2,1,0:T(8,128)S(1)}, f32[3,7,256]{2,1,0:T(8,128)}, u32[]{:S(2)}) copy-start(f32[3,7,256]{2,1,0:T(8,128)} %param.9) | copy-start | bytes 64516
  3.1 19.6 %all-to-all-start = ((bf16[4,144,512]{2,1,0:T(8,128)(2,1)}), bf16[4,144,512]{2,1,0:T(8,128)(2,1)S(1)}, u32[]{:S(2)}, u32[]{:S(2)}) async-start(bf16[4,144,512]{2,1,0:T(8,128)(2,1)} %get-tuple-element.48), calls=%async_computation | async-start | bytes 1179648 | tf_op jit(solution)/shard_map/all_to_all | solution.py:437
  7.7 15.0 %collective-permute-start.1 = (bf16[288,512]{1,0:T(8,128)(2,1)S(1)}, bf16[288,512]{1,0:T(8,128)(2,1)S(1)}, u32[]{:S(2)}, u32[]{:S(2)}) collective-permute-start(bf16[288,512]{1,0:T(8,128)(2,1)S(1)} %copy-done.18), channel_id=1, source_target_pairs={{8,0},{16,8},{24,16},{32,24},{40,32},{48,40},{56,48},{64,56},{72,6... | collective-permute-start | bytes 884744 | tf_op jit(solution)/shard_map/ppermute | solution.py:454
  9.0 11.3 %collective-permute-start = (bf16[280,512]{1,0:T(8,128)(2,1)S(1)}, bf16[280,512]{1,0:T(8,128)(2,1)S(1)}, u32[]{:S(2)}, u32[]{:S(2)}) collective-permute-start(bf16[280,512]{1,0:T(8,128)(2,1)S(1)} %copy-done.19), channel_id=1, source_target_pairs={{0,8},{8,16},{16,24},{24,32},{32,40},{40,48},{48,56},{56,64},{64,7... | collective-permute-start | bytes 860168 | tf_op jit(solution)/shard_map/ppermute | solution.py:453
  20.3 11.5 %copy-start.8 = (bf16[280,512]{1,0:T(8,128)(2,1)}, bf16[280,512]{1,0:T(8,128)(2,1)S(1)}, u32[]{:S(2)}) copy-start(bf16[280,512]{1,0:T(8,128)(2,1)S(1)} %collective-permute-done.prev_ref) | copy-start | bytes 860164
  22.7 9.1 %copy-start.7 = (bf16[288,512]{1,0:T(8,128)(2,1)}, bf16[288,512]{1,0:T(8,128)(2,1)S(1)}, u32[]{:S(2)}) copy-start(bf16[288,512]{1,0:T(8,128)(2,1)S(1)} %collective-permute-done.1.next_ref) | copy-start | bytes 884740
  22.7 17.8 %copy-start = (bf16[4,144,512]{2,1,0:T(8,128)(2,1)}, bf16[4,144,512]{2,1,0:T(8,128)(2,1)S(1)}, u32[]{:S(2)}) copy-start(bf16[4,144,512]{2,1,0:T(8,128)(2,1)S(1)} %all-to-all-done) | copy-start | bytes 1769476
  22.7 19.9 %collective-permute-start.2 = (bf16[576,512]{1,0:T(8,128)(2,1)S(1)}, bf16[576,512]{1,0:T(8,128)(2,1)S(1)}, u32[]{:S(2)}, u32[]{:S(2)}) collective-permute-start(bf16[576,512]{1,0:T(8,128)(2,1)S(1)} %bitcast.13), channel_id=1, source_target_pairs={{0,32},{32,64},{64,96},{96,128},{128,160},{160,192},{192,224},{224... | collective-permute-start | bytes 1769480 | tf_op jit(solution)/shard_map/ppermute | solution.py:460
  26.7 15.9 %collective-permute-start.3 = (bf16[576,512]{1,0:T(8,128)(2,1)S(1)}, bf16[576,512]{1,0:T(8,128)(2,1)S(1)}, u32[]{:S(2)}, u32[]{:S(2)}) collective-permute-start(bf16[576,512]{1,0:T(8,128)(2,1)S(1)} %bitcast.14), channel_id=1, source_target_pairs={{0,224},{32,0},{64,32},{96,64},{128,96},{160,128},{192,160},{224,1... | collective-permute-start | bytes 1769480 | tf_op jit(solution)/shard_map/ppermute | solution.py:460
  42.6 12.1 %copy-start.3 = (bf16[576,512]{1,0:T(8,128)(2,1)}, bf16[576,512]{1,0:T(8,128)(2,1)S(1)}, u32[]{:S(2)}) copy-start(bf16[576,512]{1,0:T(8,128)(2,1)S(1)} %collective-permute-done.2.refs_1_) | copy-start | bytes 1769476
  42.6 12.1 %copy-start.4 = (bf16[576,512]{1,0:T(8,128)(2,1)}, bf16[576,512]{1,0:T(8,128)(2,1)S(1)}, u32[]{:S(2)}) copy-start(bf16[576,512]{1,0:T(8,128)(2,1)S(1)} %collective-permute-done.3.refs_4_) | copy-start | bytes 1769476
  42.6 13.9 %collective-permute-start.4 = (bf16[576,512]{1,0:T(8,128)(2,1)S(1)}, bf16[576,512]{1,0:T(8,128)(2,1)S(1)}, u32[]{:S(2)}, u32[]{:S(2)}) collective-permute-start(bf16[576,512]{1,0:T(8,128)(2,1)S(1)} %collective-permute-done.2.refs_1_), channel_id=1, source_target_pairs={{0,32},{32,64},{64,96},{96,128},{128,160},{160,192},{192,224},{224... | collective-permute-start | bytes 1769480 | tf_op jit(solution)/shard_map/ppermute | solution.py:460
  42.7 13.8 %collective-permute-start.5 = (bf16[576,512]{1,0:T(8,128)(2,1)S(1)}, bf16[576,512]{1,0:T(8,128)(2,1)S(1)}, u32[]{:S(2)}, u32[]{:S(2)}) collective-permute-start(bf16[576,512]{1,0:T(8,128)(2,1)S(1)} %collective-permute-done.3.refs_4_), channel_id=1, source_target_pairs={{0,224},{32,0},{64,32},{96,64},{128,96},{160,128},{192,160},{224,1... | collective-permute-start | bytes 1769480 | tf_op jit(solution)/shard_map/ppermute | solution.py:460
  45.9 8.8 %copy-start.13 = (f32[128,128]{1,0:T(8,128)S(1)}, f32[128,128]{1,0:T(8,128)}, u32[]{:S(2)}) copy-start(f32[128,128]{1,0:T(8,128)} %get-tuple-element.75) | copy-start | bytes 196612
  56.5 3.1 %copy-start.1 = (bf16[576,512]{1,0:T(8,128)(2,1)}, bf16[576,512]{1,0:T(8,128)(2,1)S(1)}, u32[]{:S(2)}) copy-start(bf16[576,512]{1,0:T(8,128)(2,1)S(1)} %collective-permute-done.4.refs_2_) | copy-start | bytes 1769476
  56.5 3.1 %copy-start.2 = (bf16[576,512]{1,0:T(8,128)(2,1)}, bf16[576,512]{1,0:T(8,128)(2,1)S(1)}, u32[]{:S(2)}) copy-start(bf16[576,512]{1,0:T(8,128)(2,1)S(1)} %collective-permute-done.5.refs_5_) | copy-start | bytes 1769476
  56.6 4.2 %copy-start.14 = (f32[128,128]{1,0:T(8,128)S(1)}, f32[128,128]{1,0:T(8,128)}, u32[]{:S(2)}) copy-start(f32[128,128]{1,0:T(8,128)} %get-tuple-element.76) | copy-start | bytes 196612
  56.6 8.2 %collective-permute-start.7 = (bf16[576,256]{1,0:T(8,128)(2,1)S(1)}, bf16[576,256]{1,0:T(8,128)(2,1)S(1)}, u32[]{:S(2)}, u32[]{:S(2)}) collective-permute-start(bf16[576,256]{1,0:T(8,128)(2,1)S(1)} %constant_dynamic-slice_fusion), channel_id=1, source_target_pairs={{0,224},{32,0},{64,32},{96,64},{128,96},{160,128},{192,160},{224,1... | collective-permute-start | bytes 884744 | tf_op jit(solution)/shard_map/ppermute | solution.py:460
  59.7 1.1 copy-start.16
  59.7 8.0 %collective-permute-start.6 = (bf16[576,256]{1,0:T(8,128)(2,1)S(1)}, bf16[576,256]{1,0:T(8,128)(2,1)S(1)}, u32[]{:S(2)}, u32[]{:S(2)}) collective-permute-start(bf16[576,256]{1,0:T(8,128)(2,1)S(1)} %constant_dynamic-slice_fusion.1), channel_id=1, source_target_pairs={{0,32},{32,64},{64,96},{96,128},{128,160},{160,192},{192,224},{224... | collective-permute-start | bytes 884744 | tf_op jit(solution)/shard_map/ppermute | solution.py:460
  60.8 8.9 %copy-start.17 = (f32[3,8,128]{2,1,0:T(8,128)S(1)}, f32[3,8,128]{2,1,0:T(8,128)}, u32[]{:S(2)}) copy-start(f32[3,8,128]{2,1,0:T(8,128)} %get-tuple-element.78) | copy-start | bytes 36868
  64.7 13.0 %copy-start.5 = (bf16[576,256]{1,0:T(8,128)(2,1)}, bf16[576,256]{1,0:T(8,128)(2,1)S(1)}, u32[]{:S(2)}) copy-start(bf16[576,256]{1,0:T(8,128)(2,1)S(1)} %collective-permute-done.7.refs_6_) | copy-start | bytes 884740
  67.7 10.1 %copy-start.6 = (bf16[576,256]{1,0:T(8,128)(2,1)}, bf16[576,256]{1,0:T(8,128)(2,1)S(1)}, u32[]{:S(2)}) copy-start(bf16[576,256]{1,0:T(8,128)(2,1)S(1)} %collective-permute-done.6.refs_3_) | copy-start | bytes 884740
  67.7 2.0 %collective-permute-start.8 = (bf16[576,256]{1,0:T(8,128)(2,1)S(1)}, bf16[576,256]{1,0:T(8,128)(2,1)S(1)}, u32[]{:S(2)}, u32[]{:S(2)}) collective-permute-start(bf16[576,256]{1,0:T(8,128)(2,1)S(1)} %collective-permute-done.6.refs_3_), channel_id=1, source_target_pairs={{96,128},{128,160},{160,192},{192,224},{97,129},{129,161},{161,193... | collective-permute-start | bytes 884744 | tf_op jit(solution)/shard_map/ppermute | solution.py:489
  68.4 8.6 %collective-permute-start.9 = (bf16[576,256]{1,0:T(8,128)(2,1)S(1)}, bf16[576,256]{1,0:T(8,128)(2,1)S(1)}, u32[]{:S(2)}, u32[]{:S(2)}) collective-permute-start(bf16[576,256]{1,0:T(8,128)(2,1)S(1)} %collective-permute-done.7.refs_6_), channel_id=1, source_target_pairs={{32,0},{64,32},{96,64},{128,96},{33,1},{65,33},{97,65},{129,97},{3... | collective-permute-start | bytes 884744 | tf_op jit(solution)/shard_map/ppermute | solution.py:490
  69.7 14.0 %copy-start.10 = (bf16[576,256]{1,0:T(8,128)(2,1)}, bf16[576,256]{1,0:T(8,128)(2,1)S(1)}, u32[]{:S(2)}) copy-start(bf16[576,256]{1,0:T(8,128)(2,1)S(1)} %collective-permute-done.8.refs_7_) | copy-start | bytes 884740
  77.0 0.8 copy-start.9
  77.8 14.0 %all-to-all-start.1 = ((f32[32,10,128]{2,1,0:T(8,128)}), f32[32,10,128]{2,1,0:T(8,128)S(1)}, u32[]{:S(2)}, u32[]{:S(2)}) async-start(f32[32,10,128]{2,1,0:T(8,128)} %reshape.43), calls=%async_computation.1 | async-start | bytes 524288 | tf_op jit(solution)/shard_map/all_to_all | solution.py:437
  91.8 0.8 copy-start.12
  111.1 15.4 %all-to-all-start.3 = ((f32[8,10,128]{2,1,0:T(8,128)}), f32[8,10,128]{2,1,0:T(8,128)S(1)}, u32[]{:S(2)}, u32[]{:S(2)}) async-start(f32[8,10,128]{2,1,0:T(8,128)} %broadcast_in_dim.8), calls=%async_computation.3 | async-start | bytes 131072 | tf_op jit(solution)/shard_map/all_to_all | solution.py:437
  (1 other events, 0.6 us)

commit v11 on v10

--- a/solution.py
+++ b/solution.py
@@ -10,7 +10,7 @@
 ROWS = 144
 GROUP = 576
 SEQ = 4608
-CHUNK = 512
+CHUNK = 1536
 CHUNKS = SEQ // CHUNK
 LOG2E = 1.4426950408889634
 SCALE = HD ** -0.5
@@ -245,17 +245,15 @@
         block = (z + place + 8) % 8
         needed = (block <= z) if below else (block >= z)
 
+        at = pl.ds(pl.multiple_of(block * GROUP, 64), GROUP)
+
         @pl.when(needed)
         def _():
-            out_ref[pl.ds(pl.multiple_of(block * GROUP, 64), GROUP), :] = piece[...]
-
-    spare = z + 1 if below else z - 1
-
-    @pl.when((spare >= 0) & (spare < 8))
-    def _():
-        out_ref[pl.ds(pl.multiple_of(spare * GROUP, 64), GROUP), :] = jnp.zeros(
-            (GROUP, 2 * HD), BF16
-        )
+            out_ref[at, :] = piece[...]
+
+        @pl.when(jnp.logical_not(needed))
+        def _():
+            out_ref[at, :] = jnp.zeros((GROUP, 2 * HD), BF16)
 
 
 def lane_max(x):
@@ -495,7 +493,9 @@
     out_q, small = query_pass(where, own, pieces + [far_kv])
     part = jnp.sum(received, axis=0)
     small = jnp.concatenate([small, jnp.broadcast_to(part[None], (8, 10, HD))], 1)
-    small = exchange(small, "cz")
+    small = lax.all_to_all(
+        small, "cz", 0, 0, tiled=True, axis_index_groups=[[7, 6, 5, 4, 3, 2, 1, 0]]
+    )[::-1]
     part = share(jnp.sum(small[:, 10:], axis=0), FT, 8)
     stats = small[:, :10].reshape(8, 2, 640)[:, :, :GROUP].transpose(1, 0, 2)
     stats = stats.reshape(2, CHUNKS, CHUNK).transpose(1, 0, 2)

time: 148 us -> 147 us (level)
    all_to_all x2 -> x1, blocking collectives: 33.8 us -> 16.1 us  [exchange(): return lax.all_to_all(x, axis, 0, 0, tiled=True)]
    all_to_all x0 -> x1, blocking collectives: none -> 16.4 us  [body(): lax.all_to_all(small, 'cz', 0, 0, tiled=True, axis_index_groups=[[7, 6, 5...]
where the time goes in v11:
time: 147 us; the launch traced here: 145 us
  starting transfers between devices  39.2 us (27%)
  Pallas kernels  38.8 us (26%)
  blocking collectives  32.5 us (22%)
  waiting for transfers between devices  29.5 us (20%)
  local copies, waits for them, and re-layouts  4.42 us (3%)
    pallas_call x2, Pallas kernels, hyena(): call(hyena_body, (struct((ROWS, 512), BF16), struct((3, ROWS, 512), F32),...  17.5 us
    all_to_all x1, blocking collectives, body(): lax.all_to_all(small, 'cz', 0, 0, tiled=True, axis_index_groups=[[7, 6, 5...  16.4 us
    all_to_all x1, blocking collectives, exchange(): return lax.all_to_all(x, axis, 0, 0, tiled=True)  16.1 us
    ppermute x6, starting transfers between devices, shift(): return lax.ppermute(x, 'cz', [(i, (i + by) % 8) for i in range(8)])  15.9 us
    all_to_all x3, starting transfers between devices, exchange(): return lax.all_to_all(x, axis, 0, 0, tiled=True)  15.6 us
    ppermute x6, waiting for transfers between devices, shift(): return lax.ppermute(x, 'cz', [(i, (i + by) % 8) for i in range(8)])  10.8 us
    pallas_call x1, Pallas kernels, key_pass(): call(key_body, struct((GROUP, 2 * HD), BF16), 'key_pass', grid=(1,), in_s...  8.93 us
    ppermute x1, waiting for transfers between devices, body(): far_qd = lax.ppermute(falling[3], 'cz', [(i, i - 1) for i in range(1, 5)])  7.26 us
  transfers between devices with their start and end apart: 13, of which 8 were waited for; matrix products, arithmetic and copies ran while one was open for 1% of the time, Pallas kernels for 22%

profile of v11, /device:TPU:2, one launch (start us, length us, event | category | flops | bytes accessed | tf_op | source)
XLA Modules:
  0.0 145.4 jit_solution(16757068932191827850)
XLA Ops:
  0.6 2.5 %pack.1 = (bf16[4,144,512]{2,1,0:T(8,128)(2,1)}, bf16[280,512]{1,0:T(8,128)(2,1)}, bf16[288,512]{1,0:T(8,128)(2,1)}) custom-call(bf16[144,512]{1,0:T(8,128)(2,1)} %q_ref.1, bf16[144,512]{1,0:T(8,128)(2,1)} %d_ref.1, bf16[144,512]{1,0:T(8,128)(2,1)} %k_ref.1, bf16[144,512]{1,0:T(8,128)(2,1)} %v_ref.1, bf16[3,144,512]{2,1,0:T(8,128)(2,1)} %bitcast.19, ...), custom_call_target="tpu_custom_call" | custom-call | tf_op jit(solution)/shard_map/pack/pallas_call | solution.py:65
  3.1 4.6 %all-to-all-start = ((bf16[4,144,512]{2,1,0:T(8,128)(2,1)}), bf16[4,144,512]{2,1,0:T(8,128)(2,1)S(1)}, u32[]{:S(2)}, u32[]{:S(2)}) async-start(bf16[4,144,512]{2,1,0:T(8,128)(2,1)} %get-tuple-element.48), calls=%async_computation | async-start | bytes 1179648 | tf_op jit(solution)/shard_map/all_to_all | solution.py:435
  7.7 1.3 collective-permute-start.1
  9.0 4.6 %collective-permute-start = (bf16[280,512]{1,0:T(8,128)(2,1)S(1)}, bf16[280,512]{1,0:T(8,128)(2,1)S(1)}, u32[]{:S(2)}, u32[]{:S(2)}) collective-permute-start(bf16[280,512]{1,0:T(8,128)(2,1)S(1)} %copy-done.19), channel_id=1, source_target_pairs={{0,8},{8,16},{16,24},{24,32},{32,40},{40,48},{48,56},{56,64},{64,7... | collective-permute-start | bytes 860168 | tf_op jit(solution)/shard_map/ppermute | solution.py:451
  13.6 6.7 %collective-permute-done.prev_ref = bf16[280,512]{1,0:T(8,128)(2,1)S(1)} collective-permute-done((bf16[280,512]{1,0:T(8,128)(2,1)S(1)}, bf16[280,512]{1,0:T(8,128)(2,1)S(1)}, u32[]{:S(2)}, u32[]{:S(2)}) %collective-permute-start) | collective-permute-done | bytes 286752 | tf_op jit(solution)/shard_map/ppermute | solution.py:451
  20.3 2.4 %collective-permute-done.1.next_ref = bf16[288,512]{1,0:T(8,128)(2,1)S(1)} collective-permute-done((bf16[288,512]{1,0:T(8,128)(2,1)S(1)}, bf16[288,512]{1,0:T(8,128)(2,1)S(1)}, u32[]{:S(2)}, u32[]{:S(2)}) %collective-permute-start.1) | collective-permute-done | bytes 294944 | tf_op jit(solution)/shard_map/ppermute | solution.py:452
  22.7 4.0 %collective-permute-start.2 = (bf16[576,512]{1,0:T(8,128)(2,1)S(1)}, bf16[576,512]{1,0:T(8,128)(2,1)S(1)}, u32[]{:S(2)}, u32[]{:S(2)}) collective-permute-start(bf16[576,512]{1,0:T(8,128)(2,1)S(1)} %bitcast.13), channel_id=1, source_target_pairs={{0,32},{32,64},{64,96},{96,128},{128,160},{160,192},{192,224},{224... | collective-permute-start | bytes 1769480 | tf_op jit(solution)/shard_map/ppermute | solution.py:458
  26.7 4.5 %collective-permute-start.3 = (bf16[576,512]{1,0:T(8,128)(2,1)S(1)}, bf16[576,512]{1,0:T(8,128)(2,1)S(1)}, u32[]{:S(2)}, u32[]{:S(2)}) collective-permute-start(bf16[576,512]{1,0:T(8,128)(2,1)S(1)} %bitcast.14), channel_id=1, source_target_pairs={{0,224},{32,0},{64,32},{96,64},{128,96},{160,128},{192,160},{224,1... | collective-permute-start | bytes 1769480 | tf_op jit(solution)/shard_map/ppermute | solution.py:458
  31.8 8.7 %hyena.2 = (bf16[144,512]{1,0:T(8,128)(2,1)}, f32[3,144,512]{2,1,0:T(8,128)}, f32[128,128]{1,0:T(8,128)}, f32[3,8,128]{2,1,0:T(8,128)}) custom-call(bf16[3,144,512]{2,1,0:T(8,128)(2,1)} %bitcast.20, bf16[280,512]{1,0:T(8,128)(2,1)} %copy-done.8, bf16[288,512]{1,0:T(8,128)(2,1)} %copy-done.7, bf16[144,512]{1,0:T(8,128)(2,1)} %up_ref.5, ...), custom_call_target="tpu_custom_call" | custom-call | tf_op jit(solution)/shard_map/hyena/pallas_call | solution.py:205
  40.5 2.1 %collective-permute-done.2.refs_1_ = bf16[576,512]{1,0:T(8,128)(2,1)S(1)} collective-permute-done((bf16[576,512]{1,0:T(8,128)(2,1)S(1)}, bf16[576,512]{1,0:T(8,128)(2,1)S(1)}, u32[]{:S(2)}, u32[]{:S(2)}) %collective-permute-start.2) | collective-permute-done | bytes 589856 | tf_op jit(solution)/shard_map/ppermute | solution.py:458
  42.7 3.2 %collective-permute-start.5 = (bf16[576,512]{1,0:T(8,128)(2,1)S(1)}, bf16[576,512]{1,0:T(8,128)(2,1)S(1)}, u32[]{:S(2)}, u32[]{:S(2)}) collective-permute-start(bf16[576,512]{1,0:T(8,128)(2,1)S(1)} %collective-permute-done.3.refs_4_), channel_id=1, source_target_pairs={{0,224},{32,0},{64,32},{96,64},{128,96},{160,128},{192,160},{224,1... | collective-permute-start | bytes 1769480 | tf_op jit(solution)/shard_map/ppermute | solution.py:458
  45.9 8.8 %hyena.3 = (bf16[144,512]{1,0:T(8,128)(2,1)}, f32[3,144,512]{2,1,0:T(8,128)}, f32[128,128]{1,0:T(8,128)}, f32[3,8,128]{2,1,0:T(8,128)}) custom-call(bf16[3,144,512]{2,1,0:T(8,128)(2,1)} %bitcast.21, bf16[280,512]{1,0:T(8,128)(2,1)} %copy-done.8, bf16[288,512]{1,0:T(8,128)(2,1)} %copy-done.7, ...), custom_call_target="tpu_custom_call", output_to_operand_aliasing={{0}: (6, {}), {1}: (7, {})} | custom-call | tf_op jit(solution)/shard_map/hyena/pallas_call | solution.py:205
  54.7 1.8 %collective-permute-done.4.refs_2_ = bf16[576,512]{1,0:T(8,128)(2,1)S(1)} collective-permute-done((bf16[576,512]{1,0:T(8,128)(2,1)S(1)}, bf16[576,512]{1,0:T(8,128)(2,1)S(1)}, u32[]{:S(2)}, u32[]{:S(2)}) %collective-permute-start.4) | collective-permute-done | bytes 589856 | tf_op jit(solution)/shard_map/ppermute | solution.py:458
  56.6 3.0 %collective-permute-start.7 = (bf16[576,256]{1,0:T(8,128)(2,1)S(1)}, bf16[576,256]{1,0:T(8,128)(2,1)S(1)}, u32[]{:S(2)}, u32[]{:S(2)}) collective-permute-start(bf16[576,256]{1,0:T(8,128)(2,1)S(1)} %constant_dynamic-slice_fusion), channel_id=1, source_target_pairs={{0,224},{32,0},{64,32},{96,64},{128,96},{160,128},{192,160},{224,1... | collective-permute-start | bytes 884744 | tf_op jit(solution)/shard_map/ppermute | solution.py:458
  59.7 1.1 collective-permute-start.6
  60.8 4.0 %collective-permute-done.7.refs_6_ = bf16[576,256]{1,0:T(8,128)(2,1)S(1)} collective-permute-done((bf16[576,256]{1,0:T(8,128)(2,1)S(1)}, bf16[576,256]{1,0:T(8,128)(2,1)S(1)}, u32[]{:S(2)}, u32[]{:S(2)}) %collective-permute-start.7) | collective-permute-done | bytes 294944 | tf_op jit(solution)/shard_map/ppermute | solution.py:458
  64.7 2.9 %collective-permute-done.6.refs_3_ = bf16[576,256]{1,0:T(8,128)(2,1)S(1)} collective-permute-done((bf16[576,256]{1,0:T(8,128)(2,1)S(1)}, bf16[576,256]{1,0:T(8,128)(2,1)S(1)}, u32[]{:S(2)}, u32[]{:S(2)}) %collective-permute-start.6) | collective-permute-done | bytes 294944 | tf_op jit(solution)/shard_map/ppermute | solution.py:458
  67.7 0.7 collective-permute-start.8
  68.4 1.3 collective-permute-start.9
  69.7 7.3 %collective-permute-done.9.refs_7_ = bf16[576,256]{1,0:T(8,128)(2,1)S(1)} collective-permute-done((bf16[576,256]{1,0:T(8,128)(2,1)S(1)}, bf16[576,256]{1,0:T(8,128)(2,1)S(1)}, u32[]{:S(2)}, u32[]{:S(2)}) %collective-permute-start.9) | collective-permute-done | bytes 294944 | tf_op jit(solution)/shard_map/ppermute | solution.py:488
  77.0 0.7 reshape.43
  77.8 5.9 %all-to-all-start.1 = ((f32[32,10,128]{2,1,0:T(8,128)}), f32[32,10,128]{2,1,0:T(8,128)S(1)}, u32[]{:S(2)}, u32[]{:S(2)}) async-start(f32[32,10,128]{2,1,0:T(8,128)} %reshape.43), calls=%async_computation.1 | async-start | bytes 524288 | tf_op jit(solution)/shard_map/all_to_all | solution.py:435
  83.7 5.8 %query_pass.1 = (bf16[576,256]{1,0:T(8,128)(2,1)}, f32[8,10,128]{2,1,0:T(8,128)}) custom-call(s32[1]{0:T(128)} %bitcast.2.where_ref, bf16[576,512]{1,0:T(8,128)(2,1)} %bitcast.15, bf16[576,512]{1,0:T(8,128)(2,1)} %bitcast.16, bf16[576,512]{1,0:T(8,128)(2,1)} %copy-done.3, bf16[576,512]{1,0:T(8,128)(2,1)} %copy-done.1, bf16[576,256]{1,0:T(8,128)(2,1)} %copy-done.6, ...), custom_call_target="tpu_custom_call" | custom-call | tf_op jit(solution)/shard_map/query_pass/pallas_call | solution.py:342
  89.5 2.3 %all-to-all-done.1 = f32[32,10,128]{2,1,0:T(8,128)S(1)} async-done(((f32[32,10,128]{2,1,0:T(8,128)}), f32[32,10,128]{2,1,0:T(8,128)S(1)}, u32[]{:S(2)}, u32[]{:S(2)}) %all-to-all-start.1) | async-done | bytes 163872 | tf_op jit(solution)/shard_map/all_to_all | solution.py:435
  91.8 0.8 copy-done.12
  92.7 16.4 %all_to_all.25 = f32[8,20,128]{2,1,0:T(8,128)S(1)} all-to-all(f32[8,20,128]{2,1,0:T(8,128)S(1)} %pad_maximum_fusion), channel_id=1, replica_groups={{224,192,160,128,96,64,32,0},{225,193,161,129,97,65,33,1},{226,194,162,..., dimensions={0} | all-to-all | bytes 163840 | tf_op jit(solution)/shard_map/all_to_all | solution.py:496
  109.8 5.1 %all-to-all-start.3 = ((f32[8,10,128]{2,1,0:T(8,128)}), f32[8,10,128]{2,1,0:T(8,128)S(1)}, u32[]{:S(2)}, u32[]{:S(2)}) async-start(f32[8,10,128]{2,1,0:T(8,128)} %broadcast_in_dim.8), calls=%async_computation.3 | async-start | bytes 131072 | tf_op jit(solution)/shard_map/all_to_all | solution.py:435
  115.0 0.6 copy.21
  115.6 8.9 %key_pass.1.ok_ref = bf16[576,256]{1,0:T(8,128)(2,1)} custom-call(s32[1]{0:T(128)} %bitcast.2.where_ref, bf16[576,512]{1,0:T(8,128)(2,1)} %bitcast.17, f32[3,2,1536]{2,1,0:T(2,128)} %bitcast.23, bf16[576,512]{1,0:T(8,128)(2,1)} %bitcast.18, bf16[576,512]{1,0:T(8,128)(2,1)} %copy-done.3, bf16[576,512]{1,0:T(8,128)(2,1)} %copy-done.1, ...), custom_call_target="tpu_custom_call" | custom-call | tf_op jit(solution)/shard_map/key_pass/pallas_call | solution.py:417
  125.2 2.0 %join.1 = bf16[4,168,512]{2,1,0:T(8,128)(2,1)} custom-call(bf16[576,256]{1,0:T(8,128)(2,1)} %get-tuple-element.73.oq_ref, bf16[576,256]{1,0:T(8,128)(2,1)} %key_pass.1.ok_ref, f32[8,10,128]{2,1,0:T(8,128)} %copy-done.11), custom_call_target="tpu_custom_call" | custom-call | tf_op jit(solution)/shard_map/join/pallas_call | solution.py:412
  127.2 16.1 %all_to_all.26.x_ref = bf16[4,168,512]{2,1,0:T(8,128)(2,1)} all-to-all(bf16[4,168,512]{2,1,0:T(8,128)(2,1)} %join.1), channel_id=1, replica_groups=mesh['cz'=8,'cy'=4,'fsdp'=4,'tp'=2] {'cy'}, dimensions={0} | all-to-all | bytes 1376256 | tf_op jit(solution)/shard_map/all_to_all | solution.py:435
  143.3 2.1 %unpack.1 = (bf16[144,512]{1,0:T(8,128)(2,1)}, f32[144,512]{1,0:T(8,128)}, f32[144,512]{1,0:T(8,128)}, f32[144,512]{1,0:T(8,128)}, f32[128,256]{1,0:T(8,128)}, /*index=5*/f32[3,7,256]{2,1,0:T(8,128)}) custom-call(bf16[4,168,512]{2,1,0:T(8,128)(2,1)} %all_to_all.26.x_ref), custom_call_target="tpu_custom_call" | custom-call | tf_op jit(solution)/shard_map/unpack/pallas_call | solution.py:97
  (64 shorter events, 2.4 us)
Async XLA Ops:
  3.1 4.6 %copy-start.18 = (bf16[288,512]{1,0:T(8,128)(2,1)S(1)}, bf16[288,512]{1,0:T(8,128)(2,1)}, u32[]{:S(2)}) copy-start(bf16[288,512]{1,0:T(8,128)(2,1)} %get-tuple-element.50) | copy-start | bytes 884740
  3.1 5.9 %copy-start.19 = (bf16[280,512]{1,0:T(8,128)(2,1)S(1)}, bf16[280,512]{1,0:T(8,128)(2,1)}, u32[]{:S(2)}) copy-start(bf16[280,512]{1,0:T(8,128)(2,1)} %get-tuple-element.49) | copy-start | bytes 860164
  3.1 28.1 %copy-start.15 = (f32[3,7,256]{2,1,0:T(8,128)S(1)}, f32[3,7,256]{2,1,0:T(8,128)}, u32[]{:S(2)}) copy-start(f32[3,7,256]{2,1,0:T(8,128)} %param.9) | copy-start | bytes 64516
  3.1 19.6 %all-to-all-start = ((bf16[4,144,512]{2,1,0:T(8,128)(2,1)}), bf16[4,144,512]{2,1,0:T(8,128)(2,1)S(1)}, u32[]{:S(2)}, u32[]{:S(2)}) async-start(bf16[4,144,512]{2,1,0:T(8,128)(2,1)} %get-tuple-element.48), calls=%async_computation | async-start | bytes 1179648 | tf_op jit(solution)/shard_map/all_to_all | solution.py:435
  7.7 15.0 %collective-permute-start.1 = (bf16[288,512]{1,0:T(8,128)(2,1)S(1)}, bf16[288,512]{1,0:T(8,128)(2,1)S(1)}, u32[]{:S(2)}, u32[]{:S(2)}) collective-permute-start(bf16[288,512]{1,0:T(8,128)(2,1)S(1)} %copy-done.18), channel_id=1, source_target_pairs={{8,0},{16,8},{24,16},{32,24},{40,32},{48,40},{56,48},{64,56},{72,6... | collective-permute-start | bytes 884744 | tf_op jit(solution)/shard_map/ppermute | solution.py:452
  9.0 11.3 %collective-permute-start = (bf16[280,512]{1,0:T(8,128)(2,1)S(1)}, bf16[280,512]{1,0:T(8,128)(2,1)S(1)}, u32[]{:S(2)}, u32[]{:S(2)}) collective-permute-start(bf16[280,512]{1,0:T(8,128)(2,1)S(1)} %copy-done.19), channel_id=1, source_target_pairs={{0,8},{8,16},{16,24},{24,32},{32,40},{40,48},{48,56},{56,64},{64,7... | collective-permute-start | bytes 860168 | tf_op jit(solution)/shard_map/ppermute | solution.py:451
  20.3 11.5 %copy-start.8 = (bf16[280,512]{1,0:T(8,128)(2,1)}, bf16[280,512]{1,0:T(8,128)(2,1)S(1)}, u32[]{:S(2)}) copy-start(bf16[280,512]{1,0:T(8,128)(2,1)S(1)} %collective-permute-done.prev_ref) | copy-start | bytes 860164
  22.7 9.1 %copy-start.7 = (bf16[288,512]{1,0:T(8,128)(2,1)}, bf16[288,512]{1,0:T(8,128)(2,1)S(1)}, u32[]{:S(2)}) copy-start(bf16[288,512]{1,0:T(8,128)(2,1)S(1)} %collective-permute-done.1.next_ref) | copy-start | bytes 884740
  22.7 17.8 %copy-start = (bf16[4,144,512]{2,1,0:T(8,128)(2,1)}, bf16[4,144,512]{2,1,0:T(8,128)(2,1)S(1)}, u32[]{:S(2)}) copy-start(bf16[4,144,512]{2,1,0:T(8,128)(2,1)S(1)} %all-to-all-done) | copy-start | bytes 1769476
  22.7 19.9 %collective-permute-start.2 = (bf16[576,512]{1,0:T(8,128)(2,1)S(1)}, bf16[576,512]{1,0:T(8,128)(2,1)S(1)}, u32[]{:S(2)}, u32[]{:S(2)}) collective-permute-start(bf16[576,512]{1,0:T(8,128)(2,1)S(1)} %bitcast.13), channel_id=1, source_target_pairs={{0,32},{32,64},{64,96},{96,128},{128,160},{160,192},{192,224},{224... | collective-permute-start | bytes 1769480 | tf_op jit(solution)/shard_map/ppermute | solution.py:458
  26.7 15.9 %collective-permute-start.3 = (bf16[576,512]{1,0:T(8,128)(2,1)S(1)}, bf16[576,512]{1,0:T(8,128)(2,1)S(1)}, u32[]{:S(2)}, u32[]{:S(2)}) collective-permute-start(bf16[576,512]{1,0:T(8,128)(2,1)S(1)} %bitcast.14), channel_id=1, source_target_pairs={{0,224},{32,0},{64,32},{96,64},{128,96},{160,128},{192,160},{224,1... | collective-permute-start | bytes 1769480 | tf_op jit(solution)/shard_map/ppermute | solution.py:458
  42.6 12.1 %copy-start.3 = (bf16[576,512]{1,0:T(8,128)(2,1)}, bf16[576,512]{1,0:T(8,128)(2,1)S(1)}, u32[]{:S(2)}) copy-start(bf16[576,512]{1,0:T(8,128)(2,1)S(1)} %collective-permute-done.2.refs_1_) | copy-start | bytes 1769476
  42.6 12.1 %copy-start.4 = (bf16[576,512]{1,0:T(8,128)(2,1)}, bf16[576,512]{1,0:T(8,128)(2,1)S(1)}, u32[]{:S(2)}) copy-start(bf16[576,512]{1,0:T(8,128)(2,1)S(1)} %collective-permute-done.3.refs_4_) | copy-start | bytes 1769476
  42.6 13.9 %collective-permute-start.4 = (bf16[576,512]{1,0:T(8,128)(2,1)S(1)}, bf16[576,512]{1,0:T(8,128)(2,1)S(1)}, u32[]{:S(2)}, u32[]{:S(2)}) collective-permute-start(bf16[576,512]{1,0:T(8,128)(2,1)S(1)} %collective-permute-done.2.refs_1_), channel_id=1, source_target_pairs={{0,32},{32,64},{64,96},{96,128},{128,160},{160,192},{192,224},{224... | collective-permute-start | bytes 1769480 | tf_op jit(solution)/shard_map/ppermute | solution.py:458
  42.7 13.8 %collective-permute-start.5 = (bf16[576,512]{1,0:T(8,128)(2,1)S(1)}, bf16[576,512]{1,0:T(8,128)(2,1)S(1)}, u32[]{:S(2)}, u32[]{:S(2)}) collective-permute-start(bf16[576,512]{1,0:T(8,128)(2,1)S(1)} %collective-permute-done.3.refs_4_), channel_id=1, source_target_pairs={{0,224},{32,0},{64,32},{96,64},{128,96},{160,128},{192,160},{224,1... | collective-permute-start | bytes 1769480 | tf_op jit(solution)/shard_map/ppermute | solution.py:458
  45.9 8.8 %copy-start.13 = (f32[128,128]{1,0:T(8,128)S(1)}, f32[128,128]{1,0:T(8,128)}, u32[]{:S(2)}) copy-start(f32[128,128]{1,0:T(8,128)} %get-tuple-element.75) | copy-start | bytes 196612
  56.5 3.1 %copy-start.1 = (bf16[576,512]{1,0:T(8,128)(2,1)}, bf16[576,512]{1,0:T(8,128)(2,1)S(1)}, u32[]{:S(2)}) copy-start(bf16[576,512]{1,0:T(8,128)(2,1)S(1)} %collective-permute-done.4.refs_2_) | copy-start | bytes 1769476
  56.5 3.1 %copy-start.2 = (bf16[576,512]{1,0:T(8,128)(2,1)}, bf16[576,512]{1,0:T(8,128)(2,1)S(1)}, u32[]{:S(2)}) copy-start(bf16[576,512]{1,0:T(8,128)(2,1)S(1)} %collective-permute-done.5.refs_5_) | copy-start | bytes 1769476
  56.6 4.2 %copy-start.14 = (f32[128,128]{1,0:T(8,128)S(1)}, f32[128,128]{1,0:T(8,128)}, u32[]{:S(2)}) copy-start(f32[128,128]{1,0:T(8,128)} %get-tuple-element.76) | copy-start | bytes 196612
  56.6 8.2 %collective-permute-start.7 = (bf16[576,256]{1,0:T(8,128)(2,1)S(1)}, bf16[576,256]{1,0:T(8,128)(2,1)S(1)}, u32[]{:S(2)}, u32[]{:S(2)}) collective-permute-start(bf16[576,256]{1,0:T(8,128)(2,1)S(1)} %constant_dynamic-slice_fusion), channel_id=1, source_target_pairs={{0,224},{32,0},{64,32},{96,64},{128,96},{160,128},{192,160},{224,1... | collective-permute-start | bytes 884744 | tf_op jit(solution)/shard_map/ppermute | solution.py:458
  59.7 1.1 copy-start.16
  59.7 8.0 %collective-permute-start.6 = (bf16[576,256]{1,0:T(8,128)(2,1)S(1)}, bf16[576,256]{1,0:T(8,128)(2,1)S(1)}, u32[]{:S(2)}, u32[]{:S(2)}) collective-permute-start(bf16[576,256]{1,0:T(8,128)(2,1)S(1)} %constant_dynamic-slice_fusion.1), channel_id=1, source_target_pairs={{0,32},{32,64},{64,96},{96,128},{128,160},{160,192},{192,224},{224... | collective-permute-start | bytes 884744 | tf_op jit(solution)/shard_map/ppermute | solution.py:458
  60.8 8.9 %copy-start.17 = (f32[3,8,128]{2,1,0:T(8,128)S(1)}, f32[3,8,128]{2,1,0:T(8,128)}, u32[]{:S(2)}) copy-start(f32[3,8,128]{2,1,0:T(8,128)} %get-tuple-element.78) | copy-start | bytes 36868
  64.7 13.0 %copy-start.5 = (bf16[576,256]{1,0:T(8,128)(2,1)}, bf16[576,256]{1,0:T(8,128)(2,1)S(1)}, u32[]{:S(2)}) copy-start(bf16[576,256]{1,0:T(8,128)(2,1)S(1)} %collective-permute-done.7.refs_6_) | copy-start | bytes 884740
  67.7 10.1 %copy-start.6 = (bf16[576,256]{1,0:T(8,128)(2,1)}, bf16[576,256]{1,0:T(8,128)(2,1)S(1)}, u32[]{:S(2)}) copy-start(bf16[576,256]{1,0:T(8,128)(2,1)S(1)} %collective-permute-done.6.refs_3_) | copy-start | bytes 884740
  67.7 2.0 %collective-permute-start.8 = (bf16[576,256]{1,0:T(8,128)(2,1)S(1)}, bf16[576,256]{1,0:T(8,128)(2,1)S(1)}, u32[]{:S(2)}, u32[]{:S(2)}) collective-permute-start(bf16[576,256]{1,0:T(8,128)(2,1)S(1)} %collective-permute-done.6.refs_3_), channel_id=1, source_target_pairs={{96,128},{128,160},{160,192},{192,224},{97,129},{129,161},{161,193... | collective-permute-start | bytes 884744 | tf_op jit(solution)/shard_map/ppermute | solution.py:487
  68.4 8.6 %collective-permute-start.9 = (bf16[576,256]{1,0:T(8,128)(2,1)S(1)}, bf16[576,256]{1,0:T(8,128)(2,1)S(1)}, u32[]{:S(2)}, u32[]{:S(2)}) collective-permute-start(bf16[576,256]{1,0:T(8,128)(2,1)S(1)} %collective-permute-done.7.refs_6_), channel_id=1, source_target_pairs={{32,0},{64,32},{96,64},{128,96},{33,1},{65,33},{97,65},{129,97},{3... | collective-permute-start | bytes 884744 | tf_op jit(solution)/shard_map/ppermute | solution.py:488
  69.7 14.0 %copy-start.10 = (bf16[576,256]{1,0:T(8,128)(2,1)}, bf16[576,256]{1,0:T(8,128)(2,1)S(1)}, u32[]{:S(2)}) copy-start(bf16[576,256]{1,0:T(8,128)(2,1)S(1)} %collective-permute-done.8.refs_7_) | copy-start | bytes 884740
  77.0 0.8 copy-start.9
  77.8 14.0 %all-to-all-start.1 = ((f32[32,10,128]{2,1,0:T(8,128)}), f32[32,10,128]{2,1,0:T(8,128)S(1)}, u32[]{:S(2)}, u32[]{:S(2)}) async-start(f32[32,10,128]{2,1,0:T(8,128)} %reshape.43), calls=%async_computation.1 | async-start | bytes 524288 | tf_op jit(solution)/shard_map/all_to_all | solution.py:435
  91.8 0.8 copy-start.12
  109.8 14.8 %all-to-all-start.3 = ((f32[8,10,128]{2,1,0:T(8,128)}), f32[8,10,128]{2,1,0:T(8,128)S(1)}, u32[]{:S(2)}, u32[]{:S(2)}) async-start(f32[8,10,128]{2,1,0:T(8,128)} %broadcast_in_dim.8), calls=%async_computation.3 | async-start | bytes 131072 | tf_op jit(solution)/shard_map/all_to_all | solution.py:435
  (1 other events, 0.6 us)

commit v12 on v11

--- a/solution.py
+++ b/solution.py
@@ -357,7 +357,7 @@
     )(where, own, *kv)
 
 
-def key_body(where_ref, own_ref, stat_ref, *refs):
+def key_body(where_ref, own_ref, stat_ref, oq_ref, *refs):
     out_ref, gk_ref, gv_ref, qd_ref = refs[8:]
     assemble(where_ref, refs[:8], qd_ref, False)
     first = where_ref[0] * GROUP
@@ -391,44 +391,56 @@
     def _(c):
         visit(c, False)
 
-    out_ref[:, :HD] = (gk_ref[...] * SCALE).astype(BF16)
-    out_ref[:, HD:] = gv_ref[...].astype(BF16)
-
-
-def join_body(oq_ref, ok_ref, slices_ref, out_ref, part_ref):
+    for j in range(4):
+        at = slice(j * ROWS, (j + 1) * ROWS)
+        out_ref[j, :ROWS, : 2 * HD] = oq_ref[at]
+        out_ref[j, :ROWS, 2 * HD : 3 * HD] = (gk_ref[at] * SCALE).astype(BF16)
+        out_ref[j, :ROWS, 3 * HD :] = gv_ref[at].astype(BF16)
+        out_ref[j, ROWS:] = jnp.zeros((24, 4 * HD), BF16)
+
+
+def join_body(slices_ref, kept_ref, out_ref, part_ref):
     for n in range(8):
         part_ref[10 * n : 10 * (n + 1)] = slices_ref[n]
     for j in range(4):
-        at = slice(j * ROWS, (j + 1) * ROWS)
-        out_ref[j, :ROWS, : 2 * HD] = oq_ref[at]
-        out_ref[j, :ROWS, 2 * HD :] = ok_ref[at]
         for c in range(4):
             value = part_ref[20 * c : 20 * (c + 1)].astype(BF16)
-            out_ref[j, ROWS : ROWS + 20, c * HD : (c + 1) * HD] = value
-        out_ref[j, ROWS + 20 :] = jnp.zeros((4, 4 * HD), BF16)
-
-
-def join(out_q, out_k, part):
-    return call(join_body, struct((4, ROWS + 24, 4 * HD), BF16), "join",
-                scratch_shapes=[pltpu.VMEM((80, HD), F32)])(out_q, out_k, part)
-
-
-def key_pass(where, own, qd, stats):
+            out_ref[j, 0:20, c * HD : (c + 1) * HD] = value
+        out_ref[j, 20:] = jnp.zeros((4, 4 * HD), BF16)
+
+
+def join(result, part):
+    return call(
+        join_body,
+        struct((4, ROWS + 24, 4 * HD), BF16),
+        "join",
+        grid=(1,),
+        in_specs=[
+            pl.BlockSpec((8, 10, HD), lambda i: (0, 0, 0)),
+            pl.BlockSpec(memory_space=pl.ANY),
+        ],
+        out_specs=pl.BlockSpec((4, 24, 4 * HD), lambda i: (0, 6, 0)),
+        input_output_aliases={1: 0},
+        scratch_shapes=[pltpu.VMEM((80, HD), F32)],
+    )(part, result)
+
+
+def key_pass(where, own, qd, stats, out_q):
     return call(
         key_body,
-        struct((GROUP, 2 * HD), BF16),
+        struct((4, ROWS + 24, 4 * HD), BF16),
         "key_pass",
         grid=(1,),
         in_specs=[pl.BlockSpec(memory_space=pltpu.SMEM)]
         + [part_of(1)]
-        + [pl.BlockSpec(memory_space=pltpu.VMEM)]
+        + [pl.BlockSpec(memory_space=pltpu.VMEM)] * 2
         + [part_of(0)] * 8,
         scratch_shapes=[
             pltpu.VMEM((GROUP, HD), F32),
             pltpu.VMEM((GROUP, HD), F32),
             pltpu.VMEM((SEQ, 2 * HD), BF16),
         ],
-    )(where, own, stats, *qd)
+    )(where, own, stats, out_q, *qd)
 
 
 def exchange(x, axis):
@@ -499,8 +511,8 @@
     part = share(jnp.sum(small[:, 10:], axis=0), FT, 8)
     stats = small[:, :10].reshape(8, 2, 640)[:, :, :GROUP].transpose(1, 0, 2)
     stats = stats.reshape(2, CHUNKS, CHUNK).transpose(1, 0, 2)
-    out_k = key_pass(where, own, pieces + [far_qd], stats)
-    result = join(out_q, out_k, part)
+    result = key_pass(where, own, pieces + [far_qd], stats, out_q)
+    result = join(result, part)
     attended, grad_queries, grad_keys, grad_values, grad_long, grad_short = unpack(
         exchange(result, "cy")
     )

time: 147 us -> 146 us (level)
  waiting for transfers between devices: 29.5 us -> 32.1 us
  blocking collectives: 32.5 us -> 30.4 us
    ppermute x6, waiting for transfers between devices: 10.8 us -> 13.4 us  [shift(): return lax.ppermute(x, 'cz', [(i, (i + by) % 8) for i in range(8)])]
    all_to_all x1, blocking collectives: 16.4 us -> 14.4 us  [body(): lax.all_to_all(small, 'cz', 0, 0, tiled=True, axis_index_groups=[[7, 6, 5...]
  transfers between devices with their start and end apart: 13 -> 13, of which waited for: 8 -> 9; matrix products, arithmetic and copies ran while one was open for 1% -> 1% of each run, Pallas kernels for 22% -> 22%
where the time goes in v12:
time: 146 us; the launch traced here: 145 us
  Pallas kernels  38.6 us (26%)
  starting transfers between devices  38.1 us (26%)
  waiting for transfers between devices  32.1 us (22%)
  blocking collectives  30.4 us (21%)
  local copies, waits for them, and re-layouts  5 us (3%)
    pallas_call x2, Pallas kernels, hyena(): call(hyena_body, (struct((ROWS, 512), BF16), struct((3, ROWS, 512), F32),...  17.5 us
    all_to_all x1, blocking collectives, exchange(): return lax.all_to_all(x, axis, 0, 0, tiled=True)  16.1 us
    all_to_all x3, starting transfers between devices, exchange(): return lax.all_to_all(x, axis, 0, 0, tiled=True)  15.2 us
    ppermute x6, starting transfers between devices, shift(): return lax.ppermute(x, 'cz', [(i, (i + by) % 8) for i in range(8)])  15.1 us
    all_to_all x1, blocking collectives, body(): lax.all_to_all(small, 'cz', 0, 0, tiled=True, axis_index_groups=[[7, 6, 5...  14.4 us
    ppermute x6, waiting for transfers between devices, shift(): return lax.ppermute(x, 'cz', [(i, (i + by) % 8) for i in range(8)])  13.4 us
    pallas_call x1, Pallas kernels, key_pass(): call(key_body, struct((4, ROWS + 24, 4 * HD), BF16), 'key_pass', grid=(1,...  9.19 us
    ppermute x1, waiting for transfers between devices, body(): far_qd = lax.ppermute(falling[3], 'cz', [(i, i - 1) for i in range(1, 5)])  7.26 us
  transfers between devices with their start and end apart: 13, of which 9 were waited for; matrix products, arithmetic and copies ran while one was open for 1% of the time, Pallas kernels for 22%

profile of v12, /device:TPU:2, one launch (start us, length us, event | category | flops | bytes accessed | tf_op | source)
XLA Modules:
  0.0 145.2 jit_solution(17919199415882939593)
XLA Ops:
  0.6 2.5 %pack.1 = (bf16[4,144,512]{2,1,0:T(8,128)(2,1)}, bf16[280,512]{1,0:T(8,128)(2,1)}, bf16[288,512]{1,0:T(8,128)(2,1)}) custom-call(bf16[144,512]{1,0:T(8,128)(2,1)} %q_ref.1, bf16[144,512]{1,0:T(8,128)(2,1)} %d_ref.1, bf16[144,512]{1,0:T(8,128)(2,1)} %k_ref.1, bf16[144,512]{1,0:T(8,128)(2,1)} %v_ref.1, bf16[3,144,512]{2,1,0:T(8,128)(2,1)} %bitcast.19, ...), custom_call_target="tpu_custom_call" | custom-call | tf_op jit(solution)/shard_map/pack/pallas_call | solution.py:65
  3.1 4.6 %all-to-all-start = ((bf16[4,144,512]{2,1,0:T(8,128)(2,1)}), bf16[4,144,512]{2,1,0:T(8,128)(2,1)S(1)}, u32[]{:S(2)}, u32[]{:S(2)}) async-start(bf16[4,144,512]{2,1,0:T(8,128)(2,1)} %get-tuple-element.48), calls=%async_computation | async-start | bytes 1179648 | tf_op jit(solution)/shard_map/all_to_all | solution.py:447
  7.7 1.3 collective-permute-start.1
  9.0 4.6 %collective-permute-start = (bf16[280,512]{1,0:T(8,128)(2,1)S(1)}, bf16[280,512]{1,0:T(8,128)(2,1)S(1)}, u32[]{:S(2)}, u32[]{:S(2)}) collective-permute-start(bf16[280,512]{1,0:T(8,128)(2,1)S(1)} %copy-done.19), channel_id=1, source_target_pairs={{0,8},{8,16},{16,24},{24,32},{32,40},{40,48},{48,56},{56,64},{64,7... | collective-permute-start | bytes 860168 | tf_op jit(solution)/shard_map/ppermute | solution.py:463
  13.6 6.7 %collective-permute-done.prev_ref = bf16[280,512]{1,0:T(8,128)(2,1)S(1)} collective-permute-done((bf16[280,512]{1,0:T(8,128)(2,1)S(1)}, bf16[280,512]{1,0:T(8,128)(2,1)S(1)}, u32[]{:S(2)}, u32[]{:S(2)}) %collective-permute-start) | collective-permute-done | bytes 286752 | tf_op jit(solution)/shard_map/ppermute | solution.py:463
  20.3 2.4 %collective-permute-done.1.next_ref = bf16[288,512]{1,0:T(8,128)(2,1)S(1)} collective-permute-done((bf16[288,512]{1,0:T(8,128)(2,1)S(1)}, bf16[288,512]{1,0:T(8,128)(2,1)S(1)}, u32[]{:S(2)}, u32[]{:S(2)}) %collective-permute-start.1) | collective-permute-done | bytes 294944 | tf_op jit(solution)/shard_map/ppermute | solution.py:464
  22.7 8.4 %collective-permute-start.3 = (bf16[576,512]{1,0:T(8,128)(2,1)S(1)}, bf16[576,512]{1,0:T(8,128)(2,1)S(1)}, u32[]{:S(2)}, u32[]{:S(2)}) collective-permute-start(bf16[576,512]{1,0:T(8,128)(2,1)S(1)} %bitcast.13), channel_id=1, source_target_pairs={{0,224},{32,0},{64,32},{96,64},{128,96},{160,128},{192,160},{224,1... | collective-permute-start | bytes 1769480 | tf_op jit(solution)/shard_map/ppermute | solution.py:470
  31.7 8.7 %hyena.2 = (bf16[144,512]{1,0:T(8,128)(2,1)}, f32[3,144,512]{2,1,0:T(8,128)}, f32[128,128]{1,0:T(8,128)}, f32[3,8,128]{2,1,0:T(8,128)}) custom-call(bf16[3,144,512]{2,1,0:T(8,128)(2,1)} %bitcast.20, bf16[280,512]{1,0:T(8,128)(2,1)} %copy-done.8, bf16[288,512]{1,0:T(8,128)(2,1)} %copy-done.7, bf16[144,512]{1,0:T(8,128)(2,1)} %up_ref.5, ...), custom_call_target="tpu_custom_call" | custom-call | tf_op jit(solution)/shard_map/hyena/pallas_call | solution.py:205
  40.4 1.4 collective-permute-done.3.refs_4_
  41.9 3.4 %collective-permute-done.2.refs_1_ = bf16[576,512]{1,0:T(8,128)(2,1)S(1)} collective-permute-done((bf16[576,512]{1,0:T(8,128)(2,1)S(1)}, bf16[576,512]{1,0:T(8,128)(2,1)S(1)}, u32[]{:S(2)}, u32[]{:S(2)}) %collective-permute-start.2) | collective-permute-done | bytes 589856 | tf_op jit(solution)/shard_map/ppermute | solution.py:470
  45.3 3.2 %collective-permute-start.5 = (bf16[576,512]{1,0:T(8,128)(2,1)S(1)}, bf16[576,512]{1,0:T(8,128)(2,1)S(1)}, u32[]{:S(2)}, u32[]{:S(2)}) collective-permute-start(bf16[576,512]{1,0:T(8,128)(2,1)S(1)} %collective-permute-done.3.refs_4_), channel_id=1, source_target_pairs={{0,224},{32,0},{64,32},{96,64},{128,96},{160,128},{192,160},{224,1... | collective-permute-start | bytes 1769480 | tf_op jit(solution)/shard_map/ppermute | solution.py:470
  48.5 8.8 %hyena.3 = (bf16[144,512]{1,0:T(8,128)(2,1)}, f32[3,144,512]{2,1,0:T(8,128)}, f32[128,128]{1,0:T(8,128)}, f32[3,8,128]{2,1,0:T(8,128)}) custom-call(bf16[3,144,512]{2,1,0:T(8,128)(2,1)} %bitcast.21, bf16[280,512]{1,0:T(8,128)(2,1)} %copy-done.8, bf16[288,512]{1,0:T(8,128)(2,1)} %copy-done.7, ...), custom_call_target="tpu_custom_call", output_to_operand_aliasing={{0}: (6, {}), {1}: (7, {})} | custom-call | tf_op jit(solution)/shard_map/hyena/pallas_call | solution.py:205
  57.3 1.2 collective-permute-done.4.refs_2_
  58.6 3.4 %collective-permute-start.7 = (bf16[576,256]{1,0:T(8,128)(2,1)S(1)}, bf16[576,256]{1,0:T(8,128)(2,1)S(1)}, u32[]{:S(2)}, u32[]{:S(2)}) collective-permute-start(bf16[576,256]{1,0:T(8,128)(2,1)S(1)} %constant_dynamic-slice_fusion), channel_id=1, source_target_pairs={{0,224},{32,0},{64,32},{96,64},{128,96},{160,128},{192,160},{224,1... | collective-permute-start | bytes 884744 | tf_op jit(solution)/shard_map/ppermute | solution.py:470
  62.8 3.5 %collective-permute-done.7.refs_6_ = bf16[576,256]{1,0:T(8,128)(2,1)S(1)} collective-permute-done((bf16[576,256]{1,0:T(8,128)(2,1)S(1)}, bf16[576,256]{1,0:T(8,128)(2,1)S(1)}, u32[]{:S(2)}, u32[]{:S(2)}) %collective-permute-start.7) | collective-permute-done | bytes 294944 | tf_op jit(solution)/shard_map/ppermute | solution.py:470
  66.3 3.8 %collective-permute-done.6.refs_3_ = bf16[576,256]{1,0:T(8,128)(2,1)S(1)} collective-permute-done((bf16[576,256]{1,0:T(8,128)(2,1)S(1)}, bf16[576,256]{1,0:T(8,128)(2,1)S(1)}, u32[]{:S(2)}, u32[]{:S(2)}) %collective-permute-start.6) | collective-permute-done | bytes 294944 | tf_op jit(solution)/shard_map/ppermute | solution.py:470
  70.1 0.7 collective-permute-start.8
  70.8 1.3 collective-permute-start.9
  72.1 7.3 %collective-permute-done.9.refs_7_ = bf16[576,256]{1,0:T(8,128)(2,1)S(1)} collective-permute-done((bf16[576,256]{1,0:T(8,128)(2,1)S(1)}, bf16[576,256]{1,0:T(8,128)(2,1)S(1)}, u32[]{:S(2)}, u32[]{:S(2)}) %collective-permute-start.9) | collective-permute-done | bytes 294944 | tf_op jit(solution)/shard_map/ppermute | solution.py:500
  79.4 0.8 reshape.43
  80.2 5.5 %all-to-all-start.1 = ((f32[32,10,128]{2,1,0:T(8,128)}), f32[32,10,128]{2,1,0:T(8,128)S(1)}, u32[]{:S(2)}, u32[]{:S(2)}) async-start(f32[32,10,128]{2,1,0:T(8,128)} %reshape.43), calls=%async_computation.1 | async-start | bytes 524288 | tf_op jit(solution)/shard_map/all_to_all | solution.py:447
  85.7 5.8 %query_pass.1 = (bf16[576,256]{1,0:T(8,128)(2,1)}, f32[8,10,128]{2,1,0:T(8,128)}) custom-call(s32[1]{0:T(128)} %bitcast.2.where_ref, bf16[576,512]{1,0:T(8,128)(2,1)} %bitcast.15, bf16[576,512]{1,0:T(8,128)(2,1)} %bitcast.16, bf16[576,512]{1,0:T(8,128)(2,1)} %copy-done.4, bf16[576,512]{1,0:T(8,128)(2,1)} %copy-done.1, bf16[576,256]{1,0:T(8,128)(2,1)} %copy-done.6, ...), custom_call_target="tpu_custom_call" | custom-call | tf_op jit(solution)/shard_map/query_pass/pallas_call | solution.py:342
  91.5 2.3 %all-to-all-done.1 = f32[32,10,128]{2,1,0:T(8,128)S(1)} async-done(((f32[32,10,128]{2,1,0:T(8,128)}), f32[32,10,128]{2,1,0:T(8,128)S(1)}, u32[]{:S(2)}, u32[]{:S(2)}) %all-to-all-start.1) | async-done | bytes 163872 | tf_op jit(solution)/shard_map/all_to_all | solution.py:447
  93.9 0.8 copy-done.12
  94.7 14.4 %all_to_all.25 = f32[8,20,128]{2,1,0:T(8,128)S(1)} all-to-all(f32[8,20,128]{2,1,0:T(8,128)S(1)} %pad_maximum_fusion), channel_id=1, replica_groups={{224,192,160,128,96,64,32,0},{225,193,161,129,97,65,33,1},{226,194,162,..., dimensions={0} | all-to-all | bytes 163840 | tf_op jit(solution)/shard_map/all_to_all | solution.py:508
  109.2 0.6 broadcast_in_dim.8
  109.8 5.1 %all-to-all-start.3 = ((f32[8,10,128]{2,1,0:T(8,128)}), f32[8,10,128]{2,1,0:T(8,128)S(1)}, u32[]{:S(2)}, u32[]{:S(2)}) async-start(f32[8,10,128]{2,1,0:T(8,128)} %broadcast_in_dim.8), calls=%async_computation.3 | async-start | bytes 131072 | tf_op jit(solution)/shard_map/all_to_all | solution.py:447
  115.0 0.6 copy.22
  115.6 9.2 %key_pass.1.kept_ref = bf16[4,168,512]{2,1,0:T(8,128)(2,1)} custom-call(s32[1]{0:T(128)} %bitcast.2.where_ref, bf16[576,512]{1,0:T(8,128)(2,1)} %bitcast.17, f32[3,2,1536]{2,1,0:T(2,128)} %bitcast.23, bf16[576,256]{1,0:T(8,128)(2,1)} %get-tuple-element.79.oq_ref, bf16[576,512]{1,0:T(8,128)(2,1)} %bitcast.18, bf16[576,512]{1,0:T(8,128)(2,1)} %copy-done.4, ...), custom_call_target="tpu_custom_call" | custom-call | tf_op jit(solution)/shard_map/key_pass/pallas_call | solution.py:429
  125.5 1.5 %join.1 = bf16[4,168,512]{2,1,0:T(8,128)(2,1)} custom-call(f32[8,10,128]{2,1,0:T(8,128)} %copy-done.11, bf16[4,168,512]{2,1,0:T(8,128)(2,1)} %key_pass.1.kept_ref), custom_call_target="tpu_custom_call", output_to_operand_aliasing={{}: (1, {})} | custom-call | tf_op jit(solution)/shard_map/join/pallas_call | solution.py:413
  127.0 16.1 %all_to_all.26.x_ref = bf16[4,168,512]{2,1,0:T(8,128)(2,1)} all-to-all(bf16[4,168,512]{2,1,0:T(8,128)(2,1)} %join.1), channel_id=1, replica_groups=mesh['cz'=8,'cy'=4,'fsdp'=4,'tp'=2] {'cy'}, dimensions={0} | all-to-all | bytes 1376256 | tf_op jit(solution)/shard_map/all_to_all | solution.py:447
  143.0 2.1 %unpack.1 = (bf16[144,512]{1,0:T(8,128)(2,1)}, f32[144,512]{1,0:T(8,128)}, f32[144,512]{1,0:T(8,128)}, f32[144,512]{1,0:T(8,128)}, f32[128,256]{1,0:T(8,128)}, /*index=5*/f32[3,7,256]{2,1,0:T(8,128)}) custom-call(bf16[4,168,512]{2,1,0:T(8,128)(2,1)} %all_to_all.26.x_ref), custom_call_target="tpu_custom_call" | custom-call | tf_op jit(solution)/shard_map/unpack/pallas_call | solution.py:97
  (64 shorter events, 2.3 us)
Async XLA Ops:
  3.1 4.6 %copy-start.18 = (bf16[288,512]{1,0:T(8,128)(2,1)S(1)}, bf16[288,512]{1,0:T(8,128)(2,1)}, u32[]{:S(2)}) copy-start(bf16[288,512]{1,0:T(8,128)(2,1)} %get-tuple-element.50) | copy-start | bytes 884740
  3.1 5.9 %copy-start.19 = (bf16[280,512]{1,0:T(8,128)(2,1)S(1)}, bf16[280,512]{1,0:T(8,128)(2,1)}, u32[]{:S(2)}) copy-start(bf16[280,512]{1,0:T(8,128)(2,1)} %get-tuple-element.49) | copy-start | bytes 860164
  3.1 28.0 %copy-start.15 = (f32[3,7,256]{2,1,0:T(8,128)S(1)}, f32[3,7,256]{2,1,0:T(8,128)}, u32[]{:S(2)}) copy-start(f32[3,7,256]{2,1,0:T(8,128)} %param.9) | copy-start | bytes 64516
  3.1 19.6 %all-to-all-start = ((bf16[4,144,512]{2,1,0:T(8,128)(2,1)}), bf16[4,144,512]{2,1,0:T(8,128)(2,1)S(1)}, u32[]{:S(2)}, u32[]{:S(2)}) async-start(bf16[4,144,512]{2,1,0:T(8,128)(2,1)} %get-tuple-element.48), calls=%async_computation | async-start | bytes 1179648 | tf_op jit(solution)/shard_map/all_to_all | solution.py:447
  7.7 15.0 %collective-permute-start.1 = (bf16[288,512]{1,0:T(8,128)(2,1)S(1)}, bf16[288,512]{1,0:T(8,128)(2,1)S(1)}, u32[]{:S(2)}, u32[]{:S(2)}) collective-permute-start(bf16[288,512]{1,0:T(8,128)(2,1)S(1)} %copy-done.18), channel_id=1, source_target_pairs={{8,0},{16,8},{24,16},{32,24},{40,32},{48,40},{56,48},{64,56},{72,6... | collective-permute-start | bytes 884744 | tf_op jit(solution)/shard_map/ppermute | solution.py:464
  9.0 11.3 %collective-permute-start = (bf16[280,512]{1,0:T(8,128)(2,1)S(1)}, bf16[280,512]{1,0:T(8,128)(2,1)S(1)}, u32[]{:S(2)}, u32[]{:S(2)}) collective-permute-start(bf16[280,512]{1,0:T(8,128)(2,1)S(1)} %copy-done.19), channel_id=1, source_target_pairs={{0,8},{8,16},{16,24},{24,32},{32,40},{40,48},{48,56},{56,64},{64,7... | collective-permute-start | bytes 860168 | tf_op jit(solution)/shard_map/ppermute | solution.py:463
  20.3 11.4 %copy-start.8 = (bf16[280,512]{1,0:T(8,128)(2,1)}, bf16[280,512]{1,0:T(8,128)(2,1)S(1)}, u32[]{:S(2)}) copy-start(bf16[280,512]{1,0:T(8,128)(2,1)S(1)} %collective-permute-done.prev_ref) | copy-start | bytes 860164
  22.7 9.0 %copy-start.7 = (bf16[288,512]{1,0:T(8,128)(2,1)}, bf16[288,512]{1,0:T(8,128)(2,1)S(1)}, u32[]{:S(2)}) copy-start(bf16[288,512]{1,0:T(8,128)(2,1)S(1)} %collective-permute-done.1.next_ref) | copy-start | bytes 884740
  22.7 17.7 %copy-start = (bf16[4,144,512]{2,1,0:T(8,128)(2,1)}, bf16[4,144,512]{2,1,0:T(8,128)(2,1)S(1)}, u32[]{:S(2)}) copy-start(bf16[4,144,512]{2,1,0:T(8,128)(2,1)S(1)} %all-to-all-done) | copy-start | bytes 1769476
  22.7 19.2 %collective-permute-start.3 = (bf16[576,512]{1,0:T(8,128)(2,1)S(1)}, bf16[576,512]{1,0:T(8,128)(2,1)S(1)}, u32[]{:S(2)}, u32[]{:S(2)}) collective-permute-start(bf16[576,512]{1,0:T(8,128)(2,1)S(1)} %bitcast.13), channel_id=1, source_target_pairs={{0,224},{32,0},{64,32},{96,64},{128,96},{160,128},{192,160},{224,1... | collective-permute-start | bytes 1769480 | tf_op jit(solution)/shard_map/ppermute | solution.py:470
  31.1 14.2 %collective-permute-start.2 = (bf16[576,512]{1,0:T(8,128)(2,1)S(1)}, bf16[576,512]{1,0:T(8,128)(2,1)S(1)}, u32[]{:S(2)}, u32[]{:S(2)}) collective-permute-start(bf16[576,512]{1,0:T(8,128)(2,1)S(1)} %bitcast.14), channel_id=1, source_target_pairs={{0,32},{32,64},{64,96},{96,128},{128,160},{160,192},{192,224},{224... | collective-permute-start | bytes 1769480 | tf_op jit(solution)/shard_map/ppermute | solution.py:470
  41.9 15.4 %copy-start.3 = (bf16[576,512]{1,0:T(8,128)(2,1)}, bf16[576,512]{1,0:T(8,128)(2,1)S(1)}, u32[]{:S(2)}) copy-start(bf16[576,512]{1,0:T(8,128)(2,1)S(1)} %collective-permute-done.3.refs_4_) | copy-start | bytes 1769476
  45.3 12.0 %copy-start.4 = (bf16[576,512]{1,0:T(8,128)(2,1)}, bf16[576,512]{1,0:T(8,128)(2,1)S(1)}, u32[]{:S(2)}) copy-start(bf16[576,512]{1,0:T(8,128)(2,1)S(1)} %collective-permute-done.2.refs_1_) | copy-start | bytes 1769476
  45.3 13.3 %collective-permute-start.4 = (bf16[576,512]{1,0:T(8,128)(2,1)S(1)}, bf16[576,512]{1,0:T(8,128)(2,1)S(1)}, u32[]{:S(2)}, u32[]{:S(2)}) collective-permute-start(bf16[576,512]{1,0:T(8,128)(2,1)S(1)} %collective-permute-done.2.refs_1_), channel_id=1, source_target_pairs={{0,32},{32,64},{64,96},{96,128},{128,160},{160,192},{192,224},{224... | collective-permute-start | bytes 1769480 | tf_op jit(solution)/shard_map/ppermute | solution.py:470
  45.3 13.3 %collective-permute-start.5 = (bf16[576,512]{1,0:T(8,128)(2,1)S(1)}, bf16[576,512]{1,0:T(8,128)(2,1)S(1)}, u32[]{:S(2)}, u32[]{:S(2)}) collective-permute-start(bf16[576,512]{1,0:T(8,128)(2,1)S(1)} %collective-permute-done.3.refs_4_), channel_id=1, source_target_pairs={{0,224},{32,0},{64,32},{96,64},{128,96},{160,128},{192,160},{224,1... | collective-permute-start | bytes 1769480 | tf_op jit(solution)/shard_map/ppermute | solution.py:470
  48.5 8.8 %copy-start.13 = (f32[128,128]{1,0:T(8,128)S(1)}, f32[128,128]{1,0:T(8,128)}, u32[]{:S(2)}) copy-start(f32[128,128]{1,0:T(8,128)} %get-tuple-element.74) | copy-start | bytes 196612
  58.6 3.5 %copy-start.1 = (bf16[576,512]{1,0:T(8,128)(2,1)}, bf16[576,512]{1,0:T(8,128)(2,1)S(1)}, u32[]{:S(2)}) copy-start(bf16[576,512]{1,0:T(8,128)(2,1)S(1)} %collective-permute-done.4.refs_2_) | copy-start | bytes 1769476
  58.6 3.5 %copy-start.2 = (bf16[576,512]{1,0:T(8,128)(2,1)}, bf16[576,512]{1,0:T(8,128)(2,1)S(1)}, u32[]{:S(2)}) copy-start(bf16[576,512]{1,0:T(8,128)(2,1)S(1)} %collective-permute-done.5.refs_5_) | copy-start | bytes 1769476
  58.6 3.6 %copy-start.14 = (f32[128,128]{1,0:T(8,128)S(1)}, f32[128,128]{1,0:T(8,128)}, u32[]{:S(2)}) copy-start(f32[128,128]{1,0:T(8,128)} %get-tuple-element.75) | copy-start | bytes 196612
  58.6 7.6 %collective-permute-start.7 = (bf16[576,256]{1,0:T(8,128)(2,1)S(1)}, bf16[576,256]{1,0:T(8,128)(2,1)S(1)}, u32[]{:S(2)}, u32[]{:S(2)}) collective-permute-start(bf16[576,256]{1,0:T(8,128)(2,1)S(1)} %constant_dynamic-slice_fusion), channel_id=1, source_target_pairs={{0,224},{32,0},{64,32},{96,64},{128,96},{160,128},{192,160},{224,1... | collective-permute-start | bytes 884744 | tf_op jit(solution)/shard_map/ppermute | solution.py:470
  62.1 0.7 copy-start.16
  62.1 8.0 %collective-permute-start.6 = (bf16[576,256]{1,0:T(8,128)(2,1)S(1)}, bf16[576,256]{1,0:T(8,128)(2,1)S(1)}, u32[]{:S(2)}, u32[]{:S(2)}) collective-permute-start(bf16[576,256]{1,0:T(8,128)(2,1)S(1)} %constant_dynamic-slice_fusion.1), channel_id=1, source_target_pairs={{0,32},{32,64},{64,96},{96,128},{128,160},{160,192},{192,224},{224... | collective-permute-start | bytes 884744 | tf_op jit(solution)/shard_map/ppermute | solution.py:470
  62.8 9.3 %copy-start.17 = (f32[3,8,128]{2,1,0:T(8,128)S(1)}, f32[3,8,128]{2,1,0:T(8,128)}, u32[]{:S(2)}) copy-start(f32[3,8,128]{2,1,0:T(8,128)} %get-tuple-element.77) | copy-start | bytes 36868
  66.3 13.9 %copy-start.5 = (bf16[576,256]{1,0:T(8,128)(2,1)}, bf16[576,256]{1,0:T(8,128)(2,1)S(1)}, u32[]{:S(2)}) copy-start(bf16[576,256]{1,0:T(8,128)(2,1)S(1)} %collective-permute-done.7.refs_6_) | copy-start | bytes 884740
  70.1 10.1 %copy-start.6 = (bf16[576,256]{1,0:T(8,128)(2,1)}, bf16[576,256]{1,0:T(8,128)(2,1)S(1)}, u32[]{:S(2)}) copy-start(bf16[576,256]{1,0:T(8,128)(2,1)S(1)} %collective-permute-done.6.refs_3_) | copy-start | bytes 884740
  70.1 2.0 %collective-permute-start.8 = (bf16[576,256]{1,0:T(8,128)(2,1)S(1)}, bf16[576,256]{1,0:T(8,128)(2,1)S(1)}, u32[]{:S(2)}, u32[]{:S(2)}) collective-permute-start(bf16[576,256]{1,0:T(8,128)(2,1)S(1)} %collective-permute-done.6.refs_3_), channel_id=1, source_target_pairs={{96,128},{128,160},{160,192},{192,224},{97,129},{129,161},{161,193... | collective-permute-start | bytes 884744 | tf_op jit(solution)/shard_map/ppermute | solution.py:499
  70.8 8.6 %collective-permute-start.9 = (bf16[576,256]{1,0:T(8,128)(2,1)S(1)}, bf16[576,256]{1,0:T(8,128)(2,1)S(1)}, u32[]{:S(2)}, u32[]{:S(2)}) collective-permute-start(bf16[576,256]{1,0:T(8,128)(2,1)S(1)} %collective-permute-done.7.refs_6_), channel_id=1, source_target_pairs={{32,0},{64,32},{96,64},{128,96},{33,1},{65,33},{97,65},{129,97},{3... | collective-permute-start | bytes 884744 | tf_op jit(solution)/shard_map/ppermute | solution.py:500
  72.1 13.6 %copy-start.10 = (bf16[576,256]{1,0:T(8,128)(2,1)}, bf16[576,256]{1,0:T(8,128)(2,1)S(1)}, u32[]{:S(2)}) copy-start(bf16[576,256]{1,0:T(8,128)(2,1)S(1)} %collective-permute-done.8.refs_7_) | copy-start | bytes 884740
  79.4 0.8 copy-start.9
  80.2 13.6 %all-to-all-start.1 = ((f32[32,10,128]{2,1,0:T(8,128)}), f32[32,10,128]{2,1,0:T(8,128)S(1)}, u32[]{:S(2)}, u32[]{:S(2)}) async-start(f32[32,10,128]{2,1,0:T(8,128)} %reshape.43), calls=%async_computation.1 | async-start | bytes 524288 | tf_op jit(solution)/shard_map/all_to_all | solution.py:447
  93.8 0.8 copy-start.12
  109.8 15.0 %all-to-all-start.3 = ((f32[8,10,128]{2,1,0:T(8,128)}), f32[8,10,128]{2,1,0:T(8,128)S(1)}, u32[]{:S(2)}, u32[]{:S(2)}) async-start(f32[8,10,128]{2,1,0:T(8,128)} %broadcast_in_dim.8), calls=%async_computation.3 | async-start | bytes 131072 | tf_op jit(solution)/shard_map/all_to_all | solution.py:447
  (1 other events, 0.6 us)

commit v13 on v12

--- a/solution.py
+++ b/solution.py
@@ -10,7 +10,7 @@
 ROWS = 144
 GROUP = 576
 SEQ = 4608
-CHUNK = 1536
+CHUNK = 2304
 CHUNKS = SEQ // CHUNK
 LOG2E = 1.4426950408889634
 SCALE = HD ** -0.5

time: 146 us -> 146 us (level)
  transfers between devices with their start and end apart: 13 -> 13, of which waited for: 9 -> 9; matrix products, arithmetic and copies ran while one was open for 1% -> 1% of each run, Pallas kernels for 22% -> 23%
where the time goes in v13:
time: 146 us; the launch traced here: 145 us
  Pallas kernels  39.4 us (27%)
  starting transfers between devices  37.7 us (26%)
  waiting for transfers between devices  31.1 us (21%)
  blocking collectives  30.8 us (21%)
  local copies, waits for them, and re-layouts  4.99 us (3%)
    pallas_call x2, Pallas kernels, hyena(): call(hyena_body, (struct((ROWS, 512), BF16), struct((3, ROWS, 512), F32),...  17.5 us
    all_to_all x1, blocking collectives, exchange(): return lax.all_to_all(x, axis, 0, 0, tiled=True)  16.1 us
    ppermute x6, starting transfers between devices, shift(): return lax.ppermute(x, 'cz', [(i, (i + by) % 8) for i in range(8)])  15.1 us
    all_to_all x1, blocking collectives, body(): lax.all_to_all(small, 'cz', 0, 0, tiled=True, axis_index_groups=[[7, 6, 5...  14.8 us
    all_to_all x3, starting transfers between devices, exchange(): return lax.all_to_all(x, axis, 0, 0, tiled=True)  14.8 us
    ppermute x6, waiting for transfers between devices, shift(): return lax.ppermute(x, 'cz', [(i, (i + by) % 8) for i in range(8)])  13.4 us
    pallas_call x1, Pallas kernels, key_pass(): call(key_body, struct((4, ROWS + 24, 4 * HD), BF16), 'key_pass', grid=(1,...  9.03 us
    ppermute x1, waiting for transfers between devices, body(): far_qd = lax.ppermute(falling[3], 'cz', [(i, i - 1) for i in range(1, 5)])  7.26 us
  transfers between devices with their start and end apart: 13, of which 9 were waited for; matrix products, arithmetic and copies ran while one was open for 1% of the time, Pallas kernels for 23%

profile of v13, /device:TPU:2, one launch (start us, length us, event | category | flops | bytes accessed | tf_op | source)
XLA Modules:
  0.0 145.0 jit_solution(11161474385555791856)
XLA Ops:
  0.6 2.5 %pack.1 = (bf16[4,144,512]{2,1,0:T(8,128)(2,1)}, bf16[280,512]{1,0:T(8,128)(2,1)}, bf16[288,512]{1,0:T(8,128)(2,1)}) custom-call(bf16[144,512]{1,0:T(8,128)(2,1)} %q_ref.1, bf16[144,512]{1,0:T(8,128)(2,1)} %d_ref.1, bf16[144,512]{1,0:T(8,128)(2,1)} %k_ref.1, bf16[144,512]{1,0:T(8,128)(2,1)} %v_ref.1, bf16[3,144,512]{2,1,0:T(8,128)(2,1)} %bitcast.19, ...), custom_call_target="tpu_custom_call" | custom-call | tf_op jit(solution)/shard_map/pack/pallas_call | solution.py:65
  3.1 4.6 %all-to-all-start = ((bf16[4,144,512]{2,1,0:T(8,128)(2,1)}), bf16[4,144,512]{2,1,0:T(8,128)(2,1)S(1)}, u32[]{:S(2)}, u32[]{:S(2)}) async-start(bf16[4,144,512]{2,1,0:T(8,128)(2,1)} %get-tuple-element.48), calls=%async_computation | async-start | bytes 1179648 | tf_op jit(solution)/shard_map/all_to_all | solution.py:447
  7.7 1.3 collective-permute-start.1
  9.0 4.6 %collective-permute-start = (bf16[280,512]{1,0:T(8,128)(2,1)S(1)}, bf16[280,512]{1,0:T(8,128)(2,1)S(1)}, u32[]{:S(2)}, u32[]{:S(2)}) collective-permute-start(bf16[280,512]{1,0:T(8,128)(2,1)S(1)} %copy-done.19), channel_id=1, source_target_pairs={{0,8},{8,16},{16,24},{24,32},{32,40},{40,48},{48,56},{56,64},{64,7... | collective-permute-start | bytes 860168 | tf_op jit(solution)/shard_map/ppermute | solution.py:463
  13.6 6.7 %collective-permute-done.prev_ref = bf16[280,512]{1,0:T(8,128)(2,1)S(1)} collective-permute-done((bf16[280,512]{1,0:T(8,128)(2,1)S(1)}, bf16[280,512]{1,0:T(8,128)(2,1)S(1)}, u32[]{:S(2)}, u32[]{:S(2)}) %collective-permute-start) | collective-permute-done | bytes 286752 | tf_op jit(solution)/shard_map/ppermute | solution.py:463
  20.3 2.4 %collective-permute-done.1.next_ref = bf16[288,512]{1,0:T(8,128)(2,1)S(1)} collective-permute-done((bf16[288,512]{1,0:T(8,128)(2,1)S(1)}, bf16[288,512]{1,0:T(8,128)(2,1)S(1)}, u32[]{:S(2)}, u32[]{:S(2)}) %collective-permute-start.1) | collective-permute-done | bytes 294944 | tf_op jit(solution)/shard_map/ppermute | solution.py:464
  22.7 8.4 %collective-permute-start.3 = (bf16[576,512]{1,0:T(8,128)(2,1)S(1)}, bf16[576,512]{1,0:T(8,128)(2,1)S(1)}, u32[]{:S(2)}, u32[]{:S(2)}) collective-permute-start(bf16[576,512]{1,0:T(8,128)(2,1)S(1)} %bitcast.13), channel_id=1, source_target_pairs={{0,224},{32,0},{64,32},{96,64},{128,96},{160,128},{192,160},{224,1... | collective-permute-start | bytes 1769480 | tf_op jit(solution)/shard_map/ppermute | solution.py:470
  31.7 8.7 %hyena.2 = (bf16[144,512]{1,0:T(8,128)(2,1)}, f32[3,144,512]{2,1,0:T(8,128)}, f32[128,128]{1,0:T(8,128)}, f32[3,8,128]{2,1,0:T(8,128)}) custom-call(bf16[3,144,512]{2,1,0:T(8,128)(2,1)} %bitcast.20, bf16[280,512]{1,0:T(8,128)(2,1)} %copy-done.8, bf16[288,512]{1,0:T(8,128)(2,1)} %copy-done.7, bf16[144,512]{1,0:T(8,128)(2,1)} %up_ref.5, ...), custom_call_target="tpu_custom_call" | custom-call | tf_op jit(solution)/shard_map/hyena/pallas_call | solution.py:205
  40.4 1.4 collective-permute-done.3.refs_4_
  41.9 3.4 %collective-permute-done.2.refs_1_ = bf16[576,512]{1,0:T(8,128)(2,1)S(1)} collective-permute-done((bf16[576,512]{1,0:T(8,128)(2,1)S(1)}, bf16[576,512]{1,0:T(8,128)(2,1)S(1)}, u32[]{:S(2)}, u32[]{:S(2)}) %collective-permute-start.2) | collective-permute-done | bytes 589856 | tf_op jit(solution)/shard_map/ppermute | solution.py:470
  45.3 3.2 %collective-permute-start.5 = (bf16[576,512]{1,0:T(8,128)(2,1)S(1)}, bf16[576,512]{1,0:T(8,128)(2,1)S(1)}, u32[]{:S(2)}, u32[]{:S(2)}) collective-permute-start(bf16[576,512]{1,0:T(8,128)(2,1)S(1)} %collective-permute-done.3.refs_4_), channel_id=1, source_target_pairs={{0,224},{32,0},{64,32},{96,64},{128,96},{160,128},{192,160},{224,1... | collective-permute-start | bytes 1769480 | tf_op jit(solution)/shard_map/ppermute | solution.py:470
  48.5 8.8 %hyena.3 = (bf16[144,512]{1,0:T(8,128)(2,1)}, f32[3,144,512]{2,1,0:T(8,128)}, f32[128,128]{1,0:T(8,128)}, f32[3,8,128]{2,1,0:T(8,128)}) custom-call(bf16[3,144,512]{2,1,0:T(8,128)(2,1)} %bitcast.21, bf16[280,512]{1,0:T(8,128)(2,1)} %copy-done.8, bf16[288,512]{1,0:T(8,128)(2,1)} %copy-done.7, ...), custom_call_target="tpu_custom_call", output_to_operand_aliasing={{0}: (6, {}), {1}: (7, {})} | custom-call | tf_op jit(solution)/shard_map/hyena/pallas_call | solution.py:205
  57.3 1.2 collective-permute-done.4.refs_2_
  58.6 3.4 %collective-permute-start.7 = (bf16[576,256]{1,0:T(8,128)(2,1)S(1)}, bf16[576,256]{1,0:T(8,128)(2,1)S(1)}, u32[]{:S(2)}, u32[]{:S(2)}) collective-permute-start(bf16[576,256]{1,0:T(8,128)(2,1)S(1)} %constant_dynamic-slice_fusion), channel_id=1, source_target_pairs={{0,224},{32,0},{64,32},{96,64},{128,96},{160,128},{192,160},{224,1... | collective-permute-start | bytes 884744 | tf_op jit(solution)/shard_map/ppermute | solution.py:470
  62.8 3.5 %collective-permute-done.7.refs_6_ = bf16[576,256]{1,0:T(8,128)(2,1)S(1)} collective-permute-done((bf16[576,256]{1,0:T(8,128)(2,1)S(1)}, bf16[576,256]{1,0:T(8,128)(2,1)S(1)}, u32[]{:S(2)}, u32[]{:S(2)}) %collective-permute-start.7) | collective-permute-done | bytes 294944 | tf_op jit(solution)/shard_map/ppermute | solution.py:470
  66.3 3.8 %collective-permute-done.6.refs_3_ = bf16[576,256]{1,0:T(8,128)(2,1)S(1)} collective-permute-done((bf16[576,256]{1,0:T(8,128)(2,1)S(1)}, bf16[576,256]{1,0:T(8,128)(2,1)S(1)}, u32[]{:S(2)}, u32[]{:S(2)}) %collective-permute-start.6) | collective-permute-done | bytes 294944 | tf_op jit(solution)/shard_map/ppermute | solution.py:470
  70.1 0.7 collective-permute-start.8
  70.8 1.3 collective-permute-start.9
  72.1 7.3 %collective-permute-done.9.refs_7_ = bf16[576,256]{1,0:T(8,128)(2,1)S(1)} collective-permute-done((bf16[576,256]{1,0:T(8,128)(2,1)S(1)}, bf16[576,256]{1,0:T(8,128)(2,1)S(1)}, u32[]{:S(2)}, u32[]{:S(2)}) %collective-permute-start.9) | collective-permute-done | bytes 294944 | tf_op jit(solution)/shard_map/ppermute | solution.py:500
  79.4 0.8 reshape.43
  80.2 5.5 %all-to-all-start.1 = ((f32[32,10,128]{2,1,0:T(8,128)}), f32[32,10,128]{2,1,0:T(8,128)S(1)}, u32[]{:S(2)}, u32[]{:S(2)}) async-start(f32[32,10,128]{2,1,0:T(8,128)} %reshape.43), calls=%async_computation.1 | async-start | bytes 524288 | tf_op jit(solution)/shard_map/all_to_all | solution.py:447
  85.7 6.8 %query_pass.1 = (bf16[576,256]{1,0:T(8,128)(2,1)}, f32[8,10,128]{2,1,0:T(8,128)}) custom-call(s32[1]{0:T(128)} %bitcast.2.where_ref, bf16[576,512]{1,0:T(8,128)(2,1)} %bitcast.15, bf16[576,512]{1,0:T(8,128)(2,1)} %bitcast.16, bf16[576,512]{1,0:T(8,128)(2,1)} %copy-done.4, bf16[576,512]{1,0:T(8,128)(2,1)} %copy-done.1, bf16[576,256]{1,0:T(8,128)(2,1)} %copy-done.6, ...), custom_call_target="tpu_custom_call" | custom-call | tf_op jit(solution)/shard_map/query_pass/pallas_call | solution.py:342
  92.5 1.3 all-to-all-done.1
  93.9 0.8 copy-done.12
  94.7 14.8 %all_to_all.25 = f32[8,20,128]{2,1,0:T(8,128)S(1)} all-to-all(f32[8,20,128]{2,1,0:T(8,128)S(1)} %pad_maximum_fusion), channel_id=1, replica_groups={{224,192,160,128,96,64,32,0},{225,193,161,129,97,65,33,1},{226,194,162,..., dimensions={0} | all-to-all | bytes 163840 | tf_op jit(solution)/shard_map/all_to_all | solution.py:508
  109.6 0.6 broadcast_in_dim.8
  110.2 4.7 %all-to-all-start.3 = ((f32[8,10,128]{2,1,0:T(8,128)}), f32[8,10,128]{2,1,0:T(8,128)S(1)}, u32[]{:S(2)}, u32[]{:S(2)}) async-start(f32[8,10,128]{2,1,0:T(8,128)} %broadcast_in_dim.8), calls=%async_computation.3 | async-start | bytes 131072 | tf_op jit(solution)/shard_map/all_to_all | solution.py:447
  115.0 0.6 copy.22
  115.6 9.0 %key_pass.1.kept_ref = bf16[4,168,512]{2,1,0:T(8,128)(2,1)} custom-call(s32[1]{0:T(128)} %bitcast.2.where_ref, bf16[576,512]{1,0:T(8,128)(2,1)} %bitcast.17, f32[2,2,2304]{2,1,0:T(2,128)} %bitcast.23, bf16[576,256]{1,0:T(8,128)(2,1)} %get-tuple-element.79.oq_ref, bf16[576,512]{1,0:T(8,128)(2,1)} %bitcast.18, bf16[576,512]{1,0:T(8,128)(2,1)} %copy-done.4, ...), custom_call_target="tpu_custom_call" | custom-call | tf_op jit(solution)/shard_map/key_pass/pallas_call | solution.py:429
  125.3 1.5 %join.1 = bf16[4,168,512]{2,1,0:T(8,128)(2,1)} custom-call(f32[8,10,128]{2,1,0:T(8,128)} %copy-done.11, bf16[4,168,512]{2,1,0:T(8,128)(2,1)} %key_pass.1.kept_ref), custom_call_target="tpu_custom_call", output_to_operand_aliasing={{}: (1, {})} | custom-call | tf_op jit(solution)/shard_map/join/pallas_call | solution.py:413
  126.8 16.1 %all_to_all.26.x_ref = bf16[4,168,512]{2,1,0:T(8,128)(2,1)} all-to-all(bf16[4,168,512]{2,1,0:T(8,128)(2,1)} %join.1), channel_id=1, replica_groups=mesh['cz'=8,'cy'=4,'fsdp'=4,'tp'=2] {'cy'}, dimensions={0} | all-to-all | bytes 1376256 | tf_op jit(solution)/shard_map/all_to_all | solution.py:447
  142.9 2.1 %unpack.1 = (bf16[144,512]{1,0:T(8,128)(2,1)}, f32[144,512]{1,0:T(8,128)}, f32[144,512]{1,0:T(8,128)}, f32[144,512]{1,0:T(8,128)}, f32[128,256]{1,0:T(8,128)}, /*index=5*/f32[3,7,256]{2,1,0:T(8,128)}) custom-call(bf16[4,168,512]{2,1,0:T(8,128)(2,1)} %all_to_all.26.x_ref), custom_call_target="tpu_custom_call" | custom-call | tf_op jit(solution)/shard_map/unpack/pallas_call | solution.py:97
  (64 shorter events, 2.3 us)
Async XLA Ops:
  3.1 4.6 %copy-start.18 = (bf16[288,512]{1,0:T(8,128)(2,1)S(1)}, bf16[288,512]{1,0:T(8,128)(2,1)}, u32[]{:S(2)}) copy-start(bf16[288,512]{1,0:T(8,128)(2,1)} %get-tuple-element.50) | copy-start | bytes 884740
  3.1 5.9 %copy-start.19 = (bf16[280,512]{1,0:T(8,128)(2,1)S(1)}, bf16[280,512]{1,0:T(8,128)(2,1)}, u32[]{:S(2)}) copy-start(bf16[280,512]{1,0:T(8,128)(2,1)} %get-tuple-element.49) | copy-start | bytes 860164
  3.1 28.0 %copy-start.15 = (f32[3,7,256]{2,1,0:T(8,128)S(1)}, f32[3,7,256]{2,1,0:T(8,128)}, u32[]{:S(2)}) copy-start(f32[3,7,256]{2,1,0:T(8,128)} %param.9) | copy-start | bytes 64516
  3.1 19.6 %all-to-all-start = ((bf16[4,144,512]{2,1,0:T(8,128)(2,1)}), bf16[4,144,512]{2,1,0:T(8,128)(2,1)S(1)}, u32[]{:S(2)}, u32[]{:S(2)}) async-start(bf16[4,144,512]{2,1,0:T(8,128)(2,1)} %get-tuple-element.48), calls=%async_computation | async-start | bytes 1179648 | tf_op jit(solution)/shard_map/all_to_all | solution.py:447
  7.7 15.0 %collective-permute-start.1 = (bf16[288,512]{1,0:T(8,128)(2,1)S(1)}, bf16[288,512]{1,0:T(8,128)(2,1)S(1)}, u32[]{:S(2)}, u32[]{:S(2)}) collective-permute-start(bf16[288,512]{1,0:T(8,128)(2,1)S(1)} %copy-done.18), channel_id=1, source_target_pairs={{8,0},{16,8},{24,16},{32,24},{40,32},{48,40},{56,48},{64,56},{72,6... | collective-permute-start | bytes 884744 | tf_op jit(solution)/shard_map/ppermute | solution.py:464
  9.0 11.3 %collective-permute-start = (bf16[280,512]{1,0:T(8,128)(2,1)S(1)}, bf16[280,512]{1,0:T(8,128)(2,1)S(1)}, u32[]{:S(2)}, u32[]{:S(2)}) collective-permute-start(bf16[280,512]{1,0:T(8,128)(2,1)S(1)} %copy-done.19), channel_id=1, source_target_pairs={{0,8},{8,16},{16,24},{24,32},{32,40},{40,48},{48,56},{56,64},{64,7... | collective-permute-start | bytes 860168 | tf_op jit(solution)/shard_map/ppermute | solution.py:463
  20.3 11.4 %copy-start.8 = (bf16[280,512]{1,0:T(8,128)(2,1)}, bf16[280,512]{1,0:T(8,128)(2,1)S(1)}, u32[]{:S(2)}) copy-start(bf16[280,512]{1,0:T(8,128)(2,1)S(1)} %collective-permute-done.prev_ref) | copy-start | bytes 860164
  22.7 9.0 %copy-start.7 = (bf16[288,512]{1,0:T(8,128)(2,1)}, bf16[288,512]{1,0:T(8,128)(2,1)S(1)}, u32[]{:S(2)}) copy-start(bf16[288,512]{1,0:T(8,128)(2,1)S(1)} %collective-permute-done.1.next_ref) | copy-start | bytes 884740
  22.7 17.7 %copy-start = (bf16[4,144,512]{2,1,0:T(8,128)(2,1)}, bf16[4,144,512]{2,1,0:T(8,128)(2,1)S(1)}, u32[]{:S(2)}) copy-start(bf16[4,144,512]{2,1,0:T(8,128)(2,1)S(1)} %all-to-all-done) | copy-start | bytes 1769476
  22.7 19.2 %collective-permute-start.3 = (bf16[576,512]{1,0:T(8,128)(2,1)S(1)}, bf16[576,512]{1,0:T(8,128)(2,1)S(1)}, u32[]{:S(2)}, u32[]{:S(2)}) collective-permute-start(bf16[576,512]{1,0:T(8,128)(2,1)S(1)} %bitcast.13), channel_id=1, source_target_pairs={{0,224},{32,0},{64,32},{96,64},{128,96},{160,128},{192,160},{224,1... | collective-permute-start | bytes 1769480 | tf_op jit(solution)/shard_map/ppermute | solution.py:470
  31.1 14.2 %collective-permute-start.2 = (bf16[576,512]{1,0:T(8,128)(2,1)S(1)}, bf16[576,512]{1,0:T(8,128)(2,1)S(1)}, u32[]{:S(2)}, u32[]{:S(2)}) collective-permute-start(bf16[576,512]{1,0:T(8,128)(2,1)S(1)} %bitcast.14), channel_id=1, source_target_pairs={{0,32},{32,64},{64,96},{96,128},{128,160},{160,192},{192,224},{224... | collective-permute-start | bytes 1769480 | tf_op jit(solution)/shard_map/ppermute | solution.py:470
  41.9 15.4 %copy-start.3 = (bf16[576,512]{1,0:T(8,128)(2,1)}, bf16[576,512]{1,0:T(8,128)(2,1)S(1)}, u32[]{:S(2)}) copy-start(bf16[576,512]{1,0:T(8,128)(2,1)S(1)} %collective-permute-done.3.refs_4_) | copy-start | bytes 1769476
  45.3 12.0 %copy-start.4 = (bf16[576,512]{1,0:T(8,128)(2,1)}, bf16[576,512]{1,0:T(8,128)(2,1)S(1)}, u32[]{:S(2)}) copy-start(bf16[576,512]{1,0:T(8,128)(2,1)S(1)} %collective-permute-done.2.refs_1_) | copy-start | bytes 1769476
  45.3 13.3 %collective-permute-start.4 = (bf16[576,512]{1,0:T(8,128)(2,1)S(1)}, bf16[576,512]{1,0:T(8,128)(2,1)S(1)}, u32[]{:S(2)}, u32[]{:S(2)}) collective-permute-start(bf16[576,512]{1,0:T(8,128)(2,1)S(1)} %collective-permute-done.2.refs_1_), channel_id=1, source_target_pairs={{0,32},{32,64},{64,96},{96,128},{128,160},{160,192},{192,224},{224... | collective-permute-start | bytes 1769480 | tf_op jit(solution)/shard_map/ppermute | solution.py:470
  45.3 13.3 %collective-permute-start.5 = (bf16[576,512]{1,0:T(8,128)(2,1)S(1)}, bf16[576,512]{1,0:T(8,128)(2,1)S(1)}, u32[]{:S(2)}, u32[]{:S(2)}) collective-permute-start(bf16[576,512]{1,0:T(8,128)(2,1)S(1)} %collective-permute-done.3.refs_4_), channel_id=1, source_target_pairs={{0,224},{32,0},{64,32},{96,64},{128,96},{160,128},{192,160},{224,1... | collective-permute-start | bytes 1769480 | tf_op jit(solution)/shard_map/ppermute | solution.py:470
  48.5 8.8 %copy-start.13 = (f32[128,128]{1,0:T(8,128)S(1)}, f32[128,128]{1,0:T(8,128)}, u32[]{:S(2)}) copy-start(f32[128,128]{1,0:T(8,128)} %get-tuple-element.74) | copy-start | bytes 196612
  58.6 3.5 %copy-start.1 = (bf16[576,512]{1,0:T(8,128)(2,1)}, bf16[576,512]{1,0:T(8,128)(2,1)S(1)}, u32[]{:S(2)}) copy-start(bf16[576,512]{1,0:T(8,128)(2,1)S(1)} %collective-permute-done.4.refs_2_) | copy-start | bytes 1769476
  58.6 3.5 %copy-start.2 = (bf16[576,512]{1,0:T(8,128)(2,1)}, bf16[576,512]{1,0:T(8,128)(2,1)S(1)}, u32[]{:S(2)}) copy-start(bf16[576,512]{1,0:T(8,128)(2,1)S(1)} %collective-permute-done.5.refs_5_) | copy-start | bytes 1769476
  58.6 3.6 %copy-start.14 = (f32[128,128]{1,0:T(8,128)S(1)}, f32[128,128]{1,0:T(8,128)}, u32[]{:S(2)}) copy-start(f32[128,128]{1,0:T(8,128)} %get-tuple-element.75) | copy-start | bytes 196612
  58.6 7.6 %collective-permute-start.7 = (bf16[576,256]{1,0:T(8,128)(2,1)S(1)}, bf16[576,256]{1,0:T(8,128)(2,1)S(1)}, u32[]{:S(2)}, u32[]{:S(2)}) collective-permute-start(bf16[576,256]{1,0:T(8,128)(2,1)S(1)} %constant_dynamic-slice_fusion), channel_id=1, source_target_pairs={{0,224},{32,0},{64,32},{96,64},{128,96},{160,128},{192,160},{224,1... | collective-permute-start | bytes 884744 | tf_op jit(solution)/shard_map/ppermute | solution.py:470
  62.1 0.7 copy-start.16
  62.1 8.0 %collective-permute-start.6 = (bf16[576,256]{1,0:T(8,128)(2,1)S(1)}, bf16[576,256]{1,0:T(8,128)(2,1)S(1)}, u32[]{:S(2)}, u32[]{:S(2)}) collective-permute-start(bf16[576,256]{1,0:T(8,128)(2,1)S(1)} %constant_dynamic-slice_fusion.1), channel_id=1, source_target_pairs={{0,32},{32,64},{64,96},{96,128},{128,160},{160,192},{192,224},{224... | collective-permute-start | bytes 884744 | tf_op jit(solution)/shard_map/ppermute | solution.py:470
  62.8 9.3 %copy-start.17 = (f32[3,8,128]{2,1,0:T(8,128)S(1)}, f32[3,8,128]{2,1,0:T(8,128)}, u32[]{:S(2)}) copy-start(f32[3,8,128]{2,1,0:T(8,128)} %get-tuple-element.77) | copy-start | bytes 36868
  66.3 13.9 %copy-start.5 = (bf16[576,256]{1,0:T(8,128)(2,1)}, bf16[576,256]{1,0:T(8,128)(2,1)S(1)}, u32[]{:S(2)}) copy-start(bf16[576,256]{1,0:T(8,128)(2,1)S(1)} %collective-permute-done.7.refs_6_) | copy-start | bytes 884740
  70.1 10.1 %copy-start.6 = (bf16[576,256]{1,0:T(8,128)(2,1)}, bf16[576,256]{1,0:T(8,128)(2,1)S(1)}, u32[]{:S(2)}) copy-start(bf16[576,256]{1,0:T(8,128)(2,1)S(1)} %collective-permute-done.6.refs_3_) | copy-start | bytes 884740
  70.1 2.0 %collective-permute-start.8 = (bf16[576,256]{1,0:T(8,128)(2,1)S(1)}, bf16[576,256]{1,0:T(8,128)(2,1)S(1)}, u32[]{:S(2)}, u32[]{:S(2)}) collective-permute-start(bf16[576,256]{1,0:T(8,128)(2,1)S(1)} %collective-permute-done.6.refs_3_), channel_id=1, source_target_pairs={{96,128},{128,160},{160,192},{192,224},{97,129},{129,161},{161,193... | collective-permute-start | bytes 884744 | tf_op jit(solution)/shard_map/ppermute | solution.py:499
  70.8 8.6 %collective-permute-start.9 = (bf16[576,256]{1,0:T(8,128)(2,1)S(1)}, bf16[576,256]{1,0:T(8,128)(2,1)S(1)}, u32[]{:S(2)}, u32[]{:S(2)}) collective-permute-start(bf16[576,256]{1,0:T(8,128)(2,1)S(1)} %collective-permute-done.7.refs_6_), channel_id=1, source_target_pairs={{32,0},{64,32},{96,64},{128,96},{33,1},{65,33},{97,65},{129,97},{3... | collective-permute-start | bytes 884744 | tf_op jit(solution)/shard_map/ppermute | solution.py:500
  72.1 13.6 %copy-start.10 = (bf16[576,256]{1,0:T(8,128)(2,1)}, bf16[576,256]{1,0:T(8,128)(2,1)S(1)}, u32[]{:S(2)}) copy-start(bf16[576,256]{1,0:T(8,128)(2,1)S(1)} %collective-permute-done.8.refs_7_) | copy-start | bytes 884740
  79.4 0.8 copy-start.9
  80.2 13.6 %all-to-all-start.1 = ((f32[32,10,128]{2,1,0:T(8,128)}), f32[32,10,128]{2,1,0:T(8,128)S(1)}, u32[]{:S(2)}, u32[]{:S(2)}) async-start(f32[32,10,128]{2,1,0:T(8,128)} %reshape.43), calls=%async_computation.1 | async-start | bytes 524288 | tf_op jit(solution)/shard_map/all_to_all | solution.py:447
  93.8 0.8 copy-start.12
  110.2 14.5 %all-to-all-start.3 = ((f32[8,10,128]{2,1,0:T(8,128)}), f32[8,10,128]{2,1,0:T(8,128)S(1)}, u32[]{:S(2)}, u32[]{:S(2)}) async-start(f32[8,10,128]{2,1,0:T(8,128)} %broadcast_in_dim.8), calls=%async_computation.3 | async-start | bytes 131072 | tf_op jit(solution)/shard_map/all_to_all | solution.py:447
  (1 other events, 0.6 us)
